TPU v7x, 32 devices: a whole 2x2x4 slice. The times are simulated.
32 devices in a mesh: gx: 4 (over y, x), gy: 8 (over z, core).
Axes of the slice: x: 2, y: 2, z: 4, core: 2. Of those that a mesh axis runs over, the one named last changes fastest.
Arguments:
- grid_scalars: float32 [54, 8, 16, 128], P(None, 'gx', 'gy'), may hold values from -6 to 6
- axial_speed: float32 [8, 16, 128], P('gx', 'gy'), may hold values from 0.1 to 0.4
- particles: float32 [54, 32, 16384], P(None, None, ('gx', 'gy')), may hold values from -6 to 6
- cell_owner: int32 [8, 16, 128], P('gx', 'gy'), may hold values from 0 to 7, as said below
- cell_slot: int32 [8, 16, 128], P('gx', 'gy'), may hold values from 0 to 511, as said below
- mix_rate: float32 [16384], P(('gx', 'gy')), may hold values from 0.2 to 0.6
- partner: int32 [32, 16384], P(None, ('gx', 'gy')), may hold values from 0 to 31, as said below
- chem_input: bfloat16 [256, 54], replicated, may hold values from -0.875 to 0.875
- chem_hidden: bfloat16 [256, 256], replicated, may hold values from -0.375 to 0.375
- chem_output: bfloat16 [54, 256], replicated, may hold values from -0.375 to 0.375
- react_slots: int32 [32, 256], P(('gx', 'gy')), may hold values from 0 to 511, as said below
- react_count: int32 [32], P(('gx', 'gy')), may hold values from 1 to 256, as said below
- leave_slots: int32 [32, 64], P(('gx', 'gy')), may hold values from 0 to 512, as said below
- arrive_slots: int32 [32, 64], P(('gx', 'gy')), may hold values from 0 to 512, as said below
Outputs:
- grid_out: float32 [54, 8, 16, 128], P(None, 'gx', 'gy')
- particles_out: float32 [54, 32, 16384], P(None, None, ('gx', 'gy'))
Inputs may be any that keep to these rules, and one draw needn't show every extreme that they name: `cell_owner`: within each gx index, each of the 8 owners holds exactly 512 cells of that gx index's grid boxes, each slot once; from one grid box to one owner go at most 96 cells, and exactly 96 for some pairs in every draw. `cell_slot`: slots as described for cell_owner. In each cell partner pairs the 32 particles: partner of partner is the particle itself, never itself. `react_slots`: distinct slots in each owner's row. `react_count`: some owner has 256 live entries in every draw. `leave_slots`: every device hands one or 2 cells to every device, 2 to some; the value 512 marks an empty place; the leaving slots of a device are distinct and are exactly the slots that arriving cells take there. `arrive_slots`: as for leave_slots.
All inputs are finite; a program needn't handle non-finite values.
Results may differ from a plain program's by a relative error of at most 0.0013.
Values sent between devices are 32-bit elements; how exact they have to be, the bound alone decides.
No kernel may reach another device: no remote copies, remote signals or barrier semaphores. Data moves between devices by JAX's collectives and lax.ppermute only.
A program may use at most 128 MiB of HBM per device.

v0:
```python
import jax
import jax.numpy as jnp
from jax import lax
from jax.sharding import PartitionSpec as P

SUBSTEPS = 2


DIFFUSION = 0.1
PAIR_WEIGHT = 0.4


def with_halo(cells, sides, width):
    for axis, dim in sides:
        count = lax.axis_size(axis)
        ends = count - 1
        head = lax.slice_in_dim(cells, 0, width, axis=dim)
        tail = lax.slice_in_dim(cells, cells.shape[dim] - width, cells.shape[dim], axis=dim)
        cells = jnp.concatenate(
            [
                lax.ppermute(tail, axis, [(i, (i + 1) % count) for i in range(ends)]),
                cells,
                lax.ppermute(head, axis, [((i + 1) % count, i) for i in range(ends)]),
            ],
            axis=dim,
        )
    return cells


def advance(padded, axial_speed):
    center = padded[:, 1:-1, 1:-1, :]
    upstream = padded[:, :-2, 1:-1, :]
    beside = upstream + padded[:, 2:, 1:-1, :]
    beside = beside + padded[:, 1:-1, :-2, :] + padded[:, 1:-1, 2:, :]
    beside = beside + jnp.roll(center, 1, axis=3) + jnp.roll(center, -1, axis=3)
    return center + DIFFUSION * (beside - 6.0 * center) - axial_speed[None] * (center - upstream)


def particle_section(
    state,
    filtered,
    relaxation,
    partner,
    chem_input,
    chem_hidden,
    chem_output,
    chosen_slots,
    live_count,
):
    state = state + relaxation[None, None, :] * (filtered[:, None, :] - state)
    partner_state = jnp.take_along_axis(state, partner[None, :, :], axis=1)
    state = state + PAIR_WEIGHT * (partner_state - state)
    chosen = jnp.take(state, chosen_slots, axis=2)
    feed_rows = chosen.reshape(chosen.shape[0], -1).astype(jnp.bfloat16)
    layer_one = jax.nn.silu(
        jnp.dot(chem_input, feed_rows, preferred_element_type=jnp.float32)
    ).astype(jnp.bfloat16)
    layer_two = jax.nn.silu(
        jnp.dot(chem_hidden, layer_one, preferred_element_type=jnp.float32)
    ).astype(jnp.bfloat16)
    change = jnp.dot(chem_output, layer_two, preferred_element_type=jnp.float32).astype(
        jnp.bfloat16
    )
    change = change.reshape(chosen.shape).astype(jnp.float32)
    active = jnp.arange(chosen_slots.shape[0], dtype=jnp.int32) < live_count
    change = jnp.where(active[None, None, :], change, jnp.zeros_like(change))
    state = state.at[:, :, chosen_slots].add(change)
    source = (
        jnp.zeros(filtered.shape, filtered.dtype).at[:, chosen_slots].set(jnp.mean(change, axis=1))
    )
    return (state, source)


def per_device(
    grid_scalars,
    axial_speed,
    particles,
    cell_owner,
    cell_slot,
    mix_rate,
    partner,
    chem_input,
    chem_hidden,
    chem_output,
    react_slots,
    react_count,
    leave_slots,
    arrive_slots,
):
    scalar_count = grid_scalars.shape[0]
    cell_count = cell_owner.size
    lane_count = lax.axis_size("gy")
    owners_here = cell_owner.reshape(-1)
    slots_here = cell_slot.reshape(-1)
    capacity = 3 * (cell_count // lane_count) // 2
    onehot = (owners_here[:, None] == jnp.arange(lane_count, dtype=jnp.int32)[None, :]).astype(
        jnp.int32
    )
    ranking = jnp.sum(jnp.cumsum(onehot, axis=0) * onehot, axis=1) - 1
    places = owners_here * capacity + ranking
    source_cell = (
        jnp.full((lane_count * capacity,), cell_count, jnp.int32)
        .at[places]
        .set(jnp.arange(cell_count, dtype=jnp.int32))
    )
    labels = (
        jnp.full((1, lane_count * capacity), cell_count, jnp.int32).at[0, places].set(slots_here)
    )
    grid = grid_scalars
    state = particles
    for substep in range(SUBSTEPS):
        padded = with_halo(grid, (("gx", 1), ("gy", 2)), 1)
        grid = advance(padded, axial_speed)
        flattened = grid.reshape(scalar_count, cell_count)
        outgoing = jnp.take(flattened, source_cell, axis=1, mode="fill", fill_value=0.0)
        arrived, arrived_slots = (
            lax.all_to_all(outgoing, "gy", split_axis=1, concat_axis=1, tiled=True),
            lax.all_to_all(labels, "gy", split_axis=1, concat_axis=1, tiled=True),
        )
        landed = arrived_slots[0]
        filtered = (
            jnp.zeros((scalar_count, cell_count), jnp.float32)
            .at[:, landed]
            .set(arrived, mode="drop")
        )
        state, source = particle_section(
            state,
            filtered,
            mix_rate,
            partner,
            chem_input,
            chem_hidden,
            chem_output,
            react_slots[0],
            react_count[0],
        )
        returned = jnp.take(source, landed, axis=1, mode="fill", fill_value=0.0)
        homeward = lax.all_to_all(returned, "gy", split_axis=1, concat_axis=1, tiled=True)
        feedback = jnp.take(homeward, places, axis=1)
        grid = grid + feedback.reshape(grid.shape)
    flat_parts = state.reshape(scalar_count * state.shape[1], cell_count)
    outgoing_cells = jnp.take(flat_parts, leave_slots[0], axis=1, mode="fill", fill_value=0.0)
    arrived_cells = lax.all_to_all(
        outgoing_cells, ("gx", "gy"), split_axis=1, concat_axis=1, tiled=True
    )
    relocated = flat_parts.at[:, arrive_slots[0]].set(arrived_cells, mode="drop")
    return (grid, relocated.reshape(state.shape))


def solution(mesh):
    placed = (
        P(None, "gx", "gy", None),
        P("gx", "gy", None),
        P(None, None, ("gx", "gy")),
        P("gx", "gy", None),
        P("gx", "gy", None),
        P(("gx", "gy")),
        P(None, ("gx", "gy")),
        P(),
        P(),
        P(),
        P(("gx", "gy"), None),
        P(("gx", "gy")),
        P(("gx", "gy"), None),
        P(("gx", "gy"), None),
    )
    return jax.shard_map(
        per_device,
        mesh=mesh,
        in_specs=placed,
        out_specs=(P(None, "gx", "gy", None), P(None, None, ("gx", "gy"))),
        check_vma=False,
    )
```

profile of v0, /device:TPU:0, one launch (start us, length us, event | category | flops | bytes accessed | tf_op | source)
XLA Modules:
  0.0 838.3 jit_solution(8870852533243840656)
XLA Ops:
  1.5 4.9 collective-permute-start
  11.3 2.6 scatter_custom_fusion
  14.5 4.9 all-to-all-start
  33.1 3.0 collective-permute-start.2
  41.4 8.1 all-to-all-start.1
  50.1 8.4 %all-to-all-done.1 = f32[54,8,96]{2,0,1:T(8,128)S(1)} async-done(((f32[54,8,96]{2,0,1:T(8,128)}), f32[54,8,96]{2,0,1:T(8,128)S(1)}, u32[]{:S(2)}, u32[]{:S(2)}) %all-to-all-start.1) | async-done | bytes 165920 | tf_op jit(solution)/shard_map/all_to_all | solution.py:117
  58.9 4.5 scatter_custom_fusion.2
  63.5 4.6 multiply_add_fusion.1
  68.1 6.8 copy.128
  74.9 236.8 %gather_fusion.2 = f32[16384,54]{1,0:T(8,128)} fusion(f32[54,32,512]{0,2,1:T(8,128)} %copy.128, s32[16384]{0:T(1024)S(1)} %bitcast.152), kind=kCustom, calls=%fused_computation.1.clone | custom fusion | bytes 7208960 | tf_op jit(solution)/shard_map/jit(take_along_axis)/gather | solution.py:51
  311.7 7.1 copy.157
  318.9 6.2 fusion.5
  325.1 9.1 %copy.130 = f32[54,32,512]{0,1,2:T(8,128)} copy(f32[54,32,512]{2,1,0:T(8,128)} %fusion.5) | data formatting | bytes 7077888 | tf_op jit(solution)/shard_map/add | solution.py:52
  334.1 4.4 gather_fusion.3
  341.9 4.0 multiply_convert_fusion.3
  346.0 4.4 fusion
  351.1 4.5 copy.132
  355.7 4.9 select_bitcast_fusion.1
  364.4 3.4 all-to-all-start.2
  367.8 8.9 %all-to-all-done.2 = f32[54,8,96]{2,0,1:T(8,128)S(1)} async-done(((f32[54,8,96]{2,0,1:T(8,128)}), f32[54,8,96]{2,0,1:T(8,128)S(1)}, u32[]{:S(2)}, u32[]{:S(2)}) %all-to-all-start.2) | async-done | bytes 165920 | tf_op jit(solution)/shard_map/all_to_all | solution.py:138
  378.4 4.5 collective-permute-start.4
  384.7 4.6 collective-permute-done.5
  390.9 3.0 collective-permute-start.6
  398.2 5.3 all-to-all-start.3
  404.1 33.9 %scatter_fusion = f32[54,32,512]{0,1,2:T(8,128)} fusion(f32[54,32,512]{0,1,2:T(8,128)} %copy.130, s32[256]{0:T(256)S(1)} %bitcast.184, f32[256,54,32]{1,2,0:T(8,128)} %get-tuple-element.12), kind=kCustom, calls=%fused_computation.15 | custom fusion | flops 442368 | bytes 5309440 | tf_op jit(solution)/shard_map/scatter-add | solution.py:67
  438.1 7.3 copy.143
  445.8 4.2 scatter_custom_fusion.5
  450.1 4.7 multiply_add_fusion
  454.8 7.0 copy.144
  461.8 236.8 %gather_fusion.7 = f32[16384,54]{1,0:T(8,128)} fusion(f32[54,32,512]{0,2,1:T(8,128)} %copy.144, s32[16384]{0:T(1024)S(1)} %bitcast.153), kind=kCustom, calls=%fused_computation.7.clone | custom fusion | bytes 7208960 | tf_op jit(solution)/shard_map/jit(take_along_axis)/gather | solution.py:51
  698.6 7.2 copy.158
  705.7 6.2 fusion.3
  711.9 9.1 %copy.146 = f32[54,32,512]{0,1,2:T(8,128)} copy(f32[54,32,512]{2,1,0:T(8,128)} %fusion.3) | data formatting | bytes 7077888 | tf_op jit(solution)/shard_map/add | solution.py:52
  721.0 4.4 gather_fusion.8
  725.4 2.5 copy.147
  728.7 4.1 multiply_convert_fusion.1
  732.8 4.4 fusion.1
  737.9 4.5 copy.148
  742.5 4.5 select_bitcast_fusion
  750.9 5.1 all-to-all-start.4
  755.9 33.9 %scatter_fusion.1 = f32[54,32,512]{0,1,2:T(8,128)} fusion(f32[54,32,512]{0,1,2:T(8,128)} %copy.146, s32[256]{0:T(256)S(1)} %bitcast.186, f32[256,54,32]{1,2,0:T(8,128)} %get-tuple-element.10), kind=kCustom, calls=%fused_computation.18 | custom fusion | flops 442368 | bytes 5309440 | tf_op jit(solution)/shard_map/scatter-add | solution.py:67
  789.8 7.3 copy.153
  797.2 5.0 copy.155
  802.2 3.1 gather_fusion
  806.6 6.5 all-to-all-start.5
  815.4 12.6 %all-to-all-done.5 = f32[1728,32,2]{0,2,1:T(2,128)S(1)} async-done(((f32[1728,32,2]{0,2,1:T(2,128)}), f32[1728,32,2]{0,2,1:T(2,128)S(1)}, u32[]{:S(2)}, u32[]{:S(2)}) %all-to-all-start.5) | async-done | bytes 442400 | tf_op jit(solution)/shard_map/all_to_all | solution.py:143
  828.3 4.7 scatter_custom_fusion.8
  833.0 5.1 copy.156
  (129 shorter events, 52.9 us)
Async XLA Ops:
  0.6 345.4 %copy-start = (bf16[256,256]{1,0:T(8,128)(2,1)S(1)}, bf16[256,256]{1,0:T(8,128)(2,1)}, u32[]{:S(2)}) copy-start(bf16[256,256]{1,0:T(8,128)(2,1)} %param.30) | copy-start | bytes 393220
  1.5 29.1 %collective-permute-start = (f32[54,1,2,128]{3,2,1,0:T(2,128)S(1)}, f32[54,1,2,128]{3,2,1,0:T(2,128)S(1)}, u32[]{:S(2)}, u32[]{:S(2)}) collective-permute-start(f32[54,1,2,128]{3,2,1,0:T(2,128)S(1)} %get-tuple-element.25), channel_id=1, source_target_pairs={{0,8},{8,16},{16,24},{1,9},{9,17},{17,25},{2,10},{10,18},{18,26},{... | collective-permute-start | bytes 165896 | tf_op jit(solution)/shard_map/ppermute | solution.py:21
  6.4 25.2 %collective-permute-start.1 = (f32[54,1,2,128]{3,2,1,0:T(2,128)S(1)}, f32[54,1,2,128]{3,2,1,0:T(2,128)S(1)}, u32[]{:S(2)}, u32[]{:S(2)}) collective-permute-start(f32[54,1,2,128]{3,2,1,0:T(2,128)S(1)} %get-tuple-element.24), channel_id=1, source_target_pairs={{8,0},{16,8},{24,16},{9,1},{17,9},{25,17},{10,2},{18,10},{26,18},{... | collective-permute-start | bytes 165896 | tf_op jit(solution)/shard_map/ppermute | solution.py:23
  14.5 14.8 %all-to-all-start = ((s32[1,8,96]{2,0,1:T(1,128)}), s32[1,8,96]{2,0,1:T(1,128)S(1)}, u32[]{:S(2)}, u32[]{:S(2)}) async-start(s32[1,8,96]{2,0,1:T(1,128)} %all_to_all.45), calls=%async_computation | async-start | bytes 8192 | tf_op jit(solution)/shard_map/all_to_all | solution.py:118
  24.2 39.3 %copy-start.2 = (f32[512]{0:T(512)S(1)}, f32[512]{0:T(512)}, u32[]{:S(2)}) copy-start(f32[512]{0:T(512)} %param.27) | copy-start | bytes 6148
  31.8 4.4 collective-permute-start.3
  33.1 4.0 collective-permute-start.2
  41.4 17.1 %all-to-all-start.1 = ((f32[54,8,96]{2,0,1:T(8,128)}), f32[54,8,96]{2,0,1:T(8,128)S(1)}, u32[]{:S(2)}, u32[]{:S(2)}) async-start(f32[54,8,96]{2,0,1:T(8,128)} %copy.124), calls=%async_computation.1 | async-start | bytes 458752 | tf_op jit(solution)/shard_map/all_to_all | solution.py:117
  338.5 3.4 copy-start.4
  341.9 4.1 copy-start.5
  355.7 12.1 %copy-start.1 = (s32[2,2,128]{2,1,0:T(2,128)S(1)}, s32[2,2,128]{2,1,0:T(2,128)}, u32[]{:S(2)}) copy-start(s32[2,2,128]{2,1,0:T(2,128)} %param.25) | copy-start | bytes 6148
  361.7 33.1 %copy-start.3 = (f32[2,2,128]{2,1,0:T(2,128)S(1)}, f32[2,2,128]{2,1,0:T(2,128)}, u32[]{:S(2)}) copy-start(f32[2,2,128]{2,1,0:T(2,128)} %param.23) | copy-start | bytes 6148
  364.4 12.3 %all-to-all-start.2 = ((f32[54,8,96]{2,0,1:T(8,128)}), f32[54,8,96]{2,0,1:T(8,128)S(1)}, u32[]{:S(2)}, u32[]{:S(2)}) async-start(f32[54,8,96]{2,0,1:T(8,128)} %copy.133), calls=%async_computation.2 | async-start | bytes 458752 | tf_op jit(solution)/shard_map/all_to_all | solution.py:138
  377.9 25.5 %copy-start.6 = (s32[1,64]{1,0:T(1,128)S(1)}, s32[1,64]{1,0:T(1,128)}, u32[]{:S(2)}) copy-start(s32[1,64]{1,0:T(1,128)} %param.34) | copy-start | bytes 772
  378.4 6.3 collective-permute-start.4
  382.9 6.4 collective-permute-start.5
  389.6 4.5 collective-permute-start.7
  390.9 4.0 collective-permute-start.6
  398.2 47.2 %all-to-all-start.3 = ((f32[54,8,96]{2,0,1:T(8,128)}), f32[54,8,96]{2,0,1:T(8,128)S(1)}, u32[]{:S(2)}, u32[]{:S(2)}) async-start(f32[54,8,96]{2,0,1:T(8,128)} %copy.138), calls=%async_computation.3 | async-start | bytes 458752 | tf_op jit(solution)/shard_map/all_to_all | solution.py:117
  750.9 55.8 %all-to-all-start.4 = ((f32[54,8,96]{2,0,1:T(8,128)}), f32[54,8,96]{2,0,1:T(8,128)S(1)}, u32[]{:S(2)}, u32[]{:S(2)}) async-start(f32[54,8,96]{2,0,1:T(8,128)} %copy.149), calls=%async_computation.4 | async-start | bytes 458752 | tf_op jit(solution)/shard_map/all_to_all | solution.py:138
  802.2 10.9 %copy-start.7 = (s32[1,64]{1,0:T(1,128)S(1)}, s32[1,64]{1,0:T(1,128)}, u32[]{:S(2)}) copy-start(s32[1,64]{1,0:T(1,128)} %param.35) | copy-start | bytes 772
  806.6 21.3 %all-to-all-start.5 = ((f32[1728,32,2]{0,2,1:T(2,128)}), f32[1728,32,2]{0,2,1:T(2,128)S(1)}, u32[]{:S(2)}, u32[]{:S(2)}) async-start(f32[1728,32,2]{0,2,1:T(2,128)} %broadcast_select_fusion), calls=%async_computation.5 | async-start | bytes 917504 | tf_op jit(solution)/shard_map/all_to_all | solution.py:143
where the time goes:
time: 849 us; the launch traced here: 838 us
  local copies, waits for them, and re-layouts  613 us (72%)
  other arithmetic  116 us (14%)
  starting transfers between devices  53.8 us (6%)
  waiting for transfers between devices  36.4 us (4%)
  matrix products  17 us (2%)
    gather x4, local copies, waits for them, and re-layouts, particle_section(): partner_state = jnp.take_along_axis(state, partner[None, :, :], axis=1)  488 us
    scatter-add x2, other arithmetic, particle_section(): state = state.at[:, :, chosen_slots].add(change)  67.8 us
    add x2, local copies, waits for them, and re-layouts, particle_section(): state = state + PAIR_WEIGHT * (partner_state - state)  18.1 us
  transfers between devices with their start and end apart: 14, of which 7 were waited for; matrix products, arithmetic and copies ran while one was open for 14% of the time, Pallas kernels for 0%

commit v1 on v0

v1 whole, which is shorter than its diff:
```python
import functools

import jax
import jax.numpy as jnp
from jax import lax
from jax.experimental import pallas as pl
from jax.experimental.pallas import tpu as pltpu
from jax.sharding import PartitionSpec as P

SUBSTEPS = 2
DIFFUSION = 0.1
PAIR_WEIGHT = 0.4
LANES = 128
SUB = 8
BF = jnp.bfloat16
F32 = jnp.float32
I32 = jnp.int32

NT = (((1,), (1,)), ((), ()))
NN = (((1,), (0,)), ((), ()))


def call(body, outs, ins, smem=(), scratch=(), limit=40, name=None):
    specs = [
        pl.BlockSpec(memory_space=pltpu.SMEM if i in smem else pltpu.VMEM) for i in range(len(ins))
    ]
    return pl.pallas_call(
        body,
        out_shape=[jax.ShapeDtypeStruct(s, d) for s, d in outs],
        in_specs=specs,
        out_specs=[pl.BlockSpec(memory_space=pltpu.VMEM)] * len(outs),
        scratch_shapes=list(scratch),
        compiler_params=pltpu.CompilerParams(vmem_limit_bytes=limit << 20),
        name=name,
    )(*ins)


def dot(a, b, dims):
    return lax.dot_general(a, b, dims, preferred_element_type=F32)


def dot_split(x, onehot, dims):
    high = x.astype(BF)
    low = (x - high.astype(F32)).astype(BF)
    return dot(high, onehot, dims) + dot(low, onehot, dims)


def divisor(n, most):
    return max(k for k in range(1, most + 1) if n % k == 0)


def mix_in_place(q_ref, partner_ref):
    scalars, particles, cells = q_ref.shape
    groups = particles // SUB
    for t in range(cells // LANES):
        lanes = pl.ds(t * LANES, LANES)
        rows, homes = [], []
        for j in range(groups):
            index = partner_ref[pl.ds(j * SUB, SUB), lanes]
            rows.append(index & (SUB - 1))
            homes.append(index >> 3)

        def step(s, carry):
            x = [q_ref[s, pl.ds(k * SUB, SUB), lanes] for k in range(groups)]
            for j in range(groups):
                mate = jnp.take_along_axis(x[0], rows[j], axis=0)
                for k in range(1, groups):
                    other = jnp.take_along_axis(x[k], rows[j], axis=0)
                    mate = jnp.where(homes[j] == k, other, mate)
                q_ref[s, pl.ds(j * SUB, SUB), lanes] = x[j] + PAIR_WEIGHT * (mate - x[j])
            return carry

        lax.fori_loop(0, scalars, step, 0, unroll=2)


def store_tiles(ref, first, count, stride, value):
    slab = ref.shape[0] * LANES // value.shape[1]
    for t in range(value.shape[1] // LANES):
        at = pl.ds(t * slab + first, count, stride=stride)
        ref[at, :] = value[:, t * LANES : (t + 1) * LANES]


def load_tiles(ref, tiles, first, count, stride=1):
    slab = ref.shape[0] // tiles
    parts = [ref[pl.ds(t * slab + first, count, stride=stride), :] for t in range(tiles)]
    return jnp.concatenate(parts, axis=1)


def list_cells(q_ref, onehot, keep, a_ref, rows):
    scalars, particles, cells = q_ref.shape
    block = divisor(scalars, 8)

    def step(b, carry):
        s0 = b * block
        x = q_ref[pl.ds(s0, block), :, :].reshape(block * particles, cells)
        y = dot_split(x, onehot, NT) * keep
        for i in range(block):
            store_tiles(a_ref, s0 + i, particles, rows, y[i * particles : (i + 1) * particles])
        return carry

    lax.fori_loop(0, scalars // block, step, 0)
    for s in range(scalars, rows):
        store_tiles(a_ref, s, particles, rows, jnp.zeros((particles, onehot.shape[0]), F32))


def open_body(rows, p_ref, partner_ref, rate_ref, rcol_ref, q_ref, a_ref, ot_ref, rsel_ref):
    scalars, particles, cells = p_ref.shape
    onehot = (rcol_ref[...] == lax.broadcasted_iota(I32, ot_ref.shape, 1)).astype(F32).astype(BF)
    ot_ref[...] = onehot
    rate = jnp.broadcast_to(rate_ref[...], (SUB, cells))
    rsel_ref[...] = dot_split(rate, onehot, NT)

    def step(s, carry):
        q_ref[s] = p_ref[s]
        return carry

    lax.fori_loop(0, scalars, step, 0)
    mix_in_place(q_ref, partner_ref)
    list_cells(q_ref, ot_ref[...], 1.0 - rsel_ref[0:1, :], a_ref, rows)


def settle_state(q_ref, f_ref, r_ref, ot_ref, rate_ref, out_ref, rows):
    scalars, particles, cells = q_ref.shape
    tiles = cells // LANES
    block = divisor(scalars, 8)
    listed_tiles = ot_ref.shape[0] // LANES
    rate = rate_ref[...]
    keep = 1.0 - rate

    def step(b, carry):
        s0 = b * block
        r = jnp.concatenate(
            [load_tiles(r_ref, listed_tiles, s0 + i, particles, rows) for i in range(block)],
            axis=0,
        )
        spread = dot(r.astype(BF), ot_ref[...], NN)
        for i in range(block):
            f = jnp.concatenate(
                [f_ref[pl.ds((s0 + i) * tiles + t, 1), :] for t in range(tiles)], axis=1
            )
            out_ref[s0 + i] = (
                keep * q_ref[s0 + i] + rate * f + spread[i * particles : (i + 1) * particles]
            )
        return carry

    lax.fori_loop(0, scalars // block, step, 0)


def middle_body(
    rows, q_ref, f_ref, r_ref, ot_ref, rate_ref, rsel_ref, partner_ref, out_ref, a_ref
):
    settle_state(q_ref, f_ref, r_ref, ot_ref, rate_ref, out_ref, rows)
    mix_in_place(out_ref, partner_ref)
    list_cells(out_ref, ot_ref[...], 1.0 - rsel_ref[0:1, :], a_ref, rows)


def half_silu(y):
    return y + y * jnp.tanh(y)


def chem_body(
    particles, count_ref, f_ref, a_ref, ot_ref, rsel_ref, w1_ref, w2_ref, w3_ref, r_ref, s_ref
):
    tiles = ot_ref.shape[1] // LANES
    rows = f_ref.shape[0] // tiles
    listed = ot_ref.shape[0]
    f = jnp.concatenate([f_ref[pl.ds(t, rows, stride=tiles), :] for t in range(tiles)], axis=1)
    pull = rsel_ref[0:1, :] * dot_split(f, ot_ref[...], NT)
    live = lax.broadcasted_iota(I32, (1, listed), 1) < count_ref[0]
    group = divisor(particles, 2)

    def step(b, total):
        feed = jnp.concatenate(
            [
                (load_tiles(a_ref, listed // LANES, (b * group + i) * rows, rows) + pull).astype(BF)
                for i in range(group)
            ],
            axis=1,
        )
        one = half_silu(dot(w1_ref[...], feed, NN)).astype(BF)
        two = half_silu(dot(w2_ref[...], one, NN)).astype(BF)
        change = dot(w3_ref[...], two, NN).astype(BF).astype(F32)
        for i in range(group):
            r = jnp.where(live, change[:, i * listed : (i + 1) * listed], 0.0)
            store_tiles(r_ref, (b * group + i) * rows, rows, 1, r)
            total = total + r
        return total

    total = lax.fori_loop(0, particles // group, step, jnp.zeros((rows, listed), F32))
    source = dot_split(total * (1.0 / particles), ot_ref[...], NN)
    for t in range(tiles):
        s_ref[pl.ds(t, rows, stride=tiles), :] = source[:, t * LANES : (t + 1) * LANES]


def close_body(
    rows, span, q_ref, f_ref, r_ref, ot_ref, rate_ref, lcol_ref, out_ref, leave_ref
):
    settle_state(q_ref, f_ref, r_ref, ot_ref, rate_ref, out_ref, rows)
    scalars, particles, cells = q_ref.shape
    places = lcol_ref.shape[0]
    onehot = (lcol_ref[...] == lax.broadcasted_iota(I32, (places, cells), 1)).astype(F32).astype(BF)
    per = LANES // particles

    def pick(s0, count):
        x = out_ref[pl.ds(s0, count), :, :].reshape(count * particles, cells)
        high = x.astype(BF)
        low = (x - high.astype(F32)).astype(BF)
        return dot(onehot, high, NT) + dot(onehot, low, NT)

    def step(b, carry):
        leave_ref[pl.ds(b, places, stride=span), :] = pick(b * per, per)
        return carry

    whole = scalars // per
    lax.fori_loop(0, whole, step, 0)
    left = scalars - whole * per
    zeros = jnp.zeros((places, LANES), F32)
    for b in range(whole, span):
        if b == whole and left:
            part = jnp.concatenate(
                [pick(b * per, left), zeros[:, left * particles :]], axis=1
            )
            leave_ref[pl.ds(b, places, stride=span), :] = part
        else:
            leave_ref[pl.ds(b, places, stride=span), :] = zeros


def arrive_body(span, p_ref, arr_ref, acol_ref, out_ref):
    scalars, particles, cells = p_ref.shape
    places = acol_ref.shape[0]
    hit = (acol_ref[...] == lax.broadcasted_iota(I32, (places, cells), 1)).astype(F32)
    taken = jnp.sum(hit, axis=0, keepdims=True) > 0.5
    onehot = hit.astype(BF)
    per = LANES // particles

    def place(b, count):
        x = arr_ref[pl.ds(b, places, stride=span), :].T
        y = dot_split(x, onehot, NN)
        for i in range(count):
            s = b * per + i
            out_ref[s] = jnp.where(taken, y[i * particles : (i + 1) * particles], p_ref[s])

    whole = scalars // per

    def step(b, carry):
        place(b, per)
        return carry

    lax.fori_loop(0, whole, step, 0)
    if scalars > whole * per:
        place(whole, scalars - whole * per)


def stencil(value, speed, bx, by, lanes_y):
    boxes = value[0].shape[0]
    row = lax.broadcasted_iota(I32, value[0].shape, 0) % lanes_y
    zero = jnp.zeros((lanes_y, LANES), F32)

    def x_low(v):
        return jnp.concatenate([zero, v[: boxes - lanes_y]], axis=0)

    def x_high(v):
        return jnp.concatenate([v[lanes_y:], zero], axis=0)

    def y_low(v):
        return jnp.where(row == 0, 0.0, pltpu.roll(v, 1, 0))

    def y_high(v):
        return jnp.where(row == lanes_y - 1, 0.0, pltpu.roll(v, boxes - 1, 0))

    out = []
    for i in range(bx):
        for j in range(by):
            c = value[i * by + j]
            up = value[(i - 1) * by + j] if i else x_low(value[(bx - 1) * by + j])
            down = value[(i + 1) * by + j] if i < bx - 1 else x_high(value[j])
            left = value[i * by + j - 1] if j else y_low(value[i * by + by - 1])
            right = value[i * by + j + 1] if j < by - 1 else y_high(value[i * by])
            beside = up + down + left + right + pltpu.roll(c, 1, 1) + pltpu.roll(c, LANES - 1, 1)
            out.append(c + DIFFUSION * (beside - 6.0 * c) - speed[i * by + j] * (c - up))
    return out


def route(src_ref, first_row, row_step, item_step, items, own, quads, lanes_y, rows, lanes):
    shape = (lanes_y, LANES)
    out = [[jnp.zeros(shape, F32) for _ in rows] for _ in range(own)]

    def step(y, out):
        out = [list(o) for o in out]
        for j in range(items):
            hits = [r == (j * lanes_y + y) for r in rows]
            for s in range(own):
                line = src_ref[pl.ds(first_row + y * row_step + s * quads + j * item_step, 1), :]
                line = jnp.broadcast_to(line, shape)
                for k in range(len(rows)):
                    out[s][k] = jnp.where(
                        hits[k], jnp.take_along_axis(line, lanes[k], axis=1), out[s][k]
                    )
        return tuple(tuple(o) for o in out)

    return lax.fori_loop(0, lanes_y, step, tuple(tuple(o) for o in out), unroll=2)


def load_rows(ref, offset, stride, count):
    return ref[pl.ds(offset, count, stride=stride), :]


def start_body(dims, arr_ref, g_ref, f_ref, inv_ref, lab_ref):
    nx, ny, own, bx, by = dims
    quads = bx * by
    boxes = nx * ny
    width = own * quads
    stride = width + 2 * quads
    turns = quads * ny
    speed = [load_rows(arr_ref, width + quads + j, stride, boxes) for j in range(quads)]
    for s in range(own):
        value = [load_rows(arr_ref, s * quads + j, stride, boxes) for j in range(quads)]
        for j, v in enumerate(stencil(value, speed, bx, by, ny)):
            g_ref[pl.ds(s * quads + j, boxes, stride=width), :] = v
    for j in range(quads):
        lab_ref[pl.ds(j * boxes, boxes), :] = load_rows(arr_ref, width + j, stride, boxes).astype(
            I32
        )
    lane_of = lax.broadcasted_iota(I32, (turns, LANES), 1).astype(F32)
    sub_of = lax.broadcasted_iota(I32, (turns, LANES), 0)
    sub_lane = lax.broadcasted_iota(I32, (LANES, LANES), 0)

    def group(x, carry):
        def gather(y, acc):
            left, right = [], []
            for j in range(quads):
                line = lab_ref[pl.ds(j * boxes + x * ny + y, 1), :]
                hit = jnp.broadcast_to(line >> 7, (turns, LANES)) == sub_of
                code = (j * ny + y).astype(F32)
                left.append(
                    jnp.concatenate(
                        [jnp.where(hit, code, 0.0), jnp.where(hit, lane_of, 0.0)], axis=0
                    ).astype(BF)
                )
                right.append(
                    (jnp.broadcast_to(line & (LANES - 1), (LANES, LANES)) == sub_lane)
                    .astype(F32)
                    .astype(BF)
                )
            return acc + dot(
                jnp.concatenate(left, axis=1), jnp.concatenate(right, axis=1), NT
            )

        code = lax.fori_loop(0, ny, gather, jnp.zeros((2 * turns, LANES), F32), unroll=2)
        code = code.astype(I32)
        inv_ref[pl.ds(x * 2 * turns, 2 * turns), :] = code
        return carry

    lax.fori_loop(0, nx, group, 0)
    send_filtered(dims, g_ref, inv_ref, f_ref)


def send_filtered(dims, g_ref, inv_ref, f_ref):
    nx, ny, own, bx, by = dims
    quads = bx * by
    width = own * quads
    turns = quads * ny

    def group(x, carry):
        base = x * 2 * turns
        rows = [inv_ref[pl.ds(base + k * ny, ny), :] for k in range(quads)]
        lanes = [inv_ref[pl.ds(base + turns + k * ny, ny), :] for k in range(quads)]
        out = route(g_ref, x * ny * width, width, 1, quads, own, quads, ny, rows, lanes)
        for s in range(own):
            for k in range(quads):
                f_ref[pl.ds(x * ny * width + s * quads + k, ny, stride=width), :] = out[s][k]
        return carry

    lax.fori_loop(0, nx, group, 0)


def add_source(dims, s_ref, g_ref, lab_ref, out_ref):
    nx, ny, own, bx, by = dims
    quads = bx * by
    boxes = nx * ny
    width = own * quads

    def group(x, carry):
        labels = [lab_ref[pl.ds(j * boxes + x * ny, ny), :] for j in range(quads)]
        rows = [v >> 7 for v in labels]
        lanes = [v & (LANES - 1) for v in labels]
        out = route(s_ref, x * ny * width, width, 1, quads, own, quads, ny, rows, lanes)
        for s in range(own):
            for k in range(quads):
                at = pl.ds(x * ny * width + s * quads + k, ny, stride=width)
                out_ref[at, :] = g_ref[at, :] + out[s][k]
        return carry

    lax.fori_loop(0, nx, group, 0)


def again_body(dims, s_ref, g_ref, arr_ref, inv_ref, lab_ref, out_ref, f_ref, mid_ref):
    nx, ny, own, bx, by = dims
    quads = bx * by
    boxes = nx * ny
    width = own * quads
    stride = width + 2 * quads
    add_source(dims, s_ref, g_ref, lab_ref, mid_ref)
    speed = [load_rows(arr_ref, width + quads + j, stride, boxes) for j in range(quads)]
    for s in range(own):
        value = [load_rows(mid_ref, s * quads + j, width, boxes) for j in range(quads)]
        for j, v in enumerate(stencil(value, speed, bx, by, ny)):
            out_ref[pl.ds(s * quads + j, boxes, stride=width), :] = v
    send_filtered(dims, out_ref, inv_ref, f_ref)


def last_body(dims, s_ref, g_ref, lab_ref, out_ref):
    add_source(dims, s_ref, g_ref, lab_ref, out_ref)


def per_device(
    grid_scalars,
    axial_speed,
    particles,
    cell_owner,
    cell_slot,
    mix_rate,
    partner,
    chem_input,
    chem_hidden,
    chem_output,
    react_slots,
    react_count,
    leave_slots,
    arrive_slots,
):
    both = ("gx", "gy")
    nx, ny = lax.axis_size("gx"), lax.axis_size("gy")
    devices = nx * ny
    scalars, bx, by, nz = grid_scalars.shape
    heads, cells = partner.shape
    listed = react_slots.shape[1]
    hidden = chem_hidden.shape[0]
    quads = bx * by
    own = -(-scalars // devices)
    rows = devices * own
    width = own * quads
    tiles = cells // LANES
    assert nz == LANES and tiles == quads and heads % SUB == 0 and LANES % heads == 0
    dims = (nx, ny, own, bx, by)
    flat = devices * width

    label = ((cell_slot // LANES) * ny + cell_owner) * LANES + cell_slot % LANES
    padded = jnp.pad(grid_scalars, ((0, rows - scalars), (0, 0), (0, 0), (0, 0)))
    first = jnp.concatenate(
        [
            padded.reshape(devices, width, LANES),
            jnp.broadcast_to(label.astype(F32).reshape(1, quads, LANES), (devices, quads, LANES)),
            jnp.broadcast_to(axial_speed.reshape(1, quads, LANES), (devices, quads, LANES)),
        ],
        axis=1,
    )

    def exchange(x):
        x = x.reshape(devices, -1, LANES)
        return lax.all_to_all(x, both, split_axis=0, concat_axis=0, tiled=True).reshape(-1, LANES)

    arrival = exchange(first)

    rate = mix_rate.reshape(1, cells)
    rcol = react_slots.reshape(listed, 1)
    lcol = leave_slots.reshape(-1, 1)
    acol = arrive_slots.reshape(-1, 1)
    w1 = jnp.pad(chem_input, ((0, 0), (0, rows - scalars))) * jnp.asarray(0.5, BF)
    w2 = chem_hidden * jnp.asarray(0.5, BF)
    w3 = jnp.pad(chem_output, ((0, rows - scalars), (0, 0)))

    state_shape = (scalars, heads, cells)
    q, a, ot, rsel = call(
        functools.partial(open_body, rows),
        [
            (state_shape, F32),
            ((listed // LANES * heads * rows, LANES), F32),
            ((listed, cells), BF),
            ((SUB, listed), F32),
        ],
        [particles, partner, rate, rcol],
        name="open",
    )
    grid, sent, inv, lab = call(
        functools.partial(start_body, dims),
        [
            ((flat, LANES), F32),
            ((flat, LANES), F32),
            ((nx * 2 * quads * ny, LANES), I32),
            ((quads * devices, LANES), I32),
        ],
        [arrival],
        name="start",
    )

    def chemistry(f, a):
        return call(
            functools.partial(chem_body, heads),
            [((listed // LANES * heads * rows, LANES), F32), ((flat, LANES), F32)],
            [react_count, f, a, ot, rsel, w1, w2, w3],
            smem=(0,),
            name="chem",
        )

    for substep in range(SUBSTEPS):
        f = exchange(sent)
        change, source = chemistry(f, a)
        home = exchange(source)
        if substep < SUBSTEPS - 1:
            q, a = call(
                functools.partial(middle_body, rows),
                [(state_shape, F32), ((listed // LANES * heads * rows, LANES), F32)],
                [q, f, change, ot, rate, rsel, partner],
                name="middle",
            )
            grid, sent = call(
                functools.partial(again_body, dims),
                [((flat, LANES), F32), ((flat, LANES), F32)],
                [home, grid, arrival, inv, lab],
                scratch=[pltpu.VMEM((flat, LANES), F32)],
                name="again",
            )
    per = LANES // heads
    span = SUB * (-(-scalars // (per * SUB)))
    places = leave_slots.shape[1]
    state, leaving = call(
        functools.partial(close_body, rows, span),
        [(state_shape, F32), ((places * span, LANES), F32)],
        [q, f, change, ot, rate, lcol],
        name="close",
    )
    (grid,) = call(
        functools.partial(last_body, dims), [((flat, LANES), F32)], [home, grid, lab], name="last"
    )
    moved = exchange(leaving)
    grid_out = exchange(grid).reshape(rows, bx, by, nz)[:scalars]
    (state,) = call(
        functools.partial(arrive_body, span), [(state_shape, F32)], [state, moved, acol], name="arrive"
    )
    return (grid_out, state)


def solution(mesh):
    placed = (
        P(None, "gx", "gy", None),
        P("gx", "gy", None),
        P(None, None, ("gx", "gy")),
        P("gx", "gy", None),
        P("gx", "gy", None),
        P(("gx", "gy")),
        P(None, ("gx", "gy")),
        P(),
        P(),
        P(),
        P(("gx", "gy"), None),
        P(("gx", "gy")),
        P(("gx", "gy"), None),
        P(("gx", "gy"), None),
    )
    return jax.shard_map(
        per_device,
        mesh=mesh,
        in_specs=placed,
        out_specs=(P(None, "gx", "gy", None), P(None, None, ("gx", "gy"))),
        check_vma=False,
    )
```

time: 849 us -> 172 us (0.20); the launches traced: 838 us -> 171 us
  local copies, waits for them, and re-layouts: 613 us -> 25.7 us
  other arithmetic: 116 us -> 1.52 us
  Pallas kernels: 0 us -> 68.8 us
  starting transfers between devices: 53.8 us -> 21.1 us
  blocking collectives: 0 us -> 27.6 us
  matrix products: 17 us -> 0 us
  waiting for transfers between devices: 36.4 us -> 24.6 us
    gather x16 -> x0, local copies, waits for them, and re-layouts: 514 us -> none  [the longest x4 488 us: particle_section(): partner_state = jnp.take_along_axis(state, partner[None, :, :], axis=1)]
    pallas_call x0 -> x9, Pallas kernels: none -> 68.8 us  [call(): pl.pallas_call(body, out_shape=[jax.ShapeDtypeStruct(s, d) for s, d in ou...]
    scatter-add x2 -> x0, other arithmetic: 67.8 us -> none  [particle_section(): state = state.at[:, :, chosen_slots].add(change)]
    add x4 -> x0, local copies, waits for them, and re-layouts: 31.9 us -> none  [the longest x2 18.1 us: particle_section(): state = state + PAIR_WEIGHT * (partner_state - state)]
    all_to_all x0 -> x2, blocking collectives: none -> 27.6 us  [exchange(): lax.all_to_all(x, both, split_axis=0, concat_axis=0, tiled=True)]
    scatter x8 -> x0, local copies, waits for them, and re-layouts: 23.8 us -> none  [the longest x2 9.76 us: per_device(): flat_parts.at[:, arrive_slots[0]].set(arrived_cells, mode='drop')]
    add x6 -> x0, other arithmetic: 22.4 us -> none  [the longest x2 12.4 us: particle_section(): state = state + PAIR_WEIGHT * (partner_state - state)]
    ppermute x8 -> x0, starting transfers between devices: 20.7 us -> none  [the longest x4 15.5 us: with_halo(): lax.ppermute(tail, axis, [(i, (i + 1) % count) for i in range(ends)])]
  transfers between devices with their start and end apart: 14 -> 5, of which waited for: 7 -> 2; matrix products, arithmetic and copies ran while one was open for 14% -> 2% of each run, Pallas kernels for 0% -> 13%
where the time goes in v1:
time: 172 us; the launch traced here: 171 us
  Pallas kernels  68.8 us (40%)
  blocking collectives  27.6 us (16%)
  local copies, waits for them, and re-layouts  25.7 us (15%)
  waiting for transfers between devices  24.6 us (14%)
  starting transfers between devices  21.1 us (12%)
    pallas_call x9, Pallas kernels, call(): pl.pallas_call(body, out_shape=[jax.ShapeDtypeStruct(s, d) for s, d in ou...  68.8 us
    all_to_all x2, blocking collectives, exchange(): lax.all_to_all(x, both, split_axis=0, concat_axis=0, tiled=True)  27.6 us
    all_to_all x5, waiting for transfers between devices, exchange(): lax.all_to_all(x, both, split_axis=0, concat_axis=0, tiled=True)  24.6 us
    unnamed x37, local copies, waits for them, and re-layouts  21.7 us
    all_to_all x5, starting transfers between devices, exchange(): lax.all_to_all(x, both, split_axis=0, concat_axis=0, tiled=True)  21.1 us
  transfers between devices with their start and end apart: 5, of which 2 were waited for; matrix products, arithmetic and copies ran while one was open for 2% of the time, Pallas kernels for 13%

profile of v1, /device:TPU:0, one launch (start us, length us, event | category | flops | bytes accessed | tf_op | source)
XLA Modules:
  0.0 170.8 jit_solution(11729772054545009189)
XLA Ops:
  0.6 0.0 copy-start.15
  0.6 0.7 fusion.1
  1.4 0.9 pad.12
  2.3 0.7 broadcast_in_dim.17
  3.1 0.7 pad_maximum_fusion
  3.8 7.3 %all-to-all-start = ((f32[32,16,128]{2,1,0:T(8,128)}), f32[32,16,128]{2,1,0:T(8,128)S(1)}, u32[]{:S(2)}, u32[]{:S(2)}) async-start(f32[32,16,128]{2,1,0:T(8,128)} %pad_maximum_fusion), calls=%async_computation | async-start | bytes 524288 | tf_op jit(solution)/shard_map/all_to_all | solution.py:461
  11.1 0.9 copy.20
  12.0 9.1 %all-to-all-done = f32[32,16,128]{2,1,0:T(8,128)S(1)} async-done(((f32[32,16,128]{2,1,0:T(8,128)}), f32[32,16,128]{2,1,0:T(8,128)S(1)}, u32[]{:S(2)}, u32[]{:S(2)}) %all-to-all-start) | async-done | bytes 262176 | tf_op jit(solution)/shard_map/all_to_all | solution.py:461
  21.1 8.2 %start.1 = (f32[256,128]{1,0:T(8,128)S(1)}, f32[256,128]{1,0:T(8,128)}, s32[256,128]{1,0:T(8,128)S(1)}, s32[128,128]{1,0:T(8,128)S(1)}) custom-call(f32[512,128]{1,0:T(8,128)S(1)} %bitcast.20), custom_call_target="tpu_custom_call" | custom-call | tf_op jit(solution)/shard_map/start/pallas_call | solution.py:27
  29.3 2.9 %all-to-all-start.1 = ((f32[32,8,128]{2,1,0:T(8,128)}), f32[32,8,128]{2,1,0:T(8,128)S(1)}, u32[]{:S(2)}, u32[]{:S(2)}) async-start(f32[32,8,128]{2,1,0:T(8,128)} %bitcast.4), calls=%async_computation.1 | async-start | bytes 262144 | tf_op jit(solution)/shard_map/all_to_all | solution.py:461
  32.9 0.8 copy.19.rcol_ref
  33.7 0.8 pad.14.w3_ref
  34.4 2.0 %copy-done = f32[54,32,512]{2,1,0:T(8,128)S(1)} copy-done((f32[54,32,512]{2,1,0:T(8,128)S(1)}, f32[54,32,512]{2,1,0:T(8,128)}, u32[]{:S(2)}) %copy-start) | copy-done | bytes 3538968
  36.4 0.8 copy-done.11
  37.3 0.7 copy-done.13
  38.0 7.4 %open.1 = (f32[54,32,512]{2,1,0:T(8,128)S(1)}, f32[4096,128]{1,0:T(8,128)S(1)}, bf16[256,512]{1,0:T(8,128)(2,1)S(1)}, f32[8,256]{1,0:T(8,128)S(1)}) custom-call(f32[54,32,512]{2,1,0:T(8,128)S(1)} %copy-done, s32[32,512]{1,0:T(8,128)S(1)} %copy-done.11, f32[1,512]{1,0:T(1,128)S(1)} %bitcast.31, s32[256,1]{1,0:T(8,128)S(1)} %copy.19.rcol_ref), custom_call_target="tpu_custom_call" | custom-call | tf_op jit(solution)/shard_map/open/pallas_call | solution.py:27
  45.4 0.0 copy-start.3
  45.4 1.8 %copy-done.3 = f32[54,32,512]{2,1,0:T(8,128)} copy-done((f32[54,32,512]{2,1,0:T(8,128)}, f32[54,32,512]{2,1,0:T(8,128)S(1)}, u32[]{:S(2)}) %copy-start.3) | copy-done | bytes 3538968
  47.2 0.0 all-to-all-done.1
  47.2 9.5 %chem.2 = (f32[4096,128]{1,0:T(8,128)S(1)}, f32[256,128]{1,0:T(8,128)S(1)}) custom-call(s32[1]{0:T(128)S(6)} %copy.23.count_ref, f32[256,128]{1,0:T(8,128)S(1)} %bitcast.23, f32[4096,128]{1,0:T(8,128)S(1)} %get-tuple-element.21.a_ref, bf16[256,512]{1,0:T(8,128)(2,1)S(1)} %get-tuple-element.22.ot_ref, f32[8,256]{1,0:T(8,128)S(1)} %get-tuple-element.23.rsel_ref, ...), custom_call_target="tpu_custom_call" | custom-call | tf_op jit(solution)/shard_map/chem/pallas_call | solution.py:27
  56.7 1.3 copy-done.9
  58.1 13.8 %all_to_all.35 = f32[32,8,128]{2,1,0:T(8,128)S(1)} all-to-all(f32[32,8,128]{2,1,0:T(8,128)S(1)} %bitcast.30), channel_id=1, replica_groups=mesh['gx'=4,'gy'=8] {'gx','gy'}, dimensions={0} | all-to-all | bytes 262144 | tf_op jit(solution)/shard_map/all_to_all | solution.py:461
  71.9 8.7 %again.1 = (f32[256,128]{1,0:T(8,128)S(1)}, f32[256,128]{1,0:T(8,128)}) custom-call(f32[256,128]{1,0:T(8,128)S(1)} %bitcast.28, f32[256,128]{1,0:T(8,128)S(1)} %get-tuple-element.25.g_ref, f32[512,128]{1,0:T(8,128)S(1)} %bitcast.21, s32[256,128]{1,0:T(8,128)S(1)} %get-tuple-element.26.inv_ref, s32[128,128]{1,0:T(8,128)S(1)} %get-tuple-element.27.lab_ref), custom_call_target="tpu_custom_call" | custom-call | tf_op jit(solution)/shard_map/again/pallas_call | solution.py:27
  80.5 2.6 %all-to-all-start.3 = ((f32[32,8,128]{2,1,0:T(8,128)}), f32[32,8,128]{2,1,0:T(8,128)S(1)}, u32[]{:S(2)}, u32[]{:S(2)}) async-start(f32[32,8,128]{2,1,0:T(8,128)} %bitcast.10), calls=%async_computation.3 | async-start | bytes 262144 | tf_op jit(solution)/shard_map/all_to_all | solution.py:461
  83.1 0.0 copy-start.4
  83.1 2.0 %copy-done.4 = f32[54,32,512]{2,1,0:T(8,128)S(1)} copy-done((f32[54,32,512]{2,1,0:T(8,128)S(1)}, f32[54,32,512]{2,1,0:T(8,128)}, u32[]{:S(2)}) %copy-start.4) | copy-done | bytes 3538968
  85.1 1.6 copy-done.10
  86.7 9.0 %middle.1 = (f32[54,32,512]{2,1,0:T(8,128)S(1)}, f32[4096,128]{1,0:T(8,128)S(1)}) custom-call(f32[54,32,512]{2,1,0:T(8,128)S(1)} %copy-done.4, f32[256,128]{1,0:T(8,128)S(1)} %bitcast.24, f32[4096,128]{1,0:T(8,128)S(1)} %copy-done.10, bf16[256,512]{1,0:T(8,128)(2,1)S(1)} %get-tuple-element.22.ot_ref, f32[1,512]{1,0:T(1,128)S(1)} %bitcast.32, ...), custom_call_target="tpu_custom_call" | custom-call | tf_op jit(solution)/shard_map/middle/pallas_call | solution.py:27
  95.7 0.0 copy-start.1
  95.7 1.8 %copy-done.1 = f32[54,32,512]{2,1,0:T(8,128)} copy-done((f32[54,32,512]{2,1,0:T(8,128)}, f32[54,32,512]{2,1,0:T(8,128)S(1)}, u32[]{:S(2)}) %copy-start.1) | copy-done | bytes 3538968
  97.5 1.3 copy-done.7
  98.8 0.0 all-to-all-done.3
  98.9 1.6 copy-done.8
  100.4 9.5 %chem.3 = (f32[4096,128]{1,0:T(8,128)S(1)}, f32[256,128]{1,0:T(8,128)S(1)}) custom-call(s32[1]{0:T(128)S(6)} %copy.23.count_ref, f32[256,128]{1,0:T(8,128)S(1)} %bitcast.25, f32[4096,128]{1,0:T(8,128)S(1)} %copy-done.8, bf16[256,512]{1,0:T(8,128)(2,1)S(1)} %get-tuple-element.22.ot_ref, f32[8,256]{1,0:T(8,128)S(1)} %get-tuple-element.23.rsel_ref, ...), custom_call_target="tpu_custom_call" | custom-call | tf_op jit(solution)/shard_map/chem/pallas_call | solution.py:27
  110.0 13.8 %all_to_all.36 = f32[32,8,128]{2,1,0:T(8,128)S(1)} all-to-all(f32[32,8,128]{2,1,0:T(8,128)S(1)} %bitcast.29), channel_id=1, replica_groups=mesh['gx'=4,'gy'=8] {'gx','gy'}, dimensions={0} | all-to-all | bytes 262144 | tf_op jit(solution)/shard_map/all_to_all | solution.py:461
  123.8 4.6 %last.1 = f32[256,128]{1,0:T(8,128)} custom-call(f32[256,128]{1,0:T(8,128)S(1)} %bitcast.27, f32[256,128]{1,0:T(8,128)S(1)} %get-tuple-element.33.g_ref, s32[128,128]{1,0:T(8,128)S(1)} %get-tuple-element.27.lab_ref), custom_call_target="tpu_custom_call" | custom-call | tf_op jit(solution)/shard_map/last/pallas_call | solution.py:27
  128.4 2.6 %all-to-all-start.5 = ((f32[32,8,128]{2,1,0:T(8,128)}), f32[32,8,128]{2,1,0:T(8,128)S(1)}, u32[]{:S(2)}, u32[]{:S(2)}) async-start(f32[32,8,128]{2,1,0:T(8,128)} %bitcast.14), calls=%async_computation.5 | async-start | bytes 262144 | tf_op jit(solution)/shard_map/all_to_all | solution.py:461
  130.9 0.1 copy.21.lcol_ref
  131.0 2.0 %copy-done.2 = f32[54,32,512]{2,1,0:T(8,128)S(1)} copy-done((f32[54,32,512]{2,1,0:T(8,128)S(1)}, f32[54,32,512]{2,1,0:T(8,128)}, u32[]{:S(2)}) %copy-start.2) | copy-done | bytes 3538968
  133.0 6.2 %close.1 = (f32[54,32,512]{2,1,0:T(8,128)S(1)}, f32[1024,128]{1,0:T(8,128)}) custom-call(f32[54,32,512]{2,1,0:T(8,128)S(1)} %copy-done.2, f32[256,128]{1,0:T(8,128)S(1)} %bitcast.26, f32[4096,128]{1,0:T(8,128)S(1)} %get-tuple-element.35.r_ref, bf16[256,512]{1,0:T(8,128)(2,1)S(1)} %get-tuple-element.22.ot_ref, f32[1,512]{1,0:T(1,128)S(1)} %bitcast.33, ...), custom_call_target="tpu_custom_call" | custom-call | tf_op jit(solution)/shard_map/close/pallas_call | solution.py:27
  139.2 1.8 %copy-done.5 = f32[54,32,512]{2,1,0:T(8,128)} copy-done((f32[54,32,512]{2,1,0:T(8,128)}, f32[54,32,512]{2,1,0:T(8,128)S(1)}, u32[]{:S(2)}) %copy-start.5) | copy-done | bytes 3538968
  141.0 0.0 all-to-all-done.5
  141.0 5.8 %all-to-all-start.6 = ((f32[32,32,128]{2,1,0:T(8,128)}), f32[32,32,128]{2,1,0:T(8,128)S(1)}, u32[]{:S(2)}, u32[]{:S(2)}) async-start(f32[32,32,128]{2,1,0:T(8,128)} %bitcast.17), calls=%async_computation.6 | async-start | bytes 1048576 | tf_op jit(solution)/shard_map/all_to_all | solution.py:461
  146.9 0.1 copy.22.acol_ref
  147.0 0.7 slice.8
  147.6 15.5 %all-to-all-done.6 = f32[32,32,128]{2,1,0:T(8,128)S(1)} async-done(((f32[32,32,128]{2,1,0:T(8,128)}), f32[32,32,128]{2,1,0:T(8,128)S(1)}, u32[]{:S(2)}, u32[]{:S(2)}) %all-to-all-start.6) | async-done | bytes 524320 | tf_op jit(solution)/shard_map/all_to_all | solution.py:461
  163.1 2.0 %copy-done.6 = f32[54,32,512]{2,1,0:T(8,128)S(1)} copy-done((f32[54,32,512]{2,1,0:T(8,128)S(1)}, f32[54,32,512]{2,1,0:T(8,128)}, u32[]{:S(2)}) %copy-start.6) | copy-done | bytes 3538968
  165.1 5.7 %arrive.1 = f32[54,32,512]{2,1,0:T(8,128)} custom-call(f32[54,32,512]{2,1,0:T(8,128)S(1)} %copy-done.6, f32[1024,128]{1,0:T(8,128)S(1)} %bitcast.22, s32[64,1]{1,0:T(8,128)S(1)} %copy.22.acol_ref), custom_call_target="tpu_custom_call" | custom-call | tf_op jit(solution)/shard_map/arrive/pallas_call | solution.py:27
  (22 shorter events, 0.1 us)
Async XLA Ops:
  0.6 46.5 %copy-start.15 = (bf16[256,256]{1,0:T(8,128)(2,1)S(1)}, bf16[256,256]{1,0:T(8,128)(2,1)}, u32[]{:S(2)}) copy-start(bf16[256,256]{1,0:T(8,128)(2,1)} %param.22) | copy-start | bytes 393220
  3.8 17.3 %all-to-all-start = ((f32[32,16,128]{2,1,0:T(8,128)}), f32[32,16,128]{2,1,0:T(8,128)S(1)}, u32[]{:S(2)}, u32[]{:S(2)}) async-start(f32[32,16,128]{2,1,0:T(8,128)} %pad_maximum_fusion), calls=%async_computation | async-start | bytes 524288 | tf_op jit(solution)/shard_map/all_to_all | solution.py:461
  29.3 17.9 %all-to-all-start.1 = ((f32[32,8,128]{2,1,0:T(8,128)}), f32[32,8,128]{2,1,0:T(8,128)S(1)}, u32[]{:S(2)}, u32[]{:S(2)}) async-start(f32[32,8,128]{2,1,0:T(8,128)} %bitcast.4), calls=%async_computation.1 | async-start | bytes 262144 | tf_op jit(solution)/shard_map/all_to_all | solution.py:461
  34.4 2.0 %copy-start = (f32[54,32,512]{2,1,0:T(8,128)S(1)}, f32[54,32,512]{2,1,0:T(8,128)}, u32[]{:S(2)}) copy-start(f32[54,32,512]{2,1,0:T(8,128)} %p_ref.1) | copy-start | bytes 10616836
  36.4 0.8 copy-start.11
  37.3 0.7 copy-start.13
  38.0 45.1 %copy-start.12 = (s32[32,512]{1,0:T(8,128)S(1)}, s32[32,512]{1,0:T(8,128)}, u32[]{:S(2)}) copy-start(s32[32,512]{1,0:T(8,128)} %partner_ref.3) | copy-start | bytes 196612
  38.0 45.1 %copy-start.14 = (f32[512]{0:T(512)S(1)}, f32[512]{0:T(512)}, u32[]{:S(2)}) copy-start(f32[512]{0:T(512)} %param.19) | copy-start | bytes 6148
  45.4 1.8 %copy-start.3 = (f32[54,32,512]{2,1,0:T(8,128)}, f32[54,32,512]{2,1,0:T(8,128)S(1)}, u32[]{:S(2)}) copy-start(f32[54,32,512]{2,1,0:T(8,128)S(1)} %get-tuple-element.29.q_ref) | copy-start | bytes 10616836
  56.7 1.4 copy-start.9
  80.5 18.3 %all-to-all-start.3 = ((f32[32,8,128]{2,1,0:T(8,128)}), f32[32,8,128]{2,1,0:T(8,128)S(1)}, u32[]{:S(2)}, u32[]{:S(2)}) async-start(f32[32,8,128]{2,1,0:T(8,128)} %bitcast.10), calls=%async_computation.3 | async-start | bytes 262144 | tf_op jit(solution)/shard_map/all_to_all | solution.py:461
  83.1 2.0 %copy-start.4 = (f32[54,32,512]{2,1,0:T(8,128)S(1)}, f32[54,32,512]{2,1,0:T(8,128)}, u32[]{:S(2)}) copy-start(f32[54,32,512]{2,1,0:T(8,128)} %copy-done.3) | copy-start | bytes 10616836
  85.1 1.6 copy-start.10
  86.7 44.2 %copy-start.16 = (s32[1,64]{1,0:T(1,128)S(1)}, s32[1,64]{1,0:T(1,128)}, u32[]{:S(2)}) copy-start(s32[1,64]{1,0:T(1,128)} %param.26) | copy-start | bytes 772
  95.7 1.8 %copy-start.1 = (f32[54,32,512]{2,1,0:T(8,128)}, f32[54,32,512]{2,1,0:T(8,128)S(1)}, u32[]{:S(2)}) copy-start(f32[54,32,512]{2,1,0:T(8,128)S(1)} %get-tuple-element.34.q_ref) | copy-start | bytes 10616836
  97.5 1.4 copy-start.7
  98.9 1.6 copy-start.8
  128.4 12.7 %all-to-all-start.5 = ((f32[32,8,128]{2,1,0:T(8,128)}), f32[32,8,128]{2,1,0:T(8,128)S(1)}, u32[]{:S(2)}, u32[]{:S(2)}) async-start(f32[32,8,128]{2,1,0:T(8,128)} %bitcast.14), calls=%async_computation.5 | async-start | bytes 262144 | tf_op jit(solution)/shard_map/all_to_all | solution.py:461
  131.0 2.0 %copy-start.2 = (f32[54,32,512]{2,1,0:T(8,128)S(1)}, f32[54,32,512]{2,1,0:T(8,128)}, u32[]{:S(2)}) copy-start(f32[54,32,512]{2,1,0:T(8,128)} %copy-done.1) | copy-start | bytes 10616836
  133.0 13.8 %copy-start.17 = (s32[1,64]{1,0:T(1,128)S(1)}, s32[1,64]{1,0:T(1,128)}, u32[]{:S(2)}) copy-start(s32[1,64]{1,0:T(1,128)} %param.27) | copy-start | bytes 772
  139.2 1.8 %copy-start.5 = (f32[54,32,512]{2,1,0:T(8,128)}, f32[54,32,512]{2,1,0:T(8,128)S(1)}, u32[]{:S(2)}) copy-start(f32[54,32,512]{2,1,0:T(8,128)S(1)} %get-tuple-element.36.p_ref) | copy-start | bytes 10616836
  141.0 22.1 %all-to-all-start.6 = ((f32[32,32,128]{2,1,0:T(8,128)}), f32[32,32,128]{2,1,0:T(8,128)S(1)}, u32[]{:S(2)}, u32[]{:S(2)}) async-start(f32[32,32,128]{2,1,0:T(8,128)} %bitcast.17), calls=%async_computation.6 | async-start | bytes 1048576 | tf_op jit(solution)/shard_map/all_to_all | solution.py:461
  163.1 2.0 %copy-start.6 = (f32[54,32,512]{2,1,0:T(8,128)S(1)}, f32[54,32,512]{2,1,0:T(8,128)}, u32[]{:S(2)}) copy-start(f32[54,32,512]{2,1,0:T(8,128)} %copy-done.5) | copy-start | bytes 10616836

commit v2 on v1

v2 whole, which is shorter than its diff:
```python
import functools

import jax
import jax.numpy as jnp
from jax import lax
from jax.experimental import pallas as pl
from jax.experimental.pallas import tpu as pltpu
from jax.sharding import PartitionSpec as P

SUBSTEPS = 2
DIFFUSION = 0.1
PAIR_WEIGHT = 0.4
LANES = 128
SUB = 8
BF = jnp.bfloat16
F32 = jnp.float32
I32 = jnp.int32

NT = (((1,), (1,)), ((), ()))
NN = (((1,), (0,)), ((), ()))


def call(body, outs, ins, smem=(), scratch=(), limit=16, name=None, steps=None, blocks=None):
    blocks = blocks or {}

    def spec(i, shape):
        if i in smem:
            return pl.BlockSpec(memory_space=pltpu.SMEM)
        if steps is None:
            return pl.BlockSpec(memory_space=pltpu.VMEM)
        if i in blocks:
            return pl.BlockSpec(*blocks[i])
        return pl.BlockSpec(shape, lambda *_: (0,) * len(shape))

    grid = {} if steps is None else {"grid": (steps,)}
    return pl.pallas_call(
        body,
        out_shape=[
            pltpu.HBM(o[0], o[1]) if len(o) > 2 else jax.ShapeDtypeStruct(o[0], o[1]) for o in outs
        ],
        in_specs=[spec(i, x.shape) for i, x in enumerate(ins)],
        out_specs=[spec(len(ins) + i, o[0]) for i, o in enumerate(outs)],
        scratch_shapes=list(scratch),
        compiler_params=pltpu.CompilerParams(vmem_limit_bytes=limit << 20),
        name=name,
        **grid,
    )(*ins)


def far(x):
    return pltpu.with_memory_space_constraint(x, pltpu.HBM)


def dot(a, b, dims):
    return lax.dot_general(a, b, dims, preferred_element_type=F32)


def dot_split(x, onehot, dims):
    high = x.astype(BF)
    low = (x - high.astype(F32)).astype(BF)
    return dot(high, onehot, dims) + dot(low, onehot, dims)


def divisor(n, most):
    return max(k for k in range(1, most + 1) if n % k == 0)


def mix(p_ref, partner_ref, q_ref):
    scalars, particles, cells = p_ref.shape
    groups = particles // SUB
    for t in range(cells // LANES):
        lanes = pl.ds(t * LANES, LANES)
        rows, homes = [], []
        for j in range(groups):
            index = partner_ref[pl.ds(j * SUB, SUB), lanes]
            rows.append(index & (SUB - 1))
            homes.append(index >> 3)

        def step(s, carry):
            x = [p_ref[s, pl.ds(k * SUB, SUB), lanes] for k in range(groups)]
            for j in range(groups):
                mate = jnp.take_along_axis(x[0], rows[j], axis=0)
                for k in range(1, groups):
                    other = jnp.take_along_axis(x[k], rows[j], axis=0)
                    mate = jnp.where(homes[j] == k, other, mate)
                q_ref[s, pl.ds(j * SUB, SUB), lanes] = x[j] + PAIR_WEIGHT * (mate - x[j])
            return carry

        lax.fori_loop(0, scalars, step, 0, unroll=2)


def store_tiles(ref, at, value):
    for t in range(value.shape[1] // LANES):
        ref[t, at, :] = value[:, t * LANES : (t + 1) * LANES]


def load_tiles(ref, at):
    return jnp.concatenate([ref[t, at, :] for t in range(ref.shape[0])], axis=1)


def list_cells(s0, q_ref, onehot, keep, a_ref, rows):
    block, particles, cells = q_ref.shape
    y = dot_split(q_ref[...].reshape(block * particles, cells), onehot, NT) * keep
    for i in range(block):
        at = pl.ds(s0 + i, particles, stride=rows)
        store_tiles(a_ref, at, y[i * particles : (i + 1) * particles])


def clear_rest(scalars, rows, a_ref):
    particles = a_ref.shape[1] // rows
    zeros = jnp.zeros((particles, a_ref.shape[0] * LANES), F32)
    for s in range(scalars, rows):
        store_tiles(a_ref, pl.ds(s, particles, stride=rows), zeros)


def open_body(
    scalars, rows, p_ref, partner_ref, rate_ref, rcol_ref, q_ref, a_ref, ot_ref, rsel_ref
):
    block, particles, cells = p_ref.shape

    @pl.when(pl.program_id(0) == 0)
    def _():
        onehot = (rcol_ref[...] == lax.broadcasted_iota(I32, ot_ref.shape, 1)).astype(F32)
        ot_ref[...] = onehot.astype(BF)
        rate = jnp.broadcast_to(rate_ref[...], (SUB, cells))
        rsel_ref[...] = dot_split(rate, onehot.astype(BF), NT)
        clear_rest(scalars, rows, a_ref)

    mix(p_ref, partner_ref, q_ref)
    s0 = pl.program_id(0) * block
    list_cells(s0, q_ref, ot_ref[...], 1.0 - rsel_ref[0:1, :], a_ref, rows)


def settle_state(s0, q_ref, f_ref, r_ref, ot_ref, rate_ref, out_ref, rows):
    block, particles, cells = q_ref.shape
    tiles = cells // LANES
    rate = rate_ref[...]
    keep = 1.0 - rate
    r = jnp.concatenate(
        [load_tiles(r_ref, pl.ds(s0 + i, particles, stride=rows)) for i in range(block)], axis=0
    )
    spread = dot(r.astype(BF), ot_ref[...], NN)
    for i in range(block):
        f = jnp.concatenate(
            [f_ref[pl.ds((s0 + i) * tiles + t, 1), :] for t in range(tiles)], axis=1
        )
        out_ref[i] = keep * q_ref[i] + rate * f + spread[i * particles : (i + 1) * particles]


def middle_body(
    scalars,
    rows,
    q_ref,
    f_ref,
    r_ref,
    ot_ref,
    rate_ref,
    rsel_ref,
    partner_ref,
    out_ref,
    a_ref,
    token_ref,
    now_ref,
):
    @pl.when(pl.program_id(0) == 0)
    def _():
        clear_rest(scalars, rows, a_ref)
        token_ref[...] = rsel_ref[:, :LANES]

    s0 = pl.program_id(0) * q_ref.shape[0]
    settle_state(s0, q_ref, f_ref, r_ref, ot_ref, rate_ref, now_ref, rows)
    mix(now_ref, partner_ref, out_ref)
    list_cells(s0, out_ref, ot_ref[...], 1.0 - rsel_ref[0:1, :], a_ref, rows)


def half_silu(y):
    return y + y * jnp.tanh(y)


def chem_body(
    particles,
    count_ref,
    f_ref,
    a_ref,
    ot_ref,
    rsel_ref,
    w1_ref,
    w2_ref,
    w3_ref,
    token_ref,
    r_ref,
    s_ref,
    pull_ref,
    total_ref,
):
    tiles = ot_ref.shape[1] // LANES
    rows = f_ref.shape[0] // tiles
    listed = ot_ref.shape[0]

    @pl.when(pl.program_id(0) == 0)
    def _():
        f = jnp.concatenate([f_ref[pl.ds(t, rows, stride=tiles), :] for t in range(tiles)], axis=1)
        pull_ref[...] = rsel_ref[0:1, :] * dot_split(f, ot_ref[...], NT)
        total_ref[...] = jnp.zeros_like(total_ref)

    live = lax.broadcasted_iota(I32, (1, listed), 1) < count_ref[0]
    group = divisor(a_ref.shape[1] // rows, 2)

    def step(b, total):
        pull = pull_ref[...]
        at = [pl.ds((b * group + i) * rows, rows) for i in range(group)]
        feed = jnp.concatenate([(load_tiles(a_ref, k) + pull).astype(BF) for k in at], axis=1)
        one = half_silu(dot(w1_ref[...], feed, NN)).astype(BF)
        two = half_silu(dot(w2_ref[...], one, NN)).astype(BF)
        change = dot(w3_ref[...], two, NN).astype(BF).astype(F32)
        for i, k in enumerate(at):
            r = jnp.where(live, change[:, i * listed : (i + 1) * listed], 0.0)
            store_tiles(r_ref, k, r)
            total = total + r
        return total

    total = lax.fori_loop(0, a_ref.shape[1] // (rows * group), step, total_ref[...])
    total_ref[...] = total

    @pl.when(pl.program_id(0) == pl.num_programs(0) - 1)
    def _():
        source = dot_split(total * (1.0 / particles), ot_ref[...], NN)
        for t in range(tiles):
            s_ref[pl.ds(t, rows, stride=tiles), :] = source[:, t * LANES : (t + 1) * LANES]


def cell_onehot(col_ref, cells):
    shape = (col_ref.shape[0], cells)
    return (col_ref[...] == lax.broadcasted_iota(I32, shape, 1)).astype(F32).astype(BF)


def split_dot(onehot, x, dims):
    high = x.astype(BF)
    low = (x - high.astype(F32)).astype(BF)
    return dot(onehot, high, dims) + dot(onehot, low, dims)


def leave_blocks(scalars, particles, span, store, part):
    per = LANES // particles

    def step(b, carry):
        store(b, part(b * per, per))
        return carry

    whole = scalars // per
    lax.fori_loop(0, whole, step, 0)
    left = scalars - whole * per
    for b in range(whole, span):
        if b == whole and left:
            value = part(b * per, left)
            zeros = jnp.zeros((value.shape[0], LANES - left * particles), F32)
            store(b, jnp.concatenate([value, zeros], axis=1))
        else:
            store(b, None)


def base_body(span, q_ref, rate_ref, lcol_ref, out_ref, token_ref):
    scalars, particles, cells = q_ref.shape
    onehot = cell_onehot(lcol_ref, cells)
    keep = 1.0 - rate_ref[...]

    def part(s0, count):
        x = q_ref[pl.ds(s0, count), :, :].reshape(count * particles, cells) * keep
        return split_dot(onehot, x, NT)

    def store(b, value):
        if value is not None:
            out_ref[pl.ds(b, lcol_ref.shape[0], stride=span), :] = value

    leave_blocks(scalars, particles, span, store, part)
    token_ref[...] = keep[:, :LANES]


def leave_body(
    rows,
    span,
    scalars,
    particles,
    devices,
    base_ref,
    f_ref,
    r_ref,
    rate_ref,
    lcol_ref,
    rrow_ref,
    source_ref,
    out_ref,
):
    width = source_ref.shape[0] // devices
    stride = out_ref.shape[0] // devices
    for d in range(devices):
        out_ref[d * stride : d * stride + width] = source_ref[d * width : (d + 1) * width]
    cells = rate_ref.shape[1]
    tiles = cells // LANES
    places = lcol_ref.shape[0]
    f = jnp.concatenate([f_ref[pl.ds(t, rows, stride=tiles), :] for t in range(tiles)], axis=1)
    pull = split_dot(cell_onehot(lcol_ref, cells), f * rate_ref[...], NT)
    reacts = (lcol_ref[...] == rrow_ref[...]).astype(F32).astype(BF)

    def part(s0, count):
        wide = count * particles
        r = jnp.concatenate(
            [load_tiles(r_ref, pl.ds(s0 + i, particles, stride=rows)) for i in range(count)], axis=0
        )
        of = lax.broadcasted_iota(I32, (rows, wide), 1) // particles + s0
        mine = (of == lax.broadcasted_iota(I32, (rows, wide), 0)).astype(F32).astype(BF)
        at = pl.ds(s0 * particles // LANES, places, stride=span)
        return base_ref[at, :][:, :wide] + dot_split(pull, mine, NN) + dot(reacts, r.astype(BF), NT)

    def store(b, value):
        for c in range(places // devices):
            at = pl.ds(width + c * span + b, devices, stride=stride)
            if value is None:
                out_ref[at, :] = jnp.zeros((devices, LANES), F32)
            else:
                out_ref[at, :] = value[c * devices : (c + 1) * devices]

    leave_blocks(scalars, particles, span, store, part)


def settle_body(rows, q_ref, f_ref, r_ref, ot_ref, rate_ref, out_ref):
    s0 = pl.program_id(0) * q_ref.shape[0]
    settle_state(s0, q_ref, f_ref, r_ref, ot_ref, rate_ref, out_ref, rows)


def arrive_body(span, devices, p_ref, arr_ref, acol_ref, out_ref, hit_ref, taken_ref):
    per, particles, cells = p_ref.shape
    places = acol_ref.shape[0]
    b = pl.program_id(0)

    @pl.when(b == 0)
    def _():
        hit = (acol_ref[...] == lax.broadcasted_iota(I32, (places, cells), 1)).astype(F32)
        hit_ref[...] = hit.astype(BF)
        taken_ref[...] = jnp.broadcast_to(jnp.sum(hit, axis=0, keepdims=True), taken_ref.shape)

    stride = arr_ref.shape[0] // devices
    count = places // devices
    first = stride - count * span + b
    x = jnp.concatenate(
        [arr_ref[pl.ds(first + c * span, devices, stride=stride), :] for c in range(count)], axis=0
    ).T
    y = dot_split(x, hit_ref[...], NN)
    taken = taken_ref[0:1, :] > 0.5
    for i in range(per):
        out_ref[i] = jnp.where(taken, y[i * particles : (i + 1) * particles], p_ref[i])


def stencil(value, speed, bx, by, lanes_y):
    boxes = value[0].shape[0]
    row = lax.broadcasted_iota(I32, value[0].shape, 0) % lanes_y
    zero = jnp.zeros((lanes_y, LANES), F32)

    def x_low(v):
        return jnp.concatenate([zero, v[: boxes - lanes_y]], axis=0)

    def x_high(v):
        return jnp.concatenate([v[lanes_y:], zero], axis=0)

    def y_low(v):
        return jnp.where(row == 0, 0.0, pltpu.roll(v, 1, 0))

    def y_high(v):
        return jnp.where(row == lanes_y - 1, 0.0, pltpu.roll(v, boxes - 1, 0))

    out = []
    for i in range(bx):
        for j in range(by):
            c = value[i * by + j]
            up = value[(i - 1) * by + j] if i else x_low(value[(bx - 1) * by + j])
            down = value[(i + 1) * by + j] if i < bx - 1 else x_high(value[j])
            left = value[i * by + j - 1] if j else y_low(value[i * by + by - 1])
            right = value[i * by + j + 1] if j < by - 1 else y_high(value[i * by])
            beside = up + down + left + right + pltpu.roll(c, 1, 1) + pltpu.roll(c, LANES - 1, 1)
            out.append(c + DIFFUSION * (beside - 6.0 * c) - speed[i * by + j] * (c - up))
    return out


def route(src_ref, first_row, row_step, item_step, items, own, quads, lanes_y, rows, lanes):
    shape = (lanes_y, LANES)
    out = [[jnp.zeros(shape, F32) for _ in rows] for _ in range(own)]

    def step(y, out):
        out = [list(o) for o in out]
        for j in range(items):
            hits = [r == (j * lanes_y + y) for r in rows]
            for s in range(own):
                line = src_ref[pl.ds(first_row + y * row_step + s * quads + j * item_step, 1), :]
                line = jnp.broadcast_to(line, shape)
                for k in range(len(rows)):
                    out[s][k] = jnp.where(
                        hits[k], jnp.take_along_axis(line, lanes[k], axis=1), out[s][k]
                    )
        return tuple(tuple(o) for o in out)

    return lax.fori_loop(0, lanes_y, step, tuple(tuple(o) for o in out), unroll=2)


def load_rows(ref, offset, stride, count):
    return ref[pl.ds(offset, count, stride=stride), :]


def pack_body(width, grid_ref, owner_ref, slot_ref, speed_ref, lanes_y, out_ref):
    quads = owner_ref.shape[0]
    stride = width + 2 * quads
    total = grid_ref.shape[0]
    slot = slot_ref[...]
    label = ((slot >> 7) * lanes_y + owner_ref[...]) * LANES + (slot & (LANES - 1))
    tail = jnp.concatenate([label.astype(F32), speed_ref[...]], axis=0)
    for d in range(out_ref.shape[0] // stride):
        count = max(0, min(width, total - d * width))
        if count:
            out_ref[d * stride : d * stride + count] = grid_ref[d * width : d * width + count]
        if count < width:
            zeros = jnp.zeros((width - count, LANES), F32)
            out_ref[d * stride + count : d * stride + width] = zeros
        out_ref[d * stride + width : (d + 1) * stride] = tail


def start_body(dims, arr_ref, token_ref, g_ref, f_ref, inv_ref, lab_ref):
    nx, ny, own, bx, by = dims
    quads = bx * by
    boxes = nx * ny
    width = own * quads
    stride = width + 2 * quads
    turns = quads * ny
    speed = [load_rows(arr_ref, width + quads + j, stride, boxes) for j in range(quads)]
    for s in range(own):
        value = [load_rows(arr_ref, s * quads + j, stride, boxes) for j in range(quads)]
        for j, v in enumerate(stencil(value, speed, bx, by, ny)):
            g_ref[pl.ds(s * quads + j, boxes, stride=width), :] = v
    for j in range(quads):
        lab_ref[pl.ds(j * boxes, boxes), :] = load_rows(arr_ref, width + j, stride, boxes).astype(
            I32
        )
    lane_of = lax.broadcasted_iota(I32, (turns, LANES), 1).astype(F32)
    sub_of = lax.broadcasted_iota(I32, (turns, LANES), 0)
    sub_lane = lax.broadcasted_iota(I32, (LANES, LANES), 0)

    def group(x, carry):
        def gather(y, acc):
            left, right = [], []
            for j in range(quads):
                line = lab_ref[pl.ds(j * boxes + x * ny + y, 1), :]
                hit = jnp.broadcast_to(line >> 7, (turns, LANES)) == sub_of
                code = (j * ny + y).astype(F32)
                left.append(
                    jnp.concatenate(
                        [jnp.where(hit, code, 0.0), jnp.where(hit, lane_of, 0.0)], axis=0
                    ).astype(BF)
                )
                right.append(
                    (jnp.broadcast_to(line & (LANES - 1), (LANES, LANES)) == sub_lane)
                    .astype(F32)
                    .astype(BF)
                )
            return acc + dot(
                jnp.concatenate(left, axis=1), jnp.concatenate(right, axis=1), NT
            )

        code = lax.fori_loop(0, ny, gather, jnp.zeros((2 * turns, LANES), F32), unroll=2)
        code = code.astype(I32)
        inv_ref[pl.ds(x * 2 * turns, 2 * turns), :] = code
        return carry

    lax.fori_loop(0, nx, group, 0)
    send_filtered(dims, g_ref, inv_ref, f_ref)


def send_filtered(dims, g_ref, inv_ref, f_ref):
    nx, ny, own, bx, by = dims
    quads = bx * by
    width = own * quads
    turns = quads * ny

    def group(x, carry):
        base = x * 2 * turns
        rows = [inv_ref[pl.ds(base + k * ny, ny), :] for k in range(quads)]
        lanes = [inv_ref[pl.ds(base + turns + k * ny, ny), :] for k in range(quads)]
        out = route(g_ref, x * ny * width, width, 1, quads, own, quads, ny, rows, lanes)
        for s in range(own):
            for k in range(quads):
                f_ref[pl.ds(x * ny * width + s * quads + k, ny, stride=width), :] = out[s][k]
        return carry

    lax.fori_loop(0, nx, group, 0)


def add_source(dims, s_ref, g_ref, lab_ref, out_ref):
    nx, ny, own, bx, by = dims
    quads = bx * by
    boxes = nx * ny
    width = own * quads
    stride = s_ref.shape[0] // boxes

    def group(x, carry):
        labels = [lab_ref[pl.ds(j * boxes + x * ny, ny), :] for j in range(quads)]
        rows = [v >> 7 for v in labels]
        lanes = [v & (LANES - 1) for v in labels]
        out = route(s_ref, x * ny * stride, stride, 1, quads, own, quads, ny, rows, lanes)
        for s in range(own):
            for k in range(quads):
                at = pl.ds(x * ny * width + s * quads + k, ny, stride=width)
                out_ref[at, :] = g_ref[at, :] + out[s][k]
        return carry

    lax.fori_loop(0, nx, group, 0)


def again_body(dims, s_ref, g_ref, arr_ref, inv_ref, lab_ref, token_ref, out_ref, f_ref, mid_ref):
    nx, ny, own, bx, by = dims
    quads = bx * by
    boxes = nx * ny
    width = own * quads
    stride = width + 2 * quads
    add_source(dims, s_ref, g_ref, lab_ref, mid_ref)
    speed = [load_rows(arr_ref, width + quads + j, stride, boxes) for j in range(quads)]
    for s in range(own):
        value = [load_rows(mid_ref, s * quads + j, width, boxes) for j in range(quads)]
        for j, v in enumerate(stencil(value, speed, bx, by, ny)):
            out_ref[pl.ds(s * quads + j, boxes, stride=width), :] = v
    send_filtered(dims, out_ref, inv_ref, f_ref)


def last_body(dims, s_ref, g_ref, lab_ref, out_ref):
    add_source(dims, s_ref, g_ref, lab_ref, out_ref)


def per_device(
    grid_scalars,
    axial_speed,
    particles,
    cell_owner,
    cell_slot,
    mix_rate,
    partner,
    chem_input,
    chem_hidden,
    chem_output,
    react_slots,
    react_count,
    leave_slots,
    arrive_slots,
):
    both = ("gx", "gy")
    nx, ny = lax.axis_size("gx"), lax.axis_size("gy")
    devices = nx * ny
    scalars, bx, by, nz = grid_scalars.shape
    heads, cells = partner.shape
    listed = react_slots.shape[1]
    hidden = chem_hidden.shape[0]
    quads = bx * by
    own = -(-scalars // devices)
    rows = devices * own
    width = own * quads
    tiles = cells // LANES
    assert nz == LANES and tiles == quads and heads % SUB == 0 and LANES % heads == 0
    dims = (nx, ny, own, bx, by)
    flat = devices * width

    (first,) = call(
        lambda g, o, c, u, out: pack_body(width, g, o, c, u, ny, out),
        [((devices * (width + 2 * quads), LANES), F32)],
        [
            grid_scalars.reshape(-1, LANES),
            cell_owner.reshape(quads, LANES),
            cell_slot.reshape(quads, LANES),
            axial_speed.reshape(quads, LANES),
        ],
        name="pack",
    )

    def exchange(x):
        x = x.reshape(devices, -1, LANES)
        return lax.all_to_all(x, both, split_axis=0, concat_axis=0, tiled=True).reshape(-1, LANES)

    arrival = exchange(first)

    rate = mix_rate.reshape(1, cells)
    rcol = react_slots.reshape(listed, 1)
    lcol = leave_slots.reshape(devices, -1).T.reshape(-1, 1)
    acol = arrive_slots.reshape(devices, -1).T.reshape(-1, 1)
    w1 = jnp.pad(chem_input, ((0, 0), (0, rows - scalars))) * jnp.asarray(0.5, BF)
    w2 = chem_hidden * jnp.asarray(0.5, BF)
    w3 = jnp.pad(chem_output, ((0, rows - scalars), (0, 0)))

    state_shape = (scalars, heads, cells)
    listed_shape = (listed // LANES, heads * rows, LANES)
    block = divisor(scalars, 6)
    some = ((block, heads, cells), lambda i: (i, 0, 0))
    turn = divisor(heads, 8)
    part = ((listed // LANES, turn * rows, LANES), lambda i: (0, i, 0))
    q, a, ot, rsel = call(
        functools.partial(open_body, scalars, rows),
        [
            (state_shape, F32, True),
            (listed_shape, F32, True),
            ((listed, cells), BF),
            ((SUB, listed), F32),
        ],
        [far(particles), partner, rate, rcol],
        steps=scalars // block,
        blocks={0: some, 4: some},
        name="open",
    )
    grid, sent, inv, lab = call(
        functools.partial(start_body, dims),
        [
            ((flat, LANES), F32),
            ((flat, LANES), F32),
            ((nx * 2 * quads * ny, LANES), I32),
            ((quads * devices, LANES), I32),
        ],
        [arrival, rsel],
        name="start",
    )

    def chemistry(f, a, token):
        return call(
            functools.partial(chem_body, heads),
            [(listed_shape, F32, True), ((flat, LANES), F32)],
            [react_count, f, far(a), ot, rsel, w1, w2, w3, token],
            smem=(0,),
            scratch=[pltpu.VMEM((rows, listed), F32), pltpu.VMEM((rows, listed), F32)],
            steps=heads // turn,
            blocks={2: part, 9: part},
            name="chem",
        )

    per = LANES // heads
    span = SUB * (-(-scalars // (per * SUB)))
    places = leave_slots.shape[1]
    token = rsel
    for substep in range(SUBSTEPS):
        f = exchange(sent)
        change, source = chemistry(f, a, token)
        if substep < SUBSTEPS - 1:
            home = exchange(source)
            q, a, token = call(
                functools.partial(middle_body, scalars, rows),
                [(state_shape, F32, True), (listed_shape, F32, True), ((SUB, LANES), F32)],
                [far(q), f, far(change), ot, rate, rsel, partner],
                scratch=[pltpu.VMEM((block, heads, cells), F32)],
                steps=scalars // block,
                blocks={0: some, 7: some},
                name="middle",
            )
            grid, sent = call(
                functools.partial(again_body, dims),
                [((flat, LANES), F32), ((flat, LANES), F32)],
                [home, grid, arrival, inv, lab, token],
                scratch=[pltpu.VMEM((flat, LANES), F32)],
                name="again",
            )
        if substep == SUBSTEPS - 2:
            base, token = call(
                functools.partial(base_body, span),
                [((places * span, LANES), F32, True), ((1, LANES), F32)],
                [far(q), rate, lcol],
                name="base",
            )
    (leaving,) = call(
        functools.partial(leave_body, rows, span, scalars, heads, devices),
        [((flat + places * span, LANES), F32)],
        [far(base), f, far(change), rate, lcol, react_slots, source],
        name="leave",
    )
    moved = exchange(leaving)
    (grid,) = call(
        functools.partial(last_body, dims), [((flat, LANES), F32)], [moved, grid, lab], name="last"
    )
    grid_out = exchange(grid).reshape(rows, bx, by, nz)[:scalars]
    (state,) = call(
        functools.partial(settle_body, rows),
        [(state_shape, F32, True)],
        [far(q), f, far(change), ot, rate],
        steps=scalars // block,
        blocks={0: some, 5: some},
        name="settle",
    )
    four = ((per, heads, cells), lambda i: (i, 0, 0))
    (state,) = call(
        functools.partial(arrive_body, span, devices),
        [(state_shape, F32, True)],
        [far(state), moved, acol],
        scratch=[pltpu.VMEM((places, cells), BF), pltpu.VMEM((SUB, cells), F32)],
        steps=-(-scalars // per),
        blocks={0: four, 3: four},
        name="arrive",
    )
    return (grid_out, state)


def solution(mesh):
    placed = (
        P(None, "gx", "gy", None),
        P("gx", "gy", None),
        P(None, None, ("gx", "gy")),
        P("gx", "gy", None),
        P("gx", "gy", None),
        P(("gx", "gy")),
        P(None, ("gx", "gy")),
        P(),
        P(),
        P(),
        P(("gx", "gy"), None),
        P(("gx", "gy")),
        P(("gx", "gy"), None),
        P(("gx", "gy"), None),
    )
    return jax.shard_map(
        per_device,
        mesh=mesh,
        in_specs=placed,
        out_specs=(P(None, "gx", "gy", None), P(None, None, ("gx", "gy"))),
        check_vma=False,
    )
```

time: 172 us -> 167 us (0.971)
  Pallas kernels: 68.8 us -> 98.3 us
  local copies, waits for them, and re-layouts: 25.7 us -> 7.92 us
  waiting for transfers between devices: 24.6 us -> 8.17 us
  blocking collectives: 27.6 us -> 24 us
  starting transfers between devices: 21.1 us -> 24.1 us
    pallas_call x9 -> x12, Pallas kernels: 68.8 us -> 98.3 us  [call(): pl.pallas_call(body, out_shape=[pltpu.HBM(o[0], o[1]) if len(o) > 2 else...]
    all_to_all x5, waiting for transfers between devices: 24.6 us -> 8.17 us  [exchange(): lax.all_to_all(x, both, split_axis=0, concat_axis=0, tiled=True)]
    unnamed x37 -> x28, local copies, waits for them, and re-layouts: 21.7 us -> 5.87 us
    all_to_all x2 -> x1, blocking collectives: 27.6 us -> 24 us  [exchange(): lax.all_to_all(x, both, split_axis=0, concat_axis=0, tiled=True)]
    all_to_all x5, starting transfers between devices: 21.1 us -> 24.1 us  [exchange(): lax.all_to_all(x, both, split_axis=0, concat_axis=0, tiled=True)]
  transfers between devices with their start and end apart: 5 -> 5, of which waited for: 2 -> 2; matrix products, arithmetic and copies ran while one was open for 2% -> 3% of each run, Pallas kernels for 13% -> 29%
where the time goes in v2:
time: 167 us; the launch traced here: 165 us
  Pallas kernels  98.3 us (59%)
  starting transfers between devices  24.1 us (14%)
  blocking collectives  24 us (14%)
  waiting for transfers between devices  8.17 us (5%)
  local copies, waits for them, and re-layouts  7.92 us (5%)
    pallas_call x12, Pallas kernels, call(): pl.pallas_call(body, out_shape=[pltpu.HBM(o[0], o[1]) if len(o) > 2 else...  98.3 us
    all_to_all x5, starting transfers between devices, exchange(): lax.all_to_all(x, both, split_axis=0, concat_axis=0, tiled=True)  24.1 us
    all_to_all x1, blocking collectives, exchange(): lax.all_to_all(x, both, split_axis=0, concat_axis=0, tiled=True)  24 us
    all_to_all x5, waiting for transfers between devices, exchange(): lax.all_to_all(x, both, split_axis=0, concat_axis=0, tiled=True)  8.17 us
    unnamed x28, local copies, waits for them, and re-layouts  5.87 us
  transfers between devices with their start and end apart: 5, of which 2 were waited for; matrix products, arithmetic and copies ran while one was open for 3% of the time, Pallas kernels for 29%

profile of v2, /device:TPU:0, one launch (start us, length us, event | category | flops | bytes accessed | tf_op | source)
XLA Modules:
  0.0 165.3 jit_solution(2673552861574257034)
XLA Ops:
  0.6 0.0 copy-start.2
  0.6 0.9 copy-done.2
  1.5 0.7 copy-done.6
  2.2 0.7 copy-done.7
  2.9 0.7 copy-done.8
  3.6 0.7 pack.1
  4.3 7.3 %all-to-all-start = ((f32[32,16,128]{2,1,0:T(8,128)}), f32[32,16,128]{2,1,0:T(8,128)S(1)}, u32[]{:S(2)}, u32[]{:S(2)}) async-start(f32[32,16,128]{2,1,0:T(8,128)} %bitcast.6), calls=%async_computation | async-start | bytes 524288 | tf_op jit(solution)/shard_map/all_to_all | solution.py:580
  11.6 0.8 copy.22.rcol_ref
  12.4 0.9 copy.23
  13.3 0.8 copy-done
  14.2 0.7 copy-done.3
  14.9 10.5 %open.1 = (f32[54,32,512]{2,1,0:T(8,128)}, f32[2,2048,128]{2,1,0:T(8,128)}, bf16[256,512]{1,0:T(8,128)(2,1)S(1)}, f32[8,256]{1,0:T(8,128)S(1)}) custom-call(f32[54,32,512]{2,1,0:T(8,128)} %p_ref.1, s32[32,512]{1,0:T(8,128)S(1)} %copy-done, f32[1,512]{1,0:T(1,128)S(1)} %bitcast.32, s32[256,1]{1,0:T(8,128)S(1)} %copy.22.rcol_ref), custom_call_target="tpu_custom_call" | custom-call | tf_op jit(solution)/shard_map/open/pallas_call | solution.py:36
  25.4 0.0 all-to-all-done
  25.4 8.2 %start.1 = (f32[256,128]{1,0:T(8,128)S(1)}, f32[256,128]{1,0:T(8,128)}, s32[256,128]{1,0:T(8,128)S(1)}, s32[128,128]{1,0:T(8,128)S(1)}) custom-call(f32[512,128]{1,0:T(8,128)S(1)} %bitcast.23, f32[8,256]{1,0:T(8,128)S(1)} %get-tuple-element.22.token_ref.rsel_ref), custom_call_target="tpu_custom_call" | custom-call | tf_op jit(solution)/shard_map/start/pallas_call | solution.py:36
  33.6 5.8 %all-to-all-start.1 = ((f32[32,8,128]{2,1,0:T(8,128)}), f32[32,8,128]{2,1,0:T(8,128)S(1)}, u32[]{:S(2)}, u32[]{:S(2)}) async-start(f32[32,8,128]{2,1,0:T(8,128)} %bitcast.8), calls=%async_computation.1 | async-start | bytes 262144 | tf_op jit(solution)/shard_map/all_to_all | solution.py:580
  40.1 0.0 copy-done.9
  40.2 7.4 %all-to-all-done.1 = f32[32,8,128]{2,1,0:T(8,128)S(1)} async-done(((f32[32,8,128]{2,1,0:T(8,128)}), f32[32,8,128]{2,1,0:T(8,128)S(1)}, u32[]{:S(2)}, u32[]{:S(2)}) %all-to-all-start.1) | async-done | bytes 131104 | tf_op jit(solution)/shard_map/all_to_all | solution.py:580
  47.6 11.5 %chem.2 = (f32[2,2048,128]{2,1,0:T(8,128)}, f32[256,128]{1,0:T(8,128)}) custom-call(s32[1]{0:T(128)S(6)} %copy.29.count_ref, f32[256,128]{1,0:T(8,128)S(1)} %bitcast.28, f32[2,2048,128]{2,1,0:T(8,128)} %get-tuple-element.24.a_ref, bf16[256,512]{1,0:T(8,128)(2,1)S(1)} %get-tuple-element.25.ot_ref, f32[8,256]{1,0:T(8,128)S(1)} %get-tuple-element.22.token_ref.rsel_ref, ...), custom_call_target="tpu_custom_call" | custom-call | tf_op jit(solution)/shard_map/chem/pallas_call | solution.py:36
  59.1 2.6 %all-to-all-start.2 = ((f32[32,8,128]{2,1,0:T(8,128)}), f32[32,8,128]{2,1,0:T(8,128)S(1)}, u32[]{:S(2)}, u32[]{:S(2)}) async-start(f32[32,8,128]{2,1,0:T(8,128)} %bitcast.11), calls=%async_computation.2 | async-start | bytes 262144 | tf_op jit(solution)/shard_map/all_to_all | solution.py:580
  61.7 0.0 copy-done.1
  61.7 0.0 copy-done.4
  61.7 0.0 copy-start.11
  61.8 12.1 %middle.1 = (f32[54,32,512]{2,1,0:T(8,128)}, f32[2,2048,128]{2,1,0:T(8,128)}, f32[8,128]{1,0:T(8,128)S(1)}) custom-call(f32[54,32,512]{2,1,0:T(8,128)} %get-tuple-element.21.q_ref, f32[256,128]{1,0:T(8,128)S(1)} %bitcast.29, f32[2,2048,128]{2,1,0:T(8,128)} %get-tuple-element.26.r_ref, bf16[256,512]{1,0:T(8,128)(2,1)S(1)} %get-tuple-element.25.ot_ref, ...), custom_call_target="tpu_custom_call" | custom-call | tf_op jit(solution)/shard_map/middle/pallas_call | solution.py:36
  73.9 0.0 all-to-all-done.2
  73.9 8.7 %again.1 = (f32[256,128]{1,0:T(8,128)S(1)}, f32[256,128]{1,0:T(8,128)}) custom-call(f32[256,128]{1,0:T(8,128)S(1)} %bitcast.30, f32[256,128]{1,0:T(8,128)S(1)} %get-tuple-element.30.g_ref, f32[512,128]{1,0:T(8,128)S(1)} %bitcast.24, s32[256,128]{1,0:T(8,128)S(1)} %get-tuple-element.31.inv_ref, s32[128,128]{1,0:T(8,128)S(1)} %get-tuple-element.32.lab_ref, ...), custom_call_target="tpu_custom_call" | custom-call | tf_op jit(solution)/shard_map/again/pallas_call | solution.py:36
  82.6 5.8 %all-to-all-start.3 = ((f32[32,8,128]{2,1,0:T(8,128)}), f32[32,8,128]{2,1,0:T(8,128)S(1)}, u32[]{:S(2)}, u32[]{:S(2)}) async-start(f32[32,8,128]{2,1,0:T(8,128)} %bitcast.13), calls=%async_computation.3 | async-start | bytes 262144 | tf_op jit(solution)/shard_map/all_to_all | solution.py:580
  88.4 0.5 broadcast.10
  88.9 0.0 copy-done.11
  88.9 0.7 reduce.6
  89.6 0.1 reshape.78
  89.7 0.1 copy.24
  89.8 0.1 reshape.89.lcol_ref
  89.9 5.9 %base.1 = (f32[1024,128]{1,0:T(8,128)}, f32[1,128]{1,0:T(1,128)S(1)}) custom-call(f32[54,32,512]{2,1,0:T(8,128)} %get-tuple-element.27.q_ref, f32[1,512]{1,0:T(1,128)S(1)} %bitcast.34, s32[64,1]{1,0:T(8,128)S(1)} %reshape.89.lcol_ref), custom_call_target="tpu_custom_call" | custom-call | tf_op jit(solution)/shard_map/base/pallas_call | solution.py:36
  95.9 0.7 all-to-all-done.3
  96.6 11.4 %chem.3 = (f32[2,2048,128]{2,1,0:T(8,128)}, f32[256,128]{1,0:T(8,128)S(1)}) custom-call(s32[1]{0:T(128)S(6)} %copy.29.count_ref, f32[256,128]{1,0:T(8,128)S(1)} %bitcast.25, f32[2,2048,128]{2,1,0:T(8,128)} %get-tuple-element.35.a_ref, bf16[256,512]{1,0:T(8,128)(2,1)S(1)} %get-tuple-element.25.ot_ref, f32[8,256]{1,0:T(8,128)S(1)} %get-tuple-element.22.token_ref.rsel_ref, ...), custom_call_target="tpu_custom_call" | custom-call | tf_op jit(solution)/shard_map/chem/pallas_call | solution.py:36
  108.0 5.4 %leave.1 = f32[1280,128]{1,0:T(8,128)S(1)} custom-call(f32[1024,128]{1,0:T(8,128)} %get-tuple-element.28.base_ref, f32[256,128]{1,0:T(8,128)S(1)} %bitcast.26, f32[2,2048,128]{2,1,0:T(8,128)} %get-tuple-element.37.r_ref, f32[1,512]{1,0:T(1,128)S(1)} %bitcast.35, s32[64,1]{1,0:T(8,128)S(1)} %reshape.89.lcol_ref, s32[1,256]{1,0:T(1,128)S(1)} %copy-done.5, ...), custom_call_target="tpu_custom_call" | custom-call | tf_op jit(solution)/shard_map/leave/pallas_call | solution.py:36
  113.4 24.0 %all_to_all.30 = f32[32,40,128]{2,1,0:T(8,128)S(1)} all-to-all(f32[32,40,128]{2,1,0:T(8,128)S(1)} %bitcast.22), channel_id=1, replica_groups=mesh['gx'=4,'gy'=8] {'gx','gy'}, dimensions={0} | all-to-all | bytes 1310720 | tf_op jit(solution)/shard_map/all_to_all | solution.py:580
  137.4 4.6 %last.1 = f32[256,128]{1,0:T(8,128)} custom-call(f32[1280,128]{1,0:T(8,128)S(1)} %bitcast.20, f32[256,128]{1,0:T(8,128)S(1)} %get-tuple-element.39.g_ref, s32[128,128]{1,0:T(8,128)S(1)} %get-tuple-element.32.lab_ref), custom_call_target="tpu_custom_call" | custom-call | tf_op jit(solution)/shard_map/last/pallas_call | solution.py:36
  142.0 2.5 %all-to-all-start.5 = ((f32[32,8,128]{2,1,0:T(8,128)}), f32[32,8,128]{2,1,0:T(8,128)S(1)}, u32[]{:S(2)}, u32[]{:S(2)}) async-start(f32[32,8,128]{2,1,0:T(8,128)} %bitcast.17), calls=%async_computation.5 | async-start | bytes 262144 | tf_op jit(solution)/shard_map/all_to_all | solution.py:580
  144.5 0.0 copy-done.12
  144.6 0.7 reduce.7
  145.2 0.1 reshape.87
  145.3 0.1 copy.27
  145.4 0.1 reshape.90.acol_ref
  145.5 8.5 %settle.1.p_ref = f32[54,32,512]{2,1,0:T(8,128)} custom-call(f32[54,32,512]{2,1,0:T(8,128)} %get-tuple-element.27.q_ref, f32[256,128]{1,0:T(8,128)S(1)} %bitcast.27, f32[2,2048,128]{2,1,0:T(8,128)} %get-tuple-element.37.r_ref, bf16[256,512]{1,0:T(8,128)(2,1)S(1)} %get-tuple-element.25.ot_ref, f32[1,512]{1,0:T(1,128)S(1)} %bitcast.36), custom_call_target="tpu_custom_call" | custom-call | tf_op jit(solution)/shard_map/settle/pallas_call | solution.py:36
  154.0 10.6 %arrive.1 = f32[54,32,512]{2,1,0:T(8,128)} custom-call(f32[54,32,512]{2,1,0:T(8,128)} %settle.1.p_ref, f32[1280,128]{1,0:T(8,128)S(1)} %bitcast.21, s32[64,1]{1,0:T(8,128)S(1)} %reshape.90.acol_ref), custom_call_target="tpu_custom_call" | custom-call | tf_op jit(solution)/shard_map/arrive/pallas_call | solution.py:36
  164.6 0.0 all-to-all-done.5
  164.6 0.7 slice.8
  (16 shorter events, 0.1 us)
Async XLA Ops:
  0.6 0.9 copy-start.2
  1.5 0.7 copy-start.6
  2.2 0.7 copy-start.7
  2.9 0.7 copy-start.8
  3.6 36.5 %copy-start.10 = (bf16[54,256]{1,0:T(8,128)(2,1)S(1)}, bf16[54,256]{1,0:T(8,128)(2,1)}, u32[]{:S(2)}) copy-start(bf16[54,256]{1,0:T(8,128)(2,1)} %param.23) | copy-start | bytes 82948
  3.6 36.6 %copy-start.9 = (bf16[256,256]{1,0:T(8,128)(2,1)S(1)}, bf16[256,256]{1,0:T(8,128)(2,1)}, u32[]{:S(2)}) copy-start(bf16[256,256]{1,0:T(8,128)(2,1)} %param.22) | copy-start | bytes 393220
  4.3 21.1 %all-to-all-start = ((f32[32,16,128]{2,1,0:T(8,128)}), f32[32,16,128]{2,1,0:T(8,128)S(1)}, u32[]{:S(2)}, u32[]{:S(2)}) async-start(f32[32,16,128]{2,1,0:T(8,128)} %bitcast.6), calls=%async_computation | async-start | bytes 524288 | tf_op jit(solution)/shard_map/all_to_all | solution.py:580
  13.3 0.8 copy-start
  14.2 0.7 copy-start.3
  14.9 46.9 %copy-start.1 = (s32[32,512]{1,0:T(8,128)S(1)}, s32[32,512]{1,0:T(8,128)}, u32[]{:S(2)}) copy-start(s32[32,512]{1,0:T(8,128)} %partner_ref.3) | copy-start | bytes 196612
  14.9 46.9 %copy-start.4 = (f32[512]{0:T(512)S(1)}, f32[512]{0:T(512)}, u32[]{:S(2)}) copy-start(f32[512]{0:T(512)} %param.19) | copy-start | bytes 6148
  33.6 14.0 %all-to-all-start.1 = ((f32[32,8,128]{2,1,0:T(8,128)}), f32[32,8,128]{2,1,0:T(8,128)S(1)}, u32[]{:S(2)}, u32[]{:S(2)}) async-start(f32[32,8,128]{2,1,0:T(8,128)} %bitcast.8), calls=%async_computation.1 | async-start | bytes 262144 | tf_op jit(solution)/shard_map/all_to_all | solution.py:580
  59.1 14.8 %all-to-all-start.2 = ((f32[32,8,128]{2,1,0:T(8,128)}), f32[32,8,128]{2,1,0:T(8,128)S(1)}, u32[]{:S(2)}, u32[]{:S(2)}) async-start(f32[32,8,128]{2,1,0:T(8,128)} %bitcast.11), calls=%async_computation.2 | async-start | bytes 262144 | tf_op jit(solution)/shard_map/all_to_all | solution.py:580
  61.7 27.2 %copy-start.11 = (s32[1,64]{1,0:T(1,128)S(1)}, s32[1,64]{1,0:T(1,128)}, u32[]{:S(2)}) copy-start(s32[1,64]{1,0:T(1,128)} %param.26) | copy-start | bytes 772
  73.9 34.1 %copy-start.5 = (s32[1,256]{1,0:T(1,128)S(1)}, s32[1,256]{1,0:T(1,128)}, u32[]{:S(2)}) copy-start(s32[1,256]{1,0:T(1,128)} %rrow_ref.1) | copy-start | bytes 3076
  82.6 14.0 %all-to-all-start.3 = ((f32[32,8,128]{2,1,0:T(8,128)}), f32[32,8,128]{2,1,0:T(8,128)S(1)}, u32[]{:S(2)}, u32[]{:S(2)}) async-start(f32[32,8,128]{2,1,0:T(8,128)} %bitcast.13), calls=%async_computation.3 | async-start | bytes 262144 | tf_op jit(solution)/shard_map/all_to_all | solution.py:580
  108.0 36.5 %copy-start.12 = (s32[1,64]{1,0:T(1,128)S(1)}, s32[1,64]{1,0:T(1,128)}, u32[]{:S(2)}) copy-start(s32[1,64]{1,0:T(1,128)} %param.27) | copy-start | bytes 772
  142.0 22.6 %all-to-all-start.5 = ((f32[32,8,128]{2,1,0:T(8,128)}), f32[32,8,128]{2,1,0:T(8,128)S(1)}, u32[]{:S(2)}, u32[]{:S(2)}) async-start(f32[32,8,128]{2,1,0:T(8,128)} %bitcast.17), calls=%async_computation.5 | async-start | bytes 262144 | tf_op jit(solution)/shard_map/all_to_all | solution.py:580

commit v3 on v2

--- a/solution.py
+++ b/solution.py
@@ -20,35 +20,45 @@
 NN = (((1,), (0,)), ((), ()))
 
 
-def call(body, outs, ins, smem=(), scratch=(), limit=16, name=None, steps=None, blocks=None):
-    blocks = blocks or {}
-
-    def spec(i, shape):
-        if i in smem:
-            return pl.BlockSpec(memory_space=pltpu.SMEM)
-        if steps is None:
-            return pl.BlockSpec(memory_space=pltpu.VMEM)
-        if i in blocks:
-            return pl.BlockSpec(*blocks[i])
-        return pl.BlockSpec(shape, lambda *_: (0,) * len(shape))
-
-    grid = {} if steps is None else {"grid": (steps,)}
+def call(body, outs, ins, smem=(), hbm=(), scratch=(), limit=24, name=None):
+    spaces = {**{i: pltpu.SMEM for i in smem}, **{i: pl.ANY for i in hbm}}
+    ins = [pltpu.with_memory_space_constraint(x, pltpu.HBM) if i in hbm else x for i, x in enumerate(ins)]
     return pl.pallas_call(
         body,
         out_shape=[
             pltpu.HBM(o[0], o[1]) if len(o) > 2 else jax.ShapeDtypeStruct(o[0], o[1]) for o in outs
         ],
-        in_specs=[spec(i, x.shape) for i, x in enumerate(ins)],
-        out_specs=[spec(len(ins) + i, o[0]) for i, o in enumerate(outs)],
+        in_specs=[
+            pl.BlockSpec(memory_space=spaces.get(i, pltpu.VMEM)) for i in range(len(ins))
+        ],
+        out_specs=[
+            pl.BlockSpec(memory_space=pl.ANY if len(o) > 2 else pltpu.VMEM) for o in outs
+        ],
         scratch_shapes=list(scratch),
         compiler_params=pltpu.CompilerParams(vmem_limit_bytes=limit << 20),
         name=name,
-        **grid,
     )(*ins)
 
 
-def far(x):
-    return pltpu.with_memory_space_constraint(x, pltpu.HBM)
+class Stream:
+    def __init__(self, src, dst, sem, size, dim=0):
+        self.src, self.dst, self.sem, self.size, self.dim = src, dst, sem, size, dim
+        self.count = -(-src.shape[dim] // size)
+
+    def copy(self, i, size=None):
+        at = (slice(None),) * self.dim + (pl.ds(i * self.size, size or self.size),)
+        return pltpu.make_async_copy(self.src.at[at], self.dst.at[at], self.sem.at[i])
+
+    def tail(self, i):
+        return min(self.size, self.src.shape[self.dim] - i * self.size)
+
+    def start_all(self):
+        for i in range(self.count):
+            self.copy(i, self.tail(i)).start()
+
+    def wait_all(self, first=0):
+        for i in range(first, self.count):
+            self.copy(i, self.tail(i)).wait()
 
 
 def dot(a, b, dims):
@@ -65,7 +75,7 @@
     return max(k for k in range(1, most + 1) if n % k == 0)
 
 
-def mix(p_ref, partner_ref, q_ref):
+def mix(s0, block, p_ref, partner_ref, q_ref):
     scalars, particles, cells = p_ref.shape
     groups = particles // SUB
     for t in range(cells // LANES):
@@ -86,91 +96,149 @@
                 q_ref[s, pl.ds(j * SUB, SUB), lanes] = x[j] + PAIR_WEIGHT * (mate - x[j])
             return carry
 
-        lax.fori_loop(0, scalars, step, 0, unroll=2)
-
-
-def store_tiles(ref, at, value):
-    for t in range(value.shape[1] // LANES):
-        ref[t, at, :] = value[:, t * LANES : (t + 1) * LANES]
-
-
-def load_tiles(ref, at):
-    return jnp.concatenate([ref[t, at, :] for t in range(ref.shape[0])], axis=1)
-
-
-def list_cells(s0, q_ref, onehot, keep, a_ref, rows):
-    block, particles, cells = q_ref.shape
-    y = dot_split(q_ref[...].reshape(block * particles, cells), onehot, NT) * keep
+        lax.fori_loop(s0, s0 + block, step, 0)
+
+
+def put_scalar(ref, s, value, rows):
+    for o in range(value.shape[0] // SUB):
+        for t in range(value.shape[1] // LANES):
+            part = value[o * SUB : (o + 1) * SUB, t * LANES : (t + 1) * LANES]
+            ref[t, pl.ds(o * rows * SUB + s * SUB, SUB), :] = part
+
+
+def get_scalar(ref, s, rows):
+    octets = ref.shape[1] // (rows * SUB)
+    return jnp.concatenate(
+        [
+            jnp.concatenate(
+                [ref[t, pl.ds(o * rows * SUB + s * SUB, SUB), :] for t in range(ref.shape[0])],
+                axis=1,
+            )
+            for o in range(octets)
+        ],
+        axis=0,
+    )
+
+
+def particle_rows(p, rows):
+    return pl.ds((p >> 3) * (rows * SUB) + (p & (SUB - 1)), rows, stride=SUB)
+
+
+def list_cells(s0, block, q_ref, onehot, keep, a_ref, rows):
+    scalars, particles, cells = q_ref.shape
+    x = q_ref[pl.ds(s0, block)].reshape(block * particles, cells)
+    y = dot_split(x, onehot, NT) * keep
     for i in range(block):
-        at = pl.ds(s0 + i, particles, stride=rows)
-        store_tiles(a_ref, at, y[i * particles : (i + 1) * particles])
+        put_scalar(a_ref, s0 + i, y[i * particles : (i + 1) * particles], rows)
 
 
 def clear_rest(scalars, rows, a_ref):
     particles = a_ref.shape[1] // rows
     zeros = jnp.zeros((particles, a_ref.shape[0] * LANES), F32)
     for s in range(scalars, rows):
-        store_tiles(a_ref, pl.ds(s, particles, stride=rows), zeros)
+        put_scalar(a_ref, s, zeros, rows)
 
 
 def open_body(
-    scalars, rows, p_ref, partner_ref, rate_ref, rcol_ref, q_ref, a_ref, ot_ref, rsel_ref
+    rows,
+    block,
+    p_hbm,
+    partner_ref,
+    rate_ref,
+    rcol_ref,
+    q_hbm,
+    a_hbm,
+    ot_ref,
+    rsel_ref,
+    p_ref,
+    q_ref,
+    a_ref,
+    in_sem,
+    out_sem,
+    a_sem,
 ):
-    block, particles, cells = p_ref.shape
-
-    @pl.when(pl.program_id(0) == 0)
-    def _():
-        onehot = (rcol_ref[...] == lax.broadcasted_iota(I32, ot_ref.shape, 1)).astype(F32)
-        ot_ref[...] = onehot.astype(BF)
-        rate = jnp.broadcast_to(rate_ref[...], (SUB, cells))
-        rsel_ref[...] = dot_split(rate, onehot.astype(BF), NT)
-        clear_rest(scalars, rows, a_ref)
-
-    mix(p_ref, partner_ref, q_ref)
-    s0 = pl.program_id(0) * block
-    list_cells(s0, q_ref, ot_ref[...], 1.0 - rsel_ref[0:1, :], a_ref, rows)
-
-
-def settle_state(s0, q_ref, f_ref, r_ref, ot_ref, rate_ref, out_ref, rows):
-    block, particles, cells = q_ref.shape
+    scalars, particles, cells = p_ref.shape
+    into, out = Stream(p_hbm, p_ref, in_sem, block), Stream(q_ref, q_hbm, out_sem, block)
+    into.start_all()
+    onehot = (rcol_ref[...] == lax.broadcasted_iota(I32, ot_ref.shape, 1)).astype(F32)
+    ot_ref[...] = onehot.astype(BF)
+    rate = jnp.broadcast_to(rate_ref[...], (SUB, cells))
+    rsel_ref[...] = dot_split(rate, onehot.astype(BF), NT)
+    clear_rest(scalars, rows, a_ref)
+
+    def step(b, carry):
+        into.copy(b).wait()
+        mix(b * block, block, p_ref, partner_ref, q_ref)
+        out.copy(b).start()
+        list_cells(b * block, block, q_ref, ot_ref[...], 1.0 - rsel_ref[0:1, :], a_ref, rows)
+        return carry
+
+    lax.fori_loop(0, scalars // block, step, 0)
+    last = pltpu.make_async_copy(a_ref, a_hbm, a_sem)
+    last.start()
+    out.wait_all()
+    last.wait()
+
+
+def settle_block(s0, block, q_ref, f_ref, r_ref, ot_ref, rate_ref, out_ref, rows):
+    scalars, particles, cells = q_ref.shape
     tiles = cells // LANES
     rate = rate_ref[...]
     keep = 1.0 - rate
-    r = jnp.concatenate(
-        [load_tiles(r_ref, pl.ds(s0 + i, particles, stride=rows)) for i in range(block)], axis=0
-    )
+    r = jnp.concatenate([get_scalar(r_ref, s0 + i, rows) for i in range(block)], axis=0)
     spread = dot(r.astype(BF), ot_ref[...], NN)
     for i in range(block):
         f = jnp.concatenate(
             [f_ref[pl.ds((s0 + i) * tiles + t, 1), :] for t in range(tiles)], axis=1
         )
-        out_ref[i] = keep * q_ref[i] + rate * f + spread[i * particles : (i + 1) * particles]
+        out_ref[s0 + i] = (
+            keep * q_ref[s0 + i] + rate * f + spread[i * particles : (i + 1) * particles]
+        )
 
 
 def middle_body(
-    scalars,
     rows,
-    q_ref,
+    block,
+    q_hbm,
     f_ref,
-    r_ref,
+    r_hbm,
     ot_ref,
     rate_ref,
     rsel_ref,
     partner_ref,
-    out_ref,
-    a_ref,
+    out_hbm,
+    a_hbm,
     token_ref,
+    q_ref,
     now_ref,
+    r_ref,
+    in_sem,
+    out_sem,
+    r_sem,
 ):
-    @pl.when(pl.program_id(0) == 0)
-    def _():
-        clear_rest(scalars, rows, a_ref)
-        token_ref[...] = rsel_ref[:, :LANES]
-
-    s0 = pl.program_id(0) * q_ref.shape[0]
-    settle_state(s0, q_ref, f_ref, r_ref, ot_ref, rate_ref, now_ref, rows)
-    mix(now_ref, partner_ref, out_ref)
-    list_cells(s0, out_ref, ot_ref[...], 1.0 - rsel_ref[0:1, :], a_ref, rows)
+    scalars = q_ref.shape[0]
+    into, out = Stream(q_hbm, q_ref, in_sem, block), Stream(q_ref, out_hbm, out_sem, block)
+    first = pltpu.make_async_copy(r_hbm, r_ref, r_sem)
+    first.start()
+    into.start_all()
+    token_ref[...] = rsel_ref[:, :LANES]
+    first.wait()
+
+    def step(b, carry):
+        into.copy(b).wait()
+        s0 = b * block
+        settle_block(s0, block, q_ref, f_ref, r_ref, ot_ref, rate_ref, now_ref, rows)
+        mix(s0, block, now_ref, partner_ref, q_ref)
+        out.copy(b).start()
+        list_cells(s0, block, q_ref, ot_ref[...], 1.0 - rsel_ref[0:1, :], r_ref, rows)
+        return carry
+
+    lax.fori_loop(0, scalars // block, step, 0)
+    clear_rest(scalars, rows, r_ref)
+    last = pltpu.make_async_copy(r_ref, a_hbm, r_sem)
+    last.start()
+    out.wait_all()
+    last.wait()
 
 
 def half_silu(y):
@@ -178,55 +246,91 @@
 
 
 def chem_body(
-    particles,
     count_ref,
     f_ref,
-    a_ref,
+    a_hbm,
     ot_ref,
     rsel_ref,
     w1_ref,
     w2_ref,
     w3_ref,
     token_ref,
+    r_hbm,
+    s_ref,
+    a_ref,
     r_ref,
-    s_ref,
     pull_ref,
-    total_ref,
+    one_a,
+    one_b,
+    two_a,
+    two_b,
+    in_sem,
+    out_sem,
 ):
     tiles = ot_ref.shape[1] // LANES
     rows = f_ref.shape[0] // tiles
     listed = ot_ref.shape[0]
-
-    @pl.when(pl.program_id(0) == 0)
-    def _():
-        f = jnp.concatenate([f_ref[pl.ds(t, rows, stride=tiles), :] for t in range(tiles)], axis=1)
-        pull_ref[...] = rsel_ref[0:1, :] * dot_split(f, ot_ref[...], NT)
-        total_ref[...] = jnp.zeros_like(total_ref)
-
+    particles = a_ref.shape[1] // rows
+    into = Stream(a_hbm, a_ref, in_sem, SUB * rows, 1)
+    out = Stream(r_ref, r_hbm, out_sem, SUB * rows, 1)
+    into.start_all()
+    f = jnp.concatenate([f_ref[pl.ds(t, rows, stride=tiles), :] for t in range(tiles)], axis=1)
+    pull_ref[...] = rsel_ref[0:1, :] * dot_split(f, ot_ref[...], NT)
     live = lax.broadcasted_iota(I32, (1, listed), 1) < count_ref[0]
-    group = divisor(a_ref.shape[1] // rows, 2)
-
-    def step(b, total):
-        pull = pull_ref[...]
-        at = [pl.ds((b * group + i) * rows, rows) for i in range(group)]
-        feed = jnp.concatenate([(load_tiles(a_ref, k) + pull).astype(BF) for k in at], axis=1)
-        one = half_silu(dot(w1_ref[...], feed, NN)).astype(BF)
-        two = half_silu(dot(w2_ref[...], one, NN)).astype(BF)
+
+    def first(g):
+        parts = []
+        for i in range(2):
+            at = particle_rows(2 * g + i, rows)
+            for t in range(listed // LANES):
+                pull = pull_ref[:, t * LANES : (t + 1) * LANES]
+                parts.append((a_ref[t, at, :] + pull).astype(BF))
+        return half_silu(dot(w1_ref[...], jnp.concatenate(parts, axis=1), NN)).astype(BF)
+
+    def second(one):
+        return half_silu(dot(w2_ref[...], one, NN)).astype(BF)
+
+    def third(g, two, total):
         change = dot(w3_ref[...], two, NN).astype(BF).astype(F32)
-        for i, k in enumerate(at):
+        for i in range(2):
             r = jnp.where(live, change[:, i * listed : (i + 1) * listed], 0.0)
-            store_tiles(r_ref, k, r)
+            at = particle_rows(2 * g + i, rows)
+            for t in range(listed // LANES):
+                r_ref[t, at, :] = r[:, t * LANES : (t + 1) * LANES]
             total = total + r
         return total
 
-    total = lax.fori_loop(0, a_ref.shape[1] // (rows * group), step, total_ref[...])
-    total_ref[...] = total
-
-    @pl.when(pl.program_id(0) == pl.num_programs(0) - 1)
-    def _():
-        source = dot_split(total * (1.0 / particles), ot_ref[...], NN)
-        for t in range(tiles):
-            s_ref[pl.ds(t, rows, stride=tiles), :] = source[:, t * LANES : (t + 1) * LANES]
+    def step(g, total, old, new):
+        total = third(g - 2, old[1][...], total)
+        new[1][...] = second(old[0][...])
+        new[0][...] = first(g)
+        return total
+
+    left, right = (one_a, two_a), (one_b, two_b)
+
+    def pair(m, total):
+        total = step(2 * m, total, right, left)
+        return step(2 * m + 1, total, left, right)
+
+    total = jnp.zeros((rows, listed), F32)
+    each = SUB // 4
+    for o in range(particles // SUB):
+        into.copy(o).wait()
+        if o == 0:
+            one_a[...] = first(0)
+            two_b[...] = second(one_a[...])
+            one_b[...] = first(1)
+        total = lax.fori_loop(max(1, o * each), (o + 1) * each, pair, total)
+        if o:
+            out.copy(o - 1).start()
+    last = particles // 2 - 1
+    total = third(last - 1, two_b[...], total)
+    total = third(last, second(one_b[...]), total)
+    out.copy(particles // SUB - 1).start()
+    source = dot_split(total * (1.0 / particles), ot_ref[...], NN)
+    for t in range(tiles):
+        s_ref[pl.ds(t, rows, stride=tiles), :] = source[:, t * LANES : (t + 1) * LANES]
+    out.wait_all()
 
 
 def cell_onehot(col_ref, cells):
@@ -259,12 +363,16 @@
             store(b, None)
 
 
-def base_body(span, q_ref, rate_ref, lcol_ref, out_ref, token_ref):
+def base_body(span, q_hbm, rate_ref, lcol_ref, out_ref, token_ref, q_ref, sem):
+    per = LANES // q_ref.shape[1]
+    into = Stream(q_hbm, q_ref, sem, per)
+    into.start_all()
     scalars, particles, cells = q_ref.shape
     onehot = cell_onehot(lcol_ref, cells)
     keep = 1.0 - rate_ref[...]
 
     def part(s0, count):
+        into.copy(s0 // per, count).wait()
         x = q_ref[pl.ds(s0, count), :, :].reshape(count * particles, cells) * keep
         return split_dot(onehot, x, NT)
 
@@ -282,15 +390,24 @@
     scalars,
     particles,
     devices,
-    base_ref,
+    base_hbm,
     f_ref,
-    r_ref,
+    r_hbm,
     rate_ref,
     lcol_ref,
     rrow_ref,
     source_ref,
     out_ref,
+    base_ref,
+    r_ref,
+    sem,
 ):
+    loads = [
+        pltpu.make_async_copy(r_hbm, r_ref, sem.at[0]),
+        pltpu.make_async_copy(base_hbm, base_ref, sem.at[1]),
+    ]
+    for c in loads:
+        c.start()
     width = source_ref.shape[0] // devices
     stride = out_ref.shape[0] // devices
     for d in range(devices):
@@ -301,12 +418,12 @@
     f = jnp.concatenate([f_ref[pl.ds(t, rows, stride=tiles), :] for t in range(tiles)], axis=1)
     pull = split_dot(cell_onehot(lcol_ref, cells), f * rate_ref[...], NT)
     reacts = (lcol_ref[...] == rrow_ref[...]).astype(F32).astype(BF)
+    for c in loads:
+        c.wait()
 
     def part(s0, count):
         wide = count * particles
-        r = jnp.concatenate(
-            [load_tiles(r_ref, pl.ds(s0 + i, particles, stride=rows)) for i in range(count)], axis=0
-        )
+        r = jnp.concatenate([get_scalar(r_ref, s0 + i, rows) for i in range(count)], axis=0)
         of = lax.broadcasted_iota(I32, (rows, wide), 1) // particles + s0
         mine = (of == lax.broadcasted_iota(I32, (rows, wide), 0)).astype(F32).astype(BF)
         at = pl.ds(s0 * particles // LANES, places, stride=span)
@@ -323,32 +440,76 @@
     leave_blocks(scalars, particles, span, store, part)
 
 
-def settle_body(rows, q_ref, f_ref, r_ref, ot_ref, rate_ref, out_ref):
-    s0 = pl.program_id(0) * q_ref.shape[0]
-    settle_state(s0, q_ref, f_ref, r_ref, ot_ref, rate_ref, out_ref, rows)
-
-
-def arrive_body(span, devices, p_ref, arr_ref, acol_ref, out_ref, hit_ref, taken_ref):
-    per, particles, cells = p_ref.shape
+def settle_body(
+    rows,
+    block,
+    q_hbm,
+    f_ref,
+    r_hbm,
+    ot_ref,
+    rate_ref,
+    out_hbm,
+    token_ref,
+    q_ref,
+    out_ref,
+    r_ref,
+    in_sem,
+    out_sem,
+    r_sem,
+):
+    into, out = Stream(q_hbm, q_ref, in_sem, block), Stream(out_ref, out_hbm, out_sem, block)
+    first = pltpu.make_async_copy(r_hbm, r_ref, r_sem)
+    first.start()
+    into.start_all()
+    token_ref[...] = rate_ref[:, :LANES]
+    first.wait()
+
+    def step(b, carry):
+        into.copy(b).wait()
+        settle_block(b * block, block, q_ref, f_ref, r_ref, ot_ref, rate_ref, out_ref, rows)
+        out.copy(b).start()
+        return carry
+
+    lax.fori_loop(0, q_ref.shape[0] // block, step, 0)
+    out.wait_all()
+
+
+def arrive_body(
+    span, devices, p_hbm, arr_ref, acol_ref, out_hbm, p_ref, out_ref, hit_ref, in_sem, out_sem
+):
+    scalars, particles, cells = p_ref.shape
     places = acol_ref.shape[0]
-    b = pl.program_id(0)
-
-    @pl.when(b == 0)
-    def _():
-        hit = (acol_ref[...] == lax.broadcasted_iota(I32, (places, cells), 1)).astype(F32)
-        hit_ref[...] = hit.astype(BF)
-        taken_ref[...] = jnp.broadcast_to(jnp.sum(hit, axis=0, keepdims=True), taken_ref.shape)
-
+    per = LANES // particles
+    into, out = Stream(p_hbm, p_ref, in_sem, per), Stream(out_ref, out_hbm, out_sem, per)
+    into.start_all()
+    hit = (acol_ref[...] == lax.broadcasted_iota(I32, (places, cells), 1)).astype(F32)
+    hit_ref[...] = hit.astype(BF)
+    taken = jnp.sum(hit, axis=0, keepdims=True) > 0.5
     stride = arr_ref.shape[0] // devices
     count = places // devices
-    first = stride - count * span + b
-    x = jnp.concatenate(
-        [arr_ref[pl.ds(first + c * span, devices, stride=stride), :] for c in range(count)], axis=0
-    ).T
-    y = dot_split(x, hit_ref[...], NN)
-    taken = taken_ref[0:1, :] > 0.5
-    for i in range(per):
-        out_ref[i] = jnp.where(taken, y[i * particles : (i + 1) * particles], p_ref[i])
+
+    def place(b, size):
+        first = stride - count * span + b
+        x = jnp.concatenate(
+            [arr_ref[pl.ds(first + c * span, devices, stride=stride), :] for c in range(count)],
+            axis=0,
+        ).T
+        y = dot_split(x, hit_ref[...], NN)
+        into.copy(b, size).wait()
+        for i in range(size):
+            s = b * per + i
+            out_ref[s] = jnp.where(taken, y[i * particles : (i + 1) * particles], p_ref[s])
+        out.copy(b, size).start()
+
+    def step(b, carry):
+        place(b, per)
+        return carry
+
+    whole = scalars // per
+    lax.fori_loop(0, whole, step, 0)
+    if scalars > whole * per:
+        place(whole, scalars - whole * per)
+    out.wait_all()
 
 
 def stencil(value, speed, bx, by, lanes_y):
@@ -383,22 +544,27 @@
 
 def route(src_ref, first_row, row_step, item_step, items, own, quads, lanes_y, rows, lanes):
     shape = (lanes_y, LANES)
-    out = [[jnp.zeros(shape, F32) for _ in rows] for _ in range(own)]
-
-    def step(y, out):
-        out = [list(o) for o in out]
-        for j in range(items):
-            hits = [r == (j * lanes_y + y) for r in rows]
-            for s in range(own):
-                line = src_ref[pl.ds(first_row + y * row_step + s * quads + j * item_step, 1), :]
-                line = jnp.broadcast_to(line, shape)
-                for k in range(len(rows)):
-                    out[s][k] = jnp.where(
-                        hits[k], jnp.take_along_axis(line, lanes[k], axis=1), out[s][k]
+    out = []
+    for k in range(len(rows)):
+
+        def step(y, acc):
+            for j in range(items):
+                hit = rows[k] == (j * lanes_y + y)
+                at = first_row + y * row_step + j * item_step
+                lines = [src_ref[pl.ds(at + s * quads, 1), :] for s in range(own)]
+                acc = [
+                    jnp.where(
+                        hit,
+                        jnp.take_along_axis(jnp.broadcast_to(v, shape), lanes[k], axis=1),
+                        old,
                     )
-        return tuple(tuple(o) for o in out)
-
-    return lax.fori_loop(0, lanes_y, step, tuple(tuple(o) for o in out), unroll=2)
+                    for v, old in zip(lines, acc)
+                ]
+            return tuple(acc)
+
+        zero = tuple(jnp.zeros(shape, F32) for _ in range(own))
+        out.append(lax.fori_loop(0, lanes_y, step, zero, unroll=min(lanes_y, 8)))
+    return [[out[k][s] for k in range(len(rows))] for s in range(own)]
 
 
 def load_rows(ref, offset, stride, count):
@@ -527,7 +693,7 @@
     send_filtered(dims, out_ref, inv_ref, f_ref)
 
 
-def last_body(dims, s_ref, g_ref, lab_ref, out_ref):
+def last_body(dims, s_ref, g_ref, lab_ref, token_ref, out_ref):
     add_source(dims, s_ref, g_ref, lab_ref, out_ref)
 
 
@@ -592,20 +758,22 @@
     state_shape = (scalars, heads, cells)
     listed_shape = (listed // LANES, heads * rows, LANES)
     block = divisor(scalars, 6)
-    some = ((block, heads, cells), lambda i: (i, 0, 0))
-    turn = divisor(heads, 8)
-    part = ((listed // LANES, turn * rows, LANES), lambda i: (0, i, 0))
+    octets = heads // SUB
+    state_vmem = pltpu.VMEM(state_shape, F32)
+    listed_vmem = pltpu.VMEM(listed_shape, F32)
+    dma = pltpu.SemaphoreType.DMA
+    per_block = dma((scalars // block,))
     q, a, ot, rsel = call(
-        functools.partial(open_body, scalars, rows),
+        functools.partial(open_body, rows, block),
         [
             (state_shape, F32, True),
             (listed_shape, F32, True),
             ((listed, cells), BF),
             ((SUB, listed), F32),
         ],
-        [far(particles), partner, rate, rcol],
-        steps=scalars // block,
-        blocks={0: some, 4: some},
+        [particles, partner, rate, rcol],
+        hbm=(0,),
+        scratch=[state_vmem, state_vmem, listed_vmem, per_block, per_block, dma],
         name="open",
     )
     grid, sent, inv, lab = call(
@@ -621,14 +789,16 @@
     )
 
     def chemistry(f, a, token):
+        pair = pltpu.VMEM((hidden, 2 * listed), BF)
         return call(
-            functools.partial(chem_body, heads),
+            chem_body,
             [(listed_shape, F32, True), ((flat, LANES), F32)],
-            [react_count, f, far(a), ot, rsel, w1, w2, w3, token],
+            [react_count, f, a, ot, rsel, w1, w2, w3, token],
             smem=(0,),
-            scratch=[pltpu.VMEM((rows, listed), F32), pltpu.VMEM((rows, listed), F32)],
-            steps=heads // turn,
-            blocks={2: part, 9: part},
+            hbm=(2,),
+            scratch=[listed_vmem, listed_vmem, pltpu.VMEM((rows, listed), F32)]
+            + [pair] * 4
+            + [dma((octets,)), dma((octets,))],
             name="chem",
         )
 
@@ -642,12 +812,11 @@
         if substep < SUBSTEPS - 1:
             home = exchange(source)
             q, a, token = call(
-                functools.partial(middle_body, scalars, rows),
+                functools.partial(middle_body, rows, block),
                 [(state_shape, F32, True), (listed_shape, F32, True), ((SUB, LANES), F32)],
-                [far(q), f, far(change), ot, rate, rsel, partner],
-                scratch=[pltpu.VMEM((block, heads, cells), F32)],
-                steps=scalars // block,
-                blocks={0: some, 7: some},
+                [q, f, change, ot, rate, rsel, partner],
+                hbm=(0, 2),
+                scratch=[state_vmem, state_vmem, listed_vmem, per_block, per_block, dma],
                 name="middle",
             )
             grid, sent = call(
@@ -660,37 +829,49 @@
         if substep == SUBSTEPS - 2:
             base, token = call(
                 functools.partial(base_body, span),
-                [((places * span, LANES), F32, True), ((1, LANES), F32)],
-                [far(q), rate, lcol],
+                [((places * span, LANES), F32), ((1, LANES), F32)],
+                [q, rate, lcol],
+                hbm=(0,),
+                scratch=[state_vmem, dma((-(-scalars // per),))],
                 name="base",
             )
     (leaving,) = call(
         functools.partial(leave_body, rows, span, scalars, heads, devices),
         [((flat + places * span, LANES), F32)],
-        [far(base), f, far(change), rate, lcol, react_slots, source],
+        [base, f, change, rate, lcol, react_slots, source],
+        hbm=(0, 2),
+        scratch=[pltpu.VMEM((places * span, LANES), F32), listed_vmem, dma((2,))],
         name="leave",
     )
     moved = exchange(leaving)
+    state, token = call(
+        functools.partial(settle_body, rows, block),
+        [(state_shape, F32, True), ((1, LANES), F32)],
+        [q, f, change, ot, rate],
+        hbm=(0, 2),
+        scratch=[state_vmem, state_vmem, listed_vmem, per_block, per_block, dma],
+        name="settle",
+    )
     (grid,) = call(
-        functools.partial(last_body, dims), [((flat, LANES), F32)], [moved, grid, lab], name="last"
+        functools.partial(last_body, dims),
+        [((flat, LANES), F32)],
+        [moved, grid, lab, token],
+        name="last",
     )
     grid_out = exchange(grid).reshape(rows, bx, by, nz)[:scalars]
-    (state,) = call(
-        functools.partial(settle_body, rows),
-        [(state_shape, F32, True)],
-        [far(q), f, far(change), ot, rate],
-        steps=scalars // block,
-        blocks={0: some, 5: some},
-        name="settle",
-    )
-    four = ((per, heads, cells), lambda i: (i, 0, 0))
+    steps = -(-scalars // per)
     (state,) = call(
         functools.partial(arrive_body, span, devices),
         [(state_shape, F32, True)],
-        [far(state), moved, acol],
-        scratch=[pltpu.VMEM((places, cells), BF), pltpu.VMEM((SUB, cells), F32)],
-        steps=-(-scalars // per),
-        blocks={0: four, 3: four},
+        [state, moved, acol],
+        hbm=(0,),
+        scratch=[
+            state_vmem,
+            state_vmem,
+            pltpu.VMEM((places, cells), BF),
+            dma((steps,)),
+            dma((steps,)),
+        ],
         name="arrive",
     )
     return (grid_out, state)

time: 167 us -> 134 us (0.80)
  Pallas kernels: 98.3 us -> 68.8 us
  blocking collectives: 24 us -> 0 us
  waiting for transfers between devices: 8.17 us -> 24.2 us
  starting transfers between devices: 24.1 us -> 28.3 us
    pallas_call x12, Pallas kernels: 98.3 us -> 68.8 us  [call(): pl.pallas_call(body, out_shape=[pltpu.HBM(o[0], o[1]) if len(o) > 2 else...]
    all_to_all x1 -> x0, blocking collectives: 24 us -> none  [exchange(): lax.all_to_all(x, both, split_axis=0, concat_axis=0, tiled=True)]
    all_to_all x5 -> x6, waiting for transfers between devices: 8.17 us -> 24.2 us  [exchange(): lax.all_to_all(x, both, split_axis=0, concat_axis=0, tiled=True)]
    all_to_all x5 -> x6, starting transfers between devices: 24.1 us -> 28.3 us  [exchange(): lax.all_to_all(x, both, split_axis=0, concat_axis=0, tiled=True)]
    unnamed x28 -> x30, local copies, waits for them, and re-layouts: 5.87 us -> 6.66 us
  transfers between devices with their start and end apart: 5 -> 6, of which waited for: 2 -> 4; matrix products, arithmetic and copies ran while one was open for 3% -> 3% of each run, Pallas kernels for 29% -> 27%
where the time goes in v3:
time: 134 us; the launch traced here: 133 us
  Pallas kernels  68.8 us (51%)
  starting transfers between devices  28.3 us (21%)
  waiting for transfers between devices  24.2 us (18%)
  local copies, waits for them, and re-layouts  8.71 us (7%)
  between operations  1.57 us (1%)
  other arithmetic  1.37 us (1%)
    pallas_call x12, Pallas kernels, call(): pl.pallas_call(body, out_shape=[pltpu.HBM(o[0], o[1]) if len(o) > 2 else...  68.8 us
    all_to_all x6, starting transfers between devices, exchange(): lax.all_to_all(x, both, split_axis=0, concat_axis=0, tiled=True)  28.3 us
    all_to_all x6, waiting for transfers between devices, exchange(): lax.all_to_all(x, both, split_axis=0, concat_axis=0, tiled=True)  24.2 us
    unnamed x30, local copies, waits for them, and re-layouts  6.66 us
  transfers between devices with their start and end apart: 6, of which 4 were waited for; matrix products, arithmetic and copies ran while one was open for 3% of the time, Pallas kernels for 27%

profile of v3, /device:TPU:0, one launch (start us, length us, event | category | flops | bytes accessed | tf_op | source)
XLA Modules:
  0.0 133.0 jit_solution(16936525269195514296)
XLA Ops:
  0.6 0.0 copy-start.3
  0.6 0.9 copy-done.3
  1.5 0.7 copy-done.7
  2.2 0.7 copy-done.8
  2.9 0.7 copy-done.9
  3.6 0.7 pack.1
  4.3 7.3 %all-to-all-start = ((f32[32,16,128]{2,1,0:T(8,128)}), f32[32,16,128]{2,1,0:T(8,128)S(1)}, u32[]{:S(2)}, u32[]{:S(2)}) async-start(f32[32,16,128]{2,1,0:T(8,128)} %bitcast.6), calls=%async_computation | async-start | bytes 524288 | tf_op jit(solution)/shard_map/all_to_all | solution.py:746
  11.6 0.8 copy.22.rcol_ref
  12.4 0.9 copy.23
  13.3 0.8 copy-done.1
  14.2 0.7 copy-done.4
  14.9 8.4 %open.1 = (f32[54,32,512]{2,1,0:T(8,128)}, f32[2,2048,128]{2,1,0:T(8,128)}, bf16[256,512]{1,0:T(8,128)(2,1)S(1)}, f32[8,256]{1,0:T(8,128)S(1)}) custom-call(f32[54,32,512]{2,1,0:T(8,128)} %p_hbm.1, s32[32,512]{1,0:T(8,128)S(1)} %copy-done.1, f32[1,512]{1,0:T(1,128)S(1)} %bitcast.31, s32[256,1]{1,0:T(8,128)S(1)} %copy.22.rcol_ref), custom_call_target="tpu_custom_call" | custom-call | tf_op jit(solution)/shard_map/open/pallas_call | solution.py:26
  23.3 0.0 all-to-all-done
  23.3 5.7 %start.1 = (f32[256,128]{1,0:T(8,128)S(1)}, f32[256,128]{1,0:T(8,128)}, s32[256,128]{1,0:T(8,128)S(1)}, s32[128,128]{1,0:T(8,128)S(1)}) custom-call(f32[512,128]{1,0:T(8,128)S(1)} %bitcast.22, f32[8,256]{1,0:T(8,128)S(1)} %get-tuple-element.24.token_ref.rsel_ref), custom_call_target="tpu_custom_call" | custom-call | tf_op jit(solution)/shard_map/start/pallas_call | solution.py:26
  28.9 5.8 %all-to-all-start.1 = ((f32[32,8,128]{2,1,0:T(8,128)}), f32[32,8,128]{2,1,0:T(8,128)S(1)}, u32[]{:S(2)}, u32[]{:S(2)}) async-start(f32[32,8,128]{2,1,0:T(8,128)} %bitcast.8), calls=%async_computation.1 | async-start | bytes 262144 | tf_op jit(solution)/shard_map/all_to_all | solution.py:746
  35.5 0.0 copy-done.11
  35.5 7.4 %all-to-all-done.1 = f32[32,8,128]{2,1,0:T(8,128)S(1)} async-done(((f32[32,8,128]{2,1,0:T(8,128)}), f32[32,8,128]{2,1,0:T(8,128)S(1)}, u32[]{:S(2)}, u32[]{:S(2)}) %all-to-all-start.1) | async-done | bytes 131104 | tf_op jit(solution)/shard_map/all_to_all | solution.py:746
  43.0 8.4 %chem.2 = (f32[2,2048,128]{2,1,0:T(8,128)}, f32[256,128]{1,0:T(8,128)}) custom-call(s32[1]{0:T(128)S(6)} %copy.29.count_ref, f32[256,128]{1,0:T(8,128)S(1)} %bitcast.27, f32[2,2048,128]{2,1,0:T(8,128)} %get-tuple-element.26.a_hbm, bf16[256,512]{1,0:T(8,128)(2,1)S(1)} %get-tuple-element.27.ot_ref, f32[8,256]{1,0:T(8,128)S(1)} %get-tuple-element.24.token_ref.rsel_ref, ...), custom_call_target="tpu_custom_call" | custom-call | tf_op jit(solution)/shard_map/chem/pallas_call | solution.py:26
  51.4 2.6 %all-to-all-start.2 = ((f32[32,8,128]{2,1,0:T(8,128)}), f32[32,8,128]{2,1,0:T(8,128)S(1)}, u32[]{:S(2)}, u32[]{:S(2)}) async-start(f32[32,8,128]{2,1,0:T(8,128)} %bitcast.11), calls=%async_computation.2 | async-start | bytes 262144 | tf_op jit(solution)/shard_map/all_to_all | solution.py:746
  54.0 0.0 copy-start.12
  54.0 11.9 %middle.1 = (f32[54,32,512]{2,1,0:T(8,128)}, f32[2,2048,128]{2,1,0:T(8,128)}, f32[8,128]{1,0:T(8,128)S(1)}) custom-call(f32[54,32,512]{2,1,0:T(8,128)} %get-tuple-element.23.q_hbm, f32[256,128]{1,0:T(8,128)S(1)} %bitcast.28, f32[2,2048,128]{2,1,0:T(8,128)} %get-tuple-element.28.r_hbm, bf16[256,512]{1,0:T(8,128)(2,1)S(1)} %get-tuple-element.27.ot_ref, ...), custom_call_target="tpu_custom_call" | custom-call | tf_op jit(solution)/shard_map/middle/pallas_call | solution.py:26
  66.0 0.0 all-to-all-done.2
  66.0 0.0 copy-start.6
  66.0 3.6 %again.1 = (f32[256,128]{1,0:T(8,128)S(1)}, f32[256,128]{1,0:T(8,128)}) custom-call(f32[256,128]{1,0:T(8,128)S(1)} %bitcast.29, f32[256,128]{1,0:T(8,128)S(1)} %get-tuple-element.32.g_ref, f32[512,128]{1,0:T(8,128)S(1)} %bitcast.23, s32[256,128]{1,0:T(8,128)S(1)} %get-tuple-element.33.inv_ref, s32[128,128]{1,0:T(8,128)S(1)} %get-tuple-element.34.lab_ref, ...), custom_call_target="tpu_custom_call" | custom-call | tf_op jit(solution)/shard_map/again/pallas_call | solution.py:26
  69.6 5.8 %all-to-all-start.3 = ((f32[32,8,128]{2,1,0:T(8,128)}), f32[32,8,128]{2,1,0:T(8,128)S(1)}, u32[]{:S(2)}, u32[]{:S(2)}) async-start(f32[32,8,128]{2,1,0:T(8,128)} %bitcast.13), calls=%async_computation.3 | async-start | bytes 262144 | tf_op jit(solution)/shard_map/all_to_all | solution.py:746
  75.5 0.5 broadcast.10
  76.0 0.7 reduce.6
  76.6 0.1 reshape.78
  76.7 0.1 copy.24
  76.8 0.1 reshape.89.lcol_ref
  76.9 4.2 %base.1 = (f32[1024,128]{1,0:T(8,128)S(1)}, f32[1,128]{1,0:T(1,128)S(1)}) custom-call(f32[54,32,512]{2,1,0:T(8,128)} %get-tuple-element.29.q_hbm, f32[1,512]{1,0:T(1,128)S(1)} %bitcast.33, s32[64,1]{1,0:T(8,128)S(1)} %reshape.89.lcol_ref), custom_call_target="tpu_custom_call" | custom-call | tf_op jit(solution)/shard_map/base/pallas_call | solution.py:26
  81.1 0.8 copy-done
  81.9 1.7 %all-to-all-done.3 = f32[32,8,128]{2,1,0:T(8,128)S(1)} async-done(((f32[32,8,128]{2,1,0:T(8,128)}), f32[32,8,128]{2,1,0:T(8,128)S(1)}, u32[]{:S(2)}, u32[]{:S(2)}) %all-to-all-start.3) | async-done | bytes 131104 | tf_op jit(solution)/shard_map/all_to_all | solution.py:746
  83.6 7.8 %chem.3 = (f32[2,2048,128]{2,1,0:T(8,128)}, f32[256,128]{1,0:T(8,128)S(1)}) custom-call(s32[1]{0:T(128)S(6)} %copy.29.count_ref, f32[256,128]{1,0:T(8,128)S(1)} %bitcast.24, f32[2,2048,128]{2,1,0:T(8,128)} %get-tuple-element.37.a_hbm, bf16[256,512]{1,0:T(8,128)(2,1)S(1)} %get-tuple-element.27.ot_ref, f32[8,256]{1,0:T(8,128)S(1)} %get-tuple-element.24.token_ref.rsel_ref, ...), custom_call_target="tpu_custom_call" | custom-call | tf_op jit(solution)/shard_map/chem/pallas_call | solution.py:26
  91.4 4.9 %leave.1 = f32[1280,128]{1,0:T(8,128)} custom-call(f32[1024,128]{1,0:T(8,128)} %copy-done, f32[256,128]{1,0:T(8,128)S(1)} %bitcast.25, f32[2,2048,128]{2,1,0:T(8,128)} %get-tuple-element.39.r_hbm, f32[1,512]{1,0:T(1,128)S(1)} %bitcast.34, s32[64,1]{1,0:T(8,128)S(1)} %reshape.89.lcol_ref, s32[1,256]{1,0:T(1,128)S(1)} %copy-done.6, ...), custom_call_target="tpu_custom_call" | custom-call | tf_op jit(solution)/shard_map/leave/pallas_call | solution.py:26
  96.3 4.1 %all-to-all-start.4 = ((f32[32,40,128]{2,1,0:T(8,128)}), f32[32,40,128]{2,1,0:T(8,128)S(1)}, u32[]{:S(2)}, u32[]{:S(2)}) async-start(f32[32,40,128]{2,1,0:T(8,128)} %bitcast.15), calls=%async_computation.4 | async-start | bytes 1310720 | tf_op jit(solution)/shard_map/all_to_all | solution.py:746
  100.5 0.0 copy-start.13
  100.5 5.4 %settle.1 = (f32[54,32,512]{2,1,0:T(8,128)}, f32[1,128]{1,0:T(1,128)S(1)}) custom-call(f32[54,32,512]{2,1,0:T(8,128)} %get-tuple-element.29.q_hbm, f32[256,128]{1,0:T(8,128)S(1)} %bitcast.26, f32[2,2048,128]{2,1,0:T(8,128)} %get-tuple-element.39.r_hbm, bf16[256,512]{1,0:T(8,128)(2,1)S(1)} %get-tuple-element.27.ot_ref, f32[1,512]{1,0:T(1,128)S(1)} %bitcast.35), custom_call_target="tpu_custom_call" | custom-call | tf_op jit(solution)/shard_map/settle/pallas_call | solution.py:26
  105.9 13.6 %all-to-all-done.4 = f32[32,40,128]{2,1,0:T(8,128)S(1)} async-done(((f32[32,40,128]{2,1,0:T(8,128)}), f32[32,40,128]{2,1,0:T(8,128)S(1)}, u32[]{:S(2)}, u32[]{:S(2)}) %all-to-all-start.4) | async-done | bytes 655392 | tf_op jit(solution)/shard_map/all_to_all | solution.py:746
  119.5 2.1 %last.1 = f32[256,128]{1,0:T(8,128)} custom-call(f32[1280,128]{1,0:T(8,128)S(1)} %bitcast.20, f32[256,128]{1,0:T(8,128)S(1)} %get-tuple-element.41.g_ref, s32[128,128]{1,0:T(8,128)S(1)} %get-tuple-element.34.lab_ref, f32[1,128]{1,0:T(1,128)S(1)} %get-tuple-element.42.token_ref), custom_call_target="tpu_custom_call" | custom-call | tf_op jit(solution)/shard_map/last/pallas_call | solution.py:26
  121.6 2.6 %all-to-all-start.5 = ((f32[32,8,128]{2,1,0:T(8,128)}), f32[32,8,128]{2,1,0:T(8,128)S(1)}, u32[]{:S(2)}, u32[]{:S(2)}) async-start(f32[32,8,128]{2,1,0:T(8,128)} %bitcast.17), calls=%async_computation.5 | async-start | bytes 262144 | tf_op jit(solution)/shard_map/all_to_all | solution.py:746
  124.2 0.7 reduce.7
  124.8 0.1 reshape.87
  124.9 0.1 copy.27
  125.0 0.1 reshape.90.acol_ref
  125.1 5.7 %arrive.1 = f32[54,32,512]{2,1,0:T(8,128)} custom-call(f32[54,32,512]{2,1,0:T(8,128)} %get-tuple-element.43.p_hbm, f32[1280,128]{1,0:T(8,128)S(1)} %bitcast.21, s32[64,1]{1,0:T(8,128)S(1)} %reshape.90.acol_ref), custom_call_target="tpu_custom_call" | custom-call | tf_op jit(solution)/shard_map/arrive/pallas_call | solution.py:26
  130.8 1.5 %all-to-all-done.5 = f32[32,8,128]{2,1,0:T(8,128)S(1)} async-done(((f32[32,8,128]{2,1,0:T(8,128)}), f32[32,8,128]{2,1,0:T(8,128)S(1)}, u32[]{:S(2)}, u32[]{:S(2)}) %all-to-all-start.5) | async-done | bytes 131104 | tf_op jit(solution)/shard_map/all_to_all | solution.py:746
  132.3 0.7 slice.8
  (19 shorter events, 0.1 us)
Async XLA Ops:
  0.6 0.9 copy-start.3
  1.5 0.7 copy-start.7
  2.2 0.7 copy-start.8
  2.9 0.7 copy-start.9
  3.6 31.9 %copy-start.11 = (bf16[54,256]{1,0:T(8,128)(2,1)S(1)}, bf16[54,256]{1,0:T(8,128)(2,1)}, u32[]{:S(2)}) copy-start(bf16[54,256]{1,0:T(8,128)(2,1)} %param.23) | copy-start | bytes 82948
  3.6 31.9 %copy-start.10 = (bf16[256,256]{1,0:T(8,128)(2,1)S(1)}, bf16[256,256]{1,0:T(8,128)(2,1)}, u32[]{:S(2)}) copy-start(bf16[256,256]{1,0:T(8,128)(2,1)} %param.22) | copy-start | bytes 393220
  4.3 19.0 %all-to-all-start = ((f32[32,16,128]{2,1,0:T(8,128)}), f32[32,16,128]{2,1,0:T(8,128)S(1)}, u32[]{:S(2)}, u32[]{:S(2)}) async-start(f32[32,16,128]{2,1,0:T(8,128)} %bitcast.6), calls=%async_computation | async-start | bytes 524288 | tf_op jit(solution)/shard_map/all_to_all | solution.py:746
  13.3 0.8 copy-start.1
  14.2 0.7 copy-start.4
  14.9 39.1 %copy-start.2 = (s32[32,512]{1,0:T(8,128)S(1)}, s32[32,512]{1,0:T(8,128)}, u32[]{:S(2)}) copy-start(s32[32,512]{1,0:T(8,128)} %partner_ref.3) | copy-start | bytes 196612
  14.9 39.1 %copy-start.5 = (f32[512]{0:T(512)S(1)}, f32[512]{0:T(512)}, u32[]{:S(2)}) copy-start(f32[512]{0:T(512)} %param.19) | copy-start | bytes 6148
  28.9 14.0 %all-to-all-start.1 = ((f32[32,8,128]{2,1,0:T(8,128)}), f32[32,8,128]{2,1,0:T(8,128)S(1)}, u32[]{:S(2)}, u32[]{:S(2)}) async-start(f32[32,8,128]{2,1,0:T(8,128)} %bitcast.8), calls=%async_computation.1 | async-start | bytes 262144 | tf_op jit(solution)/shard_map/all_to_all | solution.py:746
  51.4 14.6 %all-to-all-start.2 = ((f32[32,8,128]{2,1,0:T(8,128)}), f32[32,8,128]{2,1,0:T(8,128)S(1)}, u32[]{:S(2)}, u32[]{:S(2)}) async-start(f32[32,8,128]{2,1,0:T(8,128)} %bitcast.11), calls=%async_computation.2 | async-start | bytes 262144 | tf_op jit(solution)/shard_map/all_to_all | solution.py:746
  54.0 22.0 %copy-start.12 = (s32[1,64]{1,0:T(1,128)S(1)}, s32[1,64]{1,0:T(1,128)}, u32[]{:S(2)}) copy-start(s32[1,64]{1,0:T(1,128)} %param.26) | copy-start | bytes 772
  66.0 25.4 %copy-start.6 = (s32[1,256]{1,0:T(1,128)S(1)}, s32[1,256]{1,0:T(1,128)}, u32[]{:S(2)}) copy-start(s32[1,256]{1,0:T(1,128)} %rrow_ref.1) | copy-start | bytes 3076
  69.6 14.0 %all-to-all-start.3 = ((f32[32,8,128]{2,1,0:T(8,128)}), f32[32,8,128]{2,1,0:T(8,128)S(1)}, u32[]{:S(2)}, u32[]{:S(2)}) async-start(f32[32,8,128]{2,1,0:T(8,128)} %bitcast.13), calls=%async_computation.3 | async-start | bytes 262144 | tf_op jit(solution)/shard_map/all_to_all | solution.py:746
  81.1 0.8 copy-start
  96.3 23.2 %all-to-all-start.4 = ((f32[32,40,128]{2,1,0:T(8,128)}), f32[32,40,128]{2,1,0:T(8,128)S(1)}, u32[]{:S(2)}, u32[]{:S(2)}) async-start(f32[32,40,128]{2,1,0:T(8,128)} %bitcast.15), calls=%async_computation.4 | async-start | bytes 1310720 | tf_op jit(solution)/shard_map/all_to_all | solution.py:746
  100.5 23.7 %copy-start.13 = (s32[1,64]{1,0:T(1,128)S(1)}, s32[1,64]{1,0:T(1,128)}, u32[]{:S(2)}) copy-start(s32[1,64]{1,0:T(1,128)} %param.27) | copy-start | bytes 772
  121.6 10.7 %all-to-all-start.5 = ((f32[32,8,128]{2,1,0:T(8,128)}), f32[32,8,128]{2,1,0:T(8,128)S(1)}, u32[]{:S(2)}, u32[]{:S(2)}) async-start(f32[32,8,128]{2,1,0:T(8,128)} %bitcast.17), calls=%async_computation.5 | async-start | bytes 262144 | tf_op jit(solution)/shard_map/all_to_all | solution.py:746

commit v4 on v3

--- a/solution.py
+++ b/solution.py
@@ -65,10 +65,15 @@
     return lax.dot_general(a, b, dims, preferred_element_type=F32)
 
 
+def halves(x):
+    high = x.astype(BF)
+    return high, (x - high.astype(F32)).astype(BF)
+
+
 def dot_split(x, onehot, dims):
-    high = x.astype(BF)
-    low = (x - high.astype(F32)).astype(BF)
-    return dot(high, onehot, dims) + dot(low, onehot, dims)
+    high, low = halves(x)
+    y = dot(jnp.concatenate([high, low], axis=0), onehot, dims)
+    return y[: x.shape[0]] + y[x.shape[0] :]
 
 
 def divisor(n, most):
@@ -132,6 +137,67 @@
         put_scalar(a_ref, s0 + i, y[i * particles : (i + 1) * particles], rows)
 
 
+def list_body(
+    rows,
+    span,
+    q_hbm,
+    rate_ref,
+    rsel_ref,
+    ot_ref,
+    lcol_ref,
+    a_hbm,
+    base_hbm,
+    token_ref,
+    q_ref,
+    a_ref,
+    base_ref,
+    in_sem,
+    out_sem,
+):
+    scalars, particles, cells = q_ref.shape
+    per = LANES // particles
+    into = Stream(q_hbm, q_ref, in_sem, per)
+    into.start_all()
+    token_ref[...] = rate_ref[:, :LANES]
+    leaves = cell_onehot(lcol_ref, cells)
+    places = lcol_ref.shape[0]
+    keep = 1.0 - rate_ref[...]
+
+    def part(b, count):
+        into.copy(b, count).wait()
+        x = q_ref[pl.ds(b * per, count)].reshape(count * particles, cells) * keep
+        high, low = halves(x)
+        y = dot(jnp.concatenate([high, low], axis=0), ot_ref[...], NT)
+        half = count * particles
+        y = y[:half] + y[half:]
+        for i in range(count):
+            put_scalar(a_ref, b * per + i, y[i * particles : (i + 1) * particles], rows)
+        base_ref[pl.ds(b, places, stride=span), :half] = dot(leaves, high, NT) + dot(
+            leaves, low, NT
+        )
+
+    def step(b, carry):
+        part(b, per)
+        return carry
+
+    whole = scalars // per
+    lax.fori_loop(0, whole, step, 0)
+    zeros = jnp.zeros((places, LANES), F32)
+    for b in range(whole, span):
+        base_ref[pl.ds(b, places, stride=span), :] = zeros
+    if scalars > whole * per:
+        part(whole, scalars - whole * per)
+    clear_rest(scalars, rows, a_ref)
+    copies = [
+        pltpu.make_async_copy(a_ref, a_hbm, out_sem.at[0]),
+        pltpu.make_async_copy(base_ref, base_hbm, out_sem.at[1]),
+    ]
+    for c in copies:
+        c.start()
+    for c in copies:
+        c.wait()
+
+
 def clear_rest(scalars, rows, a_ref):
     particles = a_ref.shape[1] // rows
     zeros = jnp.zeros((particles, a_ref.shape[0] * LANES), F32)
@@ -143,9 +209,9 @@
     rows,
     block,
     p_hbm,
-    partner_ref,
-    rate_ref,
-    rcol_ref,
+    partner_hbm,
+    rate_hbm,
+    list_hbm,
     q_hbm,
     a_hbm,
     ot_ref,
@@ -153,14 +219,30 @@
     p_ref,
     q_ref,
     a_ref,
+    partner_ref,
+    rate_ref,
+    list_ref,
     in_sem,
     out_sem,
     a_sem,
+    few_sem,
 ):
     scalars, particles, cells = p_ref.shape
     into, out = Stream(p_hbm, p_ref, in_sem, block), Stream(q_ref, q_hbm, out_sem, block)
+    few = [
+        pltpu.make_async_copy(src, dst, few_sem.at[i])
+        for i, (src, dst) in enumerate(
+            [(list_hbm, list_ref), (rate_hbm, rate_ref), (partner_hbm, partner_ref)]
+        )
+    ]
+    for c in few:
+        c.start()
     into.start_all()
-    onehot = (rcol_ref[...] == lax.broadcasted_iota(I32, ot_ref.shape, 1)).astype(F32)
+    for c in few:
+        c.wait()
+    column = jnp.broadcast_to(list_ref[...].astype(F32), (SUB, list_ref.shape[1])).T[:, :1]
+    cell = lax.broadcasted_iota(I32, ot_ref.shape, 1).astype(F32)
+    onehot = (column == cell).astype(F32)
     ot_ref[...] = onehot.astype(BF)
     rate = jnp.broadcast_to(rate_ref[...], (SUB, cells))
     rsel_ref[...] = dot_split(rate, onehot.astype(BF), NT)
@@ -204,10 +286,8 @@
     r_hbm,
     ot_ref,
     rate_ref,
-    rsel_ref,
     partner_ref,
     out_hbm,
-    a_hbm,
     token_ref,
     q_ref,
     now_ref,
@@ -221,7 +301,7 @@
     first = pltpu.make_async_copy(r_hbm, r_ref, r_sem)
     first.start()
     into.start_all()
-    token_ref[...] = rsel_ref[:, :LANES]
+    token_ref[...] = rate_ref[:, :LANES]
     first.wait()
 
     def step(b, carry):
@@ -230,22 +310,19 @@
         settle_block(s0, block, q_ref, f_ref, r_ref, ot_ref, rate_ref, now_ref, rows)
         mix(s0, block, now_ref, partner_ref, q_ref)
         out.copy(b).start()
-        list_cells(s0, block, q_ref, ot_ref[...], 1.0 - rsel_ref[0:1, :], r_ref, rows)
         return carry
 
     lax.fori_loop(0, scalars // block, step, 0)
-    clear_rest(scalars, rows, r_ref)
-    last = pltpu.make_async_copy(r_ref, a_hbm, r_sem)
-    last.start()
     out.wait_all()
-    last.wait()
 
 
 def half_silu(y):
+    y = y.astype(BF)
     return y + y * jnp.tanh(y)
 
 
 def chem_body(
+    leave,
     count_ref,
     f_ref,
     a_hbm,
@@ -255,18 +332,10 @@
     w2_ref,
     w3_ref,
     token_ref,
-    r_hbm,
-    s_ref,
-    a_ref,
-    r_ref,
-    pull_ref,
-    one_a,
-    one_b,
-    two_a,
-    two_b,
-    in_sem,
-    out_sem,
+    *refs,
 ):
+    leave_refs, refs = (refs[:4], refs[4:]) if leave else (None, refs)
+    r_hbm, s_ref, a_ref, r_ref, pull_ref, one_a, one_b, two_a, two_b, in_sem, out_sem, *more = refs
     tiles = ot_ref.shape[1] // LANES
     rows = f_ref.shape[0] // tiles
     listed = ot_ref.shape[0]
@@ -274,6 +343,9 @@
     into = Stream(a_hbm, a_ref, in_sem, SUB * rows, 1)
     out = Stream(r_ref, r_hbm, out_sem, SUB * rows, 1)
     into.start_all()
+    if leave:
+        base = pltpu.make_async_copy(leave_refs[0], more[0], more[1])
+        base.start()
     f = jnp.concatenate([f_ref[pl.ds(t, rows, stride=tiles), :] for t in range(tiles)], axis=1)
     pull_ref[...] = rsel_ref[0:1, :] * dot_split(f, ot_ref[...], NT)
     live = lax.broadcasted_iota(I32, (1, listed), 1) < count_ref[0]
@@ -285,10 +357,10 @@
             for t in range(listed // LANES):
                 pull = pull_ref[:, t * LANES : (t + 1) * LANES]
                 parts.append((a_ref[t, at, :] + pull).astype(BF))
-        return half_silu(dot(w1_ref[...], jnp.concatenate(parts, axis=1), NN)).astype(BF)
+        return half_silu(dot(w1_ref[...], jnp.concatenate(parts, axis=1), NN))
 
     def second(one):
-        return half_silu(dot(w2_ref[...], one, NN)).astype(BF)
+        return half_silu(dot(w2_ref[...], one, NN))
 
     def third(g, two, total):
         change = dot(w3_ref[...], two, NN).astype(BF).astype(F32)
@@ -328,8 +400,13 @@
     total = third(last, second(one_b[...]), total)
     out.copy(particles // SUB - 1).start()
     source = dot_split(total * (1.0 / particles), ot_ref[...], NN)
-    for t in range(tiles):
-        s_ref[pl.ds(t, rows, stride=tiles), :] = source[:, t * LANES : (t + 1) * LANES]
+    if leave:
+        base.wait()
+        source_rows(source, rows, tiles, leave, s_ref)
+        leave_rows(leave, f, r_ref, more[0], *leave_refs[1:], s_ref)
+    else:
+        for t in range(tiles):
+            s_ref[pl.ds(t, rows, stride=tiles), :] = source[:, t * LANES : (t + 1) * LANES]
     out.wait_all()
 
 
@@ -344,100 +421,53 @@
     return dot(onehot, high, dims) + dot(onehot, low, dims)
 
 
-def leave_blocks(scalars, particles, span, store, part):
+def source_rows(source, rows, tiles, leave, out_ref):
+    devices, own = leave["devices"], rows // leave["devices"]
+    stride = out_ref.shape[0] // devices
+    for i in range(own):
+        mine = source.reshape(devices, own, source.shape[1])[:, i] if own > 1 else source
+        for t in range(tiles):
+            at = pl.ds(i * tiles + t, devices, stride=stride)
+            out_ref[at, :] = mine[:, t * LANES : (t + 1) * LANES]
+
+
+def leave_rows(leave, f, r_ref, base_ref, rate_ref, lcol_ref, rrow_ref, out_ref):
+    devices, span, scalars = leave["devices"], leave["span"], leave["scalars"]
+    rows, cells = f.shape
+    particles = r_ref.shape[1] // rows
     per = LANES // particles
-
-    def step(b, carry):
-        store(b, part(b * per, per))
-        return carry
-
-    whole = scalars // per
-    lax.fori_loop(0, whole, step, 0)
-    left = scalars - whole * per
-    for b in range(whole, span):
-        if b == whole and left:
-            value = part(b * per, left)
-            zeros = jnp.zeros((value.shape[0], LANES - left * particles), F32)
-            store(b, jnp.concatenate([value, zeros], axis=1))
-        else:
-            store(b, None)
-
-
-def base_body(span, q_hbm, rate_ref, lcol_ref, out_ref, token_ref, q_ref, sem):
-    per = LANES // q_ref.shape[1]
-    into = Stream(q_hbm, q_ref, sem, per)
-    into.start_all()
-    scalars, particles, cells = q_ref.shape
-    onehot = cell_onehot(lcol_ref, cells)
-    keep = 1.0 - rate_ref[...]
-
-    def part(s0, count):
-        into.copy(s0 // per, count).wait()
-        x = q_ref[pl.ds(s0, count), :, :].reshape(count * particles, cells) * keep
-        return split_dot(onehot, x, NT)
-
-    def store(b, value):
-        if value is not None:
-            out_ref[pl.ds(b, lcol_ref.shape[0], stride=span), :] = value
-
-    leave_blocks(scalars, particles, span, store, part)
-    token_ref[...] = keep[:, :LANES]
-
-
-def leave_body(
-    rows,
-    span,
-    scalars,
-    particles,
-    devices,
-    base_hbm,
-    f_ref,
-    r_hbm,
-    rate_ref,
-    lcol_ref,
-    rrow_ref,
-    source_ref,
-    out_ref,
-    base_ref,
-    r_ref,
-    sem,
-):
-    loads = [
-        pltpu.make_async_copy(r_hbm, r_ref, sem.at[0]),
-        pltpu.make_async_copy(base_hbm, base_ref, sem.at[1]),
-    ]
-    for c in loads:
-        c.start()
-    width = source_ref.shape[0] // devices
+    places = lcol_ref.shape[0]
     stride = out_ref.shape[0] // devices
-    for d in range(devices):
-        out_ref[d * stride : d * stride + width] = source_ref[d * width : (d + 1) * width]
-    cells = rate_ref.shape[1]
-    tiles = cells // LANES
-    places = lcol_ref.shape[0]
-    f = jnp.concatenate([f_ref[pl.ds(t, rows, stride=tiles), :] for t in range(tiles)], axis=1)
-    pull = split_dot(cell_onehot(lcol_ref, cells), f * rate_ref[...], NT)
+    width = stride - places // devices * span
+    leaves = cell_onehot(lcol_ref, cells)
+    high, low = halves(f * rate_ref[...])
+    pull = dot(leaves, high, NT) + dot(leaves, low, NT)
     reacts = (lcol_ref[...] == rrow_ref[...]).astype(F32).astype(BF)
-    for c in loads:
-        c.wait()
-
-    def part(s0, count):
+    pull = jnp.concatenate([*halves(pull), reacts], axis=1)
+
+    def part(b, count):
         wide = count * particles
-        r = jnp.concatenate([get_scalar(r_ref, s0 + i, rows) for i in range(count)], axis=0)
-        of = lax.broadcasted_iota(I32, (rows, wide), 1) // particles + s0
-        mine = (of == lax.broadcasted_iota(I32, (rows, wide), 0)).astype(F32).astype(BF)
-        at = pl.ds(s0 * particles // LANES, places, stride=span)
-        return base_ref[at, :][:, :wide] + dot_split(pull, mine, NN) + dot(reacts, r.astype(BF), NT)
-
-    def store(b, value):
+        r = jnp.concatenate([get_scalar(r_ref, b * per + i, rows) for i in range(count)], axis=0)
+        of = lax.broadcasted_iota(I32, (wide, rows), 0) // particles + b * per
+        mine = (of == lax.broadcasted_iota(I32, (wide, rows), 1)).astype(F32).astype(BF)
+        value = dot(pull, jnp.concatenate([mine, mine, r.astype(BF)], axis=1), NT)
+        value = base_ref[pl.ds(b, places, stride=span), :][:, :wide] + value
         for c in range(places // devices):
             at = pl.ds(width + c * span + b, devices, stride=stride)
-            if value is None:
-                out_ref[at, :] = jnp.zeros((devices, LANES), F32)
-            else:
-                out_ref[at, :] = value[c * devices : (c + 1) * devices]
-
-    leave_blocks(scalars, particles, span, store, part)
+            out_ref[at, :wide] = value[c * devices : (c + 1) * devices]
+
+    def step(b, carry):
+        part(b, per)
+        return carry
+
+    whole = scalars // per
+    lax.fori_loop(0, whole, step, 0, unroll=2)
+    zeros = jnp.zeros((devices, LANES), F32)
+    for c in range(places // devices):
+        for b in range(whole, span):
+            out_ref[pl.ds(width + c * span + b, devices, stride=stride), :] = zeros
+    if scalars > whole * per:
+        part(whole, scalars - whole * per)
 
 
 def settle_body(
@@ -571,7 +601,31 @@
     return ref[pl.ds(offset, count, stride=stride), :]
 
 
-def pack_body(width, grid_ref, owner_ref, slot_ref, speed_ref, lanes_y, out_ref):
+def pack_body(
+    width,
+    lanes_y,
+    grid_hbm,
+    owner_hbm,
+    slot_hbm,
+    speed_hbm,
+    out_ref,
+    grid_ref,
+    owner_ref,
+    slot_ref,
+    speed_ref,
+    sem,
+):
+    pairs = [
+        (grid_hbm, grid_ref),
+        (owner_hbm, owner_ref),
+        (slot_hbm, slot_ref),
+        (speed_hbm, speed_ref),
+    ]
+    copies = [pltpu.make_async_copy(a, b, sem.at[i]) for i, (a, b) in enumerate(pairs)]
+    for c in copies:
+        c.start()
+    for c in copies:
+        c.wait()
     quads = owner_ref.shape[0]
     stride = width + 2 * quads
     total = grid_ref.shape[0]
@@ -586,6 +640,14 @@
             zeros = jnp.zeros((width - count, LANES), F32)
             out_ref[d * stride + count : d * stride + width] = zeros
         out_ref[d * stride + width : (d + 1) * stride] = tail
+
+
+def weights_body(w1_ref, w2_ref, w3_ref, token_ref, a_ref, b_ref, c_ref):
+    scalars, hidden = w1_ref.shape
+    rest = jnp.zeros((a_ref.shape[1] - scalars, hidden), F32)
+    a_ref[...] = jnp.concatenate([w1_ref[...].astype(F32) * 0.5, rest], axis=0).T.astype(BF)
+    b_ref[...] = (w2_ref[...].astype(F32) * 0.5).astype(BF)
+    c_ref[...] = jnp.concatenate([w3_ref[...].astype(F32), rest], axis=0).astype(BF)
 
 
 def start_body(dims, arr_ref, token_ref, g_ref, f_ref, inv_ref, lab_ref):
@@ -729,15 +791,18 @@
     dims = (nx, ny, own, bx, by)
     flat = devices * width
 
+    box = [
+        grid_scalars.reshape(-1, LANES),
+        cell_owner.reshape(quads, LANES),
+        cell_slot.reshape(quads, LANES),
+        axial_speed.reshape(quads, LANES),
+    ]
     (first,) = call(
-        lambda g, o, c, u, out: pack_body(width, g, o, c, u, ny, out),
+        functools.partial(pack_body, width, ny),
         [((devices * (width + 2 * quads), LANES), F32)],
-        [
-            grid_scalars.reshape(-1, LANES),
-            cell_owner.reshape(quads, LANES),
-            cell_slot.reshape(quads, LANES),
-            axial_speed.reshape(quads, LANES),
-        ],
+        box,
+        hbm=(0, 1, 2, 3),
+        scratch=[pltpu.VMEM(x.shape, x.dtype) for x in box] + [pltpu.SemaphoreType.DMA((4,))],
         name="pack",
     )
 
@@ -748,13 +813,8 @@
     arrival = exchange(first)
 
     rate = mix_rate.reshape(1, cells)
-    rcol = react_slots.reshape(listed, 1)
     lcol = leave_slots.reshape(devices, -1).T.reshape(-1, 1)
     acol = arrive_slots.reshape(devices, -1).T.reshape(-1, 1)
-    w1 = jnp.pad(chem_input, ((0, 0), (0, rows - scalars))) * jnp.asarray(0.5, BF)
-    w2 = chem_hidden * jnp.asarray(0.5, BF)
-    w3 = jnp.pad(chem_output, ((0, rows - scalars), (0, 0)))
-
     state_shape = (scalars, heads, cells)
     listed_shape = (listed // LANES, heads * rows, LANES)
     block = divisor(scalars, 6)
@@ -771,9 +831,20 @@
             ((listed, cells), BF),
             ((SUB, listed), F32),
         ],
-        [particles, partner, rate, rcol],
-        hbm=(0,),
-        scratch=[state_vmem, state_vmem, listed_vmem, per_block, per_block, dma],
+        [particles, partner, rate, react_slots],
+        hbm=(0, 1, 2, 3),
+        scratch=[
+            state_vmem,
+            state_vmem,
+            listed_vmem,
+            pltpu.VMEM(partner.shape, I32),
+            pltpu.VMEM(rate.shape, F32),
+            pltpu.VMEM(react_slots.shape, I32),
+            per_block,
+            per_block,
+            dma,
+            dma((3,)),
+        ],
         name="open",
     )
     grid, sent, inv, lab = call(
@@ -788,61 +859,71 @@
         name="start",
     )
 
-    def chemistry(f, a, token):
-        pair = pltpu.VMEM((hidden, 2 * listed), BF)
-        return call(
-            chem_body,
-            [(listed_shape, F32, True), ((flat, LANES), F32)],
-            [react_count, f, a, ot, rsel, w1, w2, w3, token],
-            smem=(0,),
-            hbm=(2,),
-            scratch=[listed_vmem, listed_vmem, pltpu.VMEM((rows, listed), F32)]
-            + [pair] * 4
-            + [dma((octets,)), dma((octets,))],
-            name="chem",
-        )
+    w1, w2, w3 = call(
+        weights_body,
+        [((hidden, rows), BF), ((hidden, hidden), BF), ((rows, hidden), BF)],
+        [chem_input.T, chem_hidden, chem_output, lab],
+        name="weights",
+    )
 
     per = LANES // heads
     span = SUB * (-(-scalars // (per * SUB)))
     places = leave_slots.shape[1]
+    pair = pltpu.VMEM((hidden, 2 * listed), BF)
+
+    def chemistry(f, a, token, leave=None, more=()):
+        out = (flat + places * span, LANES) if leave else (flat, LANES)
+        extra = [pltpu.VMEM((places * span, LANES), F32), dma] if leave else []
+        return call(
+            functools.partial(chem_body, leave),
+            [(listed_shape, F32, True), (out, F32)],
+            [react_count, f, a, ot, rsel, w1, w2, w3, token, *more],
+            smem=(0,),
+            hbm=(2, 9) if leave else (2,),
+            scratch=[listed_vmem, listed_vmem, pltpu.VMEM((rows, listed), F32)]
+            + [pair] * 4
+            + [dma((octets,)), dma((octets,))]
+            + extra,
+            name="chem",
+        )
+
     token = rsel
-    for substep in range(SUBSTEPS):
+    for substep in range(SUBSTEPS - 1):
         f = exchange(sent)
         change, source = chemistry(f, a, token)
-        if substep < SUBSTEPS - 1:
-            home = exchange(source)
-            q, a, token = call(
-                functools.partial(middle_body, rows, block),
-                [(state_shape, F32, True), (listed_shape, F32, True), ((SUB, LANES), F32)],
-                [q, f, change, ot, rate, rsel, partner],
-                hbm=(0, 2),
-                scratch=[state_vmem, state_vmem, listed_vmem, per_block, per_block, dma],
-                name="middle",
-            )
-            grid, sent = call(
-                functools.partial(again_body, dims),
-                [((flat, LANES), F32), ((flat, LANES), F32)],
-                [home, grid, arrival, inv, lab, token],
-                scratch=[pltpu.VMEM((flat, LANES), F32)],
-                name="again",
-            )
-        if substep == SUBSTEPS - 2:
-            base, token = call(
-                functools.partial(base_body, span),
-                [((places * span, LANES), F32), ((1, LANES), F32)],
-                [q, rate, lcol],
-                hbm=(0,),
-                scratch=[state_vmem, dma((-(-scalars // per),))],
-                name="base",
-            )
-    (leaving,) = call(
-        functools.partial(leave_body, rows, span, scalars, heads, devices),
-        [((flat + places * span, LANES), F32)],
-        [base, f, change, rate, lcol, react_slots, source],
-        hbm=(0, 2),
-        scratch=[pltpu.VMEM((places * span, LANES), F32), listed_vmem, dma((2,))],
-        name="leave",
-    )
+        home = exchange(source)
+        q, token = call(
+            functools.partial(middle_body, rows, block),
+            [(state_shape, F32, True), ((1, LANES), F32)],
+            [q, f, change, ot, rate, partner],
+            hbm=(0, 2),
+            scratch=[state_vmem, state_vmem, listed_vmem, per_block, per_block, dma],
+            name="middle",
+        )
+        grid, sent = call(
+            functools.partial(again_body, dims),
+            [((flat, LANES), F32), ((flat, LANES), F32)],
+            [home, grid, arrival, inv, lab, token],
+            scratch=[pltpu.VMEM((flat, LANES), F32)],
+            name="again",
+        )
+        a, base, token = call(
+            functools.partial(list_body, rows, span),
+            [(listed_shape, F32, True), ((places * span, LANES), F32, True), ((1, LANES), F32)],
+            [q, rate, rsel, ot, lcol],
+            hbm=(0,),
+            scratch=[
+                state_vmem,
+                listed_vmem,
+                pltpu.VMEM((places * span, LANES), F32),
+                dma((-(-scalars // per),)),
+                dma((2,)),
+            ],
+            name="list",
+        )
+    f = exchange(sent)
+    leave = dict(devices=devices, span=span, scalars=scalars)
+    change, leaving = chemistry(f, a, token, leave, [base, rate, lcol, react_slots])
     moved = exchange(leaving)
     state, token = call(
         functools.partial(settle_body, rows, block),

time: 134 us -> 126 us (0.940)
  local copies, waits for them, and re-layouts: 8.71 us -> 1.79 us
    unnamed x30 -> x17, local copies, waits for them, and re-layouts: 6.66 us -> 0.56 us
  transfers between devices with their start and end apart: 6 -> 6, of which waited for: 4 -> 4; matrix products, arithmetic and copies ran while one was open for 3% -> 2% of each run, Pallas kernels for 27% -> 29%
where the time goes in v4:
time: 126 us; the launch traced here: 125 us
  Pallas kernels  67.9 us (54%)
  starting transfers between devices  29.4 us (23%)
  waiting for transfers between devices  23.1 us (18%)
  local copies, waits for them, and re-layouts  1.79 us (1%)
  between operations  1.56 us (1%)
  other arithmetic  1.33 us (1%)
    pallas_call x12, Pallas kernels, call(): pl.pallas_call(body, out_shape=[pltpu.HBM(o[0], o[1]) if len(o) > 2 else...  67.9 us
    all_to_all x6, starting transfers between devices, exchange(): lax.all_to_all(x, both, split_axis=0, concat_axis=0, tiled=True)  29.4 us
    all_to_all x6, waiting for transfers between devices, exchange(): lax.all_to_all(x, both, split_axis=0, concat_axis=0, tiled=True)  23.1 us
  transfers between devices with their start and end apart: 6, of which 4 were waited for; matrix products, arithmetic and copies ran while one was open for 2% of the time, Pallas kernels for 29%

profile of v4, /device:TPU:0, one launch (start us, length us, event | category | flops | bytes accessed | tf_op | source)
XLA Modules:
  0.0 125.0 jit_solution(17554755908929512528)
XLA Ops:
  0.6 0.0 copy-start.3
  0.6 0.0 copy-start.1
  0.7 0.0 copy-start.4
  0.7 1.7 %pack.1 = f32[512,128]{1,0:T(8,128)} custom-call(f32[216,128]{1,0:T(8,128)} %bitcast.35, s32[4,128]{1,0:T(4,128)} %bitcast.39, s32[4,128]{1,0:T(4,128)} %bitcast.40, f32[4,128]{1,0:T(4,128)} %bitcast.41), custom_call_target="tpu_custom_call" | custom-call | tf_op jit(solution)/shard_map/pack/pallas_call | solution.py:26
  2.4 7.3 %all-to-all-start = ((f32[32,16,128]{2,1,0:T(8,128)}), f32[32,16,128]{2,1,0:T(8,128)S(1)}, u32[]{:S(2)}, u32[]{:S(2)}) async-start(f32[32,16,128]{2,1,0:T(8,128)} %bitcast.4), calls=%async_computation | async-start | bytes 524288 | tf_op jit(solution)/shard_map/all_to_all | solution.py:811
  9.7 0.0 copy-start
  9.7 0.0 copy-start.2
  9.7 9.4 %open.1 = (f32[54,32,512]{2,1,0:T(8,128)}, f32[2,2048,128]{2,1,0:T(8,128)}, bf16[256,512]{1,0:T(8,128)(2,1)S(1)}, f32[8,256]{1,0:T(8,128)S(1)}) custom-call(f32[54,32,512]{2,1,0:T(8,128)} %p_hbm.1, s32[32,512]{1,0:T(8,128)} %partner_ref.1, f32[1,512]{1,0:T(1,128)} %bitcast.29, s32[1,256]{1,0:T(1,128)} %refs_3_.1), custom_call_target="tpu_custom_call" | custom-call | tf_op jit(solution)/shard_map/open/pallas_call | solution.py:26
  19.1 0.6 all-to-all-done
  19.7 5.7 %start.1 = (f32[256,128]{1,0:T(8,128)S(1)}, f32[256,128]{1,0:T(8,128)}, s32[256,128]{1,0:T(8,128)S(1)}, s32[128,128]{1,0:T(8,128)S(1)}) custom-call(f32[512,128]{1,0:T(8,128)S(1)} %bitcast.22, f32[8,256]{1,0:T(8,128)S(1)} %get-tuple-element.26.token_ref.rsel_ref), custom_call_target="tpu_custom_call" | custom-call | tf_op jit(solution)/shard_map/start/pallas_call | solution.py:26
  25.4 5.2 %all-to-all-start.1 = ((f32[32,8,128]{2,1,0:T(8,128)}), f32[32,8,128]{2,1,0:T(8,128)S(1)}, u32[]{:S(2)}, u32[]{:S(2)}) async-start(f32[32,8,128]{2,1,0:T(8,128)} %bitcast.7), calls=%async_computation.1 | async-start | bytes 262144 | tf_op jit(solution)/shard_map/all_to_all | solution.py:811
  31.3 0.0 copy-done.3
  31.3 0.0 copy-done.1
  31.3 0.0 copy-done.4
  31.3 0.1 weights.1
  31.4 7.4 %all-to-all-done.1 = f32[32,8,128]{2,1,0:T(8,128)S(1)} async-done(((f32[32,8,128]{2,1,0:T(8,128)}), f32[32,8,128]{2,1,0:T(8,128)S(1)}, u32[]{:S(2)}, u32[]{:S(2)}) %all-to-all-start.1) | async-done | bytes 131104 | tf_op jit(solution)/shard_map/all_to_all | solution.py:811
  38.8 8.4 %chem.2 = (f32[2,2048,128]{2,1,0:T(8,128)}, f32[256,128]{1,0:T(8,128)}) custom-call(s32[1]{0:T(128)S(6)} %copy.26.count_ref, f32[256,128]{1,0:T(8,128)S(1)} %bitcast.26, f32[2,2048,128]{2,1,0:T(8,128)} %get-tuple-element.28.a_hbm, bf16[256,512]{1,0:T(8,128)(2,1)S(1)} %get-tuple-element.29.ot_ref, f32[8,256]{1,0:T(8,128)S(1)} %get-tuple-element.26.token_ref.rsel_ref, ...), custom_call_target="tpu_custom_call" | custom-call | tf_op jit(solution)/shard_map/chem/pallas_call | solution.py:26
  47.2 2.6 %all-to-all-start.2 = ((f32[32,8,128]{2,1,0:T(8,128)}), f32[32,8,128]{2,1,0:T(8,128)S(1)}, u32[]{:S(2)}, u32[]{:S(2)}) async-start(f32[32,8,128]{2,1,0:T(8,128)} %bitcast.10), calls=%async_computation.2 | async-start | bytes 262144 | tf_op jit(solution)/shard_map/all_to_all | solution.py:811
  49.8 0.0 copy-done
  49.8 0.0 copy-done.2
  49.8 0.0 copy-start.6
  49.8 8.4 %middle.1 = (f32[54,32,512]{2,1,0:T(8,128)}, f32[1,128]{1,0:T(1,128)S(1)}) custom-call(f32[54,32,512]{2,1,0:T(8,128)} %get-tuple-element.37.q_hbm, f32[256,128]{1,0:T(8,128)S(1)} %bitcast.27, f32[2,2048,128]{2,1,0:T(8,128)} %get-tuple-element.38.r_hbm, bf16[256,512]{1,0:T(8,128)(2,1)S(1)} %get-tuple-element.29.ot_ref, f32[1,512]{1,0:T(1,128)S(1)} %bitcast.30, ...), custom_call_target="tpu_custom_call" | custom-call | tf_op jit(solution)/shard_map/middle/pallas_call | solution.py:26
  58.2 0.0 copy-start.5
  58.2 0.0 all-to-all-done.2
  58.2 3.6 %again.1 = (f32[256,128]{1,0:T(8,128)S(1)}, f32[256,128]{1,0:T(8,128)}) custom-call(f32[256,128]{1,0:T(8,128)S(1)} %bitcast.28, f32[256,128]{1,0:T(8,128)S(1)} %get-tuple-element.35.g_ref, f32[512,128]{1,0:T(8,128)S(1)} %bitcast.23, s32[256,128]{1,0:T(8,128)S(1)} %get-tuple-element.36.inv_ref, s32[128,128]{1,0:T(8,128)S(1)} %get-tuple-element.30.token_ref.lab_ref, ...), custom_call_target="tpu_custom_call" | custom-call | tf_op jit(solution)/shard_map/again/pallas_call | solution.py:26
  61.8 5.8 %all-to-all-start.3 = ((f32[32,8,128]{2,1,0:T(8,128)}), f32[32,8,128]{2,1,0:T(8,128)S(1)}, u32[]{:S(2)}, u32[]{:S(2)}) async-start(f32[32,8,128]{2,1,0:T(8,128)} %bitcast.12), calls=%async_computation.3 | async-start | bytes 262144 | tf_op jit(solution)/shard_map/all_to_all | solution.py:811
  67.6 0.5 broadcast.6
  68.2 0.0 copy-done.6
  68.2 0.7 reduce.6
  68.8 0.1 reshape.78
  68.9 0.1 copy.21
  69.0 0.1 reshape.85.lcol_ref.refs_2_
  69.1 7.3 %list.1 = (f32[2,2048,128]{2,1,0:T(8,128)}, f32[1024,128]{1,0:T(8,128)}, f32[1,128]{1,0:T(1,128)S(1)}) custom-call(f32[54,32,512]{2,1,0:T(8,128)} %get-tuple-element.41.q_hbm, f32[1,512]{1,0:T(1,128)S(1)} %bitcast.31, f32[8,256]{1,0:T(8,128)S(1)} %get-tuple-element.26.token_ref.rsel_ref, bf16[256,512]{1,0:T(8,128)(2,1)S(1)} %get-tuple-element.29.ot_ref, ...), custom_call_target="tpu_custom_call" | custom-call | tf_op jit(solution)/shard_map/list/pallas_call | solution.py:26
  76.4 0.0 all-to-all-done.3
  76.4 10.3 %chem.3 = (f32[2,2048,128]{2,1,0:T(8,128)}, f32[1280,128]{1,0:T(8,128)}) custom-call(s32[1]{0:T(128)S(6)} %copy.26.count_ref, f32[256,128]{1,0:T(8,128)S(1)} %bitcast.24, f32[2,2048,128]{2,1,0:T(8,128)} %get-tuple-element.42.a_hbm, bf16[256,512]{1,0:T(8,128)(2,1)S(1)} %get-tuple-element.29.ot_ref, f32[8,256]{1,0:T(8,128)S(1)} %get-tuple-element.26.token_ref.rsel_ref, ...), custom_call_target="tpu_custom_call" | custom-call | tf_op jit(solution)/shard_map/chem/pallas_call | solution.py:26
  86.7 5.8 %all-to-all-start.4 = ((f32[32,40,128]{2,1,0:T(8,128)}), f32[32,40,128]{2,1,0:T(8,128)S(1)}, u32[]{:S(2)}, u32[]{:S(2)}) async-start(f32[32,40,128]{2,1,0:T(8,128)} %bitcast.15), calls=%async_computation.4 | async-start | bytes 1310720 | tf_op jit(solution)/shard_map/all_to_all | solution.py:811
  92.6 0.0 copy-start.7
  92.6 5.4 %settle.1 = (f32[54,32,512]{2,1,0:T(8,128)}, f32[1,128]{1,0:T(1,128)S(1)}) custom-call(f32[54,32,512]{2,1,0:T(8,128)} %get-tuple-element.41.q_hbm, f32[256,128]{1,0:T(8,128)S(1)} %bitcast.25, f32[2,2048,128]{2,1,0:T(8,128)} %get-tuple-element.47.r_hbm, bf16[256,512]{1,0:T(8,128)(2,1)S(1)} %get-tuple-element.29.ot_ref, f32[1,512]{1,0:T(1,128)S(1)} %bitcast.33), custom_call_target="tpu_custom_call" | custom-call | tf_op jit(solution)/shard_map/settle/pallas_call | solution.py:26
  98.0 13.6 %all-to-all-done.4 = f32[32,40,128]{2,1,0:T(8,128)S(1)} async-done(((f32[32,40,128]{2,1,0:T(8,128)}), f32[32,40,128]{2,1,0:T(8,128)S(1)}, u32[]{:S(2)}, u32[]{:S(2)}) %all-to-all-start.4) | async-done | bytes 655392 | tf_op jit(solution)/shard_map/all_to_all | solution.py:811
  111.6 2.1 %last.1 = f32[256,128]{1,0:T(8,128)} custom-call(f32[1280,128]{1,0:T(8,128)S(1)} %bitcast.20, f32[256,128]{1,0:T(8,128)S(1)} %get-tuple-element.46.g_ref, s32[128,128]{1,0:T(8,128)S(1)} %get-tuple-element.30.token_ref.lab_ref, f32[1,128]{1,0:T(1,128)S(1)} %get-tuple-element.48.token_ref), custom_call_target="tpu_custom_call" | custom-call | tf_op jit(solution)/shard_map/last/pallas_call | solution.py:26
  113.7 2.6 %all-to-all-start.5 = ((f32[32,8,128]{2,1,0:T(8,128)}), f32[32,8,128]{2,1,0:T(8,128)S(1)}, u32[]{:S(2)}, u32[]{:S(2)}) async-start(f32[32,8,128]{2,1,0:T(8,128)} %bitcast.17), calls=%async_computation.5 | async-start | bytes 262144 | tf_op jit(solution)/shard_map/all_to_all | solution.py:811
  116.2 0.7 reduce.7
  116.9 0.1 reshape.83
  117.0 0.1 copy.24
  117.1 0.1 reshape.86.acol_ref
  117.2 5.7 %arrive.1 = f32[54,32,512]{2,1,0:T(8,128)} custom-call(f32[54,32,512]{2,1,0:T(8,128)} %get-tuple-element.49.p_hbm, f32[1280,128]{1,0:T(8,128)S(1)} %bitcast.21, s32[64,1]{1,0:T(8,128)S(1)} %reshape.86.acol_ref), custom_call_target="tpu_custom_call" | custom-call | tf_op jit(solution)/shard_map/arrive/pallas_call | solution.py:26
  122.9 1.5 %all-to-all-done.5 = f32[32,8,128]{2,1,0:T(8,128)S(1)} async-done(((f32[32,8,128]{2,1,0:T(8,128)}), f32[32,8,128]{2,1,0:T(8,128)S(1)}, u32[]{:S(2)}, u32[]{:S(2)}) %all-to-all-start.5) | async-done | bytes 131104 | tf_op jit(solution)/shard_map/all_to_all | solution.py:811
  124.4 0.7 slice.8
  (2 shorter events, 0.0 us)
Async XLA Ops:
  0.6 30.7 %copy-start.3 = (bf16[256,54]{0,1:T(8,128)(2,1)S(1)}, bf16[256,54]{0,1:T(8,128)(2,1)}, u32[]{:S(2)}) copy-start(bf16[256,54]{0,1:T(8,128)(2,1)} %param.21) | copy-start | bytes 82948
  0.6 30.7 %copy-start.1 = (bf16[256,256]{1,0:T(8,128)(2,1)S(1)}, bf16[256,256]{1,0:T(8,128)(2,1)}, u32[]{:S(2)}) copy-start(bf16[256,256]{1,0:T(8,128)(2,1)} %w2_ref.1) | copy-start | bytes 393220
  0.7 30.7 %copy-start.4 = (bf16[54,256]{1,0:T(8,128)(2,1)S(1)}, bf16[54,256]{1,0:T(8,128)(2,1)}, u32[]{:S(2)}) copy-start(bf16[54,256]{1,0:T(8,128)(2,1)} %w3_ref.1) | copy-start | bytes 82948
  2.4 17.3 %all-to-all-start = ((f32[32,16,128]{2,1,0:T(8,128)}), f32[32,16,128]{2,1,0:T(8,128)S(1)}, u32[]{:S(2)}, u32[]{:S(2)}) async-start(f32[32,16,128]{2,1,0:T(8,128)} %bitcast.4), calls=%async_computation | async-start | bytes 524288 | tf_op jit(solution)/shard_map/all_to_all | solution.py:811
  9.7 40.1 %copy-start = (s32[32,512]{1,0:T(8,128)S(1)}, s32[32,512]{1,0:T(8,128)}, u32[]{:S(2)}) copy-start(s32[32,512]{1,0:T(8,128)} %partner_ref.1) | copy-start | bytes 196612
  9.7 40.1 %copy-start.2 = (f32[512]{0:T(512)S(1)}, f32[512]{0:T(512)}, u32[]{:S(2)}) copy-start(f32[512]{0:T(512)} %param.19) | copy-start | bytes 6148
  25.4 13.4 %all-to-all-start.1 = ((f32[32,8,128]{2,1,0:T(8,128)}), f32[32,8,128]{2,1,0:T(8,128)S(1)}, u32[]{:S(2)}, u32[]{:S(2)}) async-start(f32[32,8,128]{2,1,0:T(8,128)} %bitcast.7), calls=%async_computation.1 | async-start | bytes 262144 | tf_op jit(solution)/shard_map/all_to_all | solution.py:811
  47.2 11.0 %all-to-all-start.2 = ((f32[32,8,128]{2,1,0:T(8,128)}), f32[32,8,128]{2,1,0:T(8,128)S(1)}, u32[]{:S(2)}, u32[]{:S(2)}) async-start(f32[32,8,128]{2,1,0:T(8,128)} %bitcast.10), calls=%async_computation.2 | async-start | bytes 262144 | tf_op jit(solution)/shard_map/all_to_all | solution.py:811
  49.8 18.4 %copy-start.6 = (s32[1,64]{1,0:T(1,128)S(1)}, s32[1,64]{1,0:T(1,128)}, u32[]{:S(2)}) copy-start(s32[1,64]{1,0:T(1,128)} %param.26) | copy-start | bytes 772
  58.2 18.3 %copy-start.5 = (s32[1,256]{1,0:T(1,128)S(1)}, s32[1,256]{1,0:T(1,128)}, u32[]{:S(2)}) copy-start(s32[1,256]{1,0:T(1,128)} %refs_3_.1) | copy-start | bytes 3076
  61.8 14.6 %all-to-all-start.3 = ((f32[32,8,128]{2,1,0:T(8,128)}), f32[32,8,128]{2,1,0:T(8,128)S(1)}, u32[]{:S(2)}, u32[]{:S(2)}) async-start(f32[32,8,128]{2,1,0:T(8,128)} %bitcast.12), calls=%async_computation.3 | async-start | bytes 262144 | tf_op jit(solution)/shard_map/all_to_all | solution.py:811
  86.7 24.9 %all-to-all-start.4 = ((f32[32,40,128]{2,1,0:T(8,128)}), f32[32,40,128]{2,1,0:T(8,128)S(1)}, u32[]{:S(2)}, u32[]{:S(2)}) async-start(f32[32,40,128]{2,1,0:T(8,128)} %bitcast.15), calls=%async_computation.4 | async-start | bytes 1310720 | tf_op jit(solution)/shard_map/all_to_all | solution.py:811
  92.6 23.7 %copy-start.7 = (s32[1,64]{1,0:T(1,128)S(1)}, s32[1,64]{1,0:T(1,128)}, u32[]{:S(2)}) copy-start(s32[1,64]{1,0:T(1,128)} %param.27) | copy-start | bytes 772
  113.7 10.7 %all-to-all-start.5 = ((f32[32,8,128]{2,1,0:T(8,128)}), f32[32,8,128]{2,1,0:T(8,128)S(1)}, u32[]{:S(2)}, u32[]{:S(2)}) async-start(f32[32,8,128]{2,1,0:T(8,128)} %bitcast.17), calls=%async_computation.5 | async-start | bytes 262144 | tf_op jit(solution)/shard_map/all_to_all | solution.py:811

commit v5 on v4

--- a/solution.py
+++ b/solution.py
@@ -7,7 +7,6 @@
 from jax.experimental.pallas import tpu as pltpu
 from jax.sharding import PartitionSpec as P
 
-SUBSTEPS = 2
 DIFFUSION = 0.1
 PAIR_WEIGHT = 0.4
 LANES = 128
@@ -76,6 +75,23 @@
     return y[: x.shape[0]] + y[x.shape[0] :]
 
 
+def load_filtered(f_ref, devices, rows, tiles):
+    stride = f_ref.shape[0] // devices
+    return jnp.concatenate(
+        [
+            jnp.concatenate(
+                [
+                    f_ref[pl.ds(i * tiles + t, devices, stride=stride), :]
+                    for i in range(rows // devices)
+                ],
+                axis=0,
+            )
+            for t in range(tiles)
+        ],
+        axis=1,
+    )
+
+
 def divisor(n, most):
     return max(k for k in range(1, most + 1) if n % k == 0)
 
@@ -139,7 +155,6 @@
 
 def list_body(
     rows,
-    span,
     q_hbm,
     rate_ref,
     rsel_ref,
@@ -161,20 +176,28 @@
     token_ref[...] = rate_ref[:, :LANES]
     leaves = cell_onehot(lcol_ref, cells)
     places = lcol_ref.shape[0]
+    side = max(1, LANES // places)
     keep = 1.0 - rate_ref[...]
 
     def part(b, count):
         into.copy(b, count).wait()
         x = q_ref[pl.ds(b * per, count)].reshape(count * particles, cells) * keep
         high, low = halves(x)
-        y = dot(jnp.concatenate([high, low], axis=0), ot_ref[...], NT)
+        both = jnp.concatenate([high, low], axis=0)
         half = count * particles
+        y = dot(both, ot_ref[...], NT)
         y = y[:half] + y[half:]
+        z = dot(both, leaves, NT)
+        z = z[:half] + z[half:]
         for i in range(count):
             put_scalar(a_ref, b * per + i, y[i * particles : (i + 1) * particles], rows)
-        base_ref[pl.ds(b, places, stride=span), :half] = dot(leaves, high, NT) + dot(
-            leaves, low, NT
-        )
+            for o in range(0, particles // SUB, side):
+                first = i * particles + o * SUB
+                octets = [z[first + u * SUB : first + (u + 1) * SUB] for u in range(side)]
+                at = pl.ds(o // side * rows * SUB + (b * per + i) * SUB, SUB)
+                wide = jnp.concatenate(octets, axis=1)
+                for t in range(base_ref.shape[0]):
+                    base_ref[t, at, :] = wide[:, t * LANES : (t + 1) * LANES]
 
     def step(b, carry):
         part(b, per)
@@ -182,12 +205,13 @@
 
     whole = scalars // per
     lax.fori_loop(0, whole, step, 0)
-    zeros = jnp.zeros((places, LANES), F32)
-    for b in range(whole, span):
-        base_ref[pl.ds(b, places, stride=span), :] = zeros
     if scalars > whole * per:
         part(whole, scalars - whole * per)
     clear_rest(scalars, rows, a_ref)
+    for o in range(particles // SUB // side):
+        rest = (rows - scalars) * SUB
+        at = pl.ds(o * rows * SUB + scalars * SUB, rest)
+        base_ref[:, at, :] = jnp.zeros((base_ref.shape[0], rest, LANES), F32)
     copies = [
         pltpu.make_async_copy(a_ref, a_hbm, out_sem.at[0]),
         pltpu.make_async_copy(base_ref, base_hbm, out_sem.at[1]),
@@ -262,7 +286,7 @@
     last.wait()
 
 
-def settle_block(s0, block, q_ref, f_ref, r_ref, ot_ref, rate_ref, out_ref, rows):
+def settle_block(s0, block, q_ref, f_ref, r_ref, ot_ref, rate_ref, out_ref, rows, devices):
     scalars, particles, cells = q_ref.shape
     tiles = cells // LANES
     rate = rate_ref[...]
@@ -270,9 +294,9 @@
     r = jnp.concatenate([get_scalar(r_ref, s0 + i, rows) for i in range(block)], axis=0)
     spread = dot(r.astype(BF), ot_ref[...], NN)
     for i in range(block):
-        f = jnp.concatenate(
-            [f_ref[pl.ds((s0 + i) * tiles + t, 1), :] for t in range(tiles)], axis=1
-        )
+        s = s0 + i
+        at = lax.rem(s, devices) * (f_ref.shape[0] // devices) + lax.div(s, devices) * tiles
+        f = jnp.concatenate([f_ref[pl.ds(at + t, 1), :] for t in range(tiles)], axis=1)
         out_ref[s0 + i] = (
             keep * q_ref[s0 + i] + rate * f + spread[i * particles : (i + 1) * particles]
         )
@@ -281,6 +305,7 @@
 def middle_body(
     rows,
     block,
+    devices,
     q_hbm,
     f_ref,
     r_hbm,
@@ -307,7 +332,7 @@
     def step(b, carry):
         into.copy(b).wait()
         s0 = b * block
-        settle_block(s0, block, q_ref, f_ref, r_ref, ot_ref, rate_ref, now_ref, rows)
+        settle_block(s0, block, q_ref, f_ref, r_ref, ot_ref, rate_ref, now_ref, rows, devices)
         mix(s0, block, now_ref, partner_ref, q_ref)
         out.copy(b).start()
         return carry
@@ -317,12 +342,12 @@
 
 
 def half_silu(y):
-    y = y.astype(BF)
-    return y + y * jnp.tanh(y)
+    return (y + y * jnp.tanh(y)).astype(BF)
 
 
 def chem_body(
-    leave,
+    devices,
+    rows,
     count_ref,
     f_ref,
     a_hbm,
@@ -334,19 +359,15 @@
     token_ref,
     *refs,
 ):
-    leave_refs, refs = (refs[:4], refs[4:]) if leave else (None, refs)
-    r_hbm, s_ref, a_ref, r_ref, pull_ref, one_a, one_b, two_a, two_b, in_sem, out_sem, *more = refs
+    pos_refs, refs = refs[:-11], refs[-11:]
+    r_hbm, s_ref, a_ref, r_ref, pull_ref, one_a, one_b, two_a, two_b, in_sem, out_sem = refs
     tiles = ot_ref.shape[1] // LANES
-    rows = f_ref.shape[0] // tiles
     listed = ot_ref.shape[0]
     particles = a_ref.shape[1] // rows
     into = Stream(a_hbm, a_ref, in_sem, SUB * rows, 1)
     out = Stream(r_ref, r_hbm, out_sem, SUB * rows, 1)
     into.start_all()
-    if leave:
-        base = pltpu.make_async_copy(leave_refs[0], more[0], more[1])
-        base.start()
-    f = jnp.concatenate([f_ref[pl.ds(t, rows, stride=tiles), :] for t in range(tiles)], axis=1)
+    f = load_filtered(f_ref, devices, rows, tiles)
     pull_ref[...] = rsel_ref[0:1, :] * dot_split(f, ot_ref[...], NT)
     live = lax.broadcasted_iota(I32, (1, listed), 1) < count_ref[0]
 
@@ -399,62 +420,99 @@
     total = third(last - 1, two_b[...], total)
     total = third(last, second(one_b[...]), total)
     out.copy(particles // SUB - 1).start()
-    source = dot_split(total * (1.0 / particles), ot_ref[...], NN)
-    if leave:
-        base.wait()
-        source_rows(source, rows, tiles, leave, s_ref)
-        leave_rows(leave, f, r_ref, more[0], *leave_refs[1:], s_ref)
+    source = total * (1.0 / particles)
+    if pos_refs:
+        boxes_source(source, *pos_refs, s_ref)
     else:
-        for t in range(tiles):
-            s_ref[pl.ds(t, rows, stride=tiles), :] = source[:, t * LANES : (t + 1) * LANES]
+        source = dot_split(source, ot_ref[...], NN)
+        stride = s_ref.shape[0] // devices
+        for i in range(rows // devices):
+            for t in range(tiles):
+                part = source[i * devices : (i + 1) * devices, t * LANES : (t + 1) * LANES]
+                s_ref[pl.ds(i * tiles + t, devices, stride=stride), :] = part
     out.wait_all()
 
 
-def cell_onehot(col_ref, cells):
-    shape = (col_ref.shape[0], cells)
-    return (col_ref[...] == lax.broadcasted_iota(I32, shape, 1)).astype(F32).astype(BF)
-
-
-def split_dot(onehot, x, dims):
-    high = x.astype(BF)
-    low = (x - high.astype(F32)).astype(BF)
-    return dot(onehot, high, dims) + dot(onehot, low, dims)
-
-
-def source_rows(source, rows, tiles, leave, out_ref):
-    devices, own = leave["devices"], rows // leave["devices"]
+def boxes_source(source, pos_ref, s_ref):
+    listed = source.shape[1]
+    boxes = s_ref.shape[0]
+    put = lax.broadcasted_iota(I32, (listed, boxes * LANES), 1).astype(F32) == pos_ref[:, :1]
+    sent = dot_split(source, put.astype(F32).astype(BF), NN)
+    for b in range(boxes):
+        s_ref[b] = sent[: s_ref.shape[1], b * LANES : (b + 1) * LANES]
+
+
+def early_body(
+    devices,
+    rows,
+    span,
+    scalars,
+    particles,
+    count_ref,
+    f_ref,
+    base_ref,
+    ot_ref,
+    rate_ref,
+    lcol_ref,
+    w1_ref,
+    w2_ref,
+    w3_ref,
+    token_ref,
+    out_ref,
+    end_ref,
+    v_ref,
+):
+    listed, cells = ot_ref.shape
+    tiles = cells // LANES
+    places = lcol_ref.shape[0]
+    side = max(1, LANES // places)
+    wide = base_ref.shape[0]
+    end_ref[...] = rate_ref[:, :LANES]
+    f = load_filtered(f_ref, devices, rows, tiles)
+    leaves = cell_onehot(lcol_ref, cells)
+    rate = dot_split(jnp.broadcast_to(rate_ref[...], (SUB, cells)), leaves, NT)[:1]
+    pull = rate * dot_split(f, leaves, NT)
+    live = (lax.broadcasted_iota(I32, (SUB, listed), 1) < count_ref[0]).astype(F32).astype(BF)
+    live = dot(dot(live, ot_ref[...], NN).astype(BF), leaves, NT)[:1]
+    pull = jnp.concatenate([pull] * side, axis=1)
+    live = jnp.concatenate([live] * side, axis=1) > 0.5
+    count = 4 // wide
+
+    for o in range(particles // SUB // side):
+        for i in range(0, SUB, count):
+            ats = [pl.ds(o * rows * SUB + i + u, rows, stride=SUB) for u in range(count)]
+            x = jnp.concatenate(
+                [base_ref[t, at, :] + pull[:, t * LANES : (t + 1) * LANES] for at in ats for t in range(wide)],
+                axis=1,
+            )
+            one = half_silu(dot(w1_ref[...], x.astype(BF), NN))
+            two = half_silu(dot(w2_ref[...], one, NN))
+            change = dot(w3_ref[...], two, NN).astype(BF).astype(F32)
+            for n, (at, t) in enumerate((at, t) for at in ats for t in range(wide)):
+                cols = slice(n * LANES, (n + 1) * LANES)
+                mask = live[:, t * LANES : (t + 1) * LANES]
+                v_ref[t, at, :] = x[:, cols] + jnp.where(mask, change[:, cols], 0.0)
+
+    per = LANES // particles
     stride = out_ref.shape[0] // devices
-    for i in range(own):
-        mine = source.reshape(devices, own, source.shape[1])[:, i] if own > 1 else source
-        for t in range(tiles):
-            at = pl.ds(i * tiles + t, devices, stride=stride)
-            out_ref[at, :] = mine[:, t * LANES : (t + 1) * LANES]
-
-
-def leave_rows(leave, f, r_ref, base_ref, rate_ref, lcol_ref, rrow_ref, out_ref):
-    devices, span, scalars = leave["devices"], leave["span"], leave["scalars"]
-    rows, cells = f.shape
-    particles = r_ref.shape[1] // rows
-    per = LANES // particles
-    places = lcol_ref.shape[0]
-    stride = out_ref.shape[0] // devices
-    width = stride - places // devices * span
-    leaves = cell_onehot(lcol_ref, cells)
-    high, low = halves(f * rate_ref[...])
-    pull = dot(leaves, high, NT) + dot(leaves, low, NT)
-    reacts = (lcol_ref[...] == rrow_ref[...]).astype(F32).astype(BF)
-    pull = jnp.concatenate([*halves(pull), reacts], axis=1)
+
+    def scalar(s):
+        parts = []
+        for o in range(particles // SUB // side):
+            at = pl.ds(o * rows * SUB + s * SUB, SUB)
+            row = jnp.concatenate([v_ref[t, at, :] for t in range(wide)], axis=1)
+            parts += [row[:, u * places : (u + 1) * places] for u in range(side)]
+        return jnp.concatenate(parts, axis=0)
 
     def part(b, count):
-        wide = count * particles
-        r = jnp.concatenate([get_scalar(r_ref, b * per + i, rows) for i in range(count)], axis=0)
-        of = lax.broadcasted_iota(I32, (wide, rows), 0) // particles + b * per
-        mine = (of == lax.broadcasted_iota(I32, (wide, rows), 1)).astype(F32).astype(BF)
-        value = dot(pull, jnp.concatenate([mine, mine, r.astype(BF)], axis=1), NT)
-        value = base_ref[pl.ds(b, places, stride=span), :][:, :wide] + value
+        value = jnp.concatenate([scalar(b * per + i) for i in range(count)], axis=0)
+        if count < per:
+            rest = jnp.zeros(((per - count) * particles, places), F32)
+            value = jnp.concatenate([value, rest], axis=0)
+        value = value.T
         for c in range(places // devices):
-            at = pl.ds(width + c * span + b, devices, stride=stride)
-            out_ref[at, :wide] = value[c * devices : (c + 1) * devices]
+            at = pl.ds(c * span + b, devices, stride=stride)
+            out_ref[at, :] = value[c * devices : (c + 1) * devices]
 
     def step(b, carry):
         part(b, per)
@@ -465,14 +523,69 @@
     zeros = jnp.zeros((devices, LANES), F32)
     for c in range(places // devices):
         for b in range(whole, span):
-            out_ref[pl.ds(width + c * span + b, devices, stride=stride), :] = zeros
+            out_ref[pl.ds(c * span + b, devices, stride=stride), :] = zeros
     if scalars > whole * per:
         part(whole, scalars - whole * per)
+
+
+def maps_body(dims, me_ref, inv_ref, ot_ref, owner_ref, slot_ref, pos_ref, put_ref):
+    nx, ny, own, bx, by = dims
+    quads = bx * by
+    turns = quads * ny
+    listed, cells = ot_ref.shape
+    at = me_ref[0] * 2 * turns + me_ref[1]
+    code = jnp.concatenate([inv_ref[pl.ds(at + k * ny, 1), :] for k in range(quads)], axis=1)
+    box = lax.rem(code, ny).astype(F32)
+    boxes = lax.broadcasted_iota(I32, (ny, cells), 0).astype(F32)
+    mine = (jnp.broadcast_to(box, (ny, cells)) == boxes).astype(F32)
+    before = lax.broadcasted_iota(I32, (cells, cells), 0) < lax.broadcasted_iota(
+        I32, (cells, cells), 1
+    )
+    count = dot(mine.astype(BF), before.astype(F32).astype(BF), NN)
+    rank = jnp.sum(mine * count, axis=0, keepdims=True)
+    rest = jnp.zeros((SUB - 2, cells), F32)
+    found = dot(ot_ref[...], jnp.concatenate([box, rank, rest], axis=0).astype(BF), NT)
+    pos = found[:, :1] * LANES + found[:, 1:2]
+    pos_ref[...] = jnp.broadcast_to(pos, pos_ref.shape)
+    flat = lambda ref: jnp.concatenate([ref[j : j + 1, :] for j in range(quads)], axis=1)
+    owner, slot = flat(owner_ref).astype(F32), flat(slot_ref).astype(F32)
+    first = owner * cells
+    key = first + slot
+    column = jnp.broadcast_to(key, (SUB, cells)).T[:, :1]
+    ahead = (column < key) & (column >= first)
+    place = owner * LANES + jnp.sum(ahead.astype(F32), axis=0, keepdims=True)
+    step = min(cells, put_ref.shape[0])
+    for b in range(put_ref.shape[0] // step):
+        row = lax.broadcasted_iota(I32, (step, cells), 0).astype(F32) + b * step
+        put_ref[b * step : (b + 1) * step] = (row == place).astype(F32).astype(BF)
+
+
+def unpack_body(devices, own, s_ref, arr_ref, put_ref, out_ref):
+    boxes, rows = s_ref.shape[:2]
+    cells = put_ref.shape[1]
+    quads = cells // LANES
+    scalars = out_ref.shape[0] // quads
+    stride = arr_ref.shape[0] // devices
+    got = jnp.concatenate([s_ref[b] for b in range(boxes)], axis=1)
+    source = dot_split(got, put_ref[...], NN)
+    for j in range(quads):
+        for i in range(own):
+            n = min(devices, scalars - i * devices)
+            if n > 0:
+                grid = arr_ref[pl.ds(stride - own * quads + i * quads + j, n, stride=stride), :]
+                part = source[i * devices : i * devices + n, j * LANES : (j + 1) * LANES]
+                out_ref[pl.ds(i * devices * quads + j, n, stride=quads), :] = grid + part
+
+
+def cell_onehot(col_ref, cells):
+    shape = (col_ref.shape[0], cells)
+    return (col_ref[...] == lax.broadcasted_iota(I32, shape, 1)).astype(F32).astype(BF)
 
 
 def settle_body(
     rows,
     block,
+    devices,
     q_hbm,
     f_ref,
     r_hbm,
@@ -496,7 +609,7 @@
 
     def step(b, carry):
         into.copy(b).wait()
-        settle_block(b * block, block, q_ref, f_ref, r_ref, ot_ref, rate_ref, out_ref, rows)
+        settle_block(b * block, block, q_ref, f_ref, r_ref, ot_ref, rate_ref, out_ref, rows, devices)
         out.copy(b).start()
         return carry
 
@@ -632,13 +745,15 @@
     slot = slot_ref[...]
     label = ((slot >> 7) * lanes_y + owner_ref[...]) * LANES + (slot & (LANES - 1))
     tail = jnp.concatenate([label.astype(F32), speed_ref[...]], axis=0)
-    for d in range(out_ref.shape[0] // stride):
-        count = max(0, min(width, total - d * width))
-        if count:
-            out_ref[d * stride : d * stride + count] = grid_ref[d * width : d * width + count]
-        if count < width:
-            zeros = jnp.zeros((width - count, LANES), F32)
-            out_ref[d * stride + count : d * stride + width] = zeros
+    devices = out_ref.shape[0] // stride
+    for d in range(devices):
+        for i in range(width // quads):
+            at = d * stride + i * quads
+            src = (i * devices + d) * quads
+            if src < total:
+                out_ref[at : at + quads] = grid_ref[src : src + quads]
+            else:
+                out_ref[at : at + quads] = jnp.zeros((quads, LANES), F32)
         out_ref[d * stride + width : (d + 1) * stride] = tail
 
 
@@ -697,23 +812,26 @@
         return carry
 
     lax.fori_loop(0, nx, group, 0)
-    send_filtered(dims, g_ref, inv_ref, f_ref)
-
-
-def send_filtered(dims, g_ref, inv_ref, f_ref):
+    send_filtered(dims, g_ref, width, 0, inv_ref, f_ref)
+
+
+def send_filtered(dims, g_ref, g_stride, g_first, inv_ref, f_ref):
     nx, ny, own, bx, by = dims
     quads = bx * by
     width = own * quads
     turns = quads * ny
+    f_stride = f_ref.shape[0] // (nx * ny)
 
     def group(x, carry):
         base = x * 2 * turns
         rows = [inv_ref[pl.ds(base + k * ny, ny), :] for k in range(quads)]
         lanes = [inv_ref[pl.ds(base + turns + k * ny, ny), :] for k in range(quads)]
-        out = route(g_ref, x * ny * width, width, 1, quads, own, quads, ny, rows, lanes)
+        first = x * ny * g_stride + g_first
+        out = route(g_ref, first, g_stride, 1, quads, own, quads, ny, rows, lanes)
         for s in range(own):
             for k in range(quads):
-                f_ref[pl.ds(x * ny * width + s * quads + k, ny, stride=width), :] = out[s][k]
+                at = pl.ds(x * ny * f_stride + s * quads + k, ny, stride=f_stride)
+                f_ref[at, :] = out[s][k]
         return carry
 
     lax.fori_loop(0, nx, group, 0)
@@ -740,7 +858,7 @@
     lax.fori_loop(0, nx, group, 0)
 
 
-def again_body(dims, s_ref, g_ref, arr_ref, inv_ref, lab_ref, token_ref, out_ref, f_ref, mid_ref):
+def again_body(dims, s_ref, g_ref, arr_ref, inv_ref, lab_ref, token_ref, f_ref, mid_ref):
     nx, ny, own, bx, by = dims
     quads = bx * by
     boxes = nx * ny
@@ -751,12 +869,8 @@
     for s in range(own):
         value = [load_rows(mid_ref, s * quads + j, width, boxes) for j in range(quads)]
         for j, v in enumerate(stencil(value, speed, bx, by, ny)):
-            out_ref[pl.ds(s * quads + j, boxes, stride=width), :] = v
-    send_filtered(dims, out_ref, inv_ref, f_ref)
-
-
-def last_body(dims, s_ref, g_ref, lab_ref, token_ref, out_ref):
-    add_source(dims, s_ref, g_ref, lab_ref, out_ref)
+            f_ref[pl.ds(width + s * quads + j, boxes, stride=2 * width), :] = v
+    send_filtered(dims, f_ref, 2 * width, width, inv_ref, f_ref)
 
 
 def per_device(
@@ -869,77 +983,91 @@
     per = LANES // heads
     span = SUB * (-(-scalars // (per * SUB)))
     places = leave_slots.shape[1]
+    side = max(1, LANES // places)
+    base_shape = (max(1, places // LANES), octets // side * rows * SUB, LANES)
+    kept = SUB * (-(-scalars // SUB))
     pair = pltpu.VMEM((hidden, 2 * listed), BF)
-
-    def chemistry(f, a, token, leave=None, more=()):
-        out = (flat + places * span, LANES) if leave else (flat, LANES)
-        extra = [pltpu.VMEM((places * span, LANES), F32), dma] if leave else []
+    me = jnp.stack([lax.axis_index("gx"), lax.axis_index("gy")]).astype(I32)
+    pos, put = call(
+        functools.partial(maps_body, dims),
+        [((listed, LANES), F32), ((ny * LANES, cells), BF)],
+        [me, inv, ot, box[1], box[2]],
+        smem=(0,),
+        name="maps",
+    )
+
+    def chemistry(f, a, token, out, more=()):
         return call(
-            functools.partial(chem_body, leave),
+            functools.partial(chem_body, devices, rows),
             [(listed_shape, F32, True), (out, F32)],
             [react_count, f, a, ot, rsel, w1, w2, w3, token, *more],
             smem=(0,),
-            hbm=(2, 9) if leave else (2,),
+            hbm=(2,),
             scratch=[listed_vmem, listed_vmem, pltpu.VMEM((rows, listed), F32)]
             + [pair] * 4
-            + [dma((octets,)), dma((octets,))]
-            + extra,
+            + [dma((octets,)), dma((octets,))],
             name="chem",
         )
 
-    token = rsel
-    for substep in range(SUBSTEPS - 1):
-        f = exchange(sent)
-        change, source = chemistry(f, a, token)
-        home = exchange(source)
-        q, token = call(
-            functools.partial(middle_body, rows, block),
-            [(state_shape, F32, True), ((1, LANES), F32)],
-            [q, f, change, ot, rate, partner],
-            hbm=(0, 2),
-            scratch=[state_vmem, state_vmem, listed_vmem, per_block, per_block, dma],
-            name="middle",
-        )
-        grid, sent = call(
-            functools.partial(again_body, dims),
-            [((flat, LANES), F32), ((flat, LANES), F32)],
-            [home, grid, arrival, inv, lab, token],
-            scratch=[pltpu.VMEM((flat, LANES), F32)],
-            name="again",
-        )
-        a, base, token = call(
-            functools.partial(list_body, rows, span),
-            [(listed_shape, F32, True), ((places * span, LANES), F32, True), ((1, LANES), F32)],
-            [q, rate, rsel, ot, lcol],
-            hbm=(0,),
-            scratch=[
-                state_vmem,
-                listed_vmem,
-                pltpu.VMEM((places * span, LANES), F32),
-                dma((-(-scalars // per),)),
-                dma((2,)),
-            ],
-            name="list",
-        )
     f = exchange(sent)
-    leave = dict(devices=devices, span=span, scalars=scalars)
-    change, leaving = chemistry(f, a, token, leave, [base, rate, lcol, react_slots])
+    change, source = chemistry(f, a, pos, (flat, LANES))
+    home = exchange(source)
+    q, token = call(
+        functools.partial(middle_body, rows, block, devices),
+        [(state_shape, F32, True), ((1, LANES), F32)],
+        [q, f, change, ot, rate, partner],
+        hbm=(0, 2),
+        scratch=[state_vmem, state_vmem, listed_vmem, per_block, per_block, dma],
+        name="middle",
+    )
+    (sent,) = call(
+        functools.partial(again_body, dims),
+        [((2 * flat, LANES), F32)],
+        [home, grid, arrival, inv, lab, token],
+        scratch=[pltpu.VMEM((flat, LANES), F32)],
+        name="again",
+    )
+    a, base, token = call(
+        functools.partial(list_body, rows),
+        [(listed_shape, F32, True), (base_shape, F32, True), ((1, LANES), F32)],
+        [q, rate, rsel, ot, lcol],
+        hbm=(0,),
+        scratch=[
+            state_vmem,
+            listed_vmem,
+            pltpu.VMEM(base_shape, F32),
+            dma((-(-scalars // per),)),
+            dma((2,)),
+        ],
+        name="list",
+    )
+    f = exchange(sent)
+    leaving, token = call(
+        functools.partial(early_body, devices, rows, span, scalars, heads),
+        [((places * span, LANES), F32), ((1, LANES), F32)],
+        [react_count, f, base, ot, rate, lcol, w1, w2, w3, token],
+        smem=(0,),
+        scratch=[pltpu.VMEM(base_shape, F32)],
+        name="early",
+    )
+    change, source = chemistry(f, a, token, (ny, kept, LANES), [pos])
     moved = exchange(leaving)
     state, token = call(
-        functools.partial(settle_body, rows, block),
+        functools.partial(settle_body, rows, block, devices),
         [(state_shape, F32, True), ((1, LANES), F32)],
         [q, f, change, ot, rate],
         hbm=(0, 2),
         scratch=[state_vmem, state_vmem, listed_vmem, per_block, per_block, dma],
         name="settle",
     )
+    source = lax.all_to_all(source, "gy", split_axis=0, concat_axis=0, tiled=True)
     (grid,) = call(
-        functools.partial(last_body, dims),
-        [((flat, LANES), F32)],
-        [moved, grid, lab, token],
-        name="last",
-    )
-    grid_out = exchange(grid).reshape(rows, bx, by, nz)[:scalars]
+        functools.partial(unpack_body, devices, own),
+        [((scalars * quads, LANES), F32)],
+        [source, f, put],
+        name="unpack",
+    )
+    grid_out = grid.reshape(grid_scalars.shape)
     steps = -(-scalars // per)
     (state,) = call(
         functools.partial(arrive_body, span, devices),

time: 126 us -> 129 us (1.024)
  blocking collectives: 0 us -> 12.5 us
  waiting for transfers between devices: 23.1 us -> 15.9 us
  starting transfers between devices: 29.4 us -> 24.5 us
  Pallas kernels: 67.9 us -> 70.8 us
    all_to_all x0 -> x1, blocking collectives: none -> 12.5 us  [per_device(): lax.all_to_all(source, 'gy', split_axis=0, concat_axis=0, tiled=True)]
    all_to_all x6 -> x5, waiting for transfers between devices: 23.1 us -> 15.9 us  [exchange(): lax.all_to_all(x, both, split_axis=0, concat_axis=0, tiled=True)]
    all_to_all x6 -> x5, starting transfers between devices: 29.4 us -> 24.5 us  [exchange(): lax.all_to_all(x, both, split_axis=0, concat_axis=0, tiled=True)]
    pallas_call x12 -> x14, Pallas kernels: 67.9 us -> 70.8 us  [call(): pl.pallas_call(body, out_shape=[pltpu.HBM(o[0], o[1]) if len(o) > 2 else...]
  transfers between devices with their start and end apart: 6 -> 5, of which waited for: 4 -> 4; matrix products, arithmetic and copies ran while one was open for 2% -> 2% of each run, Pallas kernels for 29% -> 26%
where the time goes in v5:
time: 129 us
  Pallas kernels  70.8 us (55%)
  starting transfers between devices  24.5 us (19%)
  waiting for transfers between devices  15.9 us (12%)
  blocking collectives  12.5 us (10%)
  local copies, waits for them, and re-layouts  2.18 us (2%)
  between operations  1.55 us (1%)
  other arithmetic  1.41 us (1%)
    pallas_call x14, Pallas kernels, call(): pl.pallas_call(body, out_shape=[pltpu.HBM(o[0], o[1]) if len(o) > 2 else...  70.8 us
    all_to_all x5, starting transfers between devices, exchange(): lax.all_to_all(x, both, split_axis=0, concat_axis=0, tiled=True)  24.5 us
    all_to_all x5, waiting for transfers between devices, exchange(): lax.all_to_all(x, both, split_axis=0, concat_axis=0, tiled=True)  15.9 us
    all_to_all x1, blocking collectives, per_device(): lax.all_to_all(source, 'gy', split_axis=0, concat_axis=0, tiled=True)  12.5 us
  transfers between devices with their start and end apart: 5, of which 4 were waited for; matrix products, arithmetic and copies ran while one was open for 2% of the time, Pallas kernels for 26%

profile of v5, /device:TPU:0, one launch (start us, length us, event | category | flops | bytes accessed | tf_op | source)
XLA Modules:
  0.0 128.9 jit_solution(14748540496410389619)
XLA Ops:
  0.6 0.0 copy-start.6
  0.6 0.0 copy-start.7
  0.7 0.0 copy-start.4
  0.7 0.0 copy-start.2
  0.7 0.0 copy-start.5
  0.7 1.7 %pack.1 = f32[512,128]{1,0:T(8,128)} custom-call(f32[216,128]{1,0:T(8,128)} %bitcast.42, s32[4,128]{1,0:T(4,128)} %bitcast.37, s32[4,128]{1,0:T(4,128)} %bitcast.39, f32[4,128]{1,0:T(4,128)} %bitcast.45), custom_call_target="tpu_custom_call" | custom-call | tf_op jit(solution)/shard_map/pack/pallas_call | solution.py:25
  2.4 7.3 %all-to-all-start = ((f32[32,16,128]{2,1,0:T(8,128)}), f32[32,16,128]{2,1,0:T(8,128)S(1)}, u32[]{:S(2)}, u32[]{:S(2)}) async-start(f32[32,16,128]{2,1,0:T(8,128)} %bitcast.4), calls=%async_computation | async-start | bytes 524288 | tf_op jit(solution)/shard_map/all_to_all | solution.py:925
  9.7 0.0 copy-start.1
  9.8 0.0 copy-start.3
  9.8 9.4 %open.1 = (f32[54,32,512]{2,1,0:T(8,128)}, f32[2,2048,128]{2,1,0:T(8,128)}, bf16[256,512]{1,0:T(8,128)(2,1)S(1)}, f32[8,256]{1,0:T(8,128)S(1)}) custom-call(f32[54,32,512]{2,1,0:T(8,128)} %p_hbm.1, s32[32,512]{1,0:T(8,128)} %partner_ref.1, f32[1,512]{1,0:T(1,128)} %bitcast.31, s32[1,256]{1,0:T(1,128)} %list_hbm.1), custom_call_target="tpu_custom_call" | custom-call | tf_op jit(solution)/shard_map/open/pallas_call | solution.py:25
  19.1 0.6 all-to-all-done
  19.7 5.7 %start.1 = (f32[256,128]{1,0:T(8,128)S(1)}, f32[256,128]{1,0:T(8,128)}, s32[256,128]{1,0:T(8,128)S(1)}, s32[128,128]{1,0:T(8,128)S(1)}) custom-call(f32[512,128]{1,0:T(8,128)S(1)} %bitcast.25, f32[8,256]{1,0:T(8,128)S(1)} %get-tuple-element.27.token_ref.rsel_ref), custom_call_target="tpu_custom_call" | custom-call | tf_op jit(solution)/shard_map/start/pallas_call | solution.py:25
  25.4 5.2 %all-to-all-start.1 = ((f32[32,8,128]{2,1,0:T(8,128)}), f32[32,8,128]{2,1,0:T(8,128)S(1)}, u32[]{:S(2)}, u32[]{:S(2)}) async-start(f32[32,8,128]{2,1,0:T(8,128)} %bitcast.7), calls=%async_computation.1 | async-start | bytes 262144 | tf_op jit(solution)/shard_map/all_to_all | solution.py:925
  31.3 0.1 pad_add_fusion.me_ref
  31.4 1.5 %maps.1 = (f32[256,128]{1,0:T(8,128)S(1)}, bf16[1024,512]{1,0:T(8,128)(2,1)S(1)}) custom-call(s32[2]{0:T(128)S(1)} %pad_add_fusion.me_ref, s32[256,128]{1,0:T(8,128)S(1)} %get-tuple-element.35.inv_ref, bf16[256,512]{1,0:T(8,128)(2,1)S(1)} %get-tuple-element.30.ot_ref, s32[4,128]{1,0:T(4,128)S(1)} %bitcast.38, s32[4,128]{1,0:T(4,128)S(1)} %bitcast.40), custom_call_target="tpu_custom_call" | custom-call | tf_op jit(solution)/shard_map/maps/pallas_call | solution.py:25
  32.9 0.1 weights.1
  33.0 5.8 %all-to-all-done.1 = f32[32,8,128]{2,1,0:T(8,128)S(1)} async-done(((f32[32,8,128]{2,1,0:T(8,128)}), f32[32,8,128]{2,1,0:T(8,128)S(1)}, u32[]{:S(2)}, u32[]{:S(2)}) %all-to-all-start.1) | async-done | bytes 131104 | tf_op jit(solution)/shard_map/all_to_all | solution.py:925
  38.8 8.3 %chem.2 = (f32[2,2048,128]{2,1,0:T(8,128)}, f32[256,128]{1,0:T(8,128)}) custom-call(s32[1]{0:T(128)S(6)} %copy.26.count_ref, f32[256,128]{1,0:T(8,128)S(1)} %bitcast.28, f32[2,2048,128]{2,1,0:T(8,128)} %get-tuple-element.29.a_hbm, bf16[256,512]{1,0:T(8,128)(2,1)S(1)} %get-tuple-element.30.ot_ref, f32[8,256]{1,0:T(8,128)S(1)} %get-tuple-element.27.token_ref.rsel_ref, ...), custom_call_target="tpu_custom_call" | custom-call | tf_op jit(solution)/shard_map/chem/pallas_call | solution.py:25
  47.2 2.6 %all-to-all-start.2 = ((f32[32,8,128]{2,1,0:T(8,128)}), f32[32,8,128]{2,1,0:T(8,128)S(1)}, u32[]{:S(2)}, u32[]{:S(2)}) async-start(f32[32,8,128]{2,1,0:T(8,128)} %bitcast.12), calls=%async_computation.2 | async-start | bytes 262144 | tf_op jit(solution)/shard_map/all_to_all | solution.py:925
  49.8 0.0 copy-done.1
  49.8 0.0 copy-done.3
  49.8 0.0 copy-start.8
  49.8 8.4 %middle.1 = (f32[54,32,512]{2,1,0:T(8,128)}, f32[1,128]{1,0:T(1,128)S(1)}) custom-call(f32[54,32,512]{2,1,0:T(8,128)} %get-tuple-element.39.q_hbm, f32[256,128]{1,0:T(8,128)S(1)} %bitcast.29, f32[2,2048,128]{2,1,0:T(8,128)} %get-tuple-element.40.r_hbm, bf16[256,512]{1,0:T(8,128)(2,1)S(1)} %get-tuple-element.30.ot_ref, f32[1,512]{1,0:T(1,128)S(1)} %bitcast.32, ...), custom_call_target="tpu_custom_call" | custom-call | tf_op jit(solution)/shard_map/middle/pallas_call | solution.py:25
  58.2 0.0 all-to-all-done.2
  58.2 3.7 %again.1 = f32[512,128]{1,0:T(8,128)} custom-call(f32[256,128]{1,0:T(8,128)S(1)} %bitcast.30, f32[256,128]{1,0:T(8,128)S(1)} %get-tuple-element.38.g_ref, f32[512,128]{1,0:T(8,128)S(1)} %bitcast.26, s32[256,128]{1,0:T(8,128)S(1)} %get-tuple-element.35.inv_ref, s32[128,128]{1,0:T(8,128)S(1)} %get-tuple-element.31.token_ref.lab_ref, ...), custom_call_target="tpu_custom_call" | custom-call | tf_op jit(solution)/shard_map/again/pallas_call | solution.py:25
  61.9 5.8 %all-to-all-start.3 = ((f32[32,16,128]{2,1,0:T(8,128)}), f32[32,16,128]{2,1,0:T(8,128)S(1)}, u32[]{:S(2)}, u32[]{:S(2)}) async-start(f32[32,16,128]{2,1,0:T(8,128)} %bitcast.14), calls=%async_computation.3 | async-start | bytes 524288 | tf_op jit(solution)/shard_map/all_to_all | solution.py:925
  67.7 0.5 broadcast.6
  68.3 0.7 reduce.6
  68.9 0.1 reshape.77
  69.0 0.1 copy.21
  69.1 0.1 reshape.84.lcol_ref
  69.2 7.3 %list.1 = (f32[2,2048,128]{2,1,0:T(8,128)}, f32[1,1024,128]{2,1,0:T(8,128)}, f32[1,128]{1,0:T(1,128)S(1)}) custom-call(f32[54,32,512]{2,1,0:T(8,128)} %get-tuple-element.42.q_hbm, f32[1,512]{1,0:T(1,128)S(1)} %bitcast.33, f32[8,256]{1,0:T(8,128)S(1)} %get-tuple-element.27.token_ref.rsel_ref, bf16[256,512]{1,0:T(8,128)(2,1)S(1)} %get-tuple-element.30.ot_ref, ...), custom_call_target="tpu_custom_call" | custom-call | tf_op jit(solution)/shard_map/list/pallas_call | solution.py:25
  76.5 0.0 copy-start.9
  76.6 1.2 all-to-all-done.3
  77.7 1.0 copy-done
  78.8 4.2 %early.1 = (f32[1024,128]{1,0:T(8,128)}, f32[1,128]{1,0:T(1,128)S(1)}) custom-call(s32[1]{0:T(128)S(6)} %copy.26.count_ref, f32[512,128]{1,0:T(8,128)S(1)} %bitcast.21, f32[1,1024,128]{2,1,0:T(8,128)S(1)} %copy-done, bf16[256,512]{1,0:T(8,128)(2,1)S(1)} %get-tuple-element.30.ot_ref, f32[1,512]{1,0:T(1,128)S(1)} %bitcast.34, s32[64,1]{1,0:T(8,128)S(1)} %reshape.84.lcol_ref, ...), custom_call_target="tpu_custom_call" | custom-call | tf_op jit(solution)/shard_map/early/pallas_call | solution.py:25
  83.0 7.8 %chem.3 = (f32[2,2048,128]{2,1,0:T(8,128)}, f32[8,56,128]{2,1,0:T(8,128)S(1)}) custom-call(s32[1]{0:T(128)S(6)} %copy.26.count_ref, f32[512,128]{1,0:T(8,128)S(1)} %bitcast.22, f32[2,2048,128]{2,1,0:T(8,128)} %get-tuple-element.43.a_hbm, bf16[256,512]{1,0:T(8,128)(2,1)S(1)} %get-tuple-element.30.ot_ref, f32[8,256]{1,0:T(8,128)S(1)} %get-tuple-element.27.token_ref.rsel_ref, ...), custom_call_target="tpu_custom_call" | custom-call | tf_op jit(solution)/shard_map/chem/pallas_call | solution.py:25
  90.8 12.5 %all_to_all.30.s_ref = f32[8,56,128]{2,1,0:T(8,128)S(1)} all-to-all(f32[8,56,128]{2,1,0:T(8,128)S(1)} %get-tuple-element.47), channel_id=1, replica_groups=mesh['gx'=4,'gy'=8] {'gy'}, dimensions={0} | all-to-all | bytes 458752 | tf_op jit(solution)/shard_map/all_to_all | solution.py:1063
  103.3 3.5 %all-to-all-start.5 = ((f32[32,32,128]{2,1,0:T(8,128)}), f32[32,32,128]{2,1,0:T(8,128)S(1)}, u32[]{:S(2)}, u32[]{:S(2)}) async-start(f32[32,32,128]{2,1,0:T(8,128)} %bitcast.18), calls=%async_computation.5 | async-start | bytes 1048576 | tf_op jit(solution)/shard_map/all_to_all | solution.py:925
  106.8 0.0 copy-done.9
  106.8 0.7 reduce.7
  107.5 0.1 reshape.82
  107.6 0.1 copy.24
  107.7 0.1 reshape.85.acol_ref
  107.8 6.0 %settle.1 = (f32[54,32,512]{2,1,0:T(8,128)}, f32[1,128]{1,0:T(1,128)}) custom-call(f32[54,32,512]{2,1,0:T(8,128)} %get-tuple-element.42.q_hbm, f32[512,128]{1,0:T(8,128)S(1)} %bitcast.23, f32[2,2048,128]{2,1,0:T(8,128)} %get-tuple-element.49.r_hbm, bf16[256,512]{1,0:T(8,128)(2,1)S(1)} %get-tuple-element.30.ot_ref, f32[1,512]{1,0:T(1,128)S(1)} %bitcast.35), custom_call_target="tpu_custom_call" | custom-call | tf_op jit(solution)/shard_map/settle/pallas_call | solution.py:25
  113.8 1.0 unpack.1
  114.8 8.3 %all-to-all-done.5 = f32[32,32,128]{2,1,0:T(8,128)S(1)} async-done(((f32[32,32,128]{2,1,0:T(8,128)}), f32[32,32,128]{2,1,0:T(8,128)S(1)}, u32[]{:S(2)}, u32[]{:S(2)}) %all-to-all-start.5) | async-done | bytes 524320 | tf_op jit(solution)/shard_map/all_to_all | solution.py:925
  123.1 5.8 %arrive.1 = f32[54,32,512]{2,1,0:T(8,128)} custom-call(f32[54,32,512]{2,1,0:T(8,128)} %get-tuple-element.50.p_hbm, f32[1024,128]{1,0:T(8,128)S(1)} %bitcast.27, s32[64,1]{1,0:T(8,128)S(1)} %reshape.85.acol_ref), custom_call_target="tpu_custom_call" | custom-call | tf_op jit(solution)/shard_map/arrive/pallas_call | solution.py:25
  (7 shorter events, 0.0 us)
Async XLA Ops:
  0.6 30.8 %copy-start.6 = (s32[2,2,128]{2,1,0:T(2,128)S(1)}, s32[2,2,128]{2,1,0:T(2,128)}, u32[]{:S(2)}) copy-start(s32[2,2,128]{2,1,0:T(2,128)} %param.17) | copy-start | bytes 6148
  0.6 30.8 %copy-start.7 = (s32[2,2,128]{2,1,0:T(2,128)S(1)}, s32[2,2,128]{2,1,0:T(2,128)}, u32[]{:S(2)}) copy-start(s32[2,2,128]{2,1,0:T(2,128)} %param.18) | copy-start | bytes 6148
  0.7 32.2 %copy-start.4 = (bf16[256,54]{0,1:T(8,128)(2,1)S(1)}, bf16[256,54]{0,1:T(8,128)(2,1)}, u32[]{:S(2)}) copy-start(bf16[256,54]{0,1:T(8,128)(2,1)} %param.21) | copy-start | bytes 82948
  0.7 32.2 %copy-start.2 = (bf16[256,256]{1,0:T(8,128)(2,1)S(1)}, bf16[256,256]{1,0:T(8,128)(2,1)}, u32[]{:S(2)}) copy-start(bf16[256,256]{1,0:T(8,128)(2,1)} %w2_ref.1) | copy-start | bytes 393220
  0.7 32.2 %copy-start.5 = (bf16[54,256]{1,0:T(8,128)(2,1)S(1)}, bf16[54,256]{1,0:T(8,128)(2,1)}, u32[]{:S(2)}) copy-start(bf16[54,256]{1,0:T(8,128)(2,1)} %w3_ref.1) | copy-start | bytes 82948
  2.4 17.3 %all-to-all-start = ((f32[32,16,128]{2,1,0:T(8,128)}), f32[32,16,128]{2,1,0:T(8,128)S(1)}, u32[]{:S(2)}, u32[]{:S(2)}) async-start(f32[32,16,128]{2,1,0:T(8,128)} %bitcast.4), calls=%async_computation | async-start | bytes 524288 | tf_op jit(solution)/shard_map/all_to_all | solution.py:925
  9.7 40.1 %copy-start.1 = (s32[32,512]{1,0:T(8,128)S(1)}, s32[32,512]{1,0:T(8,128)}, u32[]{:S(2)}) copy-start(s32[32,512]{1,0:T(8,128)} %partner_ref.1) | copy-start | bytes 196612
  9.8 40.1 %copy-start.3 = (f32[512]{0:T(512)S(1)}, f32[512]{0:T(512)}, u32[]{:S(2)}) copy-start(f32[512]{0:T(512)} %param.19) | copy-start | bytes 6148
  25.4 13.4 %all-to-all-start.1 = ((f32[32,8,128]{2,1,0:T(8,128)}), f32[32,8,128]{2,1,0:T(8,128)S(1)}, u32[]{:S(2)}, u32[]{:S(2)}) async-start(f32[32,8,128]{2,1,0:T(8,128)} %bitcast.7), calls=%async_computation.1 | async-start | bytes 262144 | tf_op jit(solution)/shard_map/all_to_all | solution.py:925
  47.2 11.0 %all-to-all-start.2 = ((f32[32,8,128]{2,1,0:T(8,128)}), f32[32,8,128]{2,1,0:T(8,128)S(1)}, u32[]{:S(2)}, u32[]{:S(2)}) async-start(f32[32,8,128]{2,1,0:T(8,128)} %bitcast.12), calls=%async_computation.2 | async-start | bytes 262144 | tf_op jit(solution)/shard_map/all_to_all | solution.py:925
  49.8 18.4 %copy-start.8 = (s32[1,64]{1,0:T(1,128)S(1)}, s32[1,64]{1,0:T(1,128)}, u32[]{:S(2)}) copy-start(s32[1,64]{1,0:T(1,128)} %param.26) | copy-start | bytes 772
  61.9 15.8 %all-to-all-start.3 = ((f32[32,16,128]{2,1,0:T(8,128)}), f32[32,16,128]{2,1,0:T(8,128)S(1)}, u32[]{:S(2)}, u32[]{:S(2)}) async-start(f32[32,16,128]{2,1,0:T(8,128)} %bitcast.14), calls=%async_computation.3 | async-start | bytes 524288 | tf_op jit(solution)/shard_map/all_to_all | solution.py:925
  76.5 30.3 %copy-start.9 = (s32[1,64]{1,0:T(1,128)S(1)}, s32[1,64]{1,0:T(1,128)}, u32[]{:S(2)}) copy-start(s32[1,64]{1,0:T(1,128)} %param.27) | copy-start | bytes 772
  77.7 1.0 copy-start
  103.3 19.7 %all-to-all-start.5 = ((f32[32,32,128]{2,1,0:T(8,128)}), f32[32,32,128]{2,1,0:T(8,128)S(1)}, u32[]{:S(2)}, u32[]{:S(2)}) async-start(f32[32,32,128]{2,1,0:T(8,128)} %bitcast.18), calls=%async_computation.5 | async-start | bytes 1048576 | tf_op jit(solution)/shard_map/all_to_all | solution.py:925

commit v6 on v5

--- a/solution.py
+++ b/solution.py
@@ -6,6 +6,7 @@
 from jax.experimental import pallas as pl
 from jax.experimental.pallas import tpu as pltpu
 from jax.sharding import PartitionSpec as P
+
 
 DIFFUSION = 0.1
 PAIR_WEIGHT = 0.4
@@ -19,7 +20,7 @@
 NN = (((1,), (0,)), ((), ()))
 
 
-def call(body, outs, ins, smem=(), hbm=(), scratch=(), limit=24, name=None):
+def call(body, outs, ins, smem=(), hbm=(), scratch=(), limit=24):
     spaces = {**{i: pltpu.SMEM for i in smem}, **{i: pl.ANY for i in hbm}}
     ins = [pltpu.with_memory_space_constraint(x, pltpu.HBM) if i in hbm else x for i, x in enumerate(ins)]
     return pl.pallas_call(
@@ -35,7 +36,6 @@
         ],
         scratch_shapes=list(scratch),
         compiler_params=pltpu.CompilerParams(vmem_limit_bytes=limit << 20),
-        name=name,
     )(*ins)
 
 
@@ -97,7 +97,7 @@
 
 
 def mix(s0, block, p_ref, partner_ref, q_ref):
-    scalars, particles, cells = p_ref.shape
+    _, particles, cells = p_ref.shape
     groups = particles // SUB
     for t in range(cells // LANES):
         lanes = pl.ds(t * LANES, LANES)
@@ -146,7 +146,7 @@
 
 
 def list_cells(s0, block, q_ref, onehot, keep, a_ref, rows):
-    scalars, particles, cells = q_ref.shape
+    _, particles, cells = q_ref.shape
     x = q_ref[pl.ds(s0, block)].reshape(block * particles, cells)
     y = dot_split(x, onehot, NT) * keep
     for i in range(block):
@@ -251,7 +251,7 @@
     a_sem,
     few_sem,
 ):
-    scalars, particles, cells = p_ref.shape
+    scalars, _, cells = p_ref.shape
     into, out = Stream(p_hbm, p_ref, in_sem, block), Stream(q_ref, q_hbm, out_sem, block)
     few = [
         pltpu.make_async_copy(src, dst, few_sem.at[i])
@@ -287,7 +287,7 @@
 
 
 def settle_block(s0, block, q_ref, f_ref, r_ref, ot_ref, rate_ref, out_ref, rows, devices):
-    scalars, particles, cells = q_ref.shape
+    _, particles, cells = q_ref.shape
     tiles = cells // LANES
     rate = rate_ref[...]
     keep = 1.0 - rate
@@ -450,7 +450,7 @@
     particles,
     count_ref,
     f_ref,
-    base_ref,
+    base_hbm,
     ot_ref,
     rate_ref,
     lcol_ref,
@@ -461,7 +461,11 @@
     out_ref,
     end_ref,
     v_ref,
+    base_ref,
+    sem,
 ):
+    load = pltpu.make_async_copy(base_hbm, base_ref, sem)
+    load.start()
     listed, cells = ot_ref.shape
     tiles = cells // LANES
     places = lcol_ref.shape[0]
@@ -477,6 +481,7 @@
     pull = jnp.concatenate([pull] * side, axis=1)
     live = jnp.concatenate([live] * side, axis=1) > 0.5
     count = 4 // wide
+    load.wait()
 
     for o in range(particles // SUB // side):
         for i in range(0, SUB, count):
@@ -528,11 +533,37 @@
         part(whole, scalars - whole * per)
 
 
-def maps_body(dims, me_ref, inv_ref, ot_ref, owner_ref, slot_ref, pos_ref, put_ref):
-    nx, ny, own, bx, by = dims
+def columns(row_ref, devices, out_ref, turn_ref):
+    places = row_ref.shape[1]
+    count = places // devices
+    column = jnp.broadcast_to(row_ref[...].astype(F32), (SUB, places)).T[:, :1]
+    turn_ref[...] = jnp.broadcast_to(column, turn_ref.shape)
+    for c in range(count):
+        part = turn_ref[pl.ds(c, devices, stride=count), :]
+        out_ref[c * devices : (c + 1) * devices] = part.astype(I32)
+
+
+def maps_body(
+    dims,
+    me_ref,
+    inv_ref,
+    ot_ref,
+    owner_ref,
+    slot_ref,
+    leave_ref,
+    arrive_ref,
+    pos_ref,
+    put_ref,
+    lcol_ref,
+    acol_ref,
+    turn_ref,
+):
+    nx, ny, _, bx, by = dims
+    columns(leave_ref, nx * ny, lcol_ref, turn_ref)
+    columns(arrive_ref, nx * ny, acol_ref, turn_ref)
     quads = bx * by
     turns = quads * ny
-    listed, cells = ot_ref.shape
+    _, cells = ot_ref.shape
     at = me_ref[0] * 2 * turns + me_ref[1]
     code = jnp.concatenate([inv_ref[pl.ds(at + k * ny, 1), :] for k in range(quads)], axis=1)
     box = lax.rem(code, ny).astype(F32)
@@ -561,7 +592,7 @@
 
 
 def unpack_body(devices, own, s_ref, arr_ref, put_ref, out_ref):
-    boxes, rows = s_ref.shape[:2]
+    boxes, _ = s_ref.shape[:2]
     cells = put_ref.shape[1]
     quads = cells // LANES
     scalars = out_ref.shape[0] // quads
@@ -579,7 +610,7 @@
 
 def cell_onehot(col_ref, cells):
     shape = (col_ref.shape[0], cells)
-    return (col_ref[...] == lax.broadcasted_iota(I32, shape, 1)).astype(F32).astype(BF)
+    return (col_ref[:, :1] == lax.broadcasted_iota(I32, shape, 1)).astype(F32).astype(BF)
 
 
 def settle_body(
@@ -625,7 +656,7 @@
     per = LANES // particles
     into, out = Stream(p_hbm, p_ref, in_sem, per), Stream(out_ref, out_hbm, out_sem, per)
     into.start_all()
-    hit = (acol_ref[...] == lax.broadcasted_iota(I32, (places, cells), 1)).astype(F32)
+    hit = (acol_ref[:, :1] == lax.broadcasted_iota(I32, (places, cells), 1)).astype(F32)
     hit_ref[...] = hit.astype(BF)
     taken = jnp.sum(hit, axis=0, keepdims=True) > 0.5
     stride = arr_ref.shape[0] // devices
@@ -818,7 +849,6 @@
 def send_filtered(dims, g_ref, g_stride, g_first, inv_ref, f_ref):
     nx, ny, own, bx, by = dims
     quads = bx * by
-    width = own * quads
     turns = quads * ny
     f_stride = f_ref.shape[0] // (nx * ny)
 
@@ -917,7 +947,6 @@
         box,
         hbm=(0, 1, 2, 3),
         scratch=[pltpu.VMEM(x.shape, x.dtype) for x in box] + [pltpu.SemaphoreType.DMA((4,))],
-        name="pack",
     )
 
     def exchange(x):
@@ -927,8 +956,6 @@
     arrival = exchange(first)
 
     rate = mix_rate.reshape(1, cells)
-    lcol = leave_slots.reshape(devices, -1).T.reshape(-1, 1)
-    acol = arrive_slots.reshape(devices, -1).T.reshape(-1, 1)
     state_shape = (scalars, heads, cells)
     listed_shape = (listed // LANES, heads * rows, LANES)
     block = divisor(scalars, 6)
@@ -959,7 +986,6 @@
             dma,
             dma((3,)),
         ],
-        name="open",
     )
     grid, sent, inv, lab = call(
         functools.partial(start_body, dims),
@@ -970,14 +996,12 @@
             ((quads * devices, LANES), I32),
         ],
         [arrival, rsel],
-        name="start",
     )
 
     w1, w2, w3 = call(
         weights_body,
         [((hidden, rows), BF), ((hidden, hidden), BF), ((rows, hidden), BF)],
         [chem_input.T, chem_hidden, chem_output, lab],
-        name="weights",
     )
 
     per = LANES // heads
@@ -988,12 +1012,17 @@
     kept = SUB * (-(-scalars // SUB))
     pair = pltpu.VMEM((hidden, 2 * listed), BF)
     me = jnp.stack([lax.axis_index("gx"), lax.axis_index("gy")]).astype(I32)
-    pos, put = call(
+    pos, put, lcol, acol = call(
         functools.partial(maps_body, dims),
-        [((listed, LANES), F32), ((ny * LANES, cells), BF)],
-        [me, inv, ot, box[1], box[2]],
+        [
+            ((listed, LANES), F32),
+            ((ny * LANES, cells), BF),
+            ((places, LANES), I32),
+            ((places, LANES), I32),
+        ],
+        [me, inv, ot, box[1], box[2], leave_slots, arrive_slots],
         smem=(0,),
-        name="maps",
+        scratch=[pltpu.VMEM((places, LANES), F32)],
     )
 
     def chemistry(f, a, token, out, more=()):
@@ -1006,7 +1035,6 @@
             scratch=[listed_vmem, listed_vmem, pltpu.VMEM((rows, listed), F32)]
             + [pair] * 4
             + [dma((octets,)), dma((octets,))],
-            name="chem",
         )
 
     f = exchange(sent)
@@ -1018,14 +1046,12 @@
         [q, f, change, ot, rate, partner],
         hbm=(0, 2),
         scratch=[state_vmem, state_vmem, listed_vmem, per_block, per_block, dma],
-        name="middle",
     )
     (sent,) = call(
         functools.partial(again_body, dims),
         [((2 * flat, LANES), F32)],
         [home, grid, arrival, inv, lab, token],
         scratch=[pltpu.VMEM((flat, LANES), F32)],
-        name="again",
     )
     a, base, token = call(
         functools.partial(list_body, rows),
@@ -1039,7 +1065,6 @@
             dma((-(-scalars // per),)),
             dma((2,)),
         ],
-        name="list",
     )
     f = exchange(sent)
     leaving, token = call(
@@ -1047,8 +1072,8 @@
         [((places * span, LANES), F32), ((1, LANES), F32)],
         [react_count, f, base, ot, rate, lcol, w1, w2, w3, token],
         smem=(0,),
-        scratch=[pltpu.VMEM(base_shape, F32)],
-        name="early",
+        hbm=(2,),
+        scratch=[pltpu.VMEM(base_shape, F32), pltpu.VMEM(base_shape, F32), dma],
     )
     change, source = chemistry(f, a, token, (ny, kept, LANES), [pos])
     moved = exchange(leaving)
@@ -1058,14 +1083,12 @@
         [q, f, change, ot, rate],
         hbm=(0, 2),
         scratch=[state_vmem, state_vmem, listed_vmem, per_block, per_block, dma],
-        name="settle",
     )
     source = lax.all_to_all(source, "gy", split_axis=0, concat_axis=0, tiled=True)
     (grid,) = call(
         functools.partial(unpack_body, devices, own),
         [((scalars * quads, LANES), F32)],
         [source, f, put],
-        name="unpack",
     )
     grid_out = grid.reshape(grid_scalars.shape)
     steps = -(-scalars // per)
@@ -1081,7 +1104,6 @@
             dma((steps,)),
             dma((steps,)),
         ],
-        name="arrive",
     )
     return (grid_out, state)
 
@@ -1103,6 +1125,7 @@
         P(("gx", "gy"), None),
         P(("gx", "gy"), None),
     )
+
     return jax.shard_map(
         per_device,
         mesh=mesh,

time: 129 us -> 128 us (level)
  waiting for transfers between devices: 15.9 us -> 18.4 us
  local copies, waits for them, and re-layouts: 2.18 us -> 0.04 us
  other arithmetic: 1.41 us -> 0.08 us
    all_to_all x5, waiting for transfers between devices: 15.9 us -> 18.4 us  [exchange(): lax.all_to_all(x, both, split_axis=0, concat_axis=0, tiled=True)]
    unnamed x21 -> x18, local copies, waits for them, and re-layouts: 1.6 us -> 0.04 us
    unnamed x2 -> x0, other arithmetic: 1.33 us -> none
  transfers between devices with their start and end apart: 5 -> 5, of which waited for: 4 -> 4; matrix products, arithmetic and copies ran while one was open for 2% -> 0% of each run, Pallas kernels for 26% -> 26%
where the time goes in v6:
time: 128 us; the launch traced here: 127 us
  Pallas kernels  71.6 us (56%)
  starting transfers between devices  23.9 us (19%)
  waiting for transfers between devices  18.4 us (14%)
  blocking collectives  11.7 us (9%)
  between operations  1.53 us (1%)
    pallas_call x14, Pallas kernels, call(): pl.pallas_call(body, out_shape=[pltpu.HBM(o[0], o[1]) if len(o) > 2 else...  71.6 us
    all_to_all x5, starting transfers between devices, exchange(): lax.all_to_all(x, both, split_axis=0, concat_axis=0, tiled=True)  23.9 us
    all_to_all x5, waiting for transfers between devices, exchange(): lax.all_to_all(x, both, split_axis=0, concat_axis=0, tiled=True)  18.4 us
    all_to_all x1, blocking collectives, per_device(): lax.all_to_all(source, 'gy', split_axis=0, concat_axis=0, tiled=True)  11.7 us
  transfers between devices with their start and end apart: 5, of which 4 were waited for; matrix products, arithmetic and copies ran while one was open for 0% of the time, Pallas kernels for 26%

profile of v6, /device:TPU:0, one launch (start us, length us, event | category | flops | bytes accessed | tf_op | source)
XLA Modules:
  0.0 127.1 jit_solution(4403378985966877825)
XLA Ops:
  0.6 0.0 copy-start.6
  0.6 0.0 copy-start.5
  0.7 0.0 copy-start.4
  0.7 0.0 copy-start.1
  0.7 0.0 copy-start.3
  0.7 0.0 copy-start.8
  0.7 0.0 copy-start.7
  0.7 1.7 %shard_map.149 = f32[512,128]{1,0:T(8,128)} custom-call(f32[216,128]{1,0:T(8,128)} %bitcast.40, s32[4,128]{1,0:T(4,128)} %bitcast.35, s32[4,128]{1,0:T(4,128)} %bitcast.37, f32[4,128]{1,0:T(4,128)} %bitcast.41), custom_call_target="tpu_custom_call" | custom-call | tf_op jit(solution)/shard_map/pallas_call | solution.py:26
  2.4 7.3 %all-to-all-start = ((f32[32,16,128]{2,1,0:T(8,128)}), f32[32,16,128]{2,1,0:T(8,128)S(1)}, u32[]{:S(2)}, u32[]{:S(2)}) async-start(f32[32,16,128]{2,1,0:T(8,128)} %bitcast.4), calls=%async_computation | async-start | bytes 524288 | tf_op jit(solution)/shard_map/all_to_all | solution.py:954
  9.8 0.0 copy-start
  9.8 0.0 copy-start.2
  9.8 9.4 %shard_map.150 = (f32[54,32,512]{2,1,0:T(8,128)}, f32[2,2048,128]{2,1,0:T(8,128)}, bf16[256,512]{1,0:T(8,128)(2,1)S(1)}, f32[8,256]{1,0:T(8,128)S(1)}) custom-call(f32[54,32,512]{2,1,0:T(8,128)} %p_hbm.1, s32[32,512]{1,0:T(8,128)} %partner_ref.1, f32[1,512]{1,0:T(1,128)} %bitcast.29, s32[1,256]{1,0:T(1,128)} %list_hbm.1), custom_call_target="tpu_custom_call" | custom-call | tf_op jit(solution)/shard_map/pallas_call | solution.py:26
  19.2 0.6 all-to-all-done
  19.8 5.7 %shard_map.151 = (f32[256,128]{1,0:T(8,128)S(1)}, f32[256,128]{1,0:T(8,128)}, s32[256,128]{1,0:T(8,128)S(1)}, s32[128,128]{1,0:T(8,128)S(1)}) custom-call(f32[512,128]{1,0:T(8,128)S(1)} %bitcast.23, f32[8,256]{1,0:T(8,128)S(1)} %get-tuple-element.29.token_ref.rsel_ref), custom_call_target="tpu_custom_call" | custom-call | tf_op jit(solution)/shard_map/pallas_call | solution.py:26
  25.4 5.3 %all-to-all-start.1 = ((f32[32,8,128]{2,1,0:T(8,128)}), f32[32,8,128]{2,1,0:T(8,128)S(1)}, u32[]{:S(2)}, u32[]{:S(2)}) async-start(f32[32,8,128]{2,1,0:T(8,128)} %bitcast.7), calls=%async_computation.1 | async-start | bytes 262144 | tf_op jit(solution)/shard_map/all_to_all | solution.py:954
  31.4 0.1 pad_add_fusion.me_ref
  31.5 0.0 copy-done.4
  31.5 0.0 copy-done.1
  31.5 0.0 copy-done.3
  31.5 0.1 shard_map.152
  31.6 0.0 copy-done.6
  31.6 0.0 copy-done.5
  31.6 0.0 copy-done.8
  31.6 0.0 copy-done.7
  31.6 1.5 %shard_map.153 = (f32[256,128]{1,0:T(8,128)S(1)}, bf16[1024,512]{1,0:T(8,128)(2,1)S(1)}, s32[64,128]{1,0:T(8,128)S(1)}, s32[64,128]{1,0:T(8,128)S(1)}) custom-call(s32[2]{0:T(128)S(1)} %pad_add_fusion.me_ref, s32[256,128]{1,0:T(8,128)S(1)} %get-tuple-element.37.inv_ref, bf16[256,512]{1,0:T(8,128)(2,1)S(1)} %get-tuple-element.32.ot_ref, ...), custom_call_target="tpu_custom_call" | custom-call | tf_op jit(solution)/shard_map/pallas_call | solution.py:26
  33.1 5.8 %all-to-all-done.1 = f32[32,8,128]{2,1,0:T(8,128)S(1)} async-done(((f32[32,8,128]{2,1,0:T(8,128)}), f32[32,8,128]{2,1,0:T(8,128)S(1)}, u32[]{:S(2)}, u32[]{:S(2)}) %all-to-all-start.1) | async-done | bytes 131104 | tf_op jit(solution)/shard_map/all_to_all | solution.py:954
  38.9 8.4 %shard_map.154 = (f32[2,2048,128]{2,1,0:T(8,128)}, f32[256,128]{1,0:T(8,128)}) custom-call(s32[1]{0:T(128)S(6)} %copy.16.count_ref, f32[256,128]{1,0:T(8,128)S(1)} %bitcast.26, f32[2,2048,128]{2,1,0:T(8,128)} %get-tuple-element.31.a_hbm, bf16[256,512]{1,0:T(8,128)(2,1)S(1)} %get-tuple-element.32.ot_ref, f32[8,256]{1,0:T(8,128)S(1)} %get-tuple-element.29.token_ref.rsel_ref, ...), custom_call_target="tpu_custom_call" | custom-call | tf_op jit(solution)/shard_map/pallas_call | solution.py:26
  47.3 2.6 %all-to-all-start.2 = ((f32[32,8,128]{2,1,0:T(8,128)}), f32[32,8,128]{2,1,0:T(8,128)S(1)}, u32[]{:S(2)}, u32[]{:S(2)}) async-start(f32[32,8,128]{2,1,0:T(8,128)} %bitcast.12), calls=%async_computation.2 | async-start | bytes 262144 | tf_op jit(solution)/shard_map/all_to_all | solution.py:954
  49.9 0.0 copy-done
  49.9 0.0 copy-done.2
  49.9 8.4 %shard_map.155 = (f32[54,32,512]{2,1,0:T(8,128)}, f32[1,128]{1,0:T(1,128)S(1)}) custom-call(f32[54,32,512]{2,1,0:T(8,128)} %get-tuple-element.41.q_hbm, f32[256,128]{1,0:T(8,128)S(1)} %bitcast.27, f32[2,2048,128]{2,1,0:T(8,128)} %get-tuple-element.42.r_hbm, bf16[256,512]{1,0:T(8,128)(2,1)S(1)} %get-tuple-element.32.ot_ref, f32[1,512]{1,0:T(1,128)S(1)} %bitcast.30, ...), custom_call_target="tpu_custom_call" | custom-call | tf_op jit(solution)/shard_map/pallas_call | solution.py:26
  58.2 0.0 all-to-all-done.2
  58.3 3.7 %shard_map.156 = f32[512,128]{1,0:T(8,128)} custom-call(f32[256,128]{1,0:T(8,128)S(1)} %bitcast.28, f32[256,128]{1,0:T(8,128)S(1)} %get-tuple-element.40.g_ref, f32[512,128]{1,0:T(8,128)S(1)} %bitcast.24, s32[256,128]{1,0:T(8,128)S(1)} %get-tuple-element.37.inv_ref, s32[128,128]{1,0:T(8,128)S(1)} %get-tuple-element.33.token_ref.lab_ref, ...), custom_call_target="tpu_custom_call" | custom-call | tf_op jit(solution)/shard_map/pallas_call | solution.py:26
  62.0 5.8 %all-to-all-start.3 = ((f32[32,16,128]{2,1,0:T(8,128)}), f32[32,16,128]{2,1,0:T(8,128)S(1)}, u32[]{:S(2)}, u32[]{:S(2)}) async-start(f32[32,16,128]{2,1,0:T(8,128)} %bitcast.14), calls=%async_computation.3 | async-start | bytes 524288 | tf_op jit(solution)/shard_map/all_to_all | solution.py:954
  67.8 7.3 %shard_map.157 = (f32[2,2048,128]{2,1,0:T(8,128)}, f32[1,1024,128]{2,1,0:T(8,128)}, f32[1,128]{1,0:T(1,128)S(1)}) custom-call(f32[54,32,512]{2,1,0:T(8,128)} %get-tuple-element.44.q_hbm, f32[1,512]{1,0:T(1,128)S(1)} %bitcast.31, f32[8,256]{1,0:T(8,128)S(1)} %get-tuple-element.29.token_ref.rsel_ref, bf16[256,512]{1,0:T(8,128)(2,1)S(1)} %get-tuple-element.32.ot_ref, ...), custom_call_target="tpu_custom_call" | custom-call | tf_op jit(solution)/shard_map/pallas_call | solution.py:26
  75.1 2.7 %all-to-all-done.3 = f32[32,16,128]{2,1,0:T(8,128)S(1)} async-done(((f32[32,16,128]{2,1,0:T(8,128)}), f32[32,16,128]{2,1,0:T(8,128)S(1)}, u32[]{:S(2)}, u32[]{:S(2)}) %all-to-all-start.3) | async-done | bytes 262176 | tf_op jit(solution)/shard_map/all_to_all | solution.py:954
  77.8 5.0 %shard_map.158 = (f32[1024,128]{1,0:T(8,128)}, f32[1,128]{1,0:T(1,128)S(1)}) custom-call(s32[1]{0:T(128)S(6)} %copy.16.count_ref, f32[512,128]{1,0:T(8,128)S(1)} %bitcast.19, f32[1,1024,128]{2,1,0:T(8,128)} %get-tuple-element.47.base_hbm, bf16[256,512]{1,0:T(8,128)(2,1)S(1)} %get-tuple-element.32.ot_ref, f32[1,512]{1,0:T(1,128)S(1)} %bitcast.32, ...), custom_call_target="tpu_custom_call" | custom-call | tf_op jit(solution)/shard_map/pallas_call | solution.py:26
  82.8 7.7 %shard_map.159 = (f32[2,2048,128]{2,1,0:T(8,128)}, f32[8,56,128]{2,1,0:T(8,128)S(1)}) custom-call(s32[1]{0:T(128)S(6)} %copy.16.count_ref, f32[512,128]{1,0:T(8,128)S(1)} %bitcast.20, f32[2,2048,128]{2,1,0:T(8,128)} %get-tuple-element.46.a_hbm, bf16[256,512]{1,0:T(8,128)(2,1)S(1)} %get-tuple-element.32.ot_ref, ...), custom_call_target="tpu_custom_call" | custom-call | tf_op jit(solution)/shard_map/pallas_call | solution.py:26
  90.6 11.7 %all_to_all.30.s_ref = f32[8,56,128]{2,1,0:T(8,128)S(1)} all-to-all(f32[8,56,128]{2,1,0:T(8,128)S(1)} %get-tuple-element.50), channel_id=1, replica_groups=mesh['gx'=4,'gy'=8] {'gy'}, dimensions={0} | all-to-all | bytes 458752 | tf_op jit(solution)/shard_map/all_to_all | solution.py:1087
  102.3 2.8 %all-to-all-start.5 = ((f32[32,32,128]{2,1,0:T(8,128)}), f32[32,32,128]{2,1,0:T(8,128)S(1)}, u32[]{:S(2)}, u32[]{:S(2)}) async-start(f32[32,32,128]{2,1,0:T(8,128)} %bitcast.17), calls=%async_computation.5 | async-start | bytes 1048576 | tf_op jit(solution)/shard_map/all_to_all | solution.py:954
  105.1 6.0 %shard_map.161 = (f32[54,32,512]{2,1,0:T(8,128)}, f32[1,128]{1,0:T(1,128)}) custom-call(f32[54,32,512]{2,1,0:T(8,128)} %get-tuple-element.44.q_hbm, f32[512,128]{1,0:T(8,128)S(1)} %bitcast.21, f32[2,2048,128]{2,1,0:T(8,128)} %get-tuple-element.52.r_hbm, bf16[256,512]{1,0:T(8,128)(2,1)S(1)} %get-tuple-element.32.ot_ref, f32[1,512]{1,0:T(1,128)S(1)} %bitcast.33), custom_call_target="tpu_custom_call" | custom-call | tf_op jit(solution)/shard_map/pallas_call | solution.py:26
  111.1 1.0 shard_map.160
  112.0 9.3 %all-to-all-done.5 = f32[32,32,128]{2,1,0:T(8,128)S(1)} async-done(((f32[32,32,128]{2,1,0:T(8,128)}), f32[32,32,128]{2,1,0:T(8,128)S(1)}, u32[]{:S(2)}, u32[]{:S(2)}) %all-to-all-start.5) | async-done | bytes 524320 | tf_op jit(solution)/shard_map/all_to_all | solution.py:954
  121.3 5.8 %shard_map.162 = f32[54,32,512]{2,1,0:T(8,128)} custom-call(f32[54,32,512]{2,1,0:T(8,128)} %get-tuple-element.53.p_hbm, f32[1024,128]{1,0:T(8,128)S(1)} %bitcast.25, s32[64,128]{1,0:T(8,128)S(1)} %get-tuple-element.55.acol_ref), custom_call_target="tpu_custom_call" | custom-call | tf_op jit(solution)/shard_map/pallas_call | solution.py:26
Async XLA Ops:
  0.6 30.9 %copy-start.6 = (s32[2,2,128]{2,1,0:T(2,128)S(1)}, s32[2,2,128]{2,1,0:T(2,128)}, u32[]{:S(2)}) copy-start(s32[2,2,128]{2,1,0:T(2,128)} %param.18) | copy-start | bytes 6148
  0.6 30.9 %copy-start.5 = (s32[2,2,128]{2,1,0:T(2,128)S(1)}, s32[2,2,128]{2,1,0:T(2,128)}, u32[]{:S(2)}) copy-start(s32[2,2,128]{2,1,0:T(2,128)} %param.17) | copy-start | bytes 6148
  0.7 30.8 %copy-start.4 = (bf16[54,256]{1,0:T(8,128)(2,1)S(1)}, bf16[54,256]{1,0:T(8,128)(2,1)}, u32[]{:S(2)}) copy-start(bf16[54,256]{1,0:T(8,128)(2,1)} %w3_ref.1) | copy-start | bytes 82948
  0.7 30.8 %copy-start.1 = (bf16[256,256]{1,0:T(8,128)(2,1)S(1)}, bf16[256,256]{1,0:T(8,128)(2,1)}, u32[]{:S(2)}) copy-start(bf16[256,256]{1,0:T(8,128)(2,1)} %w2_ref.1) | copy-start | bytes 393220
  0.7 30.8 %copy-start.3 = (bf16[256,54]{0,1:T(8,128)(2,1)S(1)}, bf16[256,54]{0,1:T(8,128)(2,1)}, u32[]{:S(2)}) copy-start(bf16[256,54]{0,1:T(8,128)(2,1)} %param.21) | copy-start | bytes 82948
  0.7 30.9 %copy-start.8 = (s32[1,64]{1,0:T(1,128)S(1)}, s32[1,64]{1,0:T(1,128)}, u32[]{:S(2)}) copy-start(s32[1,64]{1,0:T(1,128)} %arrive_ref.1) | copy-start | bytes 772
  0.7 30.9 %copy-start.7 = (s32[1,64]{1,0:T(1,128)S(1)}, s32[1,64]{1,0:T(1,128)}, u32[]{:S(2)}) copy-start(s32[1,64]{1,0:T(1,128)} %leave_ref.1) | copy-start | bytes 772
  2.4 17.3 %all-to-all-start = ((f32[32,16,128]{2,1,0:T(8,128)}), f32[32,16,128]{2,1,0:T(8,128)S(1)}, u32[]{:S(2)}, u32[]{:S(2)}) async-start(f32[32,16,128]{2,1,0:T(8,128)} %bitcast.4), calls=%async_computation | async-start | bytes 524288 | tf_op jit(solution)/shard_map/all_to_all | solution.py:954
  9.8 40.1 %copy-start = (s32[32,512]{1,0:T(8,128)S(1)}, s32[32,512]{1,0:T(8,128)}, u32[]{:S(2)}) copy-start(s32[32,512]{1,0:T(8,128)} %partner_ref.1) | copy-start | bytes 196612
  9.8 40.1 %copy-start.2 = (f32[512]{0:T(512)S(1)}, f32[512]{0:T(512)}, u32[]{:S(2)}) copy-start(f32[512]{0:T(512)} %param.19) | copy-start | bytes 6148
  25.4 13.4 %all-to-all-start.1 = ((f32[32,8,128]{2,1,0:T(8,128)}), f32[32,8,128]{2,1,0:T(8,128)S(1)}, u32[]{:S(2)}, u32[]{:S(2)}) async-start(f32[32,8,128]{2,1,0:T(8,128)} %bitcast.7), calls=%async_computation.1 | async-start | bytes 262144 | tf_op jit(solution)/shard_map/all_to_all | solution.py:954
  47.3 11.0 %all-to-all-start.2 = ((f32[32,8,128]{2,1,0:T(8,128)}), f32[32,8,128]{2,1,0:T(8,128)S(1)}, u32[]{:S(2)}, u32[]{:S(2)}) async-start(f32[32,8,128]{2,1,0:T(8,128)} %bitcast.12), calls=%async_computation.2 | async-start | bytes 262144 | tf_op jit(solution)/shard_map/all_to_all | solution.py:954
  62.0 15.8 %all-to-all-start.3 = ((f32[32,16,128]{2,1,0:T(8,128)}), f32[32,16,128]{2,1,0:T(8,128)S(1)}, u32[]{:S(2)}, u32[]{:S(2)}) async-start(f32[32,16,128]{2,1,0:T(8,128)} %bitcast.14), calls=%async_computation.3 | async-start | bytes 524288 | tf_op jit(solution)/shard_map/all_to_all | solution.py:954
  102.3 19.1 %all-to-all-start.5 = ((f32[32,32,128]{2,1,0:T(8,128)}), f32[32,32,128]{2,1,0:T(8,128)S(1)}, u32[]{:S(2)}, u32[]{:S(2)}) async-start(f32[32,32,128]{2,1,0:T(8,128)} %bitcast.17), calls=%async_computation.5 | async-start | bytes 1048576 | tf_op jit(solution)/shard_map/all_to_all | solution.py:954

commit v7 on v6

--- a/solution.py
+++ b/solution.py
@@ -120,41 +120,35 @@
         lax.fori_loop(s0, s0 + block, step, 0)
 
 
-def put_scalar(ref, s, value, rows):
-    for o in range(value.shape[0] // SUB):
-        for t in range(value.shape[1] // LANES):
+def put_scalar(ref, s, value):
+    for o in range(ref.shape[1]):
+        for t in range(ref.shape[0]):
             part = value[o * SUB : (o + 1) * SUB, t * LANES : (t + 1) * LANES]
-            ref[t, pl.ds(o * rows * SUB + s * SUB, SUB), :] = part
-
-
-def get_scalar(ref, s, rows):
-    octets = ref.shape[1] // (rows * SUB)
+            ref[t, o, pl.ds(s * SUB, SUB), :] = part
+
+
+def get_scalar(ref, s):
     return jnp.concatenate(
         [
             jnp.concatenate(
-                [ref[t, pl.ds(o * rows * SUB + s * SUB, SUB), :] for t in range(ref.shape[0])],
-                axis=1,
+                [ref[t, o, pl.ds(s * SUB, SUB), :] for t in range(ref.shape[0])], axis=1
             )
-            for o in range(octets)
+            for o in range(ref.shape[1])
         ],
         axis=0,
     )
 
 
-def particle_rows(p, rows):
-    return pl.ds((p >> 3) * (rows * SUB) + (p & (SUB - 1)), rows, stride=SUB)
-
-
-def list_cells(s0, block, q_ref, onehot, keep, a_ref, rows):
+def list_cells(s0, block, q_ref, onehot, keep, a_ref):
     _, particles, cells = q_ref.shape
     x = q_ref[pl.ds(s0, block)].reshape(block * particles, cells)
     y = dot_split(x, onehot, NT) * keep
     for i in range(block):
-        put_scalar(a_ref, s0 + i, y[i * particles : (i + 1) * particles], rows)
+        put_scalar(a_ref, s0 + i, y[i * particles : (i + 1) * particles])
 
 
 def list_body(
-    rows,
+    block,
     q_hbm,
     rate_ref,
     rsel_ref,
@@ -167,70 +161,61 @@
     a_ref,
     base_ref,
     in_sem,
-    out_sem,
+    a_sem,
+    base_sem,
 ):
     scalars, particles, cells = q_ref.shape
-    per = LANES // particles
-    into = Stream(q_hbm, q_ref, in_sem, per)
+    into = Stream(q_hbm, q_ref, in_sem, block)
+    out_a = Stream(a_ref, a_hbm, a_sem, block * SUB, 2)
+    out_base = Stream(base_ref, base_hbm, base_sem, block * SUB, 2)
     into.start_all()
     token_ref[...] = rate_ref[:, :LANES]
     leaves = cell_onehot(lcol_ref, cells)
     places = lcol_ref.shape[0]
     side = max(1, LANES // places)
     keep = 1.0 - rate_ref[...]
-
-    def part(b, count):
-        into.copy(b, count).wait()
-        x = q_ref[pl.ds(b * per, count)].reshape(count * particles, cells) * keep
-        high, low = halves(x)
-        both = jnp.concatenate([high, low], axis=0)
-        half = count * particles
+    half = block * particles
+
+    def step(b, carry):
+        into.copy(b).wait()
+        x = q_ref[pl.ds(b * block, block)].reshape(half, cells) * keep
+        both = jnp.concatenate(halves(x), axis=0)
         y = dot(both, ot_ref[...], NT)
         y = y[:half] + y[half:]
         z = dot(both, leaves, NT)
         z = z[:half] + z[half:]
-        for i in range(count):
-            put_scalar(a_ref, b * per + i, y[i * particles : (i + 1) * particles], rows)
-            for o in range(0, particles // SUB, side):
-                first = i * particles + o * SUB
-                octets = [z[first + u * SUB : first + (u + 1) * SUB] for u in range(side)]
-                at = pl.ds(o // side * rows * SUB + (b * per + i) * SUB, SUB)
+        for i in range(block):
+            put_scalar(a_ref, b * block + i, y[i * particles : (i + 1) * particles])
+            mine = z[i * particles : (i + 1) * particles]
+            for o in range(base_ref.shape[1]):
+                octets = [
+                    mine[(o * side + u) * SUB : (o * side + u + 1) * SUB] for u in range(side)
+                ]
                 wide = jnp.concatenate(octets, axis=1)
                 for t in range(base_ref.shape[0]):
-                    base_ref[t, at, :] = wide[:, t * LANES : (t + 1) * LANES]
-
-    def step(b, carry):
-        part(b, per)
+                    at = pl.ds((b * block + i) * SUB, SUB)
+                    base_ref[t, o, at, :] = wide[:, t * LANES : (t + 1) * LANES]
+        out_a.copy(b).start()
+        out_base.copy(b).start()
         return carry
 
-    whole = scalars // per
-    lax.fori_loop(0, whole, step, 0)
-    if scalars > whole * per:
-        part(whole, scalars - whole * per)
-    clear_rest(scalars, rows, a_ref)
-    for o in range(particles // SUB // side):
-        rest = (rows - scalars) * SUB
-        at = pl.ds(o * rows * SUB + scalars * SUB, rest)
-        base_ref[:, at, :] = jnp.zeros((base_ref.shape[0], rest, LANES), F32)
-    copies = [
-        pltpu.make_async_copy(a_ref, a_hbm, out_sem.at[0]),
-        pltpu.make_async_copy(base_ref, base_hbm, out_sem.at[1]),
-    ]
-    for c in copies:
-        c.start()
-    for c in copies:
-        c.wait()
-
-
-def clear_rest(scalars, rows, a_ref):
-    particles = a_ref.shape[1] // rows
-    zeros = jnp.zeros((particles, a_ref.shape[0] * LANES), F32)
-    for s in range(scalars, rows):
-        put_scalar(a_ref, s, zeros, rows)
+    lax.fori_loop(0, scalars // block, step, 0)
+    for ref, out in ((a_ref, out_a), (base_ref, out_base)):
+        clear_rest(scalars, ref)
+        for b in range(scalars // block, out.count):
+            out.copy(b, out.tail(b)).start()
+    out_a.wait_all()
+    out_base.wait_all()
+
+
+def clear_rest(scalars, ref):
+    rest = ref.shape[2] - scalars * SUB
+    for t in range(ref.shape[0]):
+        for o in range(ref.shape[1]):
+            ref[t, o, pl.ds(scalars * SUB, rest), :] = jnp.zeros((rest, LANES), F32)
 
 
 def open_body(
-    rows,
     block,
     p_hbm,
     partner_hbm,
@@ -270,13 +255,13 @@
     ot_ref[...] = onehot.astype(BF)
     rate = jnp.broadcast_to(rate_ref[...], (SUB, cells))
     rsel_ref[...] = dot_split(rate, onehot.astype(BF), NT)
-    clear_rest(scalars, rows, a_ref)
+    clear_rest(scalars, a_ref)
 
     def step(b, carry):
         into.copy(b).wait()
         mix(b * block, block, p_ref, partner_ref, q_ref)
         out.copy(b).start()
-        list_cells(b * block, block, q_ref, ot_ref[...], 1.0 - rsel_ref[0:1, :], a_ref, rows)
+        list_cells(b * block, block, q_ref, ot_ref[...], 1.0 - rsel_ref[0:1, :], a_ref)
         return carry
 
     lax.fori_loop(0, scalars // block, step, 0)
@@ -286,12 +271,12 @@
     last.wait()
 
 
-def settle_block(s0, block, q_ref, f_ref, r_ref, ot_ref, rate_ref, out_ref, rows, devices):
+def settle_block(s0, block, q_ref, f_ref, r_ref, ot_ref, rate_ref, out_ref, devices):
     _, particles, cells = q_ref.shape
     tiles = cells // LANES
     rate = rate_ref[...]
     keep = 1.0 - rate
-    r = jnp.concatenate([get_scalar(r_ref, s0 + i, rows) for i in range(block)], axis=0)
+    r = jnp.concatenate([get_scalar(r_ref, s0 + i) for i in range(block)], axis=0)
     spread = dot(r.astype(BF), ot_ref[...], NN)
     for i in range(block):
         s = s0 + i
@@ -303,7 +288,6 @@
 
 
 def middle_body(
-    rows,
     block,
     devices,
     q_hbm,
@@ -323,16 +307,17 @@
 ):
     scalars = q_ref.shape[0]
     into, out = Stream(q_hbm, q_ref, in_sem, block), Stream(q_ref, out_hbm, out_sem, block)
-    first = pltpu.make_async_copy(r_hbm, r_ref, r_sem)
-    first.start()
-    into.start_all()
+    changes = Stream(r_hbm, r_ref, r_sem, block * SUB, 2)
+    for b in range(q_ref.shape[0] // block):
+        changes.copy(b).start()
+        into.copy(b).start()
     token_ref[...] = rate_ref[:, :LANES]
-    first.wait()
 
     def step(b, carry):
+        changes.copy(b).wait()
         into.copy(b).wait()
         s0 = b * block
-        settle_block(s0, block, q_ref, f_ref, r_ref, ot_ref, rate_ref, now_ref, rows, devices)
+        settle_block(s0, block, q_ref, f_ref, r_ref, ot_ref, rate_ref, now_ref, devices)
         mix(s0, block, now_ref, partner_ref, q_ref)
         out.copy(b).start()
         return carry
@@ -363,9 +348,8 @@
     r_hbm, s_ref, a_ref, r_ref, pull_ref, one_a, one_b, two_a, two_b, in_sem, out_sem = refs
     tiles = ot_ref.shape[1] // LANES
     listed = ot_ref.shape[0]
-    particles = a_ref.shape[1] // rows
-    into = Stream(a_hbm, a_ref, in_sem, SUB * rows, 1)
-    out = Stream(r_ref, r_hbm, out_sem, SUB * rows, 1)
+    particles = a_ref.shape[1] * SUB
+    into, out = Stream(a_hbm, a_ref, in_sem, 1, 1), Stream(r_ref, r_hbm, out_sem, 1, 1)
     into.start_all()
     f = load_filtered(f_ref, devices, rows, tiles)
     pull_ref[...] = rsel_ref[0:1, :] * dot_split(f, ot_ref[...], NT)
@@ -374,10 +358,11 @@
     def first(g):
         parts = []
         for i in range(2):
-            at = particle_rows(2 * g + i, rows)
+            p = 2 * g + i
+            at = pl.ds(p & (SUB - 1), rows, stride=SUB)
             for t in range(listed // LANES):
                 pull = pull_ref[:, t * LANES : (t + 1) * LANES]
-                parts.append((a_ref[t, at, :] + pull).astype(BF))
+                parts.append((a_ref[t, p >> 3, at, :] + pull).astype(BF))
         return half_silu(dot(w1_ref[...], jnp.concatenate(parts, axis=1), NN))
 
     def second(one):
@@ -387,17 +372,17 @@
         change = dot(w3_ref[...], two, NN).astype(BF).astype(F32)
         for i in range(2):
             r = jnp.where(live, change[:, i * listed : (i + 1) * listed], 0.0)
-            at = particle_rows(2 * g + i, rows)
+            p = 2 * g + i
+            at = pl.ds(p & (SUB - 1), rows, stride=SUB)
             for t in range(listed // LANES):
-                r_ref[t, at, :] = r[:, t * LANES : (t + 1) * LANES]
+                r_ref[t, p >> 3, at, :] = r[:, t * LANES : (t + 1) * LANES]
             total = total + r
         return total
 
     def step(g, total, old, new):
-        total = third(g - 2, old[1][...], total)
+        new[0][...] = first(g)
         new[1][...] = second(old[0][...])
-        new[0][...] = first(g)
-        return total
+        return third(g - 2, old[1][...], total)
 
     left, right = (one_a, two_a), (one_b, two_b)
 
@@ -485,9 +470,13 @@
 
     for o in range(particles // SUB // side):
         for i in range(0, SUB, count):
-            ats = [pl.ds(o * rows * SUB + i + u, rows, stride=SUB) for u in range(count)]
+            ats = [pl.ds(i + u, rows, stride=SUB) for u in range(count)]
             x = jnp.concatenate(
-                [base_ref[t, at, :] + pull[:, t * LANES : (t + 1) * LANES] for at in ats for t in range(wide)],
+                [
+                    base_ref[t, o, at, :] + pull[:, t * LANES : (t + 1) * LANES]
+                    for at in ats
+                    for t in range(wide)
+                ],
                 axis=1,
             )
             one = half_silu(dot(w1_ref[...], x.astype(BF), NN))
@@ -496,7 +485,7 @@
             for n, (at, t) in enumerate((at, t) for at in ats for t in range(wide)):
                 cols = slice(n * LANES, (n + 1) * LANES)
                 mask = live[:, t * LANES : (t + 1) * LANES]
-                v_ref[t, at, :] = x[:, cols] + jnp.where(mask, change[:, cols], 0.0)
+                v_ref[t, o, at, :] = x[:, cols] + jnp.where(mask, change[:, cols], 0.0)
 
     per = LANES // particles
     stride = out_ref.shape[0] // devices
@@ -504,8 +493,8 @@
     def scalar(s):
         parts = []
         for o in range(particles // SUB // side):
-            at = pl.ds(o * rows * SUB + s * SUB, SUB)
-            row = jnp.concatenate([v_ref[t, at, :] for t in range(wide)], axis=1)
+            at = pl.ds(s * SUB, SUB)
+            row = jnp.concatenate([v_ref[t, o, at, :] for t in range(wide)], axis=1)
             parts += [row[:, u * places : (u + 1) * places] for u in range(side)]
         return jnp.concatenate(parts, axis=0)
 
@@ -614,7 +603,6 @@
 
 
 def settle_body(
-    rows,
     block,
     devices,
     q_hbm,
@@ -632,15 +620,16 @@
     r_sem,
 ):
     into, out = Stream(q_hbm, q_ref, in_sem, block), Stream(out_ref, out_hbm, out_sem, block)
-    first = pltpu.make_async_copy(r_hbm, r_ref, r_sem)
-    first.start()
-    into.start_all()
+    changes = Stream(r_hbm, r_ref, r_sem, block * SUB, 2)
+    for b in range(q_ref.shape[0] // block):
+        changes.copy(b).start()
+        into.copy(b).start()
     token_ref[...] = rate_ref[:, :LANES]
-    first.wait()
 
     def step(b, carry):
+        changes.copy(b).wait()
         into.copy(b).wait()
-        settle_block(b * block, block, q_ref, f_ref, r_ref, ot_ref, rate_ref, out_ref, rows, devices)
+        settle_block(b * block, block, q_ref, f_ref, r_ref, ot_ref, rate_ref, out_ref, devices)
         out.copy(b).start()
         return carry
 
@@ -812,32 +801,29 @@
         lab_ref[pl.ds(j * boxes, boxes), :] = load_rows(arr_ref, width + j, stride, boxes).astype(
             I32
         )
-    lane_of = lax.broadcasted_iota(I32, (turns, LANES), 1).astype(F32)
-    sub_of = lax.broadcasted_iota(I32, (turns, LANES), 0)
-    sub_lane = lax.broadcasted_iota(I32, (LANES, LANES), 0)
+    lane_of = lax.broadcasted_iota(I32, (turns, LANES), 1).astype(F32).astype(BF)
+    sub_of = lax.broadcasted_iota(I32, (turns, LANES), 0).astype(F32).astype(BF)
+    sub_lane = lax.broadcasted_iota(I32, (LANES, LANES), 0).astype(F32).astype(BF)
+    none = jnp.zeros((turns, LANES), BF)
+    unit = jnp.ones((LANES, LANES), BF)
 
     def group(x, carry):
         def gather(y, acc):
             left, right = [], []
             for j in range(quads):
                 line = lab_ref[pl.ds(j * boxes + x * ny + y, 1), :]
-                hit = jnp.broadcast_to(line >> 7, (turns, LANES)) == sub_of
-                code = (j * ny + y).astype(F32)
+                hit = jnp.broadcast_to((line >> 7).astype(F32).astype(BF), (turns, LANES)) == sub_of
+                code = jnp.full((turns, LANES), j * ny + y).astype(F32).astype(BF)
                 left.append(
-                    jnp.concatenate(
-                        [jnp.where(hit, code, 0.0), jnp.where(hit, lane_of, 0.0)], axis=0
-                    ).astype(BF)
+                    jnp.concatenate([jnp.where(hit, code, none), jnp.where(hit, lane_of, none)], axis=0)
                 )
-                right.append(
-                    (jnp.broadcast_to(line & (LANES - 1), (LANES, LANES)) == sub_lane)
-                    .astype(F32)
-                    .astype(BF)
-                )
+                lane = jnp.broadcast_to((line & (LANES - 1)).astype(F32).astype(BF), (LANES, LANES))
+                right.append(jnp.where(lane == sub_lane, unit, jnp.zeros_like(unit)))
             return acc + dot(
                 jnp.concatenate(left, axis=1), jnp.concatenate(right, axis=1), NT
             )
 
-        code = lax.fori_loop(0, ny, gather, jnp.zeros((2 * turns, LANES), F32), unroll=2)
+        code = lax.fori_loop(0, ny, gather, jnp.zeros((2 * turns, LANES), F32), unroll=8)
         code = code.astype(I32)
         inv_ref[pl.ds(x * 2 * turns, 2 * turns), :] = code
         return carry
@@ -957,15 +943,16 @@
 
     rate = mix_rate.reshape(1, cells)
     state_shape = (scalars, heads, cells)
-    listed_shape = (listed // LANES, heads * rows, LANES)
+    listed_shape = (listed // LANES, heads // SUB, rows * SUB, LANES)
     block = divisor(scalars, 6)
     octets = heads // SUB
     state_vmem = pltpu.VMEM(state_shape, F32)
     listed_vmem = pltpu.VMEM(listed_shape, F32)
     dma = pltpu.SemaphoreType.DMA
     per_block = dma((scalars // block,))
+    per_listed = dma((-(-rows // block),))
     q, a, ot, rsel = call(
-        functools.partial(open_body, rows, block),
+        functools.partial(open_body, block),
         [
             (state_shape, F32, True),
             (listed_shape, F32, True),
@@ -1008,7 +995,7 @@
     span = SUB * (-(-scalars // (per * SUB)))
     places = leave_slots.shape[1]
     side = max(1, LANES // places)
-    base_shape = (max(1, places // LANES), octets // side * rows * SUB, LANES)
+    base_shape = (max(1, places // LANES), octets // side, rows * SUB, LANES)
     kept = SUB * (-(-scalars // SUB))
     pair = pltpu.VMEM((hidden, 2 * listed), BF)
     me = jnp.stack([lax.axis_index("gx"), lax.axis_index("gy")]).astype(I32)
@@ -1041,11 +1028,11 @@
     change, source = chemistry(f, a, pos, (flat, LANES))
     home = exchange(source)
     q, token = call(
-        functools.partial(middle_body, rows, block, devices),
+        functools.partial(middle_body, block, devices),
         [(state_shape, F32, True), ((1, LANES), F32)],
         [q, f, change, ot, rate, partner],
         hbm=(0, 2),
-        scratch=[state_vmem, state_vmem, listed_vmem, per_block, per_block, dma],
+        scratch=[state_vmem, state_vmem, listed_vmem, per_block, per_block, per_listed],
     )
     (sent,) = call(
         functools.partial(again_body, dims),
@@ -1054,7 +1041,7 @@
         scratch=[pltpu.VMEM((flat, LANES), F32)],
     )
     a, base, token = call(
-        functools.partial(list_body, rows),
+        functools.partial(list_body, block),
         [(listed_shape, F32, True), (base_shape, F32, True), ((1, LANES), F32)],
         [q, rate, rsel, ot, lcol],
         hbm=(0,),
@@ -1062,8 +1049,9 @@
             state_vmem,
             listed_vmem,
             pltpu.VMEM(base_shape, F32),
-            dma((-(-scalars // per),)),
-            dma((2,)),
+            per_block,
+            per_listed,
+            per_listed,
         ],
     )
     f = exchange(sent)
@@ -1078,11 +1066,11 @@
     change, source = chemistry(f, a, token, (ny, kept, LANES), [pos])
     moved = exchange(leaving)
     state, token = call(
-        functools.partial(settle_body, rows, block, devices),
+        functools.partial(settle_body, block, devices),
         [(state_shape, F32, True), ((1, LANES), F32)],
         [q, f, change, ot, rate],
         hbm=(0, 2),
-        scratch=[state_vmem, state_vmem, listed_vmem, per_block, per_block, dma],
+        scratch=[state_vmem, state_vmem, listed_vmem, per_block, per_block, per_listed],
     )
     source = lax.all_to_all(source, "gy", split_axis=0, concat_axis=0, tiled=True)
     (grid,) = call(

time: 128 us -> 123 us (0.961)
  Pallas kernels: 71.6 us -> 63.9 us
  waiting for transfers between devices: 18.4 us -> 22.1 us
  starting transfers between devices: 23.9 us -> 22.6 us
    pallas_call x14, Pallas kernels: 71.6 us -> 63.9 us  [call(): pl.pallas_call(body, out_shape=[pltpu.HBM(o[0], o[1]) if len(o) > 2 else...]
    all_to_all x5, waiting for transfers between devices: 18.4 us -> 22.1 us  [exchange(): lax.all_to_all(x, both, split_axis=0, concat_axis=0, tiled=True)]
    all_to_all x5, starting transfers between devices: 23.9 us -> 22.6 us  [exchange(): lax.all_to_all(x, both, split_axis=0, concat_axis=0, tiled=True)]
  transfers between devices with their start and end apart: 5 -> 5, of which waited for: 4 -> 5; matrix products, arithmetic and copies ran while one was open for 0% -> 0% of each run, Pallas kernels for 26% -> 24%
where the time goes in v7:
time: 123 us; the launch traced here: 122 us
  Pallas kernels  63.9 us (52%)
  starting transfers between devices  22.6 us (18%)
  waiting for transfers between devices  22.1 us (18%)
  blocking collectives  11.7 us (10%)
  between operations  1.52 us (1%)
    pallas_call x14, Pallas kernels, call(): pl.pallas_call(body, out_shape=[pltpu.HBM(o[0], o[1]) if len(o) > 2 else...  63.9 us
    all_to_all x5, starting transfers between devices, exchange(): lax.all_to_all(x, both, split_axis=0, concat_axis=0, tiled=True)  22.6 us
    all_to_all x5, waiting for transfers between devices, exchange(): lax.all_to_all(x, both, split_axis=0, concat_axis=0, tiled=True)  22.1 us
    all_to_all x1, blocking collectives, per_device(): lax.all_to_all(source, 'gy', split_axis=0, concat_axis=0, tiled=True)  11.7 us
  transfers between devices with their start and end apart: 5, of which 5 were waited for; matrix products, arithmetic and copies ran while one was open for 0% of the time, Pallas kernels for 24%

profile of v7, /device:TPU:0, one launch (start us, length us, event | category | flops | bytes accessed | tf_op | source)
XLA Modules:
  0.0 121.9 jit_solution(10239331347570018237)
XLA Ops:
  0.6 0.0 copy-start.6
  0.6 0.0 copy-start.5
  0.7 0.0 copy-start.4
  0.7 0.0 copy-start.1
  0.7 0.0 copy-start.3
  0.7 0.0 copy-start.8
  0.7 0.0 copy-start.7
  0.7 1.7 %shard_map.149 = f32[512,128]{1,0:T(8,128)} custom-call(f32[216,128]{1,0:T(8,128)} %bitcast.40, s32[4,128]{1,0:T(4,128)} %bitcast.35, s32[4,128]{1,0:T(4,128)} %bitcast.37, f32[4,128]{1,0:T(4,128)} %bitcast.41), custom_call_target="tpu_custom_call" | custom-call | tf_op jit(solution)/shard_map/pallas_call | solution.py:26
  2.4 7.3 %all-to-all-start = ((f32[32,16,128]{2,1,0:T(8,128)}), f32[32,16,128]{2,1,0:T(8,128)S(1)}, u32[]{:S(2)}, u32[]{:S(2)}) async-start(f32[32,16,128]{2,1,0:T(8,128)} %bitcast.4), calls=%async_computation | async-start | bytes 524288 | tf_op jit(solution)/shard_map/all_to_all | solution.py:940
  9.8 0.0 copy-start
  9.8 0.0 copy-start.2
  9.8 9.4 %shard_map.150 = (f32[54,32,512]{2,1,0:T(8,128)}, f32[2,4,512,128]{3,2,1,0:T(8,128)}, bf16[256,512]{1,0:T(8,128)(2,1)S(1)}, f32[8,256]{1,0:T(8,128)S(1)}) custom-call(f32[54,32,512]{2,1,0:T(8,128)} %p_hbm.1, s32[32,512]{1,0:T(8,128)} %partner_ref.1, f32[1,512]{1,0:T(1,128)} %bitcast.29, s32[1,256]{1,0:T(1,128)} %list_hbm.1), custom_call_target="tpu_custom_call" | custom-call | tf_op jit(solution)/shard_map/pallas_call | solution.py:26
  19.2 0.6 all-to-all-done
  19.8 4.2 %shard_map.151 = (f32[256,128]{1,0:T(8,128)S(1)}, f32[256,128]{1,0:T(8,128)}, s32[256,128]{1,0:T(8,128)S(1)}, s32[128,128]{1,0:T(8,128)S(1)}) custom-call(f32[512,128]{1,0:T(8,128)S(1)} %bitcast.23, f32[8,256]{1,0:T(8,128)S(1)} %get-tuple-element.29.token_ref.rsel_ref), custom_call_target="tpu_custom_call" | custom-call | tf_op jit(solution)/shard_map/pallas_call | solution.py:26
  23.9 5.3 %all-to-all-start.1 = ((f32[32,8,128]{2,1,0:T(8,128)}), f32[32,8,128]{2,1,0:T(8,128)S(1)}, u32[]{:S(2)}, u32[]{:S(2)}) async-start(f32[32,8,128]{2,1,0:T(8,128)} %bitcast.7), calls=%async_computation.1 | async-start | bytes 262144 | tf_op jit(solution)/shard_map/all_to_all | solution.py:940
  29.9 0.1 pad_add_fusion.me_ref
  30.0 0.0 copy-done.4
  30.0 0.0 copy-done.1
  30.0 0.0 copy-done.3
  30.0 0.1 shard_map.152
  30.1 0.0 copy-done.6
  30.1 0.0 copy-done.5
  30.1 0.0 copy-done.8
  30.1 0.0 copy-done.7
  30.1 1.5 %shard_map.153 = (f32[256,128]{1,0:T(8,128)S(1)}, bf16[1024,512]{1,0:T(8,128)(2,1)S(1)}, s32[64,128]{1,0:T(8,128)S(1)}, s32[64,128]{1,0:T(8,128)S(1)}) custom-call(s32[2]{0:T(128)S(1)} %pad_add_fusion.me_ref, s32[256,128]{1,0:T(8,128)S(1)} %get-tuple-element.37.inv_ref, bf16[256,512]{1,0:T(8,128)(2,1)S(1)} %get-tuple-element.32.ot_ref, ...), custom_call_target="tpu_custom_call" | custom-call | tf_op jit(solution)/shard_map/pallas_call | solution.py:26
  31.6 5.8 %all-to-all-done.1 = f32[32,8,128]{2,1,0:T(8,128)S(1)} async-done(((f32[32,8,128]{2,1,0:T(8,128)}), f32[32,8,128]{2,1,0:T(8,128)S(1)}, u32[]{:S(2)}, u32[]{:S(2)}) %all-to-all-start.1) | async-done | bytes 131104 | tf_op jit(solution)/shard_map/all_to_all | solution.py:940
  37.4 7.3 %shard_map.154 = (f32[2,4,512,128]{3,2,1,0:T(8,128)}, f32[256,128]{1,0:T(8,128)}) custom-call(s32[1]{0:T(128)S(6)} %copy.16.count_ref, f32[256,128]{1,0:T(8,128)S(1)} %bitcast.26, f32[2,4,512,128]{3,2,1,0:T(8,128)} %get-tuple-element.31.a_hbm, bf16[256,512]{1,0:T(8,128)(2,1)S(1)} %get-tuple-element.32.ot_ref, ...), custom_call_target="tpu_custom_call" | custom-call | tf_op jit(solution)/shard_map/pallas_call | solution.py:26
  44.7 2.6 %all-to-all-start.2 = ((f32[32,8,128]{2,1,0:T(8,128)}), f32[32,8,128]{2,1,0:T(8,128)S(1)}, u32[]{:S(2)}, u32[]{:S(2)}) async-start(f32[32,8,128]{2,1,0:T(8,128)} %bitcast.12), calls=%async_computation.2 | async-start | bytes 262144 | tf_op jit(solution)/shard_map/all_to_all | solution.py:940
  47.3 0.0 copy-done
  47.3 0.0 copy-done.2
  47.3 7.0 %shard_map.155 = (f32[54,32,512]{2,1,0:T(8,128)}, f32[1,128]{1,0:T(1,128)S(1)}) custom-call(f32[54,32,512]{2,1,0:T(8,128)} %get-tuple-element.41.q_hbm, f32[256,128]{1,0:T(8,128)S(1)} %bitcast.27, f32[2,4,512,128]{3,2,1,0:T(8,128)} %get-tuple-element.42.r_hbm, bf16[256,512]{1,0:T(8,128)(2,1)S(1)} %get-tuple-element.32.ot_ref, f32[1,512]{1,0:T(1,128)S(1)} %bitcast.30, ...), custom_call_target="tpu_custom_call" | custom-call | tf_op jit(solution)/shard_map/pallas_call | solution.py:26
  54.3 1.1 all-to-all-done.2
  55.5 3.7 %shard_map.156 = f32[512,128]{1,0:T(8,128)} custom-call(f32[256,128]{1,0:T(8,128)S(1)} %bitcast.28, f32[256,128]{1,0:T(8,128)S(1)} %get-tuple-element.40.g_ref, f32[512,128]{1,0:T(8,128)S(1)} %bitcast.24, s32[256,128]{1,0:T(8,128)S(1)} %get-tuple-element.37.inv_ref, s32[128,128]{1,0:T(8,128)S(1)} %get-tuple-element.33.token_ref.lab_ref, ...), custom_call_target="tpu_custom_call" | custom-call | tf_op jit(solution)/shard_map/pallas_call | solution.py:26
  59.2 4.7 %all-to-all-start.3 = ((f32[32,16,128]{2,1,0:T(8,128)}), f32[32,16,128]{2,1,0:T(8,128)S(1)}, u32[]{:S(2)}, u32[]{:S(2)}) async-start(f32[32,16,128]{2,1,0:T(8,128)} %bitcast.14), calls=%async_computation.3 | async-start | bytes 524288 | tf_op jit(solution)/shard_map/all_to_all | solution.py:940
  63.9 5.8 %shard_map.157 = (f32[2,4,512,128]{3,2,1,0:T(8,128)}, f32[1,2,512,128]{3,2,1,0:T(8,128)}, f32[1,128]{1,0:T(1,128)S(1)}) custom-call(f32[54,32,512]{2,1,0:T(8,128)} %get-tuple-element.44.q_hbm, f32[1,512]{1,0:T(1,128)S(1)} %bitcast.31, f32[8,256]{1,0:T(8,128)S(1)} %get-tuple-element.29.token_ref.rsel_ref, bf16[256,512]{1,0:T(8,128)(2,1)S(1)} %get-tuple-element.32.ot_ref, ...), custom_call_target="tpu_custom_call" | custom-call | tf_op jit(solution)/shard_map/pallas_call | solution.py:26
  69.7 4.2 %all-to-all-done.3 = f32[32,16,128]{2,1,0:T(8,128)S(1)} async-done(((f32[32,16,128]{2,1,0:T(8,128)}), f32[32,16,128]{2,1,0:T(8,128)S(1)}, u32[]{:S(2)}, u32[]{:S(2)}) %all-to-all-start.3) | async-done | bytes 262176 | tf_op jit(solution)/shard_map/all_to_all | solution.py:940
  73.9 5.0 %shard_map.158 = (f32[1024,128]{1,0:T(8,128)}, f32[1,128]{1,0:T(1,128)S(1)}) custom-call(s32[1]{0:T(128)S(6)} %copy.16.count_ref, f32[512,128]{1,0:T(8,128)S(1)} %bitcast.19, f32[1,2,512,128]{3,2,1,0:T(8,128)} %get-tuple-element.47.base_hbm, bf16[256,512]{1,0:T(8,128)(2,1)S(1)} %get-tuple-element.32.ot_ref, f32[1,512]{1,0:T(1,128)S(1)} %bitcast.32, ...), custom_call_target="tpu_custom_call" | custom-call | tf_op jit(solution)/shard_map/pallas_call | solution.py:26
  78.9 6.7 %shard_map.159 = (f32[2,4,512,128]{3,2,1,0:T(8,128)}, f32[8,56,128]{2,1,0:T(8,128)S(1)}) custom-call(s32[1]{0:T(128)S(6)} %copy.16.count_ref, f32[512,128]{1,0:T(8,128)S(1)} %bitcast.20, f32[2,4,512,128]{3,2,1,0:T(8,128)} %get-tuple-element.46.a_hbm, bf16[256,512]{1,0:T(8,128)(2,1)S(1)} %get-tuple-element.32.ot_ref, ...), custom_call_target="tpu_custom_call" | custom-call | tf_op jit(solution)/shard_map/pallas_call | solution.py:26
  85.6 11.7 %all_to_all.30.s_ref = f32[8,56,128]{2,1,0:T(8,128)S(1)} all-to-all(f32[8,56,128]{2,1,0:T(8,128)S(1)} %get-tuple-element.50), channel_id=1, replica_groups=mesh['gx'=4,'gy'=8] {'gy'}, dimensions={0} | all-to-all | bytes 458752 | tf_op jit(solution)/shard_map/all_to_all | solution.py:1075
  97.3 2.6 %all-to-all-start.5 = ((f32[32,32,128]{2,1,0:T(8,128)}), f32[32,32,128]{2,1,0:T(8,128)S(1)}, u32[]{:S(2)}, u32[]{:S(2)}) async-start(f32[32,32,128]{2,1,0:T(8,128)} %bitcast.17), calls=%async_computation.5 | async-start | bytes 1048576 | tf_op jit(solution)/shard_map/all_to_all | solution.py:940
  99.9 4.8 %shard_map.161 = (f32[54,32,512]{2,1,0:T(8,128)}, f32[1,128]{1,0:T(1,128)}) custom-call(f32[54,32,512]{2,1,0:T(8,128)} %get-tuple-element.44.q_hbm, f32[512,128]{1,0:T(8,128)S(1)} %bitcast.21, f32[2,4,512,128]{3,2,1,0:T(8,128)} %get-tuple-element.52.r_hbm, bf16[256,512]{1,0:T(8,128)(2,1)S(1)} %get-tuple-element.32.ot_ref, f32[1,512]{1,0:T(1,128)S(1)} %bitcast.33), custom_call_target="tpu_custom_call" | custom-call | tf_op jit(solution)/shard_map/pallas_call | solution.py:26
  104.7 1.0 shard_map.160
  105.7 10.4 %all-to-all-done.5 = f32[32,32,128]{2,1,0:T(8,128)S(1)} async-done(((f32[32,32,128]{2,1,0:T(8,128)}), f32[32,32,128]{2,1,0:T(8,128)S(1)}, u32[]{:S(2)}, u32[]{:S(2)}) %all-to-all-start.5) | async-done | bytes 524320 | tf_op jit(solution)/shard_map/all_to_all | solution.py:940
  116.1 5.8 %shard_map.162 = f32[54,32,512]{2,1,0:T(8,128)} custom-call(f32[54,32,512]{2,1,0:T(8,128)} %get-tuple-element.53.p_hbm, f32[1024,128]{1,0:T(8,128)S(1)} %bitcast.25, s32[64,128]{1,0:T(8,128)S(1)} %get-tuple-element.55.acol_ref), custom_call_target="tpu_custom_call" | custom-call | tf_op jit(solution)/shard_map/pallas_call | solution.py:26
Async XLA Ops:
  0.6 29.5 %copy-start.6 = (s32[2,2,128]{2,1,0:T(2,128)S(1)}, s32[2,2,128]{2,1,0:T(2,128)}, u32[]{:S(2)}) copy-start(s32[2,2,128]{2,1,0:T(2,128)} %param.18) | copy-start | bytes 6148
  0.6 29.5 %copy-start.5 = (s32[2,2,128]{2,1,0:T(2,128)S(1)}, s32[2,2,128]{2,1,0:T(2,128)}, u32[]{:S(2)}) copy-start(s32[2,2,128]{2,1,0:T(2,128)} %param.17) | copy-start | bytes 6148
  0.7 29.3 %copy-start.4 = (bf16[54,256]{1,0:T(8,128)(2,1)S(1)}, bf16[54,256]{1,0:T(8,128)(2,1)}, u32[]{:S(2)}) copy-start(bf16[54,256]{1,0:T(8,128)(2,1)} %w3_ref.1) | copy-start | bytes 82948
  0.7 29.3 %copy-start.1 = (bf16[256,256]{1,0:T(8,128)(2,1)S(1)}, bf16[256,256]{1,0:T(8,128)(2,1)}, u32[]{:S(2)}) copy-start(bf16[256,256]{1,0:T(8,128)(2,1)} %w2_ref.1) | copy-start | bytes 393220
  0.7 29.3 %copy-start.3 = (bf16[256,54]{0,1:T(8,128)(2,1)S(1)}, bf16[256,54]{0,1:T(8,128)(2,1)}, u32[]{:S(2)}) copy-start(bf16[256,54]{0,1:T(8,128)(2,1)} %param.21) | copy-start | bytes 82948
  0.7 29.4 %copy-start.8 = (s32[1,64]{1,0:T(1,128)S(1)}, s32[1,64]{1,0:T(1,128)}, u32[]{:S(2)}) copy-start(s32[1,64]{1,0:T(1,128)} %arrive_ref.1) | copy-start | bytes 772
  0.7 29.4 %copy-start.7 = (s32[1,64]{1,0:T(1,128)S(1)}, s32[1,64]{1,0:T(1,128)}, u32[]{:S(2)}) copy-start(s32[1,64]{1,0:T(1,128)} %leave_ref.1) | copy-start | bytes 772
  2.4 17.3 %all-to-all-start = ((f32[32,16,128]{2,1,0:T(8,128)}), f32[32,16,128]{2,1,0:T(8,128)S(1)}, u32[]{:S(2)}, u32[]{:S(2)}) async-start(f32[32,16,128]{2,1,0:T(8,128)} %bitcast.4), calls=%async_computation | async-start | bytes 524288 | tf_op jit(solution)/shard_map/all_to_all | solution.py:940
  9.8 37.5 %copy-start = (s32[32,512]{1,0:T(8,128)S(1)}, s32[32,512]{1,0:T(8,128)}, u32[]{:S(2)}) copy-start(s32[32,512]{1,0:T(8,128)} %partner_ref.1) | copy-start | bytes 196612
  9.8 37.5 %copy-start.2 = (f32[512]{0:T(512)S(1)}, f32[512]{0:T(512)}, u32[]{:S(2)}) copy-start(f32[512]{0:T(512)} %param.19) | copy-start | bytes 6148
  23.9 13.5 %all-to-all-start.1 = ((f32[32,8,128]{2,1,0:T(8,128)}), f32[32,8,128]{2,1,0:T(8,128)S(1)}, u32[]{:S(2)}, u32[]{:S(2)}) async-start(f32[32,8,128]{2,1,0:T(8,128)} %bitcast.7), calls=%async_computation.1 | async-start | bytes 262144 | tf_op jit(solution)/shard_map/all_to_all | solution.py:940
  44.7 10.8 %all-to-all-start.2 = ((f32[32,8,128]{2,1,0:T(8,128)}), f32[32,8,128]{2,1,0:T(8,128)S(1)}, u32[]{:S(2)}, u32[]{:S(2)}) async-start(f32[32,8,128]{2,1,0:T(8,128)} %bitcast.12), calls=%async_computation.2 | async-start | bytes 262144 | tf_op jit(solution)/shard_map/all_to_all | solution.py:940
  59.2 14.7 %all-to-all-start.3 = ((f32[32,16,128]{2,1,0:T(8,128)}), f32[32,16,128]{2,1,0:T(8,128)S(1)}, u32[]{:S(2)}, u32[]{:S(2)}) async-start(f32[32,16,128]{2,1,0:T(8,128)} %bitcast.14), calls=%async_computation.3 | async-start | bytes 524288 | tf_op jit(solution)/shard_map/all_to_all | solution.py:940
  97.3 18.8 %all-to-all-start.5 = ((f32[32,32,128]{2,1,0:T(8,128)}), f32[32,32,128]{2,1,0:T(8,128)S(1)}, u32[]{:S(2)}, u32[]{:S(2)}) async-start(f32[32,32,128]{2,1,0:T(8,128)} %bitcast.17), calls=%async_computation.5 | async-start | bytes 1048576 | tf_op jit(solution)/shard_map/all_to_all | solution.py:940

commit v8 on v7

--- a/solution.py
+++ b/solution.py
@@ -107,7 +107,8 @@
             rows.append(index & (SUB - 1))
             homes.append(index >> 3)
 
-        def step(s, carry):
+        def step(i, carry):
+            s = s0 + i
             x = [p_ref[s, pl.ds(k * SUB, SUB), lanes] for k in range(groups)]
             for j in range(groups):
                 mate = jnp.take_along_axis(x[0], rows[j], axis=0)
@@ -117,7 +118,7 @@
                 q_ref[s, pl.ds(j * SUB, SUB), lanes] = x[j] + PAIR_WEIGHT * (mate - x[j])
             return carry
 
-        lax.fori_loop(s0, s0 + block, step, 0)
+        lax.fori_loop(0, block, step, 0, unroll=True)
 
 
 def put_scalar(ref, s, value):
@@ -155,19 +156,16 @@
     ot_ref,
     lcol_ref,
     a_hbm,
-    base_hbm,
+    base_ref,
     token_ref,
     q_ref,
     a_ref,
-    base_ref,
     in_sem,
     a_sem,
-    base_sem,
 ):
     scalars, particles, cells = q_ref.shape
     into = Stream(q_hbm, q_ref, in_sem, block)
     out_a = Stream(a_ref, a_hbm, a_sem, block * SUB, 2)
-    out_base = Stream(base_ref, base_hbm, base_sem, block * SUB, 2)
     into.start_all()
     token_ref[...] = rate_ref[:, :LANES]
     leaves = cell_onehot(lcol_ref, cells)
@@ -196,16 +194,14 @@
                     at = pl.ds((b * block + i) * SUB, SUB)
                     base_ref[t, o, at, :] = wide[:, t * LANES : (t + 1) * LANES]
         out_a.copy(b).start()
-        out_base.copy(b).start()
         return carry
 
     lax.fori_loop(0, scalars // block, step, 0)
-    for ref, out in ((a_ref, out_a), (base_ref, out_base)):
-        clear_rest(scalars, ref)
-        for b in range(scalars // block, out.count):
-            out.copy(b, out.tail(b)).start()
+    clear_rest(scalars, base_ref)
+    clear_rest(scalars, a_ref)
+    for b in range(scalars // block, out_a.count):
+        out_a.copy(b, out_a.tail(b)).start()
     out_a.wait_all()
-    out_base.wait_all()
 
 
 def clear_rest(scalars, ref):
@@ -238,6 +234,7 @@
 ):
     scalars, _, cells = p_ref.shape
     into, out = Stream(p_hbm, p_ref, in_sem, block), Stream(q_ref, q_hbm, out_sem, block)
+    out_a = Stream(a_ref, a_hbm, a_sem, block * SUB, 2)
     few = [
         pltpu.make_async_copy(src, dst, few_sem.at[i])
         for i, (src, dst) in enumerate(
@@ -262,13 +259,15 @@
         mix(b * block, block, p_ref, partner_ref, q_ref)
         out.copy(b).start()
         list_cells(b * block, block, q_ref, ot_ref[...], 1.0 - rsel_ref[0:1, :], a_ref)
+        out_a.copy(b).start()
         return carry
 
-    lax.fori_loop(0, scalars // block, step, 0)
-    last = pltpu.make_async_copy(a_ref, a_hbm, a_sem)
-    last.start()
+    whole = scalars // block
+    for b in range(whole, out_a.count):
+        out_a.copy(b, out_a.tail(b)).start()
+    lax.fori_loop(0, whole, step, 0)
     out.wait_all()
-    last.wait()
+    out_a.wait_all()
 
 
 def settle_block(s0, block, q_ref, f_ref, r_ref, ot_ref, rate_ref, out_ref, devices):
@@ -435,7 +434,7 @@
     particles,
     count_ref,
     f_ref,
-    base_hbm,
+    base_ref,
     ot_ref,
     rate_ref,
     lcol_ref,
@@ -446,11 +445,7 @@
     out_ref,
     end_ref,
     v_ref,
-    base_ref,
-    sem,
 ):
-    load = pltpu.make_async_copy(base_hbm, base_ref, sem)
-    load.start()
     listed, cells = ot_ref.shape
     tiles = cells // LANES
     places = lcol_ref.shape[0]
@@ -466,7 +461,6 @@
     pull = jnp.concatenate([pull] * side, axis=1)
     live = jnp.concatenate([live] * side, axis=1) > 0.5
     count = 4 // wide
-    load.wait()
 
     for o in range(particles // SUB // side):
         for i in range(0, SUB, count):
@@ -936,7 +930,9 @@
     )
 
     def exchange(x):
-        x = x.reshape(devices, -1, LANES)
+        count = x.shape[0] // devices
+        tile = SUB if count % SUB == 0 else SUB // 2
+        x = x.reshape(devices, count // tile, tile, LANES)
         return lax.all_to_all(x, both, split_axis=0, concat_axis=0, tiled=True).reshape(-1, LANES)
 
     arrival = exchange(first)
@@ -970,7 +966,7 @@
             pltpu.VMEM(react_slots.shape, I32),
             per_block,
             per_block,
-            dma,
+            per_listed,
             dma((3,)),
         ],
     )
@@ -992,7 +988,7 @@
     )
 
     per = LANES // heads
-    span = SUB * (-(-scalars // (per * SUB)))
+    span = 2 * (-(-scalars // (per * 2)))
     places = leave_slots.shape[1]
     side = max(1, LANES // places)
     base_shape = (max(1, places // LANES), octets // side, rows * SUB, LANES)
@@ -1042,15 +1038,13 @@
     )
     a, base, token = call(
         functools.partial(list_body, block),
-        [(listed_shape, F32, True), (base_shape, F32, True), ((1, LANES), F32)],
+        [(listed_shape, F32, True), (base_shape, F32), ((1, LANES), F32)],
         [q, rate, rsel, ot, lcol],
         hbm=(0,),
         scratch=[
             state_vmem,
             listed_vmem,
-            pltpu.VMEM(base_shape, F32),
             per_block,
-            per_listed,
             per_listed,
         ],
     )
@@ -1060,8 +1054,7 @@
         [((places * span, LANES), F32), ((1, LANES), F32)],
         [react_count, f, base, ot, rate, lcol, w1, w2, w3, token],
         smem=(0,),
-        hbm=(2,),
-        scratch=[pltpu.VMEM(base_shape, F32), pltpu.VMEM(base_shape, F32), dma],
+        scratch=[pltpu.VMEM(base_shape, F32)],
     )
     change, source = chemistry(f, a, token, (ny, kept, LANES), [pos])
     moved = exchange(leaving)

time: 123 us -> 116 us (0.943)
  Pallas kernels: 63.9 us -> 58.1 us
  starting transfers between devices: 22.6 us -> 18.4 us
  waiting for transfers between devices: 22.1 us -> 25.3 us
    pallas_call x14, Pallas kernels: 63.9 us -> 58.1 us  [call(): pl.pallas_call(body, out_shape=[pltpu.HBM(o[0], o[1]) if len(o) > 2 else...]
    all_to_all x5, starting transfers between devices: 22.6 us -> 18.4 us  [exchange(): lax.all_to_all(x, both, split_axis=0, concat_axis=0, tiled=True)]
    all_to_all x5, waiting for transfers between devices: 22.1 us -> 25.3 us  [exchange(): lax.all_to_all(x, both, split_axis=0, concat_axis=0, tiled=True)]
  transfers between devices with their start and end apart: 5 -> 5, of which waited for: 5 -> 5; matrix products, arithmetic and copies ran while one was open for 0% -> 0% of each run, Pallas kernels for 24% -> 22%
where the time goes in v8:
time: 116 us; the launch traced here: 115 us
  Pallas kernels  58.1 us (50%)
  waiting for transfers between devices  25.3 us (22%)
  starting transfers between devices  18.4 us (16%)
  blocking collectives  11.7 us (10%)
  between operations  1.52 us (1%)
    pallas_call x14, Pallas kernels, call(): pl.pallas_call(body, out_shape=[pltpu.HBM(o[0], o[1]) if len(o) > 2 else...  58.1 us
    all_to_all x5, waiting for transfers between devices, exchange(): lax.all_to_all(x, both, split_axis=0, concat_axis=0, tiled=True)  25.3 us
    all_to_all x5, starting transfers between devices, exchange(): lax.all_to_all(x, both, split_axis=0, concat_axis=0, tiled=True)  18.4 us
    all_to_all x1, blocking collectives, per_device(): lax.all_to_all(source, 'gy', split_axis=0, concat_axis=0, tiled=True)  11.7 us
  transfers between devices with their start and end apart: 5, of which 5 were waited for; matrix products, arithmetic and copies ran while one was open for 0% of the time, Pallas kernels for 22%

profile of v8, /device:TPU:0, one launch (start us, length us, event | category | flops | bytes accessed | tf_op | source)
XLA Modules:
  0.0 115.0 jit_solution(15389868869327473163)
XLA Ops:
  0.6 0.0 copy-start.6
  0.6 0.0 copy-start.5
  0.7 0.0 copy-start.4
  0.7 0.0 copy-start.1
  0.7 0.0 copy-start.3
  0.7 0.0 copy-start.8
  0.7 0.0 copy-start.7
  0.7 1.7 %shard_map.149 = f32[512,128]{1,0:T(8,128)} custom-call(f32[216,128]{1,0:T(8,128)} %bitcast.44, s32[4,128]{1,0:T(4,128)} %bitcast.39, s32[4,128]{1,0:T(4,128)} %bitcast.41, f32[4,128]{1,0:T(4,128)} %bitcast.45), custom_call_target="tpu_custom_call" | custom-call | tf_op jit(solution)/shard_map/pallas_call | solution.py:26
  2.4 7.3 %all-to-all-start = ((f32[32,2,8,128]{3,2,1,0:T(8,128)}), f32[32,2,8,128]{3,2,1,0:T(8,128)S(1)}, u32[]{:S(2)}, u32[]{:S(2)}) async-start(f32[32,2,8,128]{3,2,1,0:T(8,128)} %bitcast.4), calls=%async_computation | async-start | bytes 524288 | tf_op jit(solution)/shard_map/all_to_all | solution.py:936
  9.8 0.0 copy-start
  9.8 0.0 copy-start.2
  9.8 6.8 %shard_map.150 = (f32[54,32,512]{2,1,0:T(8,128)}, f32[2,4,512,128]{3,2,1,0:T(8,128)}, bf16[256,512]{1,0:T(8,128)(2,1)S(1)}, f32[8,256]{1,0:T(8,128)S(1)}) custom-call(f32[54,32,512]{2,1,0:T(8,128)} %p_hbm.1, s32[32,512]{1,0:T(8,128)} %partner_ref.1, f32[1,512]{1,0:T(1,128)} %bitcast.33, s32[1,256]{1,0:T(1,128)} %list_hbm.1), custom_call_target="tpu_custom_call" | custom-call | tf_op jit(solution)/shard_map/pallas_call | solution.py:26
  16.6 3.2 %all-to-all-done = f32[32,2,8,128]{3,2,1,0:T(8,128)S(1)} async-done(((f32[32,2,8,128]{3,2,1,0:T(8,128)}), f32[32,2,8,128]{3,2,1,0:T(8,128)S(1)}, u32[]{:S(2)}, u32[]{:S(2)}) %all-to-all-start) | async-done | bytes 262176 | tf_op jit(solution)/shard_map/all_to_all | solution.py:936
  19.8 4.2 %shard_map.151 = (f32[256,128]{1,0:T(8,128)S(1)}, f32[256,128]{1,0:T(8,128)}, s32[256,128]{1,0:T(8,128)S(1)}, s32[128,128]{1,0:T(8,128)S(1)}) custom-call(f32[512,128]{1,0:T(8,128)S(1)} %bitcast.27, f32[8,256]{1,0:T(8,128)S(1)} %get-tuple-element.29.token_ref.rsel_ref), custom_call_target="tpu_custom_call" | custom-call | tf_op jit(solution)/shard_map/pallas_call | solution.py:26
  23.9 2.9 %all-to-all-start.1 = ((f32[32,1,8,128]{3,2,1,0:T(8,128)}), f32[32,1,8,128]{3,2,1,0:T(8,128)S(1)}, u32[]{:S(2)}, u32[]{:S(2)}) async-start(f32[32,1,8,128]{3,2,1,0:T(8,128)} %bitcast.8), calls=%async_computation.1 | async-start | bytes 262144 | tf_op jit(solution)/shard_map/all_to_all | solution.py:936
  27.5 0.1 pad_add_fusion.me_ref
  27.5 0.0 copy-done.4
  27.5 0.0 copy-done.1
  27.5 0.0 copy-done.3
  27.6 0.1 shard_map.152
  27.7 0.0 copy-done.6
  27.7 0.0 copy-done.5
  27.7 0.0 copy-done.8
  27.7 0.0 copy-done.7
  27.7 1.5 %shard_map.153 = (f32[256,128]{1,0:T(8,128)S(1)}, bf16[1024,512]{1,0:T(8,128)(2,1)S(1)}, s32[64,128]{1,0:T(8,128)S(1)}, s32[64,128]{1,0:T(8,128)S(1)}) custom-call(s32[2]{0:T(128)S(1)} %pad_add_fusion.me_ref, s32[256,128]{1,0:T(8,128)S(1)} %get-tuple-element.37.inv_ref, bf16[256,512]{1,0:T(8,128)(2,1)S(1)} %get-tuple-element.32.ot_ref, ...), custom_call_target="tpu_custom_call" | custom-call | tf_op jit(solution)/shard_map/pallas_call | solution.py:26
  29.2 5.8 %all-to-all-done.1 = f32[32,1,8,128]{3,2,1,0:T(8,128)S(1)} async-done(((f32[32,1,8,128]{3,2,1,0:T(8,128)}), f32[32,1,8,128]{3,2,1,0:T(8,128)S(1)}, u32[]{:S(2)}, u32[]{:S(2)}) %all-to-all-start.1) | async-done | bytes 131104 | tf_op jit(solution)/shard_map/all_to_all | solution.py:936
  35.0 7.3 %shard_map.154 = (f32[2,4,512,128]{3,2,1,0:T(8,128)}, f32[256,128]{1,0:T(8,128)}) custom-call(s32[1]{0:T(128)S(6)} %copy.18.count_ref, f32[256,128]{1,0:T(8,128)S(1)} %bitcast.30, f32[2,4,512,128]{3,2,1,0:T(8,128)} %get-tuple-element.31.a_hbm, bf16[256,512]{1,0:T(8,128)(2,1)S(1)} %get-tuple-element.32.ot_ref, ...), custom_call_target="tpu_custom_call" | custom-call | tf_op jit(solution)/shard_map/pallas_call | solution.py:26
  42.3 2.6 %all-to-all-start.2 = ((f32[32,1,8,128]{3,2,1,0:T(8,128)}), f32[32,1,8,128]{3,2,1,0:T(8,128)S(1)}, u32[]{:S(2)}, u32[]{:S(2)}) async-start(f32[32,1,8,128]{3,2,1,0:T(8,128)} %bitcast.14), calls=%async_computation.2 | async-start | bytes 262144 | tf_op jit(solution)/shard_map/all_to_all | solution.py:936
  44.9 0.0 copy-done
  44.9 0.0 copy-done.2
  44.9 5.3 %shard_map.155 = (f32[54,32,512]{2,1,0:T(8,128)}, f32[1,128]{1,0:T(1,128)S(1)}) custom-call(f32[54,32,512]{2,1,0:T(8,128)} %get-tuple-element.41.q_hbm, f32[256,128]{1,0:T(8,128)S(1)} %bitcast.31, f32[2,4,512,128]{3,2,1,0:T(8,128)} %get-tuple-element.42.r_hbm, bf16[256,512]{1,0:T(8,128)(2,1)S(1)} %get-tuple-element.32.ot_ref, f32[1,512]{1,0:T(1,128)S(1)} %bitcast.34, ...), custom_call_target="tpu_custom_call" | custom-call | tf_op jit(solution)/shard_map/pallas_call | solution.py:26
  50.1 2.9 %all-to-all-done.2 = f32[32,1,8,128]{3,2,1,0:T(8,128)S(1)} async-done(((f32[32,1,8,128]{3,2,1,0:T(8,128)}), f32[32,1,8,128]{3,2,1,0:T(8,128)S(1)}, u32[]{:S(2)}, u32[]{:S(2)}) %all-to-all-start.2) | async-done | bytes 131104 | tf_op jit(solution)/shard_map/all_to_all | solution.py:936
  53.0 3.7 %shard_map.156 = f32[512,128]{1,0:T(8,128)} custom-call(f32[256,128]{1,0:T(8,128)S(1)} %bitcast.32, f32[256,128]{1,0:T(8,128)S(1)} %get-tuple-element.40.g_ref, f32[512,128]{1,0:T(8,128)S(1)} %bitcast.28, s32[256,128]{1,0:T(8,128)S(1)} %get-tuple-element.37.inv_ref, s32[128,128]{1,0:T(8,128)S(1)} %get-tuple-element.33.token_ref.lab_ref, ...), custom_call_target="tpu_custom_call" | custom-call | tf_op jit(solution)/shard_map/pallas_call | solution.py:26
  56.7 3.0 %all-to-all-start.3 = ((f32[32,2,8,128]{3,2,1,0:T(8,128)}), f32[32,2,8,128]{3,2,1,0:T(8,128)S(1)}, u32[]{:S(2)}, u32[]{:S(2)}) async-start(f32[32,2,8,128]{3,2,1,0:T(8,128)} %bitcast.16), calls=%async_computation.3 | async-start | bytes 524288 | tf_op jit(solution)/shard_map/all_to_all | solution.py:936
  59.7 5.6 %shard_map.157 = (f32[2,4,512,128]{3,2,1,0:T(8,128)}, f32[1,2,512,128]{3,2,1,0:T(8,128)S(1)}, f32[1,128]{1,0:T(1,128)S(1)}) custom-call(f32[54,32,512]{2,1,0:T(8,128)} %get-tuple-element.44.q_hbm, f32[1,512]{1,0:T(1,128)S(1)} %bitcast.35, f32[8,256]{1,0:T(8,128)S(1)} %get-tuple-element.29.token_ref.rsel_ref, bf16[256,512]{1,0:T(8,128)(2,1)S(1)} %get-tuple-element.32.ot_ref, ...), custom_call_target="tpu_custom_call" | custom-call | tf_op jit(solution)/shard_map/pallas_call | solution.py:26
  65.3 4.4 %all-to-all-done.3 = f32[32,2,8,128]{3,2,1,0:T(8,128)S(1)} async-done(((f32[32,2,8,128]{3,2,1,0:T(8,128)}), f32[32,2,8,128]{3,2,1,0:T(8,128)S(1)}, u32[]{:S(2)}, u32[]{:S(2)}) %all-to-all-start.3) | async-done | bytes 262176 | tf_op jit(solution)/shard_map/all_to_all | solution.py:936
  69.7 4.0 %shard_map.158 = (f32[896,128]{1,0:T(8,128)}, f32[1,128]{1,0:T(1,128)S(1)}) custom-call(s32[1]{0:T(128)S(6)} %copy.18.count_ref, f32[512,128]{1,0:T(8,128)S(1)} %bitcast.23, f32[1,2,512,128]{3,2,1,0:T(8,128)S(1)} %get-tuple-element.47.base_ref, bf16[256,512]{1,0:T(8,128)(2,1)S(1)} %get-tuple-element.32.ot_ref, f32[1,512]{1,0:T(1,128)S(1)} %bitcast.36, ...), custom_call_target="tpu_custom_call" | custom-call | tf_op jit(solution)/shard_map/pallas_call | solution.py:26
  73.7 6.6 %shard_map.159 = (f32[2,4,512,128]{3,2,1,0:T(8,128)}, f32[8,56,128]{2,1,0:T(8,128)S(1)}) custom-call(s32[1]{0:T(128)S(6)} %copy.18.count_ref, f32[512,128]{1,0:T(8,128)S(1)} %bitcast.24, f32[2,4,512,128]{3,2,1,0:T(8,128)} %get-tuple-element.46.a_hbm, bf16[256,512]{1,0:T(8,128)(2,1)S(1)} %get-tuple-element.32.ot_ref, ...), custom_call_target="tpu_custom_call" | custom-call | tf_op jit(solution)/shard_map/pallas_call | solution.py:26
  80.3 11.7 %all_to_all.30.s_ref = f32[8,56,128]{2,1,0:T(8,128)S(1)} all-to-all(f32[8,56,128]{2,1,0:T(8,128)S(1)} %get-tuple-element.50), channel_id=1, replica_groups=mesh['gx'=4,'gy'=8] {'gy'}, dimensions={0} | all-to-all | bytes 458752 | tf_op jit(solution)/shard_map/all_to_all | solution.py:1068
  92.0 2.6 %all-to-all-start.5 = ((f32[32,7,4,128]{3,2,1,0:T(4,128)}), f32[32,7,4,128]{3,2,1,0:T(4,128)S(1)}, u32[]{:S(2)}, u32[]{:S(2)}) async-start(f32[32,7,4,128]{3,2,1,0:T(4,128)} %bitcast.19), calls=%async_computation.5 | async-start | bytes 917504 | tf_op jit(solution)/shard_map/all_to_all | solution.py:936
  94.6 4.8 %shard_map.161 = (f32[54,32,512]{2,1,0:T(8,128)}, f32[1,128]{1,0:T(1,128)}) custom-call(f32[54,32,512]{2,1,0:T(8,128)} %get-tuple-element.44.q_hbm, f32[512,128]{1,0:T(8,128)S(1)} %bitcast.25, f32[2,4,512,128]{3,2,1,0:T(8,128)} %get-tuple-element.52.r_hbm, bf16[256,512]{1,0:T(8,128)(2,1)S(1)} %get-tuple-element.32.ot_ref, f32[1,512]{1,0:T(1,128)S(1)} %bitcast.37), custom_call_target="tpu_custom_call" | custom-call | tf_op jit(solution)/shard_map/pallas_call | solution.py:26
  99.4 1.0 shard_map.160
  100.4 9.0 %all-to-all-done.5 = f32[32,7,4,128]{3,2,1,0:T(4,128)S(1)} async-done(((f32[32,7,4,128]{3,2,1,0:T(4,128)}), f32[32,7,4,128]{3,2,1,0:T(4,128)S(1)}, u32[]{:S(2)}, u32[]{:S(2)}) %all-to-all-start.5) | async-done | bytes 458784 | tf_op jit(solution)/shard_map/all_to_all | solution.py:936
  109.4 5.6 %shard_map.162 = f32[54,32,512]{2,1,0:T(8,128)} custom-call(f32[54,32,512]{2,1,0:T(8,128)} %get-tuple-element.53.p_hbm, f32[896,128]{1,0:T(8,128)S(1)} %bitcast.29, s32[64,128]{1,0:T(8,128)S(1)} %get-tuple-element.55.acol_ref), custom_call_target="tpu_custom_call" | custom-call | tf_op jit(solution)/shard_map/pallas_call | solution.py:26
Async XLA Ops:
  0.6 27.0 %copy-start.6 = (s32[2,2,128]{2,1,0:T(2,128)S(1)}, s32[2,2,128]{2,1,0:T(2,128)}, u32[]{:S(2)}) copy-start(s32[2,2,128]{2,1,0:T(2,128)} %param.18) | copy-start | bytes 6148
  0.6 27.0 %copy-start.5 = (s32[2,2,128]{2,1,0:T(2,128)S(1)}, s32[2,2,128]{2,1,0:T(2,128)}, u32[]{:S(2)}) copy-start(s32[2,2,128]{2,1,0:T(2,128)} %param.17) | copy-start | bytes 6148
  0.7 26.9 %copy-start.4 = (bf16[54,256]{1,0:T(8,128)(2,1)S(1)}, bf16[54,256]{1,0:T(8,128)(2,1)}, u32[]{:S(2)}) copy-start(bf16[54,256]{1,0:T(8,128)(2,1)} %w3_ref.1) | copy-start | bytes 82948
  0.7 26.9 %copy-start.1 = (bf16[256,256]{1,0:T(8,128)(2,1)S(1)}, bf16[256,256]{1,0:T(8,128)(2,1)}, u32[]{:S(2)}) copy-start(bf16[256,256]{1,0:T(8,128)(2,1)} %w2_ref.1) | copy-start | bytes 393220
  0.7 26.9 %copy-start.3 = (bf16[256,54]{0,1:T(8,128)(2,1)S(1)}, bf16[256,54]{0,1:T(8,128)(2,1)}, u32[]{:S(2)}) copy-start(bf16[256,54]{0,1:T(8,128)(2,1)} %param.21) | copy-start | bytes 82948
  0.7 27.0 %copy-start.8 = (s32[1,64]{1,0:T(1,128)S(1)}, s32[1,64]{1,0:T(1,128)}, u32[]{:S(2)}) copy-start(s32[1,64]{1,0:T(1,128)} %arrive_ref.1) | copy-start | bytes 772
  0.7 27.0 %copy-start.7 = (s32[1,64]{1,0:T(1,128)S(1)}, s32[1,64]{1,0:T(1,128)}, u32[]{:S(2)}) copy-start(s32[1,64]{1,0:T(1,128)} %leave_ref.1) | copy-start | bytes 772
  2.4 17.3 %all-to-all-start = ((f32[32,2,8,128]{3,2,1,0:T(8,128)}), f32[32,2,8,128]{3,2,1,0:T(8,128)S(1)}, u32[]{:S(2)}, u32[]{:S(2)}) async-start(f32[32,2,8,128]{3,2,1,0:T(8,128)} %bitcast.4), calls=%async_computation | async-start | bytes 524288 | tf_op jit(solution)/shard_map/all_to_all | solution.py:936
  9.8 35.1 %copy-start = (s32[32,512]{1,0:T(8,128)S(1)}, s32[32,512]{1,0:T(8,128)}, u32[]{:S(2)}) copy-start(s32[32,512]{1,0:T(8,128)} %partner_ref.1) | copy-start | bytes 196612
  9.8 35.1 %copy-start.2 = (f32[512]{0:T(512)S(1)}, f32[512]{0:T(512)}, u32[]{:S(2)}) copy-start(f32[512]{0:T(512)} %param.19) | copy-start | bytes 6148
  23.9 11.0 %all-to-all-start.1 = ((f32[32,1,8,128]{3,2,1,0:T(8,128)}), f32[32,1,8,128]{3,2,1,0:T(8,128)S(1)}, u32[]{:S(2)}, u32[]{:S(2)}) async-start(f32[32,1,8,128]{3,2,1,0:T(8,128)} %bitcast.8), calls=%async_computation.1 | async-start | bytes 262144 | tf_op jit(solution)/shard_map/all_to_all | solution.py:936
  42.3 10.8 %all-to-all-start.2 = ((f32[32,1,8,128]{3,2,1,0:T(8,128)}), f32[32,1,8,128]{3,2,1,0:T(8,128)S(1)}, u32[]{:S(2)}, u32[]{:S(2)}) async-start(f32[32,1,8,128]{3,2,1,0:T(8,128)} %bitcast.14), calls=%async_computation.2 | async-start | bytes 262144 | tf_op jit(solution)/shard_map/all_to_all | solution.py:936
  56.7 13.0 %all-to-all-start.3 = ((f32[32,2,8,128]{3,2,1,0:T(8,128)}), f32[32,2,8,128]{3,2,1,0:T(8,128)S(1)}, u32[]{:S(2)}, u32[]{:S(2)}) async-start(f32[32,2,8,128]{3,2,1,0:T(8,128)} %bitcast.16), calls=%async_computation.3 | async-start | bytes 524288 | tf_op jit(solution)/shard_map/all_to_all | solution.py:936
  92.0 17.4 %all-to-all-start.5 = ((f32[32,7,4,128]{3,2,1,0:T(4,128)}), f32[32,7,4,128]{3,2,1,0:T(4,128)S(1)}, u32[]{:S(2)}, u32[]{:S(2)}) async-start(f32[32,7,4,128]{3,2,1,0:T(4,128)} %bitcast.19), calls=%async_computation.5 | async-start | bytes 917504 | tf_op jit(solution)/shard_map/all_to_all | solution.py:936

commit v9 on v8

--- a/solution.py
+++ b/solution.py
@@ -343,8 +343,8 @@
     token_ref,
     *refs,
 ):
-    pos_refs, refs = refs[:-11], refs[-11:]
-    r_hbm, s_ref, a_ref, r_ref, pull_ref, one_a, one_b, two_a, two_b, in_sem, out_sem = refs
+    pos_refs, refs = refs[:-7], refs[-7:]
+    r_hbm, s_ref, a_ref, r_ref, pull_ref, in_sem, out_sem = refs
     tiles = ot_ref.shape[1] // LANES
     listed = ot_ref.shape[0]
     particles = a_ref.shape[1] * SUB
@@ -378,31 +378,20 @@
             total = total + r
         return total
 
-    def step(g, total, old, new):
-        new[0][...] = first(g)
-        new[1][...] = second(old[0][...])
-        return third(g - 2, old[1][...], total)
-
-    left, right = (one_a, two_a), (one_b, two_b)
-
-    def pair(m, total):
-        total = step(2 * m, total, right, left)
-        return step(2 * m + 1, total, left, right)
-
     total = jnp.zeros((rows, listed), F32)
-    each = SUB // 4
-    for o in range(particles // SUB):
-        into.copy(o).wait()
-        if o == 0:
-            one_a[...] = first(0)
-            two_b[...] = second(one_a[...])
-            one_b[...] = first(1)
-        total = lax.fori_loop(max(1, o * each), (o + 1) * each, pair, total)
-        if o:
-            out.copy(o - 1).start()
-    last = particles // 2 - 1
-    total = third(last - 1, two_b[...], total)
-    total = third(last, second(one_b[...]), total)
+    groups, each = particles // 2, SUB // 2
+    ones, twos = {}, {}
+    for n in range(groups + 2):
+        if n < groups:
+            if n % each == 0:
+                into.copy(n // each).wait()
+            ones[n] = first(n)
+        if 0 < n <= groups:
+            twos[n - 1] = second(ones.pop(n - 1))
+        if n > 1:
+            total = third(n - 2, twos.pop(n - 2), total)
+            if (n - 1) % each == 0 and n - 1 < groups:
+                out.copy((n - 1) // each - 1).start()
     out.copy(particles // SUB - 1).start()
     source = total * (1.0 / particles)
     if pos_refs:
@@ -441,6 +430,7 @@
     w1_ref,
     w2_ref,
     w3_ref,
+    grid_ref,
     token_ref,
     out_ref,
     end_ref,
@@ -462,27 +452,38 @@
     live = jnp.concatenate([live] * side, axis=1) > 0.5
     count = 4 // wide
 
-    for o in range(particles // SUB // side):
-        for i in range(0, SUB, count):
-            ats = [pl.ds(i + u, rows, stride=SUB) for u in range(count)]
-            x = jnp.concatenate(
+    todo = [(o, i) for o in range(particles // SUB // side) for i in range(0, SUB, count)]
+    tile = [(u, t) for u in range(count) for t in range(wide)]
+    ones, twos, fed = {}, {}, {}
+    for n in range(len(todo) + 2):
+        if n < len(todo):
+            o, i = todo[n]
+            fed[n] = jnp.concatenate(
                 [
-                    base_ref[t, o, at, :] + pull[:, t * LANES : (t + 1) * LANES]
-                    for at in ats
-                    for t in range(wide)
+                    base_ref[t, o, pl.ds(i + u, rows, stride=SUB), :]
+                    + pull[:, t * LANES : (t + 1) * LANES]
+                    for u, t in tile
                 ],
                 axis=1,
             )
-            one = half_silu(dot(w1_ref[...], x.astype(BF), NN))
-            two = half_silu(dot(w2_ref[...], one, NN))
-            change = dot(w3_ref[...], two, NN).astype(BF).astype(F32)
-            for n, (at, t) in enumerate((at, t) for at in ats for t in range(wide)):
-                cols = slice(n * LANES, (n + 1) * LANES)
+            ones[n] = half_silu(dot(w1_ref[...], fed[n].astype(BF), NN))
+        if 0 < n <= len(todo):
+            twos[n - 1] = half_silu(dot(w2_ref[...], ones[n - 1], NN))
+        if n > 1:
+            o, i = todo[n - 2]
+            change = dot(w3_ref[...], twos[n - 2], NN).astype(BF).astype(F32)
+            for c, (u, t) in enumerate(tile):
+                cols = slice(c * LANES, (c + 1) * LANES)
                 mask = live[:, t * LANES : (t + 1) * LANES]
-                v_ref[t, o, at, :] = x[:, cols] + jnp.where(mask, change[:, cols], 0.0)
+                v_ref[t, o, pl.ds(i + u, rows, stride=SUB), :] = fed[n - 2][:, cols] + jnp.where(
+                    mask, change[:, cols], 0.0
+                )
 
     per = LANES // particles
     stride = out_ref.shape[0] // devices
+    width = grid_ref.shape[0] // devices
+    for d in range(devices):
+        out_ref[(d + 1) * stride - width : (d + 1) * stride] = grid_ref[d * width : (d + 1) * width]
 
     def scalar(s):
         parts = []
@@ -646,7 +647,7 @@
     count = places // devices
 
     def place(b, size):
-        first = stride - count * span + b
+        first = b
         x = jnp.concatenate(
             [arr_ref[pl.ds(first + c * span, devices, stride=stride), :] for c in range(count)],
             axis=0,
@@ -823,25 +824,23 @@
         return carry
 
     lax.fori_loop(0, nx, group, 0)
-    send_filtered(dims, g_ref, width, 0, inv_ref, f_ref)
-
-
-def send_filtered(dims, g_ref, g_stride, g_first, inv_ref, f_ref):
+    send_filtered(dims, g_ref, inv_ref, f_ref)
+
+
+def send_filtered(dims, g_ref, inv_ref, f_ref):
     nx, ny, own, bx, by = dims
     quads = bx * by
+    width = own * quads
     turns = quads * ny
-    f_stride = f_ref.shape[0] // (nx * ny)
 
     def group(x, carry):
         base = x * 2 * turns
         rows = [inv_ref[pl.ds(base + k * ny, ny), :] for k in range(quads)]
         lanes = [inv_ref[pl.ds(base + turns + k * ny, ny), :] for k in range(quads)]
-        first = x * ny * g_stride + g_first
-        out = route(g_ref, first, g_stride, 1, quads, own, quads, ny, rows, lanes)
+        out = route(g_ref, x * ny * width, width, 1, quads, own, quads, ny, rows, lanes)
         for s in range(own):
             for k in range(quads):
-                at = pl.ds(x * ny * f_stride + s * quads + k, ny, stride=f_stride)
-                f_ref[at, :] = out[s][k]
+                f_ref[pl.ds(x * ny * width + s * quads + k, ny, stride=width), :] = out[s][k]
         return carry
 
     lax.fori_loop(0, nx, group, 0)
@@ -868,7 +867,9 @@
     lax.fori_loop(0, nx, group, 0)
 
 
-def again_body(dims, s_ref, g_ref, arr_ref, inv_ref, lab_ref, token_ref, f_ref, mid_ref):
+def again_body(
+    dims, s_ref, g_ref, arr_ref, inv_ref, lab_ref, token_ref, f_ref, out_ref, mid_ref
+):
     nx, ny, own, bx, by = dims
     quads = bx * by
     boxes = nx * ny
@@ -879,8 +880,8 @@
     for s in range(own):
         value = [load_rows(mid_ref, s * quads + j, width, boxes) for j in range(quads)]
         for j, v in enumerate(stencil(value, speed, bx, by, ny)):
-            f_ref[pl.ds(width + s * quads + j, boxes, stride=2 * width), :] = v
-    send_filtered(dims, f_ref, 2 * width, width, inv_ref, f_ref)
+            out_ref[pl.ds(s * quads + j, boxes, stride=width), :] = v
+    send_filtered(dims, out_ref, inv_ref, f_ref)
 
 
 def per_device(
@@ -993,7 +994,6 @@
     side = max(1, LANES // places)
     base_shape = (max(1, places // LANES), octets // side, rows * SUB, LANES)
     kept = SUB * (-(-scalars // SUB))
-    pair = pltpu.VMEM((hidden, 2 * listed), BF)
     me = jnp.stack([lax.axis_index("gx"), lax.axis_index("gy")]).astype(I32)
     pos, put, lcol, acol = call(
         functools.partial(maps_body, dims),
@@ -1016,7 +1016,6 @@
             smem=(0,),
             hbm=(2,),
             scratch=[listed_vmem, listed_vmem, pltpu.VMEM((rows, listed), F32)]
-            + [pair] * 4
             + [dma((octets,)), dma((octets,))],
         )
 
@@ -1030,9 +1029,9 @@
         hbm=(0, 2),
         scratch=[state_vmem, state_vmem, listed_vmem, per_block, per_block, per_listed],
     )
-    (sent,) = call(
+    sent, grid = call(
         functools.partial(again_body, dims),
-        [((2 * flat, LANES), F32)],
+        [((flat, LANES), F32), ((flat, LANES), F32)],
         [home, grid, arrival, inv, lab, token],
         scratch=[pltpu.VMEM((flat, LANES), F32)],
     )
@@ -1051,8 +1050,8 @@
     f = exchange(sent)
     leaving, token = call(
         functools.partial(early_body, devices, rows, span, scalars, heads),
-        [((places * span, LANES), F32), ((1, LANES), F32)],
-        [react_count, f, base, ot, rate, lcol, w1, w2, w3, token],
+        [((places * span + flat, LANES), F32), ((1, LANES), F32)],
+        [react_count, f, base, ot, rate, lcol, w1, w2, w3, grid, token],
         smem=(0,),
         scratch=[pltpu.VMEM(base_shape, F32)],
     )
@@ -1069,7 +1068,7 @@
     (grid,) = call(
         functools.partial(unpack_body, devices, own),
         [((scalars * quads, LANES), F32)],
-        [source, f, put],
+        [source, moved, put],
     )
     grid_out = grid.reshape(grid_scalars.shape)
     steps = -(-scalars // per)

time: 116 us -> 106 us (0.914)
  blocking collectives: 11.7 us -> 0 us
  starting transfers between devices: 18.4 us -> 22.7 us
  Pallas kernels: 58.1 us -> 56.1 us
    all_to_all x1 -> x0, blocking collectives: 11.7 us -> none  [per_device(): lax.all_to_all(source, 'gy', split_axis=0, concat_axis=0, tiled=True)]
    all_to_all x0 -> x1, starting transfers between devices: none -> 3.4 us  [per_device(): lax.all_to_all(source, 'gy', split_axis=0, concat_axis=0, tiled=True)]
    pallas_call x14, Pallas kernels: 58.1 us -> 56.1 us  [call(): pl.pallas_call(body, out_shape=[pltpu.HBM(o[0], o[1]) if len(o) > 2 else...]
  transfers between devices with their start and end apart: 5 -> 6, of which waited for: 5 -> 5; matrix products, arithmetic and copies ran while one was open for 0% -> 0% of each run, Pallas kernels for 22% -> 34%
where the time goes in v9:
time: 106 us
  Pallas kernels  56.1 us (53%)
  waiting for transfers between devices  25.4 us (24%)
  starting transfers between devices  22.7 us (21%)
  between operations  1.54 us (1%)
    pallas_call x14, Pallas kernels, call(): pl.pallas_call(body, out_shape=[pltpu.HBM(o[0], o[1]) if len(o) > 2 else...  56.1 us
    all_to_all x5, waiting for transfers between devices, exchange(): lax.all_to_all(x, both, split_axis=0, concat_axis=0, tiled=True)  25.4 us
    all_to_all x5, starting transfers between devices, exchange(): lax.all_to_all(x, both, split_axis=0, concat_axis=0, tiled=True)  19.3 us
    all_to_all x1, starting transfers between devices, per_device(): lax.all_to_all(source, 'gy', split_axis=0, concat_axis=0, tiled=True)  3.4 us
  transfers between devices with their start and end apart: 6, of which 5 were waited for; matrix products, arithmetic and copies ran while one was open for 0% of the time, Pallas kernels for 34%

profile of v9, /device:TPU:0, one launch (start us, length us, event | category | flops | bytes accessed | tf_op | source)
XLA Modules:
  0.0 105.9 jit_solution(4040666511566531667)
XLA Ops:
  0.6 0.0 copy-start.6
  0.6 0.0 copy-start.5
  0.7 0.0 copy-start.4
  0.7 0.0 copy-start.1
  0.7 0.0 copy-start.3
  0.7 0.0 copy-start.8
  0.7 0.0 copy-start.7
  0.7 1.7 %shard_map.149 = f32[512,128]{1,0:T(8,128)} custom-call(f32[216,128]{1,0:T(8,128)} %bitcast.45, s32[4,128]{1,0:T(4,128)} %bitcast.41, s32[4,128]{1,0:T(4,128)} %bitcast.43, f32[4,128]{1,0:T(4,128)} %bitcast.47), custom_call_target="tpu_custom_call" | custom-call | tf_op jit(solution)/shard_map/pallas_call | solution.py:26
  2.4 7.3 %all-to-all-start = ((f32[32,2,8,128]{3,2,1,0:T(8,128)}), f32[32,2,8,128]{3,2,1,0:T(8,128)S(1)}, u32[]{:S(2)}, u32[]{:S(2)}) async-start(f32[32,2,8,128]{3,2,1,0:T(8,128)} %bitcast.4), calls=%async_computation | async-start | bytes 524288 | tf_op jit(solution)/shard_map/all_to_all | solution.py:937
  9.8 0.0 copy-start
  9.8 0.0 copy-start.2
  9.8 6.8 %shard_map.150 = (f32[54,32,512]{2,1,0:T(8,128)}, f32[2,4,512,128]{3,2,1,0:T(8,128)}, bf16[256,512]{1,0:T(8,128)(2,1)S(1)}, f32[8,256]{1,0:T(8,128)S(1)}) custom-call(f32[54,32,512]{2,1,0:T(8,128)} %p_hbm.1, s32[32,512]{1,0:T(8,128)} %partner_ref.1, f32[1,512]{1,0:T(1,128)} %bitcast.35, s32[1,256]{1,0:T(1,128)} %list_hbm.1), custom_call_target="tpu_custom_call" | custom-call | tf_op jit(solution)/shard_map/pallas_call | solution.py:26
  16.6 3.2 %all-to-all-done = f32[32,2,8,128]{3,2,1,0:T(8,128)S(1)} async-done(((f32[32,2,8,128]{3,2,1,0:T(8,128)}), f32[32,2,8,128]{3,2,1,0:T(8,128)S(1)}, u32[]{:S(2)}, u32[]{:S(2)}) %all-to-all-start) | async-done | bytes 262176 | tf_op jit(solution)/shard_map/all_to_all | solution.py:937
  19.8 4.2 %shard_map.151 = (f32[256,128]{1,0:T(8,128)S(1)}, f32[256,128]{1,0:T(8,128)}, s32[256,128]{1,0:T(8,128)S(1)}, s32[128,128]{1,0:T(8,128)S(1)}) custom-call(f32[512,128]{1,0:T(8,128)S(1)} %bitcast.27, f32[8,256]{1,0:T(8,128)S(1)} %get-tuple-element.31.token_ref.rsel_ref), custom_call_target="tpu_custom_call" | custom-call | tf_op jit(solution)/shard_map/pallas_call | solution.py:26
  24.0 2.9 %all-to-all-start.1 = ((f32[32,1,8,128]{3,2,1,0:T(8,128)}), f32[32,1,8,128]{3,2,1,0:T(8,128)S(1)}, u32[]{:S(2)}, u32[]{:S(2)}) async-start(f32[32,1,8,128]{3,2,1,0:T(8,128)} %bitcast.8), calls=%async_computation.1 | async-start | bytes 262144 | tf_op jit(solution)/shard_map/all_to_all | solution.py:937
  27.5 0.1 pad_add_fusion.me_ref
  27.6 0.0 copy-done.4
  27.6 0.0 copy-done.1
  27.6 0.0 copy-done.3
  27.6 0.1 shard_map.152
  27.7 0.0 copy-done.6
  27.7 0.0 copy-done.5
  27.7 0.0 copy-done.8
  27.7 0.0 copy-done.7
  27.7 1.5 %shard_map.153 = (f32[256,128]{1,0:T(8,128)S(1)}, bf16[1024,512]{1,0:T(8,128)(2,1)S(1)}, s32[64,128]{1,0:T(8,128)S(1)}, s32[64,128]{1,0:T(8,128)S(1)}) custom-call(s32[2]{0:T(128)S(1)} %pad_add_fusion.me_ref, s32[256,128]{1,0:T(8,128)S(1)} %get-tuple-element.39.inv_ref, bf16[256,512]{1,0:T(8,128)(2,1)S(1)} %get-tuple-element.34.ot_ref, ...), custom_call_target="tpu_custom_call" | custom-call | tf_op jit(solution)/shard_map/pallas_call | solution.py:26
  29.2 5.8 %all-to-all-done.1 = f32[32,1,8,128]{3,2,1,0:T(8,128)S(1)} async-done(((f32[32,1,8,128]{3,2,1,0:T(8,128)}), f32[32,1,8,128]{3,2,1,0:T(8,128)S(1)}, u32[]{:S(2)}, u32[]{:S(2)}) %all-to-all-start.1) | async-done | bytes 131104 | tf_op jit(solution)/shard_map/all_to_all | solution.py:937
  35.0 6.4 %shard_map.154 = (f32[2,4,512,128]{3,2,1,0:T(8,128)}, f32[256,128]{1,0:T(8,128)}) custom-call(s32[1]{0:T(128)S(6)} %copy.19.count_ref, f32[256,128]{1,0:T(8,128)S(1)} %bitcast.32, f32[2,4,512,128]{3,2,1,0:T(8,128)} %get-tuple-element.33.a_hbm, bf16[256,512]{1,0:T(8,128)(2,1)S(1)} %get-tuple-element.34.ot_ref, ...), custom_call_target="tpu_custom_call" | custom-call | tf_op jit(solution)/shard_map/pallas_call | solution.py:26
  41.4 2.6 %all-to-all-start.2 = ((f32[32,1,8,128]{3,2,1,0:T(8,128)}), f32[32,1,8,128]{3,2,1,0:T(8,128)S(1)}, u32[]{:S(2)}, u32[]{:S(2)}) async-start(f32[32,1,8,128]{3,2,1,0:T(8,128)} %bitcast.14), calls=%async_computation.2 | async-start | bytes 262144 | tf_op jit(solution)/shard_map/all_to_all | solution.py:937
  44.0 0.0 copy-done
  44.0 0.0 copy-done.2
  44.0 5.3 %shard_map.155 = (f32[54,32,512]{2,1,0:T(8,128)}, f32[1,128]{1,0:T(1,128)S(1)}) custom-call(f32[54,32,512]{2,1,0:T(8,128)} %get-tuple-element.43.q_hbm, f32[256,128]{1,0:T(8,128)S(1)} %bitcast.33, f32[2,4,512,128]{3,2,1,0:T(8,128)} %get-tuple-element.44.r_hbm, bf16[256,512]{1,0:T(8,128)(2,1)S(1)} %get-tuple-element.34.ot_ref, f32[1,512]{1,0:T(1,128)S(1)} %bitcast.36, ...), custom_call_target="tpu_custom_call" | custom-call | tf_op jit(solution)/shard_map/pallas_call | solution.py:26
  49.3 2.9 %all-to-all-done.2 = f32[32,1,8,128]{3,2,1,0:T(8,128)S(1)} async-done(((f32[32,1,8,128]{3,2,1,0:T(8,128)}), f32[32,1,8,128]{3,2,1,0:T(8,128)S(1)}, u32[]{:S(2)}, u32[]{:S(2)}) %all-to-all-start.2) | async-done | bytes 131104 | tf_op jit(solution)/shard_map/all_to_all | solution.py:937
  52.1 3.6 %shard_map.156 = (f32[256,128]{1,0:T(8,128)}, f32[256,128]{1,0:T(8,128)S(1)}) custom-call(f32[256,128]{1,0:T(8,128)S(1)} %bitcast.34, f32[256,128]{1,0:T(8,128)S(1)} %get-tuple-element.42.g_ref, f32[512,128]{1,0:T(8,128)S(1)} %bitcast.28, s32[256,128]{1,0:T(8,128)S(1)} %get-tuple-element.39.inv_ref, s32[128,128]{1,0:T(8,128)S(1)} %get-tuple-element.35.token_ref.lab_ref, ...), custom_call_target="tpu_custom_call" | custom-call | tf_op jit(solution)/shard_map/pallas_call | solution.py:26
  55.7 3.0 %all-to-all-start.3 = ((f32[32,1,8,128]{3,2,1,0:T(8,128)}), f32[32,1,8,128]{3,2,1,0:T(8,128)S(1)}, u32[]{:S(2)}, u32[]{:S(2)}) async-start(f32[32,1,8,128]{3,2,1,0:T(8,128)} %bitcast.17), calls=%async_computation.3 | async-start | bytes 262144 | tf_op jit(solution)/shard_map/all_to_all | solution.py:937
  58.7 5.6 %shard_map.157 = (f32[2,4,512,128]{3,2,1,0:T(8,128)}, f32[1,2,512,128]{3,2,1,0:T(8,128)S(1)}, f32[1,128]{1,0:T(1,128)S(1)}) custom-call(f32[54,32,512]{2,1,0:T(8,128)} %get-tuple-element.47.q_hbm, f32[1,512]{1,0:T(1,128)S(1)} %bitcast.37, f32[8,256]{1,0:T(8,128)S(1)} %get-tuple-element.31.token_ref.rsel_ref, bf16[256,512]{1,0:T(8,128)(2,1)S(1)} %get-tuple-element.34.ot_ref, ...), custom_call_target="tpu_custom_call" | custom-call | tf_op jit(solution)/shard_map/pallas_call | solution.py:26
  64.4 2.5 %all-to-all-done.3 = f32[32,1,8,128]{3,2,1,0:T(8,128)S(1)} async-done(((f32[32,1,8,128]{3,2,1,0:T(8,128)}), f32[32,1,8,128]{3,2,1,0:T(8,128)S(1)}, u32[]{:S(2)}, u32[]{:S(2)}) %all-to-all-start.3) | async-done | bytes 131104 | tf_op jit(solution)/shard_map/all_to_all | solution.py:937
  66.9 3.2 %shard_map.158 = (f32[1152,128]{1,0:T(8,128)}, f32[1,128]{1,0:T(1,128)S(1)}) custom-call(s32[1]{0:T(128)S(6)} %copy.19.count_ref, f32[256,128]{1,0:T(8,128)S(1)} %bitcast.29, f32[1,2,512,128]{3,2,1,0:T(8,128)S(1)} %get-tuple-element.50.base_ref, bf16[256,512]{1,0:T(8,128)(2,1)S(1)} %get-tuple-element.34.ot_ref, f32[1,512]{1,0:T(1,128)S(1)} %bitcast.38, ...), custom_call_target="tpu_custom_call" | custom-call | tf_op jit(solution)/shard_map/pallas_call | solution.py:26
  70.1 3.5 %all-to-all-start.5 = ((f32[32,9,4,128]{3,2,1,0:T(4,128)}), f32[32,9,4,128]{3,2,1,0:T(4,128)S(1)}, u32[]{:S(2)}, u32[]{:S(2)}) async-start(f32[32,9,4,128]{3,2,1,0:T(4,128)} %bitcast.19), calls=%async_computation.5 | async-start | bytes 1179648 | tf_op jit(solution)/shard_map/all_to_all | solution.py:937
  73.6 6.4 %shard_map.159 = (f32[2,4,512,128]{3,2,1,0:T(8,128)}, f32[8,56,128]{2,1,0:T(8,128)}) custom-call(s32[1]{0:T(128)S(6)} %copy.19.count_ref, f32[256,128]{1,0:T(8,128)S(1)} %bitcast.30, f32[2,4,512,128]{3,2,1,0:T(8,128)} %get-tuple-element.49.a_hbm, bf16[256,512]{1,0:T(8,128)(2,1)S(1)} %get-tuple-element.34.ot_ref, ...), custom_call_target="tpu_custom_call" | custom-call | tf_op jit(solution)/shard_map/pallas_call | solution.py:26
  80.0 11.0 %all-to-all-done.5 = f32[32,9,4,128]{3,2,1,0:T(4,128)S(1)} async-done(((f32[32,9,4,128]{3,2,1,0:T(4,128)}), f32[32,9,4,128]{3,2,1,0:T(4,128)S(1)}, u32[]{:S(2)}, u32[]{:S(2)}) %all-to-all-start.5) | async-done | bytes 589856 | tf_op jit(solution)/shard_map/all_to_all | solution.py:937
  91.1 3.4 %all-to-all-start.4 = ((f32[8,56,128]{2,1,0:T(8,128)}), f32[8,56,128]{2,1,0:T(8,128)S(1)}, u32[]{:S(2)}, u32[]{:S(2)}) async-start(f32[8,56,128]{2,1,0:T(8,128)} %get-tuple-element.54), calls=%async_computation.4 | async-start | bytes 458752 | tf_op jit(solution)/shard_map/all_to_all | solution.py:1067
  94.5 4.8 %shard_map.161 = (f32[54,32,512]{2,1,0:T(8,128)}, f32[1,128]{1,0:T(1,128)}) custom-call(f32[54,32,512]{2,1,0:T(8,128)} %get-tuple-element.47.q_hbm, f32[256,128]{1,0:T(8,128)S(1)} %bitcast.31, f32[2,4,512,128]{3,2,1,0:T(8,128)} %get-tuple-element.57.r_hbm, bf16[256,512]{1,0:T(8,128)(2,1)S(1)} %get-tuple-element.34.ot_ref, f32[1,512]{1,0:T(1,128)S(1)} %bitcast.39), custom_call_target="tpu_custom_call" | custom-call | tf_op jit(solution)/shard_map/pallas_call | solution.py:26
  99.3 5.6 %shard_map.162 = f32[54,32,512]{2,1,0:T(8,128)} custom-call(f32[54,32,512]{2,1,0:T(8,128)} %get-tuple-element.58.p_hbm, f32[1152,128]{1,0:T(8,128)S(1)} %bitcast.25, s32[64,128]{1,0:T(8,128)S(1)} %get-tuple-element.59.acol_ref), custom_call_target="tpu_custom_call" | custom-call | tf_op jit(solution)/shard_map/pallas_call | solution.py:26
  104.9 0.0 all-to-all-done.4.s_ref
  104.9 1.0 shard_map.160
Async XLA Ops:
  0.6 27.1 %copy-start.6 = (s32[2,2,128]{2,1,0:T(2,128)S(1)}, s32[2,2,128]{2,1,0:T(2,128)}, u32[]{:S(2)}) copy-start(s32[2,2,128]{2,1,0:T(2,128)} %param.18) | copy-start | bytes 6148
  0.6 27.1 %copy-start.5 = (s32[2,2,128]{2,1,0:T(2,128)S(1)}, s32[2,2,128]{2,1,0:T(2,128)}, u32[]{:S(2)}) copy-start(s32[2,2,128]{2,1,0:T(2,128)} %param.17) | copy-start | bytes 6148
  0.7 26.9 %copy-start.4 = (bf16[54,256]{1,0:T(8,128)(2,1)S(1)}, bf16[54,256]{1,0:T(8,128)(2,1)}, u32[]{:S(2)}) copy-start(bf16[54,256]{1,0:T(8,128)(2,1)} %w3_ref.1) | copy-start | bytes 82948
  0.7 26.9 %copy-start.1 = (bf16[256,256]{1,0:T(8,128)(2,1)S(1)}, bf16[256,256]{1,0:T(8,128)(2,1)}, u32[]{:S(2)}) copy-start(bf16[256,256]{1,0:T(8,128)(2,1)} %w2_ref.1) | copy-start | bytes 393220
  0.7 26.9 %copy-start.3 = (bf16[256,54]{0,1:T(8,128)(2,1)S(1)}, bf16[256,54]{0,1:T(8,128)(2,1)}, u32[]{:S(2)}) copy-start(bf16[256,54]{0,1:T(8,128)(2,1)} %param.21) | copy-start | bytes 82948
  0.7 27.0 %copy-start.8 = (s32[1,64]{1,0:T(1,128)S(1)}, s32[1,64]{1,0:T(1,128)}, u32[]{:S(2)}) copy-start(s32[1,64]{1,0:T(1,128)} %arrive_ref.1) | copy-start | bytes 772
  0.7 27.0 %copy-start.7 = (s32[1,64]{1,0:T(1,128)S(1)}, s32[1,64]{1,0:T(1,128)}, u32[]{:S(2)}) copy-start(s32[1,64]{1,0:T(1,128)} %leave_ref.1) | copy-start | bytes 772
  2.4 17.3 %all-to-all-start = ((f32[32,2,8,128]{3,2,1,0:T(8,128)}), f32[32,2,8,128]{3,2,1,0:T(8,128)S(1)}, u32[]{:S(2)}, u32[]{:S(2)}) async-start(f32[32,2,8,128]{3,2,1,0:T(8,128)} %bitcast.4), calls=%async_computation | async-start | bytes 524288 | tf_op jit(solution)/shard_map/all_to_all | solution.py:937
  9.8 34.2 %copy-start = (s32[32,512]{1,0:T(8,128)S(1)}, s32[32,512]{1,0:T(8,128)}, u32[]{:S(2)}) copy-start(s32[32,512]{1,0:T(8,128)} %partner_ref.1) | copy-start | bytes 196612
  9.8 34.2 %copy-start.2 = (f32[512]{0:T(512)S(1)}, f32[512]{0:T(512)}, u32[]{:S(2)}) copy-start(f32[512]{0:T(512)} %param.19) | copy-start | bytes 6148
  24.0 11.0 %all-to-all-start.1 = ((f32[32,1,8,128]{3,2,1,0:T(8,128)}), f32[32,1,8,128]{3,2,1,0:T(8,128)S(1)}, u32[]{:S(2)}, u32[]{:S(2)}) async-start(f32[32,1,8,128]{3,2,1,0:T(8,128)} %bitcast.8), calls=%async_computation.1 | async-start | bytes 262144 | tf_op jit(solution)/shard_map/all_to_all | solution.py:937
  41.4 10.8 %all-to-all-start.2 = ((f32[32,1,8,128]{3,2,1,0:T(8,128)}), f32[32,1,8,128]{3,2,1,0:T(8,128)S(1)}, u32[]{:S(2)}, u32[]{:S(2)}) async-start(f32[32,1,8,128]{3,2,1,0:T(8,128)} %bitcast.14), calls=%async_computation.2 | async-start | bytes 262144 | tf_op jit(solution)/shard_map/all_to_all | solution.py:937
  55.7 11.1 %all-to-all-start.3 = ((f32[32,1,8,128]{3,2,1,0:T(8,128)}), f32[32,1,8,128]{3,2,1,0:T(8,128)S(1)}, u32[]{:S(2)}, u32[]{:S(2)}) async-start(f32[32,1,8,128]{3,2,1,0:T(8,128)} %bitcast.17), calls=%async_computation.3 | async-start | bytes 262144 | tf_op jit(solution)/shard_map/all_to_all | solution.py:937
  70.1 21.0 %all-to-all-start.5 = ((f32[32,9,4,128]{3,2,1,0:T(4,128)}), f32[32,9,4,128]{3,2,1,0:T(4,128)S(1)}, u32[]{:S(2)}, u32[]{:S(2)}) async-start(f32[32,9,4,128]{3,2,1,0:T(4,128)} %bitcast.19), calls=%async_computation.5 | async-start | bytes 1179648 | tf_op jit(solution)/shard_map/all_to_all | solution.py:937
  91.1 13.8 %all-to-all-start.4 = ((f32[8,56,128]{2,1,0:T(8,128)}), f32[8,56,128]{2,1,0:T(8,128)S(1)}, u32[]{:S(2)}, u32[]{:S(2)}) async-start(f32[8,56,128]{2,1,0:T(8,128)} %get-tuple-element.54), calls=%async_computation.4 | async-start | bytes 458752 | tf_op jit(solution)/shard_map/all_to_all | solution.py:1067

commit v10 on v9

--- a/solution.py
+++ b/solution.py
@@ -430,7 +430,6 @@
     w1_ref,
     w2_ref,
     w3_ref,
-    grid_ref,
     token_ref,
     out_ref,
     end_ref,
@@ -481,9 +480,6 @@
 
     per = LANES // particles
     stride = out_ref.shape[0] // devices
-    width = grid_ref.shape[0] // devices
-    for d in range(devices):
-        out_ref[(d + 1) * stride - width : (d + 1) * stride] = grid_ref[d * width : (d + 1) * width]
 
     def scalar(s):
         parts = []
@@ -530,7 +526,7 @@
 def maps_body(
     dims,
     me_ref,
-    inv_ref,
+    lab_ref,
     ot_ref,
     owner_ref,
     slot_ref,
@@ -540,9 +536,11 @@
     put_ref,
     lcol_ref,
     acol_ref,
+    inv_ref,
     turn_ref,
 ):
     nx, ny, _, bx, by = dims
+    invert(dims, lab_ref, inv_ref)
     columns(leave_ref, nx * ny, lcol_ref, turn_ref)
     columns(arrive_ref, nx * ny, acol_ref, turn_ref)
     quads = bx * by
@@ -647,7 +645,7 @@
     count = places // devices
 
     def place(b, size):
-        first = b
+        first = stride - count * span + b
         x = jnp.concatenate(
             [arr_ref[pl.ds(first + c * span, devices, stride=stride), :] for c in range(count)],
             axis=0,
@@ -780,7 +778,7 @@
     c_ref[...] = jnp.concatenate([w3_ref[...].astype(F32), rest], axis=0).astype(BF)
 
 
-def start_body(dims, arr_ref, token_ref, g_ref, f_ref, inv_ref, lab_ref):
+def start_body(dims, arr_ref, token_ref, g_ref, f_ref, lab_ref, high_ref, low_ref):
     nx, ny, own, bx, by = dims
     quads = bx * by
     boxes = nx * ny
@@ -791,11 +789,54 @@
     for s in range(own):
         value = [load_rows(arr_ref, s * quads + j, stride, boxes) for j in range(quads)]
         for j, v in enumerate(stencil(value, speed, bx, by, ny)):
-            g_ref[pl.ds(s * quads + j, boxes, stride=width), :] = v
+            at = pl.ds(s * quads + j, boxes, stride=width)
+            g_ref[at, :] = v
+            high = v.astype(BF).astype(F32)
+            high_ref[at, :] = high
+            low_ref[at, :] = v - high
     for j in range(quads):
         lab_ref[pl.ds(j * boxes, boxes), :] = load_rows(arr_ref, width + j, stride, boxes).astype(
             I32
         )
+    sub_of = lax.broadcasted_iota(I32, (turns, LANES), 0).astype(F32).astype(BF)
+    sub_lane = lax.broadcasted_iota(I32, (LANES, LANES), 0).astype(F32).astype(BF)
+    none = jnp.zeros((turns, LANES), BF)
+    unit = jnp.ones((LANES, LANES), BF)
+
+    def group(x, carry):
+        def gather(y, acc):
+            left, right = [], []
+            for j in range(quads):
+                line = lab_ref[pl.ds(j * boxes + x * ny + y, 1), :]
+                hit = jnp.broadcast_to((line >> 7).astype(F32).astype(BF), (turns, LANES)) == sub_of
+                parts = []
+                for s in range(own):
+                    at = pl.ds((x * ny + y) * width + s * quads + j, 1)
+                    for ref in (high_ref, low_ref):
+                        value = jnp.broadcast_to(ref[at, :].astype(BF), (turns, LANES))
+                        parts.append(jnp.where(hit, value, none))
+                left.append(jnp.concatenate(parts, axis=0))
+                lane = jnp.broadcast_to((line & (LANES - 1)).astype(F32).astype(BF), (LANES, LANES))
+                right.append(jnp.where(lane == sub_lane, unit, jnp.zeros_like(unit)))
+            return acc + dot(jnp.concatenate(left, axis=1), jnp.concatenate(right, axis=1), NT)
+
+        zero = jnp.zeros((2 * own * turns, LANES), F32)
+        acc = lax.fori_loop(0, ny, gather, zero, unroll=min(ny, 8))
+        for s in range(own):
+            out = acc[2 * s * turns : (2 * s + 1) * turns] + acc[(2 * s + 1) * turns :][:turns]
+            for k in range(quads):
+                at = pl.ds(x * ny * width + s * quads + k, ny, stride=width)
+                f_ref[at, :] = out[k * ny : (k + 1) * ny]
+        return carry
+
+    lax.fori_loop(0, nx, group, 0)
+
+
+def invert(dims, lab_ref, inv_ref):
+    nx, ny, _, bx, by = dims
+    quads = bx * by
+    boxes = nx * ny
+    turns = quads * ny
     lane_of = lax.broadcasted_iota(I32, (turns, LANES), 1).astype(F32).astype(BF)
     sub_of = lax.broadcasted_iota(I32, (turns, LANES), 0).astype(F32).astype(BF)
     sub_lane = lax.broadcasted_iota(I32, (LANES, LANES), 0).astype(F32).astype(BF)
@@ -824,23 +865,24 @@
         return carry
 
     lax.fori_loop(0, nx, group, 0)
-    send_filtered(dims, g_ref, inv_ref, f_ref)
-
-
-def send_filtered(dims, g_ref, inv_ref, f_ref):
+
+
+def send_filtered(dims, g_ref, g_stride, g_first, inv_ref, f_ref):
     nx, ny, own, bx, by = dims
     quads = bx * by
-    width = own * quads
     turns = quads * ny
+    f_stride = f_ref.shape[0] // (nx * ny)
 
     def group(x, carry):
         base = x * 2 * turns
         rows = [inv_ref[pl.ds(base + k * ny, ny), :] for k in range(quads)]
         lanes = [inv_ref[pl.ds(base + turns + k * ny, ny), :] for k in range(quads)]
-        out = route(g_ref, x * ny * width, width, 1, quads, own, quads, ny, rows, lanes)
+        first = x * ny * g_stride + g_first
+        out = route(g_ref, first, g_stride, 1, quads, own, quads, ny, rows, lanes)
         for s in range(own):
             for k in range(quads):
-                f_ref[pl.ds(x * ny * width + s * quads + k, ny, stride=width), :] = out[s][k]
+                at = pl.ds(x * ny * f_stride + s * quads + k, ny, stride=f_stride)
+                f_ref[at, :] = out[s][k]
         return carry
 
     lax.fori_loop(0, nx, group, 0)
@@ -867,9 +909,7 @@
     lax.fori_loop(0, nx, group, 0)
 
 
-def again_body(
-    dims, s_ref, g_ref, arr_ref, inv_ref, lab_ref, token_ref, f_ref, out_ref, mid_ref
-):
+def again_body(dims, s_ref, g_ref, arr_ref, inv_ref, lab_ref, token_ref, f_ref, mid_ref):
     nx, ny, own, bx, by = dims
     quads = bx * by
     boxes = nx * ny
@@ -880,8 +920,8 @@
     for s in range(own):
         value = [load_rows(mid_ref, s * quads + j, width, boxes) for j in range(quads)]
         for j, v in enumerate(stencil(value, speed, bx, by, ny)):
-            out_ref[pl.ds(s * quads + j, boxes, stride=width), :] = v
-    send_filtered(dims, out_ref, inv_ref, f_ref)
+            f_ref[pl.ds(width + s * quads + j, boxes, stride=2 * width), :] = v
+    send_filtered(dims, f_ref, 2 * width, width, inv_ref, f_ref)
 
 
 def per_device(
@@ -971,15 +1011,11 @@
             dma((3,)),
         ],
     )
-    grid, sent, inv, lab = call(
+    grid, sent, lab = call(
         functools.partial(start_body, dims),
-        [
-            ((flat, LANES), F32),
-            ((flat, LANES), F32),
-            ((nx * 2 * quads * ny, LANES), I32),
-            ((quads * devices, LANES), I32),
-        ],
+        [((flat, LANES), F32), ((flat, LANES), F32), ((quads * devices, LANES), I32)],
         [arrival, rsel],
+        scratch=[pltpu.VMEM((flat, LANES), F32)] * 2,
     )
 
     w1, w2, w3 = call(
@@ -995,15 +1031,16 @@
     base_shape = (max(1, places // LANES), octets // side, rows * SUB, LANES)
     kept = SUB * (-(-scalars // SUB))
     me = jnp.stack([lax.axis_index("gx"), lax.axis_index("gy")]).astype(I32)
-    pos, put, lcol, acol = call(
+    pos, put, lcol, acol, inv = call(
         functools.partial(maps_body, dims),
         [
             ((listed, LANES), F32),
             ((ny * LANES, cells), BF),
             ((places, LANES), I32),
             ((places, LANES), I32),
+            ((nx * 2 * quads * ny, LANES), I32),
         ],
-        [me, inv, ot, box[1], box[2], leave_slots, arrive_slots],
+        [me, lab, ot, box[1], box[2], leave_slots, arrive_slots],
         smem=(0,),
         scratch=[pltpu.VMEM((places, LANES), F32)],
     )
@@ -1029,9 +1066,9 @@
         hbm=(0, 2),
         scratch=[state_vmem, state_vmem, listed_vmem, per_block, per_block, per_listed],
     )
-    sent, grid = call(
+    (sent,) = call(
         functools.partial(again_body, dims),
-        [((flat, LANES), F32), ((flat, LANES), F32)],
+        [((2 * flat, LANES), F32)],
         [home, grid, arrival, inv, lab, token],
         scratch=[pltpu.VMEM((flat, LANES), F32)],
     )
@@ -1050,8 +1087,8 @@
     f = exchange(sent)
     leaving, token = call(
         functools.partial(early_body, devices, rows, span, scalars, heads),
-        [((places * span + flat, LANES), F32), ((1, LANES), F32)],
-        [react_count, f, base, ot, rate, lcol, w1, w2, w3, grid, token],
+        [((places * span, LANES), F32), ((1, LANES), F32)],
+        [react_count, f, base, ot, rate, lcol, w1, w2, w3, token],
         smem=(0,),
         scratch=[pltpu.VMEM(base_shape, F32)],
     )
@@ -1068,7 +1105,7 @@
     (grid,) = call(
         functools.partial(unpack_body, devices, own),
         [((scalars * quads, LANES), F32)],
-        [source, moved, put],
+        [source, f, put],
     )
     grid_out = grid.reshape(grid_scalars.shape)
     steps = -(-scalars // per)

time: 106 us -> 112 us (1.057)
  blocking collectives: 0 us -> 11.7 us
  starting transfers between devices: 22.7 us -> 18.5 us
  waiting for transfers between devices: 25.4 us -> 23.1 us
    all_to_all x0 -> x1, blocking collectives: none -> 11.7 us  [per_device(): lax.all_to_all(source, 'gy', split_axis=0, concat_axis=0, tiled=True)]
    all_to_all x1 -> x0, starting transfers between devices: 3.4 us -> none  [per_device(): lax.all_to_all(source, 'gy', split_axis=0, concat_axis=0, tiled=True)]
    all_to_all x5, waiting for transfers between devices: 25.4 us -> 23.1 us  [exchange(): lax.all_to_all(x, both, split_axis=0, concat_axis=0, tiled=True)]
  transfers between devices with their start and end apart: 6 -> 5, of which waited for: 5 -> 5; matrix products, arithmetic and copies ran while one was open for 0% -> 0% of each run, Pallas kernels for 34% -> 24%
where the time goes in v10:
time: 112 us; the launch traced here: 111 us
  Pallas kernels  56 us (50%)
  waiting for transfers between devices  23.1 us (21%)
  starting transfers between devices  18.5 us (17%)
  blocking collectives  11.7 us (10%)
  between operations  1.68 us (2%)
    pallas_call x14, Pallas kernels, call(): pl.pallas_call(body, out_shape=[pltpu.HBM(o[0], o[1]) if len(o) > 2 else...  56 us
    all_to_all x5, waiting for transfers between devices, exchange(): lax.all_to_all(x, both, split_axis=0, concat_axis=0, tiled=True)  23.1 us
    all_to_all x5, starting transfers between devices, exchange(): lax.all_to_all(x, both, split_axis=0, concat_axis=0, tiled=True)  18.5 us
    all_to_all x1, blocking collectives, per_device(): lax.all_to_all(source, 'gy', split_axis=0, concat_axis=0, tiled=True)  11.7 us
  transfers between devices with their start and end apart: 5, of which 5 were waited for; matrix products, arithmetic and copies ran while one was open for 0% of the time, Pallas kernels for 24%

profile of v10, /device:TPU:0, one launch (start us, length us, event | category | flops | bytes accessed | tf_op | source)
XLA Modules:
  0.0 111.2 jit_solution(8775589368809752495)
XLA Ops:
  0.6 0.0 copy-start.6
  0.6 0.0 copy-start.5
  0.7 0.0 copy-start.4
  0.7 0.0 copy-start.1
  0.7 0.0 copy-start.3
  0.7 0.0 copy-start.8
  0.7 0.0 copy-start.7
  0.7 1.7 %shard_map.149 = f32[512,128]{1,0:T(8,128)} custom-call(f32[216,128]{1,0:T(8,128)} %bitcast.44, s32[4,128]{1,0:T(4,128)} %bitcast.39, s32[4,128]{1,0:T(4,128)} %bitcast.41, f32[4,128]{1,0:T(4,128)} %bitcast.45), custom_call_target="tpu_custom_call" | custom-call | tf_op jit(solution)/shard_map/pallas_call | solution.py:26
  2.4 7.3 %all-to-all-start = ((f32[32,2,8,128]{3,2,1,0:T(8,128)}), f32[32,2,8,128]{3,2,1,0:T(8,128)S(1)}, u32[]{:S(2)}, u32[]{:S(2)}) async-start(f32[32,2,8,128]{3,2,1,0:T(8,128)} %bitcast.4), calls=%async_computation | async-start | bytes 524288 | tf_op jit(solution)/shard_map/all_to_all | solution.py:977
  9.8 0.0 copy-start
  9.8 0.0 copy-start.2
  9.8 6.8 %shard_map.150 = (f32[54,32,512]{2,1,0:T(8,128)}, f32[2,4,512,128]{3,2,1,0:T(8,128)}, bf16[256,512]{1,0:T(8,128)(2,1)S(1)}, f32[8,256]{1,0:T(8,128)S(1)}) custom-call(f32[54,32,512]{2,1,0:T(8,128)} %p_hbm.1, s32[32,512]{1,0:T(8,128)} %partner_ref.1, f32[1,512]{1,0:T(1,128)} %bitcast.33, s32[1,256]{1,0:T(1,128)} %list_hbm.1), custom_call_target="tpu_custom_call" | custom-call | tf_op jit(solution)/shard_map/pallas_call | solution.py:26
  16.6 3.2 %all-to-all-done = f32[32,2,8,128]{3,2,1,0:T(8,128)S(1)} async-done(((f32[32,2,8,128]{3,2,1,0:T(8,128)}), f32[32,2,8,128]{3,2,1,0:T(8,128)S(1)}, u32[]{:S(2)}, u32[]{:S(2)}) %all-to-all-start) | async-done | bytes 262176 | tf_op jit(solution)/shard_map/all_to_all | solution.py:977
  19.8 2.8 %shard_map.151 = (f32[256,128]{1,0:T(8,128)S(1)}, f32[256,128]{1,0:T(8,128)}, s32[128,128]{1,0:T(8,128)S(1)}) custom-call(f32[512,128]{1,0:T(8,128)S(1)} %bitcast.27, f32[8,256]{1,0:T(8,128)S(1)} %get-tuple-element.29.token_ref.rsel_ref), custom_call_target="tpu_custom_call" | custom-call | tf_op jit(solution)/shard_map/pallas_call | solution.py:26
  22.5 2.9 %all-to-all-start.1 = ((f32[32,1,8,128]{3,2,1,0:T(8,128)}), f32[32,1,8,128]{3,2,1,0:T(8,128)S(1)}, u32[]{:S(2)}, u32[]{:S(2)}) async-start(f32[32,1,8,128]{3,2,1,0:T(8,128)} %bitcast.8), calls=%async_computation.1 | async-start | bytes 262144 | tf_op jit(solution)/shard_map/all_to_all | solution.py:977
  26.1 0.1 pad_add_fusion.me_ref
  26.1 0.0 copy-done.4
  26.1 0.0 copy-done.1
  26.1 0.0 copy-done.3
  26.1 0.1 shard_map.152
  26.3 0.0 copy-done.6
  26.3 0.0 copy-done.5
  26.3 0.0 copy-done.8
  26.3 0.0 copy-done.7
  26.3 3.4 %shard_map.153 = (f32[256,128]{1,0:T(8,128)S(1)}, bf16[1024,512]{1,0:T(8,128)(2,1)S(1)}, s32[64,128]{1,0:T(8,128)S(1)}, s32[64,128]{1,0:T(8,128)S(1)}, s32[256,128]{1,0:T(8,128)S(1)}) custom-call(s32[2]{0:T(128)S(1)} %pad_add_fusion.me_ref, s32[128,128]{1,0:T(8,128)S(1)} %get-tuple-element.33.token_ref.lab_ref, ...), custom_call_target="tpu_custom_call" | custom-call | tf_op jit(solution)/shard_map/pallas_call | solution.py:26
  29.7 3.8 %all-to-all-done.1 = f32[32,1,8,128]{3,2,1,0:T(8,128)S(1)} async-done(((f32[32,1,8,128]{3,2,1,0:T(8,128)}), f32[32,1,8,128]{3,2,1,0:T(8,128)S(1)}, u32[]{:S(2)}, u32[]{:S(2)}) %all-to-all-start.1) | async-done | bytes 131104 | tf_op jit(solution)/shard_map/all_to_all | solution.py:977
  33.6 6.4 %shard_map.154 = (f32[2,4,512,128]{3,2,1,0:T(8,128)}, f32[256,128]{1,0:T(8,128)}) custom-call(s32[1]{0:T(128)S(6)} %copy.18.count_ref, f32[256,128]{1,0:T(8,128)S(1)} %bitcast.30, f32[2,4,512,128]{3,2,1,0:T(8,128)} %get-tuple-element.31.a_hbm, bf16[256,512]{1,0:T(8,128)(2,1)S(1)} %get-tuple-element.32.ot_ref, ...), custom_call_target="tpu_custom_call" | custom-call | tf_op jit(solution)/shard_map/pallas_call | solution.py:26
  40.0 2.6 %all-to-all-start.2 = ((f32[32,1,8,128]{3,2,1,0:T(8,128)}), f32[32,1,8,128]{3,2,1,0:T(8,128)S(1)}, u32[]{:S(2)}, u32[]{:S(2)}) async-start(f32[32,1,8,128]{3,2,1,0:T(8,128)} %bitcast.14), calls=%async_computation.2 | async-start | bytes 262144 | tf_op jit(solution)/shard_map/all_to_all | solution.py:977
  42.6 0.0 copy-done
  42.6 0.0 copy-done.2
  42.6 5.3 %shard_map.155 = (f32[54,32,512]{2,1,0:T(8,128)}, f32[1,128]{1,0:T(1,128)S(1)}) custom-call(f32[54,32,512]{2,1,0:T(8,128)} %get-tuple-element.41.q_hbm, f32[256,128]{1,0:T(8,128)S(1)} %bitcast.31, f32[2,4,512,128]{3,2,1,0:T(8,128)} %get-tuple-element.42.r_hbm, bf16[256,512]{1,0:T(8,128)(2,1)S(1)} %get-tuple-element.32.ot_ref, f32[1,512]{1,0:T(1,128)S(1)} %bitcast.34, ...), custom_call_target="tpu_custom_call" | custom-call | tf_op jit(solution)/shard_map/pallas_call | solution.py:26
  47.8 2.9 %all-to-all-done.2 = f32[32,1,8,128]{3,2,1,0:T(8,128)S(1)} async-done(((f32[32,1,8,128]{3,2,1,0:T(8,128)}), f32[32,1,8,128]{3,2,1,0:T(8,128)S(1)}, u32[]{:S(2)}, u32[]{:S(2)}) %all-to-all-start.2) | async-done | bytes 131104 | tf_op jit(solution)/shard_map/all_to_all | solution.py:977
  50.7 3.7 %shard_map.156 = f32[512,128]{1,0:T(8,128)} custom-call(f32[256,128]{1,0:T(8,128)S(1)} %bitcast.32, f32[256,128]{1,0:T(8,128)S(1)} %get-tuple-element.39.g_ref, f32[512,128]{1,0:T(8,128)S(1)} %bitcast.28, s32[256,128]{1,0:T(8,128)S(1)} %get-tuple-element.40.inv_ref, s32[128,128]{1,0:T(8,128)S(1)} %get-tuple-element.33.token_ref.lab_ref, ...), custom_call_target="tpu_custom_call" | custom-call | tf_op jit(solution)/shard_map/pallas_call | solution.py:26
  54.4 3.1 %all-to-all-start.3 = ((f32[32,2,8,128]{3,2,1,0:T(8,128)}), f32[32,2,8,128]{3,2,1,0:T(8,128)S(1)}, u32[]{:S(2)}, u32[]{:S(2)}) async-start(f32[32,2,8,128]{3,2,1,0:T(8,128)} %bitcast.16), calls=%async_computation.3 | async-start | bytes 524288 | tf_op jit(solution)/shard_map/all_to_all | solution.py:977
  57.5 5.6 %shard_map.157 = (f32[2,4,512,128]{3,2,1,0:T(8,128)}, f32[1,2,512,128]{3,2,1,0:T(8,128)S(1)}, f32[1,128]{1,0:T(1,128)S(1)}) custom-call(f32[54,32,512]{2,1,0:T(8,128)} %get-tuple-element.44.q_hbm, f32[1,512]{1,0:T(1,128)S(1)} %bitcast.35, f32[8,256]{1,0:T(8,128)S(1)} %get-tuple-element.29.token_ref.rsel_ref, bf16[256,512]{1,0:T(8,128)(2,1)S(1)} %get-tuple-element.32.ot_ref, ...), custom_call_target="tpu_custom_call" | custom-call | tf_op jit(solution)/shard_map/pallas_call | solution.py:26
  63.2 4.2 %all-to-all-done.3 = f32[32,2,8,128]{3,2,1,0:T(8,128)S(1)} async-done(((f32[32,2,8,128]{3,2,1,0:T(8,128)}), f32[32,2,8,128]{3,2,1,0:T(8,128)S(1)}, u32[]{:S(2)}, u32[]{:S(2)}) %all-to-all-start.3) | async-done | bytes 262176 | tf_op jit(solution)/shard_map/all_to_all | solution.py:977
  67.4 3.2 %shard_map.158 = (f32[896,128]{1,0:T(8,128)}, f32[1,128]{1,0:T(1,128)S(1)}) custom-call(s32[1]{0:T(128)S(6)} %copy.18.count_ref, f32[512,128]{1,0:T(8,128)S(1)} %bitcast.23, f32[1,2,512,128]{3,2,1,0:T(8,128)S(1)} %get-tuple-element.47.base_ref, bf16[256,512]{1,0:T(8,128)(2,1)S(1)} %get-tuple-element.32.ot_ref, f32[1,512]{1,0:T(1,128)S(1)} %bitcast.36, ...), custom_call_target="tpu_custom_call" | custom-call | tf_op jit(solution)/shard_map/pallas_call | solution.py:26
  70.5 5.7 %shard_map.159 = (f32[2,4,512,128]{3,2,1,0:T(8,128)}, f32[8,56,128]{2,1,0:T(8,128)S(1)}) custom-call(s32[1]{0:T(128)S(6)} %copy.18.count_ref, f32[512,128]{1,0:T(8,128)S(1)} %bitcast.24, f32[2,4,512,128]{3,2,1,0:T(8,128)} %get-tuple-element.46.a_hbm, bf16[256,512]{1,0:T(8,128)(2,1)S(1)} %get-tuple-element.32.ot_ref, ...), custom_call_target="tpu_custom_call" | custom-call | tf_op jit(solution)/shard_map/pallas_call | solution.py:26
  76.3 11.7 %all_to_all.30.s_ref = f32[8,56,128]{2,1,0:T(8,128)S(1)} all-to-all(f32[8,56,128]{2,1,0:T(8,128)S(1)} %get-tuple-element.50), channel_id=1, replica_groups=mesh['gx'=4,'gy'=8] {'gy'}, dimensions={0} | all-to-all | bytes 458752 | tf_op jit(solution)/shard_map/all_to_all | solution.py:1104
  88.0 2.6 %all-to-all-start.5 = ((f32[32,7,4,128]{3,2,1,0:T(4,128)}), f32[32,7,4,128]{3,2,1,0:T(4,128)S(1)}, u32[]{:S(2)}, u32[]{:S(2)}) async-start(f32[32,7,4,128]{3,2,1,0:T(4,128)} %bitcast.19), calls=%async_computation.5 | async-start | bytes 917504 | tf_op jit(solution)/shard_map/all_to_all | solution.py:977
  90.6 4.8 %shard_map.161 = (f32[54,32,512]{2,1,0:T(8,128)}, f32[1,128]{1,0:T(1,128)}) custom-call(f32[54,32,512]{2,1,0:T(8,128)} %get-tuple-element.44.q_hbm, f32[512,128]{1,0:T(8,128)S(1)} %bitcast.25, f32[2,4,512,128]{3,2,1,0:T(8,128)} %get-tuple-element.52.r_hbm, bf16[256,512]{1,0:T(8,128)(2,1)S(1)} %get-tuple-element.32.ot_ref, f32[1,512]{1,0:T(1,128)S(1)} %bitcast.37), custom_call_target="tpu_custom_call" | custom-call | tf_op jit(solution)/shard_map/pallas_call | solution.py:26
  95.4 1.0 shard_map.160
  96.4 9.0 %all-to-all-done.5 = f32[32,7,4,128]{3,2,1,0:T(4,128)S(1)} async-done(((f32[32,7,4,128]{3,2,1,0:T(4,128)}), f32[32,7,4,128]{3,2,1,0:T(4,128)S(1)}, u32[]{:S(2)}, u32[]{:S(2)}) %all-to-all-start.5) | async-done | bytes 458784 | tf_op jit(solution)/shard_map/all_to_all | solution.py:977
  105.4 5.6 %shard_map.162 = f32[54,32,512]{2,1,0:T(8,128)} custom-call(f32[54,32,512]{2,1,0:T(8,128)} %get-tuple-element.53.p_hbm, f32[896,128]{1,0:T(8,128)S(1)} %bitcast.29, s32[64,128]{1,0:T(8,128)S(1)} %get-tuple-element.55.acol_ref), custom_call_target="tpu_custom_call" | custom-call | tf_op jit(solution)/shard_map/pallas_call | solution.py:26
Async XLA Ops:
  0.6 25.6 %copy-start.6 = (s32[2,2,128]{2,1,0:T(2,128)S(1)}, s32[2,2,128]{2,1,0:T(2,128)}, u32[]{:S(2)}) copy-start(s32[2,2,128]{2,1,0:T(2,128)} %param.18) | copy-start | bytes 6148
  0.6 25.6 %copy-start.5 = (s32[2,2,128]{2,1,0:T(2,128)S(1)}, s32[2,2,128]{2,1,0:T(2,128)}, u32[]{:S(2)}) copy-start(s32[2,2,128]{2,1,0:T(2,128)} %param.17) | copy-start | bytes 6148
  0.7 25.5 %copy-start.4 = (bf16[54,256]{1,0:T(8,128)(2,1)S(1)}, bf16[54,256]{1,0:T(8,128)(2,1)}, u32[]{:S(2)}) copy-start(bf16[54,256]{1,0:T(8,128)(2,1)} %w3_ref.1) | copy-start | bytes 82948
  0.7 25.5 %copy-start.1 = (bf16[256,256]{1,0:T(8,128)(2,1)S(1)}, bf16[256,256]{1,0:T(8,128)(2,1)}, u32[]{:S(2)}) copy-start(bf16[256,256]{1,0:T(8,128)(2,1)} %w2_ref.1) | copy-start | bytes 393220
  0.7 25.5 %copy-start.3 = (bf16[256,54]{0,1:T(8,128)(2,1)S(1)}, bf16[256,54]{0,1:T(8,128)(2,1)}, u32[]{:S(2)}) copy-start(bf16[256,54]{0,1:T(8,128)(2,1)} %param.21) | copy-start | bytes 82948
  0.7 25.6 %copy-start.8 = (s32[1,64]{1,0:T(1,128)S(1)}, s32[1,64]{1,0:T(1,128)}, u32[]{:S(2)}) copy-start(s32[1,64]{1,0:T(1,128)} %arrive_ref.1) | copy-start | bytes 772
  0.7 25.6 %copy-start.7 = (s32[1,64]{1,0:T(1,128)S(1)}, s32[1,64]{1,0:T(1,128)}, u32[]{:S(2)}) copy-start(s32[1,64]{1,0:T(1,128)} %leave_ref.1) | copy-start | bytes 772
  2.4 17.3 %all-to-all-start = ((f32[32,2,8,128]{3,2,1,0:T(8,128)}), f32[32,2,8,128]{3,2,1,0:T(8,128)S(1)}, u32[]{:S(2)}, u32[]{:S(2)}) async-start(f32[32,2,8,128]{3,2,1,0:T(8,128)} %bitcast.4), calls=%async_computation | async-start | bytes 524288 | tf_op jit(solution)/shard_map/all_to_all | solution.py:977
  9.8 32.8 %copy-start = (s32[32,512]{1,0:T(8,128)S(1)}, s32[32,512]{1,0:T(8,128)}, u32[]{:S(2)}) copy-start(s32[32,512]{1,0:T(8,128)} %partner_ref.1) | copy-start | bytes 196612
  9.8 32.8 %copy-start.2 = (f32[512]{0:T(512)S(1)}, f32[512]{0:T(512)}, u32[]{:S(2)}) copy-start(f32[512]{0:T(512)} %param.19) | copy-start | bytes 6148
  22.5 11.0 %all-to-all-start.1 = ((f32[32,1,8,128]{3,2,1,0:T(8,128)}), f32[32,1,8,128]{3,2,1,0:T(8,128)S(1)}, u32[]{:S(2)}, u32[]{:S(2)}) async-start(f32[32,1,8,128]{3,2,1,0:T(8,128)} %bitcast.8), calls=%async_computation.1 | async-start | bytes 262144 | tf_op jit(solution)/shard_map/all_to_all | solution.py:977
  40.0 10.8 %all-to-all-start.2 = ((f32[32,1,8,128]{3,2,1,0:T(8,128)}), f32[32,1,8,128]{3,2,1,0:T(8,128)S(1)}, u32[]{:S(2)}, u32[]{:S(2)}) async-start(f32[32,1,8,128]{3,2,1,0:T(8,128)} %bitcast.14), calls=%async_computation.2 | async-start | bytes 262144 | tf_op jit(solution)/shard_map/all_to_all | solution.py:977
  54.4 13.0 %all-to-all-start.3 = ((f32[32,2,8,128]{3,2,1,0:T(8,128)}), f32[32,2,8,128]{3,2,1,0:T(8,128)S(1)}, u32[]{:S(2)}, u32[]{:S(2)}) async-start(f32[32,2,8,128]{3,2,1,0:T(8,128)} %bitcast.16), calls=%async_computation.3 | async-start | bytes 524288 | tf_op jit(solution)/shard_map/all_to_all | solution.py:977
  88.0 17.4 %all-to-all-start.5 = ((f32[32,7,4,128]{3,2,1,0:T(4,128)}), f32[32,7,4,128]{3,2,1,0:T(4,128)S(1)}, u32[]{:S(2)}, u32[]{:S(2)}) async-start(f32[32,7,4,128]{3,2,1,0:T(4,128)} %bitcast.19), calls=%async_computation.5 | async-start | bytes 917504 | tf_op jit(solution)/shard_map/all_to_all | solution.py:977

commit v11 on v10

--- a/solution.py
+++ b/solution.py
@@ -504,7 +504,7 @@
         return carry
 
     whole = scalars // per
-    lax.fori_loop(0, whole, step, 0, unroll=2)
+    lax.fori_loop(0, whole, step, 0, unroll=True)
     zeros = jnp.zeros((devices, LANES), F32)
     for c in range(places // devices):
         for b in range(whole, span):
@@ -867,61 +867,128 @@
     lax.fori_loop(0, nx, group, 0)
 
 
-def send_filtered(dims, g_ref, g_stride, g_first, inv_ref, f_ref):
+def scatter(parts_refs, first_row, row_step, quads, own, lanes_y, target):
+    turns = quads * lanes_y
+    sub_of = lax.broadcasted_iota(I32, (turns, LANES), 0).astype(F32).astype(BF)
+    sub_lane = lax.broadcasted_iota(I32, (LANES, LANES), 0).astype(F32).astype(BF)
+    none = jnp.zeros((turns, LANES), BF)
+    unit = jnp.ones((LANES, LANES), BF)
+
+    def step(y, acc):
+        left, right = [], []
+        for j in range(quads):
+            row, lane = target(j, y)
+            hit = jnp.broadcast_to(row.astype(F32).astype(BF), (turns, LANES)) == sub_of
+            parts = []
+            for s in range(own):
+                at = pl.ds(first_row + y * row_step + s * quads + j, 1)
+                for ref in parts_refs:
+                    value = jnp.broadcast_to(ref[at, :].astype(BF), (turns, LANES))
+                    parts.append(jnp.where(hit, value, none))
+            left.append(jnp.concatenate(parts, axis=0))
+            lane = jnp.broadcast_to(lane.astype(F32).astype(BF), (LANES, LANES))
+            right.append(jnp.where(lane == sub_lane, unit, jnp.zeros_like(unit)))
+        return acc + dot(jnp.concatenate(left, axis=1), jnp.concatenate(right, axis=1), NT)
+
+    zero = jnp.zeros((2 * own * turns, LANES), F32)
+    acc = lax.fori_loop(0, lanes_y, step, zero, unroll=min(lanes_y, 8))
+    parts = [acc[i * turns : (i + 1) * turns] for i in range(2 * own)]
+    return [parts[2 * s] + parts[2 * s + 1] for s in range(own)]
+
+
+def both_ways(dims, src_ref, high_ref, low_ref, pull, push, store):
     nx, ny, own, bx, by = dims
     quads = bx * by
-    turns = quads * ny
-    f_stride = f_ref.shape[0] // (nx * ny)
-
-    def group(x, carry):
-        base = x * 2 * turns
-        rows = [inv_ref[pl.ds(base + k * ny, ny), :] for k in range(quads)]
-        lanes = [inv_ref[pl.ds(base + turns + k * ny, ny), :] for k in range(quads)]
-        first = x * ny * g_stride + g_first
-        out = route(g_ref, first, g_stride, 1, quads, own, quads, ny, rows, lanes)
+    width = own * quads
+    high = src_ref[...].astype(BF).astype(F32)
+    high_ref[...] = high
+    low_ref[...] = src_ref[...] - high
+
+    def routed(x):
+        rows, lanes = pull(x)
+        return route(src_ref, x * ny * width, width, 1, quads, own, quads, ny, rows, lanes)
+
+    def pair(i, carry):
+        x, z = 2 * i, 2 * i + 1
+        out = routed(x)
+        other = scatter((high_ref, low_ref), z * ny * width, width, quads, own, ny, push(z))
         for s in range(own):
             for k in range(quads):
-                at = pl.ds(x * ny * f_stride + s * quads + k, ny, stride=f_stride)
-                f_ref[at, :] = out[s][k]
+                store(pl.ds(x * ny * width + s * quads + k, ny, stride=width), out[s][k])
+                at = pl.ds(z * ny * width + s * quads + k, ny, stride=width)
+                store(at, other[s][k * ny : (k + 1) * ny])
         return carry
 
-    lax.fori_loop(0, nx, group, 0)
-
-
-def add_source(dims, s_ref, g_ref, lab_ref, out_ref):
-    nx, ny, own, bx, by = dims
-    quads = bx * by
-    boxes = nx * ny
-    width = own * quads
-    stride = s_ref.shape[0] // boxes
-
-    def group(x, carry):
-        labels = [lab_ref[pl.ds(j * boxes + x * ny, ny), :] for j in range(quads)]
-        rows = [v >> 7 for v in labels]
-        lanes = [v & (LANES - 1) for v in labels]
-        out = route(s_ref, x * ny * stride, stride, 1, quads, own, quads, ny, rows, lanes)
+    lax.fori_loop(0, nx // 2, pair, 0)
+    for x in range(nx // 2 * 2, nx):
+        out = routed(x)
         for s in range(own):
             for k in range(quads):
-                at = pl.ds(x * ny * width + s * quads + k, ny, stride=width)
-                out_ref[at, :] = g_ref[at, :] + out[s][k]
-        return carry
-
-    lax.fori_loop(0, nx, group, 0)
-
-
-def again_body(dims, s_ref, g_ref, arr_ref, inv_ref, lab_ref, token_ref, f_ref, mid_ref):
+                store(pl.ds(x * ny * width + s * quads + k, ny, stride=width), out[s][k])
+
+
+def again_body(
+    dims,
+    s_ref,
+    g_ref,
+    arr_ref,
+    inv_ref,
+    lab_ref,
+    token_ref,
+    f_ref,
+    mid_ref,
+    out_ref,
+    high_ref,
+    low_ref,
+):
     nx, ny, own, bx, by = dims
     quads = bx * by
     boxes = nx * ny
     width = own * quads
     stride = width + 2 * quads
-    add_source(dims, s_ref, g_ref, lab_ref, mid_ref)
+    turns = quads * ny
+
+    def by_label(x):
+        labels = [lab_ref[pl.ds(j * boxes + x * ny, ny), :] for j in range(quads)]
+        return [v >> 7 for v in labels], [v & (LANES - 1) for v in labels]
+
+    def by_inverse(x):
+        base = x * 2 * turns
+        rows = [inv_ref[pl.ds(base + k * ny, ny), :] for k in range(quads)]
+        return rows, [inv_ref[pl.ds(base + turns + k * ny, ny), :] for k in range(quads)]
+
+    def to_label(x):
+        def target(j, y):
+            line = lab_ref[pl.ds(j * boxes + x * ny + y, 1), :]
+            return line >> 7, line & (LANES - 1)
+
+        return target
+
+    def to_inverse(x):
+        def target(k, y):
+            at = x * 2 * turns + k * ny + y
+            return inv_ref[pl.ds(at, 1), :], inv_ref[pl.ds(at + turns, 1), :]
+
+        return target
+
+    def add(at, value):
+        mid_ref[at, :] = g_ref[at, :] + value
+
+    both_ways(dims, s_ref, high_ref, low_ref, by_label, to_inverse, add)
     speed = [load_rows(arr_ref, width + quads + j, stride, boxes) for j in range(quads)]
     for s in range(own):
         value = [load_rows(mid_ref, s * quads + j, width, boxes) for j in range(quads)]
         for j, v in enumerate(stencil(value, speed, bx, by, ny)):
-            f_ref[pl.ds(width + s * quads + j, boxes, stride=2 * width), :] = v
-    send_filtered(dims, f_ref, 2 * width, width, inv_ref, f_ref)
+            out_ref[pl.ds(s * quads + j, boxes, stride=width), :] = v
+
+
+    def keep(at, value):
+        mid_ref[at, :] = value
+
+    both_ways(dims, out_ref, high_ref, low_ref, by_inverse, to_label, keep)
+    for d in range(boxes):
+        f_ref[2 * d * width : (2 * d + 1) * width] = mid_ref[d * width : (d + 1) * width]
+        f_ref[(2 * d + 1) * width : (2 * d + 2) * width] = out_ref[d * width : (d + 1) * width]
 
 
 def per_device(
@@ -1070,7 +1137,7 @@
         functools.partial(again_body, dims),
         [((2 * flat, LANES), F32)],
         [home, grid, arrival, inv, lab, token],
-        scratch=[pltpu.VMEM((flat, LANES), F32)],
+        scratch=[pltpu.VMEM((flat, LANES), F32)] * 4,
     )
     a, base, token = call(
         functools.partial(list_body, block),

time: 112 us -> 110 us (0.982)
  Pallas kernels: 56 us -> 54.4 us
    pallas_call x14, Pallas kernels: 56 us -> 54.4 us  [call(): pl.pallas_call(body, out_shape=[pltpu.HBM(o[0], o[1]) if len(o) > 2 else...]
  transfers between devices with their start and end apart: 5 -> 5, of which waited for: 5 -> 5; matrix products, arithmetic and copies ran while one was open for 0% -> 0% of each run, Pallas kernels for 24% -> 25%
where the time goes in v11:
time: 110 us
  Pallas kernels  54.4 us (49%)
  waiting for transfers between devices  23.1 us (21%)
  starting transfers between devices  18.5 us (17%)
  blocking collectives  11.7 us (11%)
  between operations  1.68 us (2%)
    pallas_call x14, Pallas kernels, call(): pl.pallas_call(body, out_shape=[pltpu.HBM(o[0], o[1]) if len(o) > 2 else...  54.4 us
    all_to_all x5, waiting for transfers between devices, exchange(): lax.all_to_all(x, both, split_axis=0, concat_axis=0, tiled=True)  23.1 us
    all_to_all x5, starting transfers between devices, exchange(): lax.all_to_all(x, both, split_axis=0, concat_axis=0, tiled=True)  18.5 us
    all_to_all x1, blocking collectives, per_device(): lax.all_to_all(source, 'gy', split_axis=0, concat_axis=0, tiled=True)  11.7 us
  transfers between devices with their start and end apart: 5, of which 5 were waited for; matrix products, arithmetic and copies ran while one was open for 0% of the time, Pallas kernels for 25%

profile of v11, /device:TPU:0, one launch (start us, length us, event | category | flops | bytes accessed | tf_op | source)
XLA Modules:
  0.0 109.6 jit_solution(8081077752520729160)
XLA Ops:
  0.6 0.0 copy-start.6
  0.6 0.0 copy-start.5
  0.7 0.0 copy-start.4
  0.7 0.0 copy-start.1
  0.7 0.0 copy-start.3
  0.7 0.0 copy-start.8
  0.7 0.0 copy-start.7
  0.7 1.7 %shard_map.149 = f32[512,128]{1,0:T(8,128)} custom-call(f32[216,128]{1,0:T(8,128)} %bitcast.44, s32[4,128]{1,0:T(4,128)} %bitcast.39, s32[4,128]{1,0:T(4,128)} %bitcast.41, f32[4,128]{1,0:T(4,128)} %bitcast.45), custom_call_target="tpu_custom_call" | custom-call | tf_op jit(solution)/shard_map/pallas_call | solution.py:26
  2.4 7.3 %all-to-all-start = ((f32[32,2,8,128]{3,2,1,0:T(8,128)}), f32[32,2,8,128]{3,2,1,0:T(8,128)S(1)}, u32[]{:S(2)}, u32[]{:S(2)}) async-start(f32[32,2,8,128]{3,2,1,0:T(8,128)} %bitcast.4), calls=%async_computation | async-start | bytes 524288 | tf_op jit(solution)/shard_map/all_to_all | solution.py:1044
  9.8 0.0 copy-start
  9.8 0.0 copy-start.2
  9.8 6.8 %shard_map.150 = (f32[54,32,512]{2,1,0:T(8,128)}, f32[2,4,512,128]{3,2,1,0:T(8,128)}, bf16[256,512]{1,0:T(8,128)(2,1)S(1)}, f32[8,256]{1,0:T(8,128)S(1)}) custom-call(f32[54,32,512]{2,1,0:T(8,128)} %p_hbm.1, s32[32,512]{1,0:T(8,128)} %partner_ref.1, f32[1,512]{1,0:T(1,128)} %bitcast.33, s32[1,256]{1,0:T(1,128)} %list_hbm.1), custom_call_target="tpu_custom_call" | custom-call | tf_op jit(solution)/shard_map/pallas_call | solution.py:26
  16.6 3.2 %all-to-all-done = f32[32,2,8,128]{3,2,1,0:T(8,128)S(1)} async-done(((f32[32,2,8,128]{3,2,1,0:T(8,128)}), f32[32,2,8,128]{3,2,1,0:T(8,128)S(1)}, u32[]{:S(2)}, u32[]{:S(2)}) %all-to-all-start) | async-done | bytes 262176 | tf_op jit(solution)/shard_map/all_to_all | solution.py:1044
  19.8 2.8 %shard_map.151 = (f32[256,128]{1,0:T(8,128)S(1)}, f32[256,128]{1,0:T(8,128)}, s32[128,128]{1,0:T(8,128)S(1)}) custom-call(f32[512,128]{1,0:T(8,128)S(1)} %bitcast.27, f32[8,256]{1,0:T(8,128)S(1)} %get-tuple-element.29.token_ref.rsel_ref), custom_call_target="tpu_custom_call" | custom-call | tf_op jit(solution)/shard_map/pallas_call | solution.py:26
  22.5 2.9 %all-to-all-start.1 = ((f32[32,1,8,128]{3,2,1,0:T(8,128)}), f32[32,1,8,128]{3,2,1,0:T(8,128)S(1)}, u32[]{:S(2)}, u32[]{:S(2)}) async-start(f32[32,1,8,128]{3,2,1,0:T(8,128)} %bitcast.8), calls=%async_computation.1 | async-start | bytes 262144 | tf_op jit(solution)/shard_map/all_to_all | solution.py:1044
  26.1 0.1 pad_add_fusion.me_ref
  26.1 0.0 copy-done.4
  26.1 0.0 copy-done.1
  26.1 0.0 copy-done.3
  26.1 0.1 shard_map.152
  26.3 0.0 copy-done.6
  26.3 0.0 copy-done.5
  26.3 0.0 copy-done.8
  26.3 0.0 copy-done.7
  26.3 3.4 %shard_map.153 = (f32[256,128]{1,0:T(8,128)S(1)}, bf16[1024,512]{1,0:T(8,128)(2,1)S(1)}, s32[64,128]{1,0:T(8,128)S(1)}, s32[64,128]{1,0:T(8,128)S(1)}, s32[256,128]{1,0:T(8,128)S(1)}) custom-call(s32[2]{0:T(128)S(1)} %pad_add_fusion.me_ref, s32[128,128]{1,0:T(8,128)S(1)} %get-tuple-element.33.token_ref.lab_ref, ...), custom_call_target="tpu_custom_call" | custom-call | tf_op jit(solution)/shard_map/pallas_call | solution.py:26
  29.7 3.8 %all-to-all-done.1 = f32[32,1,8,128]{3,2,1,0:T(8,128)S(1)} async-done(((f32[32,1,8,128]{3,2,1,0:T(8,128)}), f32[32,1,8,128]{3,2,1,0:T(8,128)S(1)}, u32[]{:S(2)}, u32[]{:S(2)}) %all-to-all-start.1) | async-done | bytes 131104 | tf_op jit(solution)/shard_map/all_to_all | solution.py:1044
  33.6 6.4 %shard_map.154 = (f32[2,4,512,128]{3,2,1,0:T(8,128)}, f32[256,128]{1,0:T(8,128)}) custom-call(s32[1]{0:T(128)S(6)} %copy.18.count_ref, f32[256,128]{1,0:T(8,128)S(1)} %bitcast.30, f32[2,4,512,128]{3,2,1,0:T(8,128)} %get-tuple-element.31.a_hbm, bf16[256,512]{1,0:T(8,128)(2,1)S(1)} %get-tuple-element.32.ot_ref, ...), custom_call_target="tpu_custom_call" | custom-call | tf_op jit(solution)/shard_map/pallas_call | solution.py:26
  40.0 2.6 %all-to-all-start.2 = ((f32[32,1,8,128]{3,2,1,0:T(8,128)}), f32[32,1,8,128]{3,2,1,0:T(8,128)S(1)}, u32[]{:S(2)}, u32[]{:S(2)}) async-start(f32[32,1,8,128]{3,2,1,0:T(8,128)} %bitcast.14), calls=%async_computation.2 | async-start | bytes 262144 | tf_op jit(solution)/shard_map/all_to_all | solution.py:1044
  42.6 0.0 copy-done
  42.6 0.0 copy-done.2
  42.6 5.3 %shard_map.155 = (f32[54,32,512]{2,1,0:T(8,128)}, f32[1,128]{1,0:T(1,128)S(1)}) custom-call(f32[54,32,512]{2,1,0:T(8,128)} %get-tuple-element.41.q_hbm, f32[256,128]{1,0:T(8,128)S(1)} %bitcast.31, f32[2,4,512,128]{3,2,1,0:T(8,128)} %get-tuple-element.42.r_hbm, bf16[256,512]{1,0:T(8,128)(2,1)S(1)} %get-tuple-element.32.ot_ref, f32[1,512]{1,0:T(1,128)S(1)} %bitcast.34, ...), custom_call_target="tpu_custom_call" | custom-call | tf_op jit(solution)/shard_map/pallas_call | solution.py:26
  47.8 2.9 %all-to-all-done.2 = f32[32,1,8,128]{3,2,1,0:T(8,128)S(1)} async-done(((f32[32,1,8,128]{3,2,1,0:T(8,128)}), f32[32,1,8,128]{3,2,1,0:T(8,128)S(1)}, u32[]{:S(2)}, u32[]{:S(2)}) %all-to-all-start.2) | async-done | bytes 131104 | tf_op jit(solution)/shard_map/all_to_all | solution.py:1044
  50.7 2.7 %shard_map.156 = f32[512,128]{1,0:T(8,128)} custom-call(f32[256,128]{1,0:T(8,128)S(1)} %bitcast.32, f32[256,128]{1,0:T(8,128)S(1)} %get-tuple-element.39.g_ref, f32[512,128]{1,0:T(8,128)S(1)} %bitcast.28, s32[256,128]{1,0:T(8,128)S(1)} %get-tuple-element.40.inv_ref, s32[128,128]{1,0:T(8,128)S(1)} %get-tuple-element.33.token_ref.lab_ref, ...), custom_call_target="tpu_custom_call" | custom-call | tf_op jit(solution)/shard_map/pallas_call | solution.py:26
  53.4 3.2 %all-to-all-start.3 = ((f32[32,2,8,128]{3,2,1,0:T(8,128)}), f32[32,2,8,128]{3,2,1,0:T(8,128)S(1)}, u32[]{:S(2)}, u32[]{:S(2)}) async-start(f32[32,2,8,128]{3,2,1,0:T(8,128)} %bitcast.16), calls=%async_computation.3 | async-start | bytes 524288 | tf_op jit(solution)/shard_map/all_to_all | solution.py:1044
  56.6 5.6 %shard_map.157 = (f32[2,4,512,128]{3,2,1,0:T(8,128)}, f32[1,2,512,128]{3,2,1,0:T(8,128)S(1)}, f32[1,128]{1,0:T(1,128)S(1)}) custom-call(f32[54,32,512]{2,1,0:T(8,128)} %get-tuple-element.44.q_hbm, f32[1,512]{1,0:T(1,128)S(1)} %bitcast.35, f32[8,256]{1,0:T(8,128)S(1)} %get-tuple-element.29.token_ref.rsel_ref, bf16[256,512]{1,0:T(8,128)(2,1)S(1)} %get-tuple-element.32.ot_ref, ...), custom_call_target="tpu_custom_call" | custom-call | tf_op jit(solution)/shard_map/pallas_call | solution.py:26
  62.2 4.2 %all-to-all-done.3 = f32[32,2,8,128]{3,2,1,0:T(8,128)S(1)} async-done(((f32[32,2,8,128]{3,2,1,0:T(8,128)}), f32[32,2,8,128]{3,2,1,0:T(8,128)S(1)}, u32[]{:S(2)}, u32[]{:S(2)}) %all-to-all-start.3) | async-done | bytes 262176 | tf_op jit(solution)/shard_map/all_to_all | solution.py:1044
  66.4 2.5 %shard_map.158 = (f32[896,128]{1,0:T(8,128)}, f32[1,128]{1,0:T(1,128)S(1)}) custom-call(s32[1]{0:T(128)S(6)} %copy.18.count_ref, f32[512,128]{1,0:T(8,128)S(1)} %bitcast.23, f32[1,2,512,128]{3,2,1,0:T(8,128)S(1)} %get-tuple-element.47.base_ref, bf16[256,512]{1,0:T(8,128)(2,1)S(1)} %get-tuple-element.32.ot_ref, f32[1,512]{1,0:T(1,128)S(1)} %bitcast.36, ...), custom_call_target="tpu_custom_call" | custom-call | tf_op jit(solution)/shard_map/pallas_call | solution.py:26
  68.9 5.8 %shard_map.159 = (f32[2,4,512,128]{3,2,1,0:T(8,128)}, f32[8,56,128]{2,1,0:T(8,128)S(1)}) custom-call(s32[1]{0:T(128)S(6)} %copy.18.count_ref, f32[512,128]{1,0:T(8,128)S(1)} %bitcast.24, f32[2,4,512,128]{3,2,1,0:T(8,128)} %get-tuple-element.46.a_hbm, bf16[256,512]{1,0:T(8,128)(2,1)S(1)} %get-tuple-element.32.ot_ref, ...), custom_call_target="tpu_custom_call" | custom-call | tf_op jit(solution)/shard_map/pallas_call | solution.py:26
  74.7 11.7 %all_to_all.30.s_ref = f32[8,56,128]{2,1,0:T(8,128)S(1)} all-to-all(f32[8,56,128]{2,1,0:T(8,128)S(1)} %get-tuple-element.50), channel_id=1, replica_groups=mesh['gx'=4,'gy'=8] {'gy'}, dimensions={0} | all-to-all | bytes 458752 | tf_op jit(solution)/shard_map/all_to_all | solution.py:1171
  86.4 2.6 %all-to-all-start.5 = ((f32[32,7,4,128]{3,2,1,0:T(4,128)}), f32[32,7,4,128]{3,2,1,0:T(4,128)S(1)}, u32[]{:S(2)}, u32[]{:S(2)}) async-start(f32[32,7,4,128]{3,2,1,0:T(4,128)} %bitcast.19), calls=%async_computation.5 | async-start | bytes 917504 | tf_op jit(solution)/shard_map/all_to_all | solution.py:1044
  89.0 4.8 %shard_map.161 = (f32[54,32,512]{2,1,0:T(8,128)}, f32[1,128]{1,0:T(1,128)}) custom-call(f32[54,32,512]{2,1,0:T(8,128)} %get-tuple-element.44.q_hbm, f32[512,128]{1,0:T(8,128)S(1)} %bitcast.25, f32[2,4,512,128]{3,2,1,0:T(8,128)} %get-tuple-element.52.r_hbm, bf16[256,512]{1,0:T(8,128)(2,1)S(1)} %get-tuple-element.32.ot_ref, f32[1,512]{1,0:T(1,128)S(1)} %bitcast.37), custom_call_target="tpu_custom_call" | custom-call | tf_op jit(solution)/shard_map/pallas_call | solution.py:26
  93.8 1.0 shard_map.160
  94.8 9.0 %all-to-all-done.5 = f32[32,7,4,128]{3,2,1,0:T(4,128)S(1)} async-done(((f32[32,7,4,128]{3,2,1,0:T(4,128)}), f32[32,7,4,128]{3,2,1,0:T(4,128)S(1)}, u32[]{:S(2)}, u32[]{:S(2)}) %all-to-all-start.5) | async-done | bytes 458784 | tf_op jit(solution)/shard_map/all_to_all | solution.py:1044
  103.8 5.6 %shard_map.162 = f32[54,32,512]{2,1,0:T(8,128)} custom-call(f32[54,32,512]{2,1,0:T(8,128)} %get-tuple-element.53.p_hbm, f32[896,128]{1,0:T(8,128)S(1)} %bitcast.29, s32[64,128]{1,0:T(8,128)S(1)} %get-tuple-element.55.acol_ref), custom_call_target="tpu_custom_call" | custom-call | tf_op jit(solution)/shard_map/pallas_call | solution.py:26
Async XLA Ops:
  0.6 25.6 %copy-start.6 = (s32[2,2,128]{2,1,0:T(2,128)S(1)}, s32[2,2,128]{2,1,0:T(2,128)}, u32[]{:S(2)}) copy-start(s32[2,2,128]{2,1,0:T(2,128)} %param.18) | copy-start | bytes 6148
  0.6 25.6 %copy-start.5 = (s32[2,2,128]{2,1,0:T(2,128)S(1)}, s32[2,2,128]{2,1,0:T(2,128)}, u32[]{:S(2)}) copy-start(s32[2,2,128]{2,1,0:T(2,128)} %param.17) | copy-start | bytes 6148
  0.7 25.5 %copy-start.4 = (bf16[54,256]{1,0:T(8,128)(2,1)S(1)}, bf16[54,256]{1,0:T(8,128)(2,1)}, u32[]{:S(2)}) copy-start(bf16[54,256]{1,0:T(8,128)(2,1)} %w3_ref.1) | copy-start | bytes 82948
  0.7 25.5 %copy-start.1 = (bf16[256,256]{1,0:T(8,128)(2,1)S(1)}, bf16[256,256]{1,0:T(8,128)(2,1)}, u32[]{:S(2)}) copy-start(bf16[256,256]{1,0:T(8,128)(2,1)} %w2_ref.1) | copy-start | bytes 393220
  0.7 25.5 %copy-start.3 = (bf16[256,54]{0,1:T(8,128)(2,1)S(1)}, bf16[256,54]{0,1:T(8,128)(2,1)}, u32[]{:S(2)}) copy-start(bf16[256,54]{0,1:T(8,128)(2,1)} %param.21) | copy-start | bytes 82948
  0.7 25.6 %copy-start.8 = (s32[1,64]{1,0:T(1,128)S(1)}, s32[1,64]{1,0:T(1,128)}, u32[]{:S(2)}) copy-start(s32[1,64]{1,0:T(1,128)} %arrive_ref.1) | copy-start | bytes 772
  0.7 25.6 %copy-start.7 = (s32[1,64]{1,0:T(1,128)S(1)}, s32[1,64]{1,0:T(1,128)}, u32[]{:S(2)}) copy-start(s32[1,64]{1,0:T(1,128)} %leave_ref.1) | copy-start | bytes 772
  2.4 17.3 %all-to-all-start = ((f32[32,2,8,128]{3,2,1,0:T(8,128)}), f32[32,2,8,128]{3,2,1,0:T(8,128)S(1)}, u32[]{:S(2)}, u32[]{:S(2)}) async-start(f32[32,2,8,128]{3,2,1,0:T(8,128)} %bitcast.4), calls=%async_computation | async-start | bytes 524288 | tf_op jit(solution)/shard_map/all_to_all | solution.py:1044
  9.8 32.8 %copy-start = (s32[32,512]{1,0:T(8,128)S(1)}, s32[32,512]{1,0:T(8,128)}, u32[]{:S(2)}) copy-start(s32[32,512]{1,0:T(8,128)} %partner_ref.1) | copy-start | bytes 196612
  9.8 32.8 %copy-start.2 = (f32[512]{0:T(512)S(1)}, f32[512]{0:T(512)}, u32[]{:S(2)}) copy-start(f32[512]{0:T(512)} %param.19) | copy-start | bytes 6148
  22.5 11.0 %all-to-all-start.1 = ((f32[32,1,8,128]{3,2,1,0:T(8,128)}), f32[32,1,8,128]{3,2,1,0:T(8,128)S(1)}, u32[]{:S(2)}, u32[]{:S(2)}) async-start(f32[32,1,8,128]{3,2,1,0:T(8,128)} %bitcast.8), calls=%async_computation.1 | async-start | bytes 262144 | tf_op jit(solution)/shard_map/all_to_all | solution.py:1044
  40.0 10.8 %all-to-all-start.2 = ((f32[32,1,8,128]{3,2,1,0:T(8,128)}), f32[32,1,8,128]{3,2,1,0:T(8,128)S(1)}, u32[]{:S(2)}, u32[]{:S(2)}) async-start(f32[32,1,8,128]{3,2,1,0:T(8,128)} %bitcast.14), calls=%async_computation.2 | async-start | bytes 262144 | tf_op jit(solution)/shard_map/all_to_all | solution.py:1044
  53.4 13.0 %all-to-all-start.3 = ((f32[32,2,8,128]{3,2,1,0:T(8,128)}), f32[32,2,8,128]{3,2,1,0:T(8,128)S(1)}, u32[]{:S(2)}, u32[]{:S(2)}) async-start(f32[32,2,8,128]{3,2,1,0:T(8,128)} %bitcast.16), calls=%async_computation.3 | async-start | bytes 524288 | tf_op jit(solution)/shard_map/all_to_all | solution.py:1044
  86.4 17.4 %all-to-all-start.5 = ((f32[32,7,4,128]{3,2,1,0:T(4,128)}), f32[32,7,4,128]{3,2,1,0:T(4,128)S(1)}, u32[]{:S(2)}, u32[]{:S(2)}) async-start(f32[32,7,4,128]{3,2,1,0:T(4,128)} %bitcast.19), calls=%async_computation.5 | async-start | bytes 917504 | tf_op jit(solution)/shard_map/all_to_all | solution.py:1044
